TPU v7x, 256 devices: a whole 4x4x8 slice. The times are simulated.
256 devices in a mesh: req: 32 (over z_hi, x, y), tp: 8 (over z_lo, core).
Axes of the slice: x: 4, y: 4, z: 8 (z_hi: 2, z_lo: 4; z = z_hi * 4 + z_lo), core: 2. Of those that a mesh axis runs over, the one named last changes fastest.
Arguments:
- hidden: bfloat16 [4096, 2048], P('req', 'tp'), may hold values from -6 to 6
- attn_gain: bfloat16 [2048], replicated, may hold values from 0.099609375 to 1.8984375
- w_qkv: bfloat16 [3, 2048, 2048], P(None, None, 'tp'), may hold values from -0.125 to 0.125
- w_out: bfloat16 [2048, 2048], P('tp'), may hold values from -0.125 to 0.125
- kv_cache: bfloat16 [2, 32, 1024, 2048], P(None, 'req', None, 'tp'), as said below
- holder_slot: int32 [32], replicated, may hold values from 0 to 31, as said below
- lengths: int32 [32], P('req'), may hold values from 1 to 1024, as said below
- ffn_gain: bfloat16 [2048], replicated, may hold values from 0.099609375 to 1.8984375
- w_router: bfloat16 [2048, 32], replicated
- expert_ids: int32 [4096, 6], P('req'), may hold values from 0 to 31, all different within a row; in each aligned block of 128 rows (0 to 127, 128 to 255, ...) at most 32 rows name the same one
- w_exp_in: bfloat16 [32, 2, 2048, 1408], P('req', None, None, 'tp'), may hold values from -0.4375 to 0.4375
- w_exp_down: bfloat16 [32, 1408, 2048], P('req', 'tp'), may hold values from -0.5 to 0.5
- w_sh_in: bfloat16 [2, 2048, 1408], P(None, None, 'tp'), may hold values from -0.125 to 0.125
- w_sh_down: bfloat16 [1408, 2048], P('tp'), may hold values from -0.15625 to 0.15625
- final_gain: bfloat16 [2048], replicated, may hold values from 0.5 to 1.5
- w_head: bfloat16 [51200, 2048], P(('req', 'tp')), may hold values from -0.5 to 0.5
Outputs:
- out_hidden: bfloat16 [4096, 2048], P('req', 'tp')
- new_cache: bfloat16 [2, 32, 128, 2048], P(None, 'req', None, 'tp')
- last_rms: float32 [32], replicated
- top_logit: float32 [32], replicated
Inputs may be any that keep to these rules, and one draw needn't show every extreme that they name: `kv_cache`: the cache in slot s lies on index s // 1 of req; request r is owned by index r. `holder_slot`: A permutation of the cache slots; about half of the requests keep their own slot. `lengths`: some request has exactly 1024 cached positions. `expert_ids`: within the rows of one device (128 aligned tokens) each expert is named by at most 32 rows, a bound that is reached.
All inputs are finite; a program needn't handle non-finite values.
Results may differ from a plain program's by a relative error of at most 0.025.
Values may be sent and summed in bfloat16 or wider, within the bound.
No kernel may reach another device: no remote copies, remote signals or barrier semaphores. Data moves between devices by JAX's collectives and lax.ppermute only.
A program may use at most 64 MiB of HBM per device.

v0:
```python
import jax
import jax.numpy as jnp
from jax import lax
from jax.sharding import PartitionSpec as P

HD = 128
TOPK = 6
CAP = 32


epsilon = 1e-06


def rms_scale(values, gain):
    return (
        values
        * lax.rsqrt(jnp.mean(values * values, axis=-1, keepdims=True) + epsilon)
        * gain.astype(jnp.float32)
    )


def rotate_half(values, positions):
    half_len = values.shape[-1] // 2
    freqs = 10000.0 ** (-2.0 * jnp.arange(half_len, dtype=jnp.float32) / values.shape[-1])
    angles = positions[..., None] * freqs
    cosine = jnp.cos(angles)[..., None, :]
    sine = jnp.sin(angles)[..., None, :]
    lead_half = values[..., :half_len]
    tail_half = values[..., half_len:]
    return jnp.concatenate(
        [lead_half * cosine - tail_half * sine, tail_half * cosine + lead_half * sine], axis=-1
    )


def attend(queries, keys_new, values_new, old_keys, old_values, lengths):
    context_len = old_keys.shape[1]
    new_len = queries.shape[1]
    all_keys = jnp.concatenate([old_keys, keys_new], axis=1)
    all_values = jnp.concatenate([old_values, values_new], axis=1)
    scores = jnp.einsum(
        "rthd,rshd->rhts", queries, all_keys, preferred_element_type=jnp.float32
    ) * queries.shape[-1] ** (-0.5)
    column = jnp.arange(context_len + new_len)[None, None, :]
    row_pos = jnp.arange(new_len)[None, :, None]
    visible = jnp.where(
        column < context_len, column < lengths[:, None, None], column - context_len <= row_pos
    )
    visible = visible[:, None]
    masked = jnp.where(visible, scores, -1e30)
    peak = jnp.max(masked, axis=-1, keepdims=True)
    raised = jnp.where(visible, jnp.exp(masked - peak), 0.0)
    weights = (raised / jnp.sum(raised, axis=-1, keepdims=True)).astype(jnp.bfloat16)
    mixed = jnp.einsum("rhts,rshd->rthd", weights, all_values, preferred_element_type=jnp.float32)
    return mixed.astype(jnp.bfloat16)


def expert_block(arrived, w_exp_in, w_exp_down):
    both = jnp.einsum("nekd,ecdf->cnekf", arrived, w_exp_in, preferred_element_type=jnp.float32)
    inner = (jax.nn.silu(both[0]) * both[1]).astype(jnp.bfloat16)
    return jnp.einsum(
        "nekf,efd->nekd", inner, w_exp_down, preferred_element_type=jnp.float32
    ).astype(jnp.bfloat16)


def local(
    hidden,
    attn_gain,
    w_qkv,
    w_out,
    kv_cache,
    holder_slot,
    lengths,
    ffn_gain,
    w_router,
    expert_ids,
    w_exp_in,
    w_exp_down,
    w_sh_in,
    w_sh_down,
    final_gain,
    w_head,
):
    req_size = lax.axis_size("req")
    tp_pos = lax.axis_index("tp")
    full_in = lax.all_gather(hidden, "tp", axis=1, tiled=True)
    tok_rows = full_in.shape[0]
    slot_count = kv_cache.shape[1]
    new_len = tok_rows // slot_count
    local_feat = hidden.shape[1]
    local_heads = w_qkv.shape[2] // HD
    normed = rms_scale(full_in.astype(jnp.float32), attn_gain).astype(jnp.bfloat16)
    projected = jnp.einsum("td,cde->cte", normed, w_qkv, preferred_element_type=jnp.float32)
    positions = (lengths[:, None] + jnp.arange(new_len, dtype=jnp.int32)[None, :]).astype(
        jnp.float32
    )
    shaped = projected.reshape(3, slot_count, new_len, local_heads, HD)
    queries = rotate_half(shaped[0], positions).astype(jnp.bfloat16)
    keys_new = rotate_half(shaped[1], positions).astype(jnp.bfloat16)
    values_new = shaped[2].astype(jnp.bfloat16)
    new_cache = jnp.stack([keys_new, values_new]).reshape(2, slot_count, new_len, local_heads * HD)
    spread = lax.all_to_all(kv_cache, "req", split_axis=2, concat_axis=1, tiled=True)
    ordered = jnp.take(spread, holder_slot, axis=1)
    fetched = lax.all_to_all(ordered, "req", split_axis=1, concat_axis=2, tiled=True)
    context_len = fetched.shape[2]
    old_pair = fetched.reshape(2, slot_count, context_len, local_heads, HD)
    attn_out = attend(queries, keys_new, values_new, old_pair[0], old_pair[1], lengths)
    attn_out = attn_out.reshape(tok_rows, local_heads * HD)
    attn_total = lax.psum(
        jnp.dot(attn_out, w_out, preferred_element_type=jnp.float32).astype(jnp.bfloat16), "tp"
    ).astype(jnp.float32)
    resid = (full_in.astype(jnp.float32) + attn_total).astype(jnp.bfloat16)
    ffn_in = rms_scale(resid.astype(jnp.float32), ffn_gain).astype(jnp.bfloat16)
    probs = jax.nn.softmax(jnp.dot(ffn_in, w_router, preferred_element_type=jnp.float32), axis=-1)
    experts_all = w_router.shape[1]
    expert_local = w_exp_in.shape[0]
    expert_iota = jnp.arange(experts_all, dtype=jnp.int32)
    gates = jnp.sum(
        probs[:, None, :]
        * (expert_ids[:, :, None] == expert_iota[None, None, :]).astype(jnp.float32),
        axis=-1,
    )
    picks = expert_ids.reshape(-1)
    pick_count = picks.shape[0]
    onehot = (picks[:, None] == expert_iota[None, :]).astype(jnp.int32)
    earlier = jnp.cumsum(onehot, axis=0) - onehot
    rank = jnp.sum(earlier * onehot, axis=1)
    slot_of_pick = picks * CAP + rank
    source = (
        jnp.full((experts_all * CAP,), tok_rows, jnp.int32)
        .at[slot_of_pick]
        .set(jnp.arange(pick_count, dtype=jnp.int32) // TOPK)
    )
    padded = jnp.concatenate([ffn_in, jnp.zeros((1, ffn_in.shape[1]), jnp.bfloat16)], axis=0)
    outgoing = jnp.take(padded, source, axis=0).reshape(
        req_size, expert_local, CAP, padded.shape[1]
    )
    served = expert_block(
        lax.all_to_all(outgoing, "req", split_axis=0, concat_axis=0, tiled=True),
        w_exp_in,
        w_exp_down,
    )
    shared_both = jnp.einsum("td,cdf->ctf", ffn_in, w_sh_in, preferred_element_type=jnp.float32)
    shared_inner = (jax.nn.silu(shared_both[0]) * shared_both[1]).astype(jnp.bfloat16)
    shared_terms = jnp.dot(shared_inner, w_sh_down, preferred_element_type=jnp.float32)
    pick_slots = slot_of_pick.reshape(tok_rows, TOPK)
    returned = lax.all_to_all(served, "req", split_axis=0, concat_axis=0, tiled=True)
    returned = returned.reshape(experts_all * CAP, returned.shape[3])
    to_reduce = shared_terms
    for pick_pos in range(TOPK):
        chosen_rows = jnp.take(returned, pick_slots[:, pick_pos], axis=0).astype(jnp.float32)
        to_reduce = to_reduce + chosen_rows * gates[:, pick_pos : pick_pos + 1]
    layer_share = lax.psum_scatter(
        to_reduce.astype(jnp.bfloat16), "tp", scatter_dimension=1, tiled=True
    ).astype(jnp.float32)
    resid_share = lax.dynamic_slice_in_dim(resid, tp_pos * local_feat, local_feat, 1)
    out_hidden = (resid_share.astype(jnp.float32) + layer_share).astype(jnp.bfloat16)
    last_share = out_hidden.reshape(slot_count, new_len, local_feat)[:, new_len - 1]
    last_rows = lax.all_gather(last_share, "tp", axis=1, tiled=True)
    last_every = lax.all_gather(last_rows, "req", axis=0, tiled=True)
    last_tok = last_every.astype(jnp.float32)
    last_rms = jnp.sqrt(jnp.mean(last_tok * last_tok, axis=-1) + epsilon)
    head_in = (last_tok / last_rms[:, None] * final_gain.astype(jnp.float32)).astype(jnp.bfloat16)
    logits = lax.dot_general(
        head_in, w_head, (((1,), (1,)), ((), ())), preferred_element_type=jnp.float32
    )
    top_logit = lax.pmax(jnp.max(logits, axis=1), ("req", "tp"))
    return (out_hidden, new_cache, last_rms, top_logit)


def solution(mesh):
    return jax.shard_map(
        local,
        mesh=mesh,
        in_specs=(
            P("req", "tp"),
            P(),
            P(None, None, "tp"),
            P("tp", None),
            P(None, "req", None, "tp"),
            P(),
            P("req"),
            P(),
            P(),
            P("req", None),
            P("req", None, None, "tp"),
            P("req", "tp", None),
            P(None, None, "tp"),
            P("tp", None),
            P(),
            P(("req", "tp"), None),
        ),
        out_specs=(P("req", "tp"), P(None, "req", None, "tp"), P(), P()),
        check_vma=False,
    )
```

profile of v0, /device:TPU:1, one launch (start us, length us, event | category | flops | bytes accessed | tf_op | source)
XLA Modules:
  0.0 697.8 jit_solution(8037834648569727721)
XLA Ops:
  7.2 3.5 copy.92
  10.7 14.8 %all-to-all-start = ((bf16[2,1,1024,256]{3,0,1,2:T(2,128)(2,1)}), bf16[2,1,1024,256]{3,0,1,2:T(2,128)(2,1)}, u32[]{:S(2)}, u32[]{:S(2)}) async-start(bf16[2,1,1024,256]{3,0,1,2:T(2,128)(2,1)} %copy.92), calls=%async_computation | async-start | bytes 2097152 | tf_op jit(solution)/shard_map/all_to_all | solution.py:101
  28.2 32.7 %all_gather.9 = bf16[128,2048]{1,0:T(8,128)(2,1)S(1)} all-gather(bf16[128,256]{1,0:T(8,128)(2,1)S(1)} %copy-done.8), channel_id=1, replica_groups=mesh['req'=32,'tp'=8] {'tp'}, dimensions={1}, use_global_device_ids=true | all-gather | bytes 589824 | tf_op jit(solution)/shard_map/all_gather | solution.py:85
  70.7 11.3 %all-to-all-start.1 = ((bf16[2,32,32,256]{3,2,0,1:T(8,128)(2,1)}), bf16[2,32,32,256]{3,2,0,1:T(8,128)(2,1)}, u32[]{:S(2)}, u32[]{:S(2)}) async-start(bf16[2,32,32,256]{3,2,0,1:T(8,128)(2,1)} %select_bitcast_fusion), calls=%async_computation.1 | async-start | bytes 2097152 | tf_op jit(solution)/shard_map/all_to_all | solution.py:103
  89.8 15.1 %all-to-all-done.1 = bf16[2,32,32,256]{3,2,0,1:T(8,128)(2,1)} async-done(((bf16[2,32,32,256]{3,2,0,1:T(8,128)(2,1)}), bf16[2,32,32,256]{3,2,0,1:T(8,128)(2,1)}, u32[]{:S(2)}, u32[]{:S(2)}) %all-to-all-start.1) | async-done | bytes 1048608 | tf_op jit(solution)/shard_map/all_to_all | solution.py:103
  115.1 3.3 fusion.79
  121.6 3.5 scatter_custom_fusion
  125.2 67.9 %all-reduce.3.cloned.1.call-done = bf16[128,2048]{1,0:T(8,128)(2,1)} async-done(((bf16[128,2048]{1,0:T(8,128)(2,1)}), bf16[128,2048]{1,0:T(8,128)(2,1)}) %all-reduce.3.cloned.1.call-update) | async-done | bytes 524304 | tf_op jit(solution)/shard_map/psum | solution.py:108
  197.4 10.0 %gather_fusion.1 = bf16[1024,2048]{1,0:T(8,128)(2,1)} fusion(bf16[129,2048]{1,0:T(8,128)(2,1)} %concatenate.47, s32[1024]{0:T(1024)S(1)} %fusion.61), kind=kCustom, calls=%fused_computation.7 | custom fusion | bytes 8392704 | tf_op jit(solution)/shard_map/jit(_take)/gather | solution.py:134
  210.0 106.0 %all_to_all.31 = bf16[32,1,32,2048]{3,2,1,0:T(8,128)(2,1)S(1)} all-to-all(bf16[32,1,32,2048]{3,2,1,0:T(8,128)(2,1)S(1)} %broadcast_select_fusion), channel_id=1, replica_groups=mesh['req'=32,'tp'=8] {'req'}, dimensions={0} | all-to-all | bytes 8388608 | tf_op jit(solution)/shard_map/all_to_all | solution.py:138
  318.4 3.3 convert_bitcast_fusion
  321.7 6.9 all-to-all-start.3
  332.5 81.5 %all-to-all-done.3 = bf16[32,1,32,2048]{3,2,1,0:T(8,128)(2,1)} async-done(((bf16[32,1,32,2048]{3,2,1,0:T(8,128)(2,1)}), bf16[32,1,32,2048]{3,2,1,0:T(8,128)(2,1)}, u32[]{:S(2)}, u32[]{:S(2)}) %all-to-all-start.3) | async-done | bytes 4194336 | tf_op jit(solution)/shard_map/all_to_all | solution.py:146
  413.9 5.0 gather_fusion.7
  418.9 5.0 gather_fusion.6
  423.9 5.0 gather_fusion.5
  428.9 5.0 gather_fusion.4
  433.8 5.0 gather_fusion.3
  438.8 5.0 gather_fusion.2
  443.8 4.0 fusion.12
  448.9 39.4 %reduce-scatter.2.cloned.1.call-done = bf16[128,256]{1,0:T(8,128)(2,1)} async-done(((bf16[128,2048]{1,0:T(8,128)(2,1)}), bf16[128,256]{1,0:T(8,128)(2,1)}) %reduce-scatter.2.cloned.1.call-update) | async-done | bytes 65552 | tf_op jit(solution)/shard_map/reduce_scatter | solution.py:152
  489.2 12.1 %all-gather = bf16[1,1,2048]{2,1,0:T(2,128)(2,1)S(1)} all-gather(bf16[1,1,256]{2,1,0:T(2,128)(2,1)S(1)} %slice.154), channel_id=2, replica_groups=mesh['req'=32,'tp'=8] {'tp'}, dimensions={2}, use_global_device_ids=true | all-gather | bytes 4608 | tf_op jit(solution)/shard_map/all_gather | solution.py:158
  501.3 101.8 %all-gather.1 = bf16[32,1,2048]{2,1,0:T(2,128)(2,1)S(1)} all-gather(bf16[1,1,2048]{2,1,0:T(2,128)(2,1)S(1)} %all-gather), channel_id=3, replica_groups=mesh['req'=32,'tp'=8] {'req'}, dimensions={0}, use_global_device_ids=true | all-gather | bytes 135168 | tf_op jit(solution)/shard_map/all_gather | solution.py:159
  605.9 85.0 %pmax.7 = f32[32]{0:T(128)} all-reduce(f32[32]{0:T(128)S(1)} %convolution_reduce_fusion), channel_id=1, replica_groups=mesh['req'=32,'tp'=8] {'req','tp'}, use_global_device_ids=true, to_apply=%region_15.17 | all-reduce | flops 32 | bytes 256 | tf_op jit(solution)/shard_map/pmax | solution.py:166
  (125 shorter events, 50.7 us)
Async XLA Ops:
  7.2 54.5 %copy-start = (bf16[3,2048,256]{2,1,0:T(8,128)(2,1)S(1)}, bf16[3,2048,256]{2,1,0:T(8,128)(2,1)}, u32[]{:S(2)}) copy-start(bf16[3,2048,256]{2,1,0:T(8,128)(2,1)} %param.20) | copy-start | bytes 9437188
  10.7 14.8 %copy-start.10 = (s32[128,6]{0,1:T(8,128)S(1)}, s32[128,6]{0,1:T(8,128)}, u32[]{:S(2)}) copy-start(s32[128,6]{0,1:T(8,128)} %param.27) | copy-start | bytes 9220
  10.7 15.2 %copy-start.12 = (bf16[2048]{0:T(1024)(128)(2,1)S(1)}, bf16[2048]{0:T(1024)(128)(2,1)}, u32[]{:S(2)}) copy-start(bf16[2048]{0:T(1024)(128)(2,1)} %param.19) | copy-start | bytes 12292
  10.7 17.5 %copy-start.17 = (s32[32]{0:T(128)S(1)}, s32[32]{0:T(128)}, u32[]{:S(2)}) copy-start(s32[32]{0:T(128)} %param.23) | copy-start | bytes 388
  10.7 17.5 %copy-start.8 = (bf16[128,256]{1,0:T(8,128)(2,1)S(1)}, bf16[128,256]{1,0:T(8,128)(2,1)}, u32[]{:S(2)}) copy-start(bf16[128,256]{1,0:T(8,128)(2,1)} %param.18) | copy-start | bytes 196612
  10.7 52.4 %all-to-all-start = ((bf16[2,1,1024,256]{3,0,1,2:T(2,128)(2,1)}), bf16[2,1,1024,256]{3,0,1,2:T(2,128)(2,1)}, u32[]{:S(2)}, u32[]{:S(2)}) async-start(bf16[2,1,1024,256]{3,0,1,2:T(2,128)(2,1)} %copy.92), calls=%async_computation | async-start | bytes 2097152 | tf_op jit(solution)/shard_map/all_to_all | solution.py:101
  60.9 0.8 copy-start.1
  70.7 12.0 %copy-start.13 = (bf16[2048]{0:T(1024)(128)(2,1)S(1)}, bf16[2048]{0:T(1024)(128)(2,1)}, u32[]{:S(2)}) copy-start(bf16[2048]{0:T(1024)(128)(2,1)} %param.25) | copy-start | bytes 12292
  70.7 34.3 %all-to-all-start.1 = ((bf16[2,32,32,256]{3,2,0,1:T(8,128)(2,1)}), bf16[2,32,32,256]{3,2,0,1:T(8,128)(2,1)}, u32[]{:S(2)}, u32[]{:S(2)}) async-start(bf16[2,32,32,256]{3,2,0,1:T(8,128)(2,1)} %select_bitcast_fusion), calls=%async_computation.1 | async-start | bytes 2097152 | tf_op jit(solution)/shard_map/all_to_all | solution.py:103
  81.9 111.3 %all-reduce.3.cloned.1.call-start = ((), (), s32[]{:S(2)}) async-start(), calls=%async_computation.5 | async-start | bytes 1048576 | tf_op jit(solution)/shard_map/psum | solution.py:108
  118.5 2.0 copy-start.5
  121.6 73.9 %copy-start.9 = (f32[2048]{0:T(1024)S(1)}, f32[2048]{0:T(1024)}, u32[]{:S(2)}) copy-start(f32[2048]{0:T(1024)} %convert_element_type.185) | copy-start | bytes 24580
  194.6 0.8 copy-start.4
  195.7 0.9 copy-start.2
  210.0 106.0 %copy-start.15 = (bf16[1,2,2048,176]{2,3,1,0:T(8,128)(2,1)S(1)}, bf16[1,2,2048,176]{2,3,1,0:T(8,128)(2,1)}, u32[]{:S(2)}) copy-start(bf16[1,2,2048,176]{2,3,1,0:T(8,128)(2,1)} %param.28) | copy-start | bytes 4325380
  316.0 2.3 copy-start.16
  321.7 7.4 %copy-start.6 = (bf16[2048,32]{0,1:T(8,128)(2,1)S(1)}, bf16[2048,32]{0,1:T(8,128)(2,1)}, u32[]{:S(2)}) copy-start(bf16[2048,32]{0,1:T(8,128)(2,1)} %param.26) | copy-start | bytes 393220
  321.7 8.8 %copy-start.11 = (s32[128,6]{0,1:T(8,128)S(1)}, s32[128,6]{0,1:T(8,128)}, u32[]{:S(2)}) copy-start(s32[128,6]{0,1:T(8,128)} %param.27) | copy-start | bytes 9220
  321.7 92.3 %all-to-all-start.3 = ((bf16[32,1,32,2048]{3,2,1,0:T(8,128)(2,1)}), bf16[32,1,32,2048]{3,2,1,0:T(8,128)(2,1)}, u32[]{:S(2)}, u32[]{:S(2)}) async-start(bf16[32,1,32,2048]{3,2,1,0:T(8,128)(2,1)} %convert_bitcast_fusion), calls=%async_computation.3 | async-start | bytes 8388608 | tf_op jit(solution)/shard_map/all_to_all | solution.py:146
  328.6 159.7 %reduce-scatter.2.cloned.1.call-start = ((), (), s32[]{:S(2)}) async-start(), calls=%async_computation.6 | async-start | bytes 589824 | tf_op jit(solution)/shard_map/reduce_scatter | solution.py:152
  328.6 1.9 copy-start.3
  443.8 4.1 copy-start.14
  489.2 116.8 %copy-start.7 = (bf16[128,256]{1,0:T(8,128)(2,1)}, bf16[128,256]{1,0:T(8,128)(2,1)S(1)}, u32[]{:S(2)}) copy-start(bf16[128,256]{1,0:T(8,128)(2,1)S(1)} %add_convert_fusion) | copy-start | bytes 196612
  603.6 87.3 %copy-start.18 = (f32[32]{0:T(128)}, f32[32]{0:T(128)S(1)}, u32[]{:S(2)}) copy-start(f32[32]{0:T(128)S(1)} %add_sqrt_fusion) | copy-start | bytes 388
Sparse Core Ops, SparseCore 0:
  121.7 71.4 all-reduce.2
  448.0 40.2 reduce-scatter.1
where the time goes:
time: 699 us; the launch traced here: 698 us
  blocking collectives  338 us (48%)
  waiting for transfers between devices  204 us (29%)
  local copies, waits for them, and re-layouts  72.3 us (10%)
  starting transfers between devices  33 us (5%)
  matrix products  22.3 us (3%)
  between operations  15.2 us (2%)
  other arithmetic  13.4 us (2%)
    all_to_all x1, blocking collectives, local(): lax.all_to_all(outgoing, 'req', split_axis=0, concat_axis=0, tiled=True)  106 us
    all_gather x1, blocking collectives, local(): last_every = lax.all_gather(last_rows, 'req', axis=0, tiled=True)  102 us
    pmax x1, blocking collectives, local(): top_logit = lax.pmax(jnp.max(logits, axis=1), ('req', 'tp'))  85 us
    all_to_all x1, waiting for transfers between devices, local(): lax.all_to_all(served, 'req', split_axis=0, concat_axis=0, tiled=True)  81.5 us
    psum x1, waiting for transfers between devices, local(): lax.psum(jnp.dot(attn_out, w_out, preferred_element_type=jnp.float32).ast...  67.9 us
    reduce_scatter x1, waiting for transfers between devices, local(): lax.psum_scatter(to_reduce.astype(jnp.bfloat16), 'tp', scatter_dimension=...  39.4 us
    all_gather x1, blocking collectives, local(): full_in = lax.all_gather(hidden, 'tp', axis=1, tiled=True)  32.7 us
    gather x6, local copies, waits for them, and re-layouts, local(): jnp.take(returned, pick_slots[:, pick_pos], axis=0).astype(jnp.float32)  29.9 us
  transfers between devices with their start and end apart: 5, of which 4 were waited for; matrix products, arithmetic and copies ran while one was open for 3% of the time, Pallas kernels for 0%

commit v1 on v0

v1 whole, which is shorter than its diff:
```python
import jax
import jax.numpy as jnp
from jax import lax
from jax.sharding import Mesh, PartitionSpec as P
from jax.experimental import pallas as pl
from jax.experimental.pallas import tpu as pltpu

HD = 128
TOPK = 6
CAP = 32

REQ = ("zh", "x", "y")
TP = ("zl", "core")
COL = ("zh", "zl", "core")
Z = ("zh", "zl")
ALL = ("zh", "x", "y", "zl", "core")
SIZES = (2, 4, 4, 4, 2)

epsilon = 1e-06
bf16 = jnp.bfloat16
f32 = jnp.float32


def rms_scale(values, gain):
    return (
        values
        * lax.rsqrt(jnp.mean(values * values, axis=-1, keepdims=True) + epsilon)
        * gain.astype(f32)
    )


def rotate_half(values, positions):
    half_len = values.shape[-1] // 2
    freqs = 10000.0 ** (-2.0 * jnp.arange(half_len, dtype=f32) / values.shape[-1])
    angles = positions[..., None] * freqs
    cosine = jnp.cos(angles)[..., None, :]
    sine = jnp.sin(angles)[..., None, :]
    lead_half = values[..., :half_len]
    tail_half = values[..., half_len:]
    return jnp.concatenate(
        [lead_half * cosine - tail_half * sine, tail_half * cosine + lead_half * sine], axis=-1
    )


def attend_body(len_ref, q_ref, k_ref, v_ref, old_ref, w_ref, o_ref):
    length = len_ref[0]
    parts, _, span, _ = old_ref.shape
    ctx = parts * span
    new = q_ref.shape[0]
    nt = (((1,), (1,)), ((), ()))
    heads = []
    for head in range(q_ref.shape[1] // HD):
        lanes = slice(head * HD, (head + 1) * HD)
        q = q_ref[:, lanes]
        old_k = old_ref[:, 0, :, lanes].reshape(ctx, HD)
        old_v = old_ref[:, 1, :, lanes].reshape(ctx, HD)
        s_old = lax.dot_general(q, old_k, nt, preferred_element_type=f32) * HD ** (-0.5)
        s_new = lax.dot_general(q, k_ref[:, lanes], nt, preferred_element_type=f32) * HD ** (-0.5)
        seen_old = lax.broadcasted_iota(jnp.int32, (new, ctx), 1) < length
        seen_new = lax.broadcasted_iota(jnp.int32, (new, new), 1) <= lax.broadcasted_iota(
            jnp.int32, (new, new), 0
        )
        s_old = jnp.where(seen_old, s_old, -1e30)
        s_new = jnp.where(seen_new, s_new, -1e30)
        peak = jnp.maximum(
            jnp.max(s_old, axis=-1, keepdims=True), jnp.max(s_new, axis=-1, keepdims=True)
        )
        e_old = jnp.where(seen_old, jnp.exp(s_old - peak), 0.0)
        e_new = jnp.where(seen_new, jnp.exp(s_new - peak), 0.0)
        total = jnp.sum(e_old, axis=-1, keepdims=True) + jnp.sum(e_new, axis=-1, keepdims=True)
        w_old = (e_old / total).astype(bf16)
        w_new = (e_new / total).astype(bf16)
        out = jnp.dot(w_old, old_v, preferred_element_type=f32) + jnp.dot(
            w_new, v_ref[:, lanes], preferred_element_type=f32
        )
        heads.append(out.astype(bf16))
    attn = jnp.concatenate(heads, axis=1)
    wide = o_ref.shape[2]
    for part in range(o_ref.shape[0]):
        o_ref[part] = jnp.dot(
            attn, w_ref[:, part * wide : (part + 1) * wide], preferred_element_type=f32
        ).astype(bf16)


def attend(lengths, q, k, v, old, w_out):
    vm = pl.BlockSpec(memory_space=pltpu.VMEM)
    new, feat = q.shape
    return pl.pallas_call(
        attend_body,
        out_shape=jax.ShapeDtypeStruct((w_out.shape[1] // feat, new, feat), bf16),
        in_specs=[pl.BlockSpec(memory_space=pltpu.SMEM), vm, vm, vm, vm, vm],
        out_specs=vm,
        name="attend",
    )(lengths, q, k, v, old, w_out)


def expert_body(
    place_ref, a_ref, b_ref, gain_ref, router_ref, in_ref, down_ref, om_ref, ot_ref, x_ref, routed
):
    first = place_ref[0] == 0
    width = x_ref.shape[1]
    feat = width // 8

    def fill(even_ref, odd_ref):
        for part in range(4):
            piece = slice(part * feat, (part + 1) * feat)
            x_ref[:, 2 * part * feat : (2 * part + 1) * feat] = even_ref[:, piece]
            x_ref[:, (2 * part + 1) * feat : (2 * part + 2) * feat] = odd_ref[:, piece]

    @pl.when(first)
    def _():
        fill(a_ref, b_ref)

    @pl.when(jnp.logical_not(first))
    def _():
        fill(b_ref, a_ref)

    x = x_ref[...].astype(f32)
    scale = lax.rsqrt(jnp.mean(x * x, axis=-1, keepdims=True) + epsilon)
    rows = (x * scale * gain_ref[...].astype(f32)).astype(bf16)
    gate = jnp.dot(rows, in_ref[0], preferred_element_type=f32)
    up = jnp.dot(rows, in_ref[1], preferred_element_type=f32)
    inner = (gate / (1.0 + jnp.exp(-gate)) * up).astype(bf16)
    out = jnp.dot(inner, down_ref[...], preferred_element_type=f32)
    if routed:
        logits = jnp.dot(rows, router_ref[...], preferred_element_type=f32)
        raised = jnp.exp(logits - jnp.max(logits, axis=-1, keepdims=True))
        own = lax.broadcasted_iota(jnp.int32, logits.shape, 1) == place_ref[1]
        picked = jnp.sum(jnp.where(own, raised, 0.0), axis=-1, keepdims=True)
        out = out * (picked / jnp.sum(raised, axis=-1, keepdims=True))
    out = out.astype(bf16)

    def drain(even_ref, odd_ref):
        for part in range(4):
            piece = slice(part * feat, (part + 1) * feat)
            even_ref[:, piece] = out[:, 2 * part * feat : (2 * part + 1) * feat]
            odd_ref[:, piece] = out[:, (2 * part + 1) * feat : (2 * part + 2) * feat]

    @pl.when(first)
    def _():
        drain(om_ref, ot_ref)

    @pl.when(jnp.logical_not(first))
    def _():
        drain(ot_ref, om_ref)


def expert_mlp(place, rows_mine, rows_theirs, gain, w_router, w_in, w_down, block, routed):
    count, half = rows_mine.shape
    width = 2 * half
    hidden = w_down.shape[0]
    row_spec = pl.BlockSpec((block, half), lambda i: (i, 0))

    def whole(array):
        zeros = (0,) * array.ndim
        return pl.BlockSpec(array.shape, lambda i: zeros)

    shape = jax.ShapeDtypeStruct((count, half), bf16)

    def body(*refs):
        expert_body(*refs, routed)

    return pl.pallas_call(
        body,
        grid=(count // block,),
        out_shape=(shape, shape),
        in_specs=[
            pl.BlockSpec(memory_space=pltpu.SMEM),
            row_spec,
            row_spec,
            whole(gain),
            whole(w_router),
            whole(w_in),
            whole(w_down),
        ],
        out_specs=(row_spec, row_spec),
        scratch_shapes=[pltpu.VMEM((block, width), bf16)],
        cost_estimate=pl.CostEstimate(
            flops=6 * count * width * hidden,
            transcendentals=count * hidden,
            bytes_accessed=8 * count * half + 6 * width * hidden,
        ),
        name="routed_mlp" if routed else "shared_mlp",
    )(place, rows_mine, rows_theirs, gain, w_router, w_in, w_down)


def head_body(last_ref, gain_ref, w_ref, top_ref, rms_ref):
    rows, width = last_ref.shape
    plane = rows // 2
    feat = width // 8
    halves = []
    for zo in range(2):
        pieces = []
        for part in range(4):
            for core in range(2):
                lanes = slice((zo * 4 + part) * feat, (zo * 4 + part + 1) * feat)
                pieces.append(last_ref[core * plane : (core + 1) * plane, lanes])
        halves.append(jnp.concatenate(pieces, axis=1))
    tok = jnp.concatenate(halves, axis=0).astype(f32)
    rms = jnp.sqrt(jnp.mean(tok * tok, axis=-1, keepdims=True) + epsilon)
    head_in = (tok / rms * gain_ref[...].astype(f32)).astype(bf16)
    logits = lax.dot_general(
        w_ref[...], head_in, (((1,), (1,)), ((), ())), preferred_element_type=f32
    )
    top_ref[...] = jnp.broadcast_to(jnp.max(logits, axis=0, keepdims=True), top_ref.shape)
    rms_ref[...] = rms


def head(last, gain, w_head):
    vm = pl.BlockSpec(memory_space=pltpu.VMEM)
    rows = last.shape[0]
    return pl.pallas_call(
        head_body,
        out_shape=(
            jax.ShapeDtypeStruct((256, rows), f32),
            jax.ShapeDtypeStruct((rows, 1), f32),
        ),
        in_specs=[vm, vm, vm],
        out_specs=(vm, vm),
        name="head",
    )(last, gain, w_head)


def spread(value, axes, count):
    wide = jnp.broadcast_to(value[None], (count,) + value.shape)
    return lax.all_to_all(wide, axes, 0, 0, tiled=True)


def swap_core(value):
    return lax.ppermute(value, "core", [(0, 1), (1, 0)])


def local(
    hidden,
    attn_gain,
    w_qkv,
    w_out,
    kv_cache,
    holder_slot,
    lengths,
    ffn_gain,
    w_router,
    expert_ids,
    w_exp_in,
    w_exp_down,
    w_sh_in,
    w_sh_down,
    final_gain,
    w_head,
):
    zh = lax.axis_index("zh")
    zl = lax.axis_index("zl")
    core = lax.axis_index("core")
    expert = lax.axis_index(REQ)
    new, feat = hidden.shape
    width = attn_gain.shape[0]
    half = width // 2
    experts_all = w_router.shape[1]
    plane = experts_all // 2
    slots = plane * 2 * CAP

    reqs = holder_slot.shape[0]
    ctx = kv_cache.shape[2]
    pieces = kv_cache.reshape(2, reqs, ctx // reqs, feat).transpose(1, 0, 2, 3)
    leg = lax.all_to_all(pieces, REQ, 0, 0, tiled=True)
    leg = leg.at[holder_slot].get(mode="promise_in_bounds")
    old = lax.all_to_all(leg, REQ, 0, 0, tiled=True)

    ids_there = lax.ppermute(expert_ids, "zh", [(0, 1), (1, 0)])
    own = lax.all_gather(hidden, TP, axis=1, tiled=True)
    normed = rms_scale(own.astype(f32), attn_gain).astype(bf16)
    projected = jnp.einsum("td,cde->cte", normed, w_qkv, preferred_element_type=f32)
    positions = (lengths[:, None] + jnp.arange(new, dtype=jnp.int32)[None, :]).astype(f32)
    shaped = projected.reshape(3, 1, new, feat // HD, HD)
    queries = rotate_half(shaped[0], positions).astype(bf16).reshape(new, feat)
    keys_new = rotate_half(shaped[1], positions).astype(bf16).reshape(new, feat)
    values_new = shaped[2].astype(bf16).reshape(new, feat)
    new_cache = jnp.stack([keys_new, values_new])[:, None]

    parts = attend(lengths, queries, keys_new, values_new, old, w_out)
    parts = lax.all_to_all(parts, TP, 0, 0, tiled=True)
    attn_total = jnp.sum(parts.astype(f32), axis=0)
    resid_share = (hidden.astype(f32) + attn_total).astype(bf16)
    resid = spread(resid_share, Z, 8).reshape(2, 4, new, feat)
    resid = resid.transpose(0, 2, 1, 3).reshape(2 * new, half)

    ids = jnp.where(
        zh == 0, jnp.stack([expert_ids, ids_there]), jnp.stack([ids_there, expert_ids])
    )
    picks = ids.reshape(2, new * TOPK)
    onehot = (picks[:, :, None] == jnp.arange(experts_all, dtype=jnp.int32)).astype(bf16)
    order = jnp.arange(new * TOPK, dtype=jnp.int32)
    before = (order[:, None] > order[None, :]).astype(bf16)
    earlier = jnp.einsum("pq,rqe->rpe", before, onehot, preferred_element_type=f32)
    rank = jnp.sum(earlier * onehot.astype(f32), axis=2).astype(jnp.int32)
    there = picks - zh * plane
    slot = (there * 2 + jnp.arange(2, dtype=jnp.int32)[:, None]) * CAP + rank
    slot = jnp.where((there >= 0) & (there < plane), slot, -1).reshape(2 * new, TOPK)
    slot_iota = jnp.arange(slots, dtype=jnp.int32)
    chosen = jnp.zeros((2 * new, slots), bf16)
    for pick in range(TOPK):
        chosen = chosen + (slot[:, pick : pick + 1] == slot_iota[None, :]).astype(bf16)

    outgoing = lax.dot_general(
        chosen, resid, (((0,), (0,)), ((), ())), preferred_element_type=f32
    ).astype(bf16)
    rows_mine = lax.all_to_all(
        outgoing.reshape(plane, 2 * CAP, half), ("x", "y"), 0, 0, tiled=True
    ).reshape(slots, half)
    rows_theirs = swap_core(rows_mine)

    place = jnp.stack([core, expert]).astype(jnp.int32)
    gain = ffn_gain[None]
    own_mine = lax.dynamic_slice_in_dim(resid, zh * new, new, 0)
    shared_mine, shared_theirs = expert_mlp(
        place, own_mine, swap_core(own_mine), gain, w_router, w_sh_in, w_sh_down, new, False
    )
    shared = shared_mine.astype(f32) + swap_core(shared_theirs).astype(f32)

    served_mine, served_theirs = expert_mlp(
        place, rows_mine, rows_theirs, gain, w_router, w_exp_in[0], w_exp_down[0], 256, True
    )
    served = (served_mine.astype(f32) + swap_core(served_theirs).astype(f32)).astype(bf16)
    returned = lax.all_to_all(
        served.reshape(plane, 2 * CAP, half), ("x", "y"), 0, 0, tiled=True
    ).reshape(slots, half)
    share = jnp.dot(chosen, returned, preferred_element_type=f32).reshape(2, new, half)
    is_own = (jnp.arange(2) == zh)[:, None, None]
    share = (share + jnp.where(is_own, shared[None], 0.0)).astype(bf16)

    cut = share.reshape(2, new, 4, feat).transpose(0, 2, 1, 3).reshape(8, new, feat)
    last = share[:, new - 1].reshape(1, 8, feat)
    packed = jnp.concatenate([cut, jnp.broadcast_to(last, (8, 8, feat))], axis=1)
    summed = jnp.sum(lax.all_to_all(packed, Z, 0, 0, tiled=True).astype(f32), axis=0)
    out_hidden = (resid_share.astype(f32) + summed[:new]).astype(bf16)
    last_resid = resid.reshape(2, new, half)[:, new - 1].astype(f32)
    last_half = (last_resid + summed[new:].reshape(2, half)).astype(bf16)

    last_all = spread(last_half.reshape(width), ("core", "x", "y"), reqs)
    tops, rms = head(last_all, final_gain[None], w_head)
    last_rms = rms.reshape(reqs)
    top_logit = jnp.max(lax.all_to_all(tops, ALL, 0, 0, tiled=True), axis=0)
    return (out_hidden, new_cache, last_rms, top_logit)


def solution(mesh):
    fine = Mesh(mesh.devices.reshape(SIZES), ALL)
    return jax.shard_map(
        local,
        mesh=fine,
        in_specs=(
            P(REQ, TP),
            P(),
            P(None, None, TP),
            P(TP, None),
            P(None, REQ, None, TP),
            P(),
            P(REQ),
            P(),
            P(),
            P(REQ, None),
            P(REQ, None, None, TP),
            P(REQ, TP, None),
            P(None, None, TP),
            P(TP, None),
            P(),
            P(REQ + TP, None),
        ),
        out_specs=(P(REQ, TP), P(None, REQ, None, TP), P(), P()),
        check_vma=False,
    )
```

time: 699 us -> 320 us (0.46)
  blocking collectives: 338 us -> 65.8 us
  waiting for transfers between devices: 204 us -> 84.2 us
  starting transfers between devices: 33 us -> 66.5 us
  local copies, waits for them, and re-layouts: 72.3 us -> 44.8 us
  Pallas kernels: 0 us -> 21.8 us
  matrix products: 22.3 us -> 6.57 us
  between operations: 15.2 us -> 1.72 us
  other arithmetic: 13.4 us -> 26.5 us
    all_gather x3 -> x1, blocking collectives: 147 us -> 34.7 us  [local(): own = lax.all_gather(hidden, TP, axis=1, tiled=True)]
    pmax x1 -> x0, blocking collectives: 85 us -> none  [local(): top_logit = lax.pmax(jnp.max(logits, axis=1), ('req', 'tp'))]
    all_to_all x1, blocking collectives: 106 us -> 31.1 us  [local(): lax.all_to_all(outgoing.reshape(plane, 2 * CAP, half), ('x', 'y'), 0, 0,...]
    psum x1 -> x0, waiting for transfers between devices: 67.9 us -> none  [local(): lax.psum(jnp.dot(attn_out, w_out, preferred_element_type=jnp.float32).ast...]
    gather x8 -> x1, local copies, waits for them, and re-layouts: 42.6 us -> 2.85 us  [local(): leg = leg.at[holder_slot].get(mode='promise_in_bounds')]
    reduce_scatter x1 -> x0, waiting for transfers between devices: 39.4 us -> none  [local(): lax.psum_scatter(to_reduce.astype(jnp.bfloat16), 'tp', scatter_dimension=...]
    all_to_all x3 -> x8, starting transfers between devices: 32.9 us -> 63.5 us  [the longest x1 14.6 us: local(): leg = lax.all_to_all(pieces, REQ, 0, 0, tiled=True)]
    pallas_call x0 -> x4, Pallas kernels: none -> 21.8 us  [the longest x2 15.6 us: expert_mlp(): pl.pallas_call(body, grid=(count // block,), out_shape=(shape, shape), in...]
  transfers between devices with their start and end apart: 5 -> 13, of which waited for: 4 -> 9; matrix products, arithmetic and copies ran while one was open for 3% -> 15% of each run, Pallas kernels for 0% -> 1%
where the time goes in v1:
time: 320 us; the launch traced here: 318 us
  waiting for transfers between devices  84.2 us (26%)
  starting transfers between devices  66.5 us (21%)
  blocking collectives  65.8 us (21%)
  local copies, waits for them, and re-layouts  44.8 us (14%)
  other arithmetic  26.5 us (8%)
  Pallas kernels  21.8 us (7%)
  matrix products  6.57 us (2%)
    all_gather x1, blocking collectives, local(): own = lax.all_gather(hidden, TP, axis=1, tiled=True)  34.7 us
    all_to_all x1, blocking collectives, local(): lax.all_to_all(outgoing.reshape(plane, 2 * CAP, half), ('x', 'y'), 0, 0,...  31.1 us
    all_to_all x1, waiting for transfers between devices, local(): lax.all_to_all(served.reshape(plane, 2 * CAP, half), ('x', 'y'), 0, 0, ti...  16.4 us
    unnamed x44, local copies, waits for them, and re-layouts  15.9 us
    pallas_call x2, Pallas kernels, expert_mlp(): pl.pallas_call(body, grid=(count // block,), out_shape=(shape, shape), in...  15.6 us
    all_to_all x1, starting transfers between devices, local(): leg = lax.all_to_all(pieces, REQ, 0, 0, tiled=True)  14.6 us
    all_to_all x1, waiting for transfers between devices, local(): parts = lax.all_to_all(parts, TP, 0, 0, tiled=True)  14.3 us
    all_to_all x1, waiting for transfers between devices, local(): lax.all_to_all(packed, Z, 0, 0, tiled=True).astype(f32)  13.7 us
  transfers between devices with their start and end apart: 13, of which 9 were waited for; matrix products, arithmetic and copies ran while one was open for 15% of the time, Pallas kernels for 1%

profile of v1, /device:TPU:1, one launch (start us, length us, event | category | flops | bytes accessed | tf_op | source)
XLA Modules:
  0.0 318.0 jit_solution(2555832487154370966)
XLA Ops:
  3.2 14.6 %all-to-all-start = ((bf16[32,2,32,256]{3,2,1,0:T(8,128)(2,1)}), bf16[32,2,32,256]{3,2,1,0:T(8,128)(2,1)}, u32[]{:S(2)}, u32[]{:S(2)}) async-start(bf16[32,2,32,256]{3,2,1,0:T(8,128)(2,1)} %copy.61), calls=%async_computation | async-start | bytes 2097152 | tf_op jit(solution)/shard_map/all_to_all | solution.py:265
  18.5 34.7 %all_gather.3 = bf16[128,2048]{1,0:T(8,128)(2,1)S(1)} all-gather(bf16[128,256]{1,0:T(8,128)(2,1)S(1)} %copy-done.7), channel_id=1, replica_groups=mesh['zh'=2,'x'=4,'y'=4,'zl'=4,'core'=2] {'zl','core'}, dimensions={1}, use_global_device_ids=true | all-gather | bytes 589824 | tf_op jit(solution)/shard_map/all_gather | solution.py:270
  57.1 11.2 %all-to-all-start.1 = ((bf16[32,2,32,256]{3,2,1,0:T(8,128)(2,1)}), bf16[32,2,32,256]{3,2,1,0:T(8,128)(2,1)}, u32[]{:S(2)}, u32[]{:S(2)}) async-start(bf16[32,2,32,256]{3,2,1,0:T(8,128)(2,1)} %gather_fusion), calls=%async_computation.1 | async-start | bytes 2097152 | tf_op jit(solution)/shard_map/all_to_all | solution.py:267
  78.4 12.9 %all-to-all-done.1.old_ref = bf16[32,2,32,256]{3,2,1,0:T(8,128)(2,1)} async-done(((bf16[32,2,32,256]{3,2,1,0:T(8,128)(2,1)}), bf16[32,2,32,256]{3,2,1,0:T(8,128)(2,1)}, u32[]{:S(2)}, u32[]{:S(2)}) %all-to-all-start.1) | async-done | bytes 1048608 | tf_op jit(solution)/shard_map/all_to_all | solution.py:267
  91.3 3.9 %attend.1 = bf16[8,128,256]{2,1,0:T(8,128)(2,1)} custom-call(s32[1]{0:T(128)} %copy.83.len_ref, bf16[128,256]{1,0:T(8,128)(2,1)} %get-tuple-element.61.q_ref, bf16[128,256]{1,0:T(8,128)(2,1)} %get-tuple-element.60.k_ref, bf16[128,256]{1,0:T(8,128)(2,1)} %slice_bitcast_fusion.1.v_ref, bf16[32,2,32,256]{3,2,1,0:T(8,128)(2,1)} %all-to-all-done.1.old_ref, ...), custom_call_target="tpu_custom_call" | custom-call | tf_op jit(solution)/shard_map/attend/pallas_call | solution.py:88
  95.2 11.2 %all-to-all-start.2 = ((bf16[8,128,256]{2,1,0:T(8,128)(2,1)}), bf16[8,128,256]{2,1,0:T(8,128)(2,1)}, u32[]{:S(2)}, u32[]{:S(2)}) async-start(bf16[8,128,256]{2,1,0:T(8,128)(2,1)} %attend.1), calls=%async_computation.2 | async-start | bytes 1048576 | tf_op jit(solution)/shard_map/all_to_all | solution.py:281
  106.8 14.3 %all-to-all-done.2 = bf16[8,128,256]{2,1,0:T(8,128)(2,1)} async-done(((bf16[8,128,256]{2,1,0:T(8,128)(2,1)}), bf16[8,128,256]{2,1,0:T(8,128)(2,1)}, u32[]{:S(2)}, u32[]{:S(2)}) %all-to-all-start.2) | async-done | bytes 524320 | tf_op jit(solution)/shard_map/all_to_all | solution.py:281
  124.6 4.1 %all-to-all-start.3 = ((bf16[8,128,256]{2,1,0:T(8,128)(2,1)}), bf16[8,128,256]{2,1,0:T(8,128)(2,1)}, u32[]{:S(2)}, u32[]{:S(2)}) async-start(bf16[8,128,256]{2,1,0:T(8,128)(2,1)} %broadcast_in_dim.35), calls=%async_computation.3 | async-start | bytes 1048576 | tf_op jit(solution)/shard_map/all_to_all | solution.py:226
  139.0 7.7 %all-to-all-done.3 = bf16[8,128,256]{2,1,0:T(8,128)(2,1)} async-done(((bf16[8,128,256]{2,1,0:T(8,128)(2,1)}), bf16[8,128,256]{2,1,0:T(8,128)(2,1)}, u32[]{:S(2)}, u32[]{:S(2)}) %all-to-all-start.3) | async-done | bytes 524320 | tf_op jit(solution)/shard_map/all_to_all | solution.py:226
  149.7 31.1 %all_to_all.52 = bf16[16,64,1024]{2,1,0:T(8,128)(2,1)} all-to-all(bf16[16,64,1024]{2,1,0:T(8,128)(2,1)S(1)} %bitcast.89), channel_id=1, replica_groups=mesh['zh'=2,'x'=4,'y'=4,'zl'=4,'core'=2] {'x','y'}, dimensions={0} | all-to-all | bytes 4194304 | tf_op jit(solution)/shard_map/all_to_all | solution.py:307
  185.4 3.6 %copy.65 = bf16[1,2,2048,176]{3,2,1,0:T(8,128)(2,1)} copy(bf16[1,2,2048,176]{2,3,1,0:T(8,128)(2,1)} %param.26) | data formatting | bytes 2883584 | tf_op args[10]
  189.7 11.7 %routed_mlp.1 = (bf16[1024,1024]{1,0:T(8,128)(2,1)}, bf16[1024,1024]{1,0:T(8,128)(2,1)}) custom-call(s32[2]{0:T(128)} %pad_add_fusion.refs_0_, bf16[1024,1024]{1,0:T(8,128)(2,1)} %bitcast.15.refs_1_, bf16[1024,1024]{1,0:T(8,128)(2,1)} %collective-permute-done.1.refs_2_, bf16[1,2048]{1,0:T(2,128)(2,1)} %broadcast_in_dim.36.refs_3_, ...), custom_call_target="tpu_custom_call" | custom-call | flops 2214592512 | bytes 10551296 | tf_op jit(solution)/shard_map/routed_mlp/pallas_call | solution.py:163
  201.4 4.3 %collective-permute-done.2 = bf16[1024,1024]{1,0:T(8,128)(2,1)S(1)} collective-permute-done((bf16[1024,1024]{1,0:T(8,128)(2,1)}, bf16[1024,1024]{1,0:T(8,128)(2,1)S(1)}, u32[]{:S(2)}, u32[]{:S(2)}) %collective-permute-start.2) | collective-permute-done | bytes 2097184 | tf_op jit(solution)/shard_map/ppermute | solution.py:230
  205.7 3.9 %add_convert_fusion = bf16[1024,1024]{1,0:T(8,128)(2,1)} fusion(bf16[1024,1024]{1,0:T(8,128)(2,1)S(1)} %collective-permute-done.2, bf16[1024,1024]{1,0:T(8,128)(2,1)} %get-tuple-element.10), kind=kLoop, calls=%fused_computation.1 | loop fusion | flops 4194304 | bytes 6291456 | tf_op jit(solution)/shard_map/convert_element_type | solution.py:323
  209.6 4.4 %all-to-all-start.5 = ((bf16[16,64,1024]{2,1,0:T(8,128)(2,1)}), bf16[16,64,1024]{2,1,0:T(8,128)(2,1)}, u32[]{:S(2)}, u32[]{:S(2)}) async-start(bf16[16,64,1024]{2,1,0:T(8,128)(2,1)} %bitcast.87), calls=%async_computation.5 | async-start | bytes 4194304 | tf_op jit(solution)/shard_map/all_to_all | solution.py:324
  215.8 3.6 %copy.68.refs_5_ = bf16[2,2048,176]{2,1,0:T(8,128)(2,1)} copy(bf16[2,2048,176]{1,2,0:T(8,128)(2,1)} %param.28) | data formatting | bytes 2883584 | tf_op args[12]
  219.5 3.9 %shared_mlp.1 = (bf16[128,1024]{1,0:T(8,128)(2,1)}, bf16[128,1024]{1,0:T(8,128)(2,1)}) custom-call(s32[2]{0:T(128)} %pad_add_fusion.refs_0_, bf16[128,1024]{1,0:T(8,128)(2,1)} %constant_dynamic-slice_fusion.refs_1_, bf16[128,1024]{1,0:T(8,128)(2,1)} %collective-permute-done.3.refs_2_, bf16[1,2048]{1,0:T(2,128)(2,1)} %broadcast_in_dim.36.refs_3_, ...), custom_call_target="tpu_custom_call" | custom-call | flops 276824064 | bytes 3211264 | tf_op jit(solution)/shard_map/shared_mlp/pallas_call | solution.py:163
  227.0 16.4 %all-to-all-done.5 = bf16[16,64,1024]{2,1,0:T(8,128)(2,1)} async-done(((bf16[16,64,1024]{2,1,0:T(8,128)(2,1)}), bf16[16,64,1024]{2,1,0:T(8,128)(2,1)}, u32[]{:S(2)}, u32[]{:S(2)}) %all-to-all-start.5) | async-done | bytes 2097184 | tf_op jit(solution)/shard_map/all_to_all | solution.py:324
  249.3 4.2 %all-to-all-start.6 = ((bf16[8,136,256]{2,1,0:T(8,128)(2,1)}), bf16[8,136,256]{2,1,0:T(8,128)(2,1)}, u32[]{:S(2)}, u32[]{:S(2)}) async-start(bf16[8,136,256]{2,1,0:T(8,128)(2,1)} %pad_maximum_fusion), calls=%async_computation.6 | async-start | bytes 1114112 | tf_op jit(solution)/shard_map/all_to_all | solution.py:334
  257.0 13.7 %all-to-all-done.6 = bf16[8,136,256]{2,1,0:T(8,128)(2,1)} async-done(((bf16[8,136,256]{2,1,0:T(8,128)(2,1)}), bf16[8,136,256]{2,1,0:T(8,128)(2,1)}, u32[]{:S(2)}, u32[]{:S(2)}) %all-to-all-start.6) | async-done | bytes 557088 | tf_op jit(solution)/shard_map/all_to_all | solution.py:334
  278.5 8.2 %all-to-all-start.7 = ((bf16[32,2,1024]{2,1,0:T(2,128)(2,1)}), bf16[32,2,1024]{2,1,0:T(2,128)(2,1)}, u32[]{:S(2)}, u32[]{:S(2)}) async-start(bf16[32,2,1024]{2,1,0:T(2,128)(2,1)} %reshape.448), calls=%async_computation.7 | async-start | bytes 262144 | tf_op jit(solution)/shard_map/all_to_all | solution.py:226
  290.4 3.9 %all-to-all-done.7 = bf16[32,2,1024]{2,1,0:T(2,128)(2,1)} async-done(((bf16[32,2,1024]{2,1,0:T(2,128)(2,1)}), bf16[32,2,1024]{2,1,0:T(2,128)(2,1)}, u32[]{:S(2)}, u32[]{:S(2)}) %all-to-all-start.7) | async-done | bytes 131104 | tf_op jit(solution)/shard_map/all_to_all | solution.py:226
  298.8 5.5 %all-to-all-start.8 = ((f32[256,1,32]{2,1,0:T(1,128)}), f32[256,1,32]{2,1,0:T(1,128)S(1)}, u32[]{:S(2)}, u32[]{:S(2)}) async-start(f32[256,1,32]{2,1,0:T(1,128)} %bitcast.99), calls=%async_computation.8 | async-start | bytes 262144 | tf_op jit(solution)/shard_map/all_to_all | solution.py:342
  307.3 10.0 %all-to-all-done.8 = f32[256,1,32]{2,1,0:T(1,128)S(1)} async-done(((f32[256,1,32]{2,1,0:T(1,128)}), f32[256,1,32]{2,1,0:T(1,128)S(1)}, u32[]{:S(2)}, u32[]{:S(2)}) %all-to-all-start.8) | async-done | bytes 32800 | tf_op jit(solution)/shard_map/all_to_all | solution.py:342
  (117 shorter events, 73.0 us)
Async XLA Ops:
  0.6 67.7 %copy-start = (bf16[3,2048,256]{2,1,0:T(8,128)(2,1)S(1)}, bf16[3,2048,256]{2,1,0:T(8,128)(2,1)}, u32[]{:S(2)}) copy-start(bf16[3,2048,256]{2,1,0:T(8,128)(2,1)} %param.18) | copy-start | bytes 9437188
  0.6 17.8 %copy-start.8 = (bf16[2048]{0:T(1024)(128)(2,1)S(1)}, bf16[2048]{0:T(1024)(128)(2,1)}, u32[]{:S(2)}) copy-start(bf16[2048]{0:T(1024)(128)(2,1)} %param.17) | copy-start | bytes 12292
  0.7 17.8 %copy-start.16 = (s32[32]{0:T(128)S(1)}, s32[32]{0:T(128)}, u32[]{:S(2)}) copy-start(s32[32]{0:T(128)} %param.21) | copy-start | bytes 388
  0.7 17.8 %copy-start.7 = (bf16[128,256]{1,0:T(8,128)(2,1)S(1)}, bf16[128,256]{1,0:T(8,128)(2,1)}, u32[]{:S(2)}) copy-start(bf16[128,256]{1,0:T(8,128)(2,1)} %param.16) | copy-start | bytes 196612
  3.2 51.1 %all-to-all-start = ((bf16[32,2,32,256]{3,2,1,0:T(8,128)(2,1)}), bf16[32,2,32,256]{3,2,1,0:T(8,128)(2,1)}, u32[]{:S(2)}, u32[]{:S(2)}) async-start(bf16[32,2,32,256]{3,2,1,0:T(8,128)(2,1)} %copy.61), calls=%async_computation | async-start | bytes 2097152 | tf_op jit(solution)/shard_map/all_to_all | solution.py:265
  57.1 34.2 %all-to-all-start.1 = ((bf16[32,2,32,256]{3,2,1,0:T(8,128)(2,1)}), bf16[32,2,32,256]{3,2,1,0:T(8,128)(2,1)}, u32[]{:S(2)}, u32[]{:S(2)}) async-start(bf16[32,2,32,256]{3,2,1,0:T(8,128)(2,1)} %gather_fusion), calls=%async_computation.1 | async-start | bytes 2097152 | tf_op jit(solution)/shard_map/all_to_all | solution.py:267
  75.7 2.1 copy-start.3
  77.7 28.6 %copy-start.9 = (s32[128,6]{0,1:T(8,128)S(1)}, s32[128,6]{0,1:T(8,128)}, u32[]{:S(2)}) copy-start(s32[128,6]{0,1:T(8,128)} %param.25) | copy-start | bytes 9220
  95.2 26.0 %all-to-all-start.2 = ((bf16[8,128,256]{2,1,0:T(8,128)(2,1)}), bf16[8,128,256]{2,1,0:T(8,128)(2,1)}, u32[]{:S(2)}, u32[]{:S(2)}) async-start(bf16[8,128,256]{2,1,0:T(8,128)(2,1)} %attend.1), calls=%async_computation.2 | async-start | bytes 1048576 | tf_op jit(solution)/shard_map/all_to_all | solution.py:281
  106.4 24.6 %collective-permute-start = (s32[128,6]{0,1:T(8,128)S(1)}, s32[128,6]{0,1:T(8,128)S(1)}, u32[]{:S(2)}, u32[]{:S(2)}) collective-permute-start(s32[128,6]{0,1:T(8,128)S(1)} %copy-done.9), channel_id=1, source_target_pairs={{0,128},{128,0},{1,129},{129,1},{2,130},{130,2},{3,131},{131,3},{4... | collective-permute-start | bytes 9224 | tf_op jit(solution)/shard_map/ppermute | solution.py:269
  124.6 22.1 %all-to-all-start.3 = ((bf16[8,128,256]{2,1,0:T(8,128)(2,1)}), bf16[8,128,256]{2,1,0:T(8,128)(2,1)}, u32[]{:S(2)}, u32[]{:S(2)}) async-start(bf16[8,128,256]{2,1,0:T(8,128)(2,1)} %broadcast_in_dim.35), calls=%async_computation.3 | async-start | bytes 1048576 | tf_op jit(solution)/shard_map/all_to_all | solution.py:226
  139.0 10.8 %copy-start.12 = (s32[256]{0:T(256)}, s32[256]{0:T(256)S(1)}, u32[]{:S(2)}) copy-start(s32[256]{0:T(256)S(1)} %get-tuple-element.43) | copy-start | bytes 3076
  149.7 33.2 %copy-start.10 = (bf16[2048]{0:T(1024)(128)(2,1)S(1)}, bf16[2048]{0:T(1024)(128)(2,1)}, u32[]{:S(2)}) copy-start(bf16[2048]{0:T(1024)(128)(2,1)} %param.23) | copy-start | bytes 12292
  180.9 8.8 %collective-permute-start.1 = (bf16[1024,1024]{1,0:T(8,128)(2,1)}, bf16[1024,1024]{1,0:T(8,128)(2,1)}, u32[]{:S(2)}, u32[]{:S(2)}) collective-permute-start(bf16[1024,1024]{1,0:T(8,128)(2,1)} %bitcast.15.refs_1_), channel_id=1, source_target_pairs={{0,1},{1,0},{2,3},{3,2},{4,5},{5,4},{6,7},{7,6},{8,9},{9,8},{10,11... | collective-permute-start | bytes 6291464 | tf_op jit(solution)/shard_map/ppermute | solution.py:230
  201.3 4.4 %collective-permute-start.2 = (bf16[1024,1024]{1,0:T(8,128)(2,1)}, bf16[1024,1024]{1,0:T(8,128)(2,1)S(1)}, u32[]{:S(2)}, u32[]{:S(2)}) collective-permute-start(bf16[1024,1024]{1,0:T(8,128)(2,1)} %get-tuple-element.11), channel_id=1, source_target_pairs={{0,1},{1,0},{2,3},{3,2},{4,5},{5,4},{6,7},{7,6},{8,9},{9,8},{10,11... | collective-permute-start | bytes 6291464 | tf_op jit(solution)/shard_map/ppermute | solution.py:230
  209.6 33.8 %all-to-all-start.5 = ((bf16[16,64,1024]{2,1,0:T(8,128)(2,1)}), bf16[16,64,1024]{2,1,0:T(8,128)(2,1)}, u32[]{:S(2)}, u32[]{:S(2)}) async-start(bf16[16,64,1024]{2,1,0:T(8,128)(2,1)} %bitcast.87), calls=%async_computation.5 | async-start | bytes 4194304 | tf_op jit(solution)/shard_map/all_to_all | solution.py:324
  215.7 3.8 %collective-permute-start.3 = (bf16[128,1024]{1,0:T(8,128)(2,1)}, bf16[128,1024]{1,0:T(8,128)(2,1)}, u32[]{:S(2)}, u32[]{:S(2)}) collective-permute-start(bf16[128,1024]{1,0:T(8,128)(2,1)} %constant_dynamic-slice_fusion.refs_1_), channel_id=1, source_target_pairs={{0,1},{1,0},{2,3},{3,2},{4,5},{5,4},{6,7},{7,6},{8,9},{9,8},{10,11... | collective-permute-start | bytes 786440 | tf_op jit(solution)/shard_map/ppermute | solution.py:230
  219.5 23.9 %copy-start.13 = (s32[256]{0:T(256)S(1)}, s32[256]{0:T(256)}, u32[]{:S(2)}) copy-start(s32[256]{0:T(256)} %copy-done.12) | copy-start | bytes 3076
  223.4 1.7 collective-permute-start.4
  249.3 21.4 %all-to-all-start.6 = ((bf16[8,136,256]{2,1,0:T(8,128)(2,1)}), bf16[8,136,256]{2,1,0:T(8,128)(2,1)}, u32[]{:S(2)}, u32[]{:S(2)}) async-start(bf16[8,136,256]{2,1,0:T(8,128)(2,1)} %pad_maximum_fusion), calls=%async_computation.6 | async-start | bytes 1114112 | tf_op jit(solution)/shard_map/all_to_all | solution.py:334
  253.5 34.8 %copy-start.11 = (bf16[2048]{0:T(1024)(128)(2,1)S(1)}, bf16[2048]{0:T(1024)(128)(2,1)}, u32[]{:S(2)}) copy-start(bf16[2048]{0:T(1024)(128)(2,1)} %param.30) | copy-start | bytes 12292
  278.5 15.8 %all-to-all-start.7 = ((bf16[32,2,1024]{2,1,0:T(2,128)(2,1)}), bf16[32,2,1024]{2,1,0:T(2,128)(2,1)}, u32[]{:S(2)}, u32[]{:S(2)}) async-start(bf16[32,2,1024]{2,1,0:T(2,128)(2,1)} %reshape.448), calls=%async_computation.7 | async-start | bytes 262144 | tf_op jit(solution)/shard_map/all_to_all | solution.py:226
  287.4 17.0 %copy-start.5 = (bf16[128,256]{1,0:T(8,128)(2,1)S(1)}, bf16[128,256]{1,0:T(8,128)(2,1)}, u32[]{:S(2)}) copy-start(bf16[128,256]{1,0:T(8,128)(2,1)} %copy-done.4) | copy-start | bytes 196612
  298.8 18.4 %all-to-all-start.8 = ((f32[256,1,32]{2,1,0:T(1,128)}), f32[256,1,32]{2,1,0:T(1,128)S(1)}, u32[]{:S(2)}, u32[]{:S(2)}) async-start(f32[256,1,32]{2,1,0:T(1,128)} %bitcast.99), calls=%async_computation.8 | async-start | bytes 262144 | tf_op jit(solution)/shard_map/all_to_all | solution.py:342
  (6 other events, 6.7 us)

commit v2 on v1

--- a/solution.py
+++ b/solution.py
@@ -8,6 +8,7 @@
 HD = 128
 TOPK = 6
 CAP = 32
+SHARE = CAP // 2
 
 REQ = ("zh", "x", "y")
 TP = ("zl", "core")
@@ -94,9 +95,13 @@
     )(lengths, q, k, v, old, w_out)
 
 
-def expert_body(
-    place_ref, a_ref, b_ref, gain_ref, router_ref, in_ref, down_ref, om_ref, ot_ref, x_ref, routed
-):
+def dot_nt(a, b):
+    return lax.dot_general(a, b, (((1,), (1,)), ((), ())), preferred_element_type=f32)
+
+
+def expert_body(place_ref, a_ref, b_ref, gain_ref, router_ref, *refs, routed):
+    om_ref, ot_ref, x_ref = refs[-3:]
+    weights = refs[:-3]
     first = place_ref[0] == 0
     width = x_ref.shape[1]
     feat = width // 8
@@ -118,12 +123,16 @@
     x = x_ref[...].astype(f32)
     scale = lax.rsqrt(jnp.mean(x * x, axis=-1, keepdims=True) + epsilon)
     rows = (x * scale * gain_ref[...].astype(f32)).astype(bf16)
-    gate = jnp.dot(rows, in_ref[0], preferred_element_type=f32)
-    up = jnp.dot(rows, in_ref[1], preferred_element_type=f32)
-    inner = (gate / (1.0 + jnp.exp(-gate)) * up).astype(bf16)
-    out = jnp.dot(inner, down_ref[...], preferred_element_type=f32)
+    out = None
+    for i in range(0, len(weights), 2):
+        in_ref, down_ref = weights[i : i + 2]
+        gate = dot_nt(rows, in_ref[0])
+        up = dot_nt(rows, in_ref[1])
+        inner = (gate / (1.0 + jnp.exp(-gate)) * up).astype(bf16)
+        term = jnp.dot(inner, down_ref[...], preferred_element_type=f32)
+        out = term if out is None else out + term
     if routed:
-        logits = jnp.dot(rows, router_ref[...], preferred_element_type=f32)
+        logits = dot_nt(rows, router_ref[...])
         raised = jnp.exp(logits - jnp.max(logits, axis=-1, keepdims=True))
         own = lax.broadcasted_iota(jnp.int32, logits.shape, 1) == place_ref[1]
         picked = jnp.sum(jnp.where(own, raised, 0.0), axis=-1, keepdims=True)
@@ -145,10 +154,10 @@
         drain(ot_ref, om_ref)
 
 
-def expert_mlp(place, rows_mine, rows_theirs, gain, w_router, w_in, w_down, block, routed):
+def expert_mlp(place, rows_mine, rows_theirs, gain, router, weights, block, routed):
     count, half = rows_mine.shape
     width = 2 * half
-    hidden = w_down.shape[0]
+    hidden = sum(w.shape[0] for w in weights[1::2])
     row_spec = pl.BlockSpec((block, half), lambda i: (i, 0))
 
     def whole(array):
@@ -158,21 +167,14 @@
     shape = jax.ShapeDtypeStruct((count, half), bf16)
 
     def body(*refs):
-        expert_body(*refs, routed)
+        expert_body(*refs, routed=routed)
 
     return pl.pallas_call(
         body,
         grid=(count // block,),
         out_shape=(shape, shape),
-        in_specs=[
-            pl.BlockSpec(memory_space=pltpu.SMEM),
-            row_spec,
-            row_spec,
-            whole(gain),
-            whole(w_router),
-            whole(w_in),
-            whole(w_down),
-        ],
+        in_specs=[pl.BlockSpec(memory_space=pltpu.SMEM), row_spec, row_spec]
+        + [whole(array) for array in (gain, router) + weights],
         out_specs=(row_spec, row_spec),
         scratch_shapes=[pltpu.VMEM((block, width), bf16)],
         cost_estimate=pl.CostEstimate(
@@ -181,22 +183,115 @@
             bytes_accessed=8 * count * half + 6 * width * hidden,
         ),
         name="routed_mlp" if routed else "shared_mlp",
-    )(place, rows_mine, rows_theirs, gain, w_router, w_in, w_down)
+    )(place, rows_mine, rows_theirs, gain, router, *weights)
+
+
+def dispatch_body(chosen_ref, parts_ref, out_ref, rows_ref):
+    new, feat = parts_ref.shape[1:]
+    for part in range(4):
+        lanes = slice(part * feat, (part + 1) * feat)
+        both = jnp.concatenate([parts_ref[part], parts_ref[4 + part]], axis=0)
+        rows_ref[:, lanes] = both
+        out_ref[:, lanes] = jnp.dot(
+            chosen_ref[...], both, preferred_element_type=f32
+        ).astype(bf16)
+
+
+def dispatch(chosen_t, parts):
+    vm = pl.BlockSpec(memory_space=pltpu.VMEM)
+    slots, tokens = chosen_t.shape
+    half = 4 * parts.shape[2]
+    return pl.pallas_call(
+        dispatch_body,
+        out_shape=(
+            jax.ShapeDtypeStruct((slots, half), bf16),
+            jax.ShapeDtypeStruct((tokens, half), bf16),
+        ),
+        in_specs=[vm, vm],
+        out_specs=(vm, vm),
+        name="dispatch",
+    )(chosen_t, parts)
+
+
+def combine_body(place_ref, chosen_ref, back_ref, mine_ref, theirs_ref, out_ref):
+    tokens = chosen_ref.shape[0]
+    new = tokens // 2
+    feat = out_ref.shape[2]
+    for zo in range(2):
+        own = (place_ref[2] == zo).astype(f32)
+        total = jnp.dot(
+            chosen_ref[zo * new : (zo + 1) * new, :], back_ref[...], preferred_element_type=f32
+        )
+        total = total + own * (mine_ref[...].astype(f32) + theirs_ref[...].astype(f32))
+        for part in range(4):
+            piece = total[:, part * feat : (part + 1) * feat]
+            out_ref[zo * 4 + part, :new, :] = piece.astype(bf16)
+            row = piece[new - 1 :, :].astype(bf16)
+            for dest in range(8):
+                out_ref[dest, new + zo * 4 + part : new + zo * 4 + part + 1, :] = row
+
+
+def combine(place, chosen, back, mine, theirs):
+    vm = pl.BlockSpec(memory_space=pltpu.VMEM)
+    tokens = chosen.shape[0]
+    half = back.shape[1]
+    return pl.pallas_call(
+        combine_body,
+        out_shape=jax.ShapeDtypeStruct((8, tokens // 2 + 8, half // 4), bf16),
+        in_specs=[pl.BlockSpec(memory_space=pltpu.SMEM), vm, vm, vm, vm],
+        out_specs=vm,
+        name="combine",
+    )(place, chosen, back, mine, theirs)
+
+
+def finish_body(parts_ref, share_ref, resid_ref, out_ref, last_ref):
+    new, feat = share_ref.shape
+    total = parts_ref[0].astype(f32)
+    for part in range(1, 8):
+        total = total + parts_ref[part].astype(f32)
+    out_ref[...] = (share_ref[...].astype(f32) + total[:new]).astype(bf16)
+    for zo in range(2):
+        for part in range(4):
+            lanes = slice(part * feat, (part + 1) * feat)
+            tail = resid_ref[(zo + 1) * new - 16 : (zo + 1) * new, lanes].astype(f32)
+            at = new + zo * 4 + part
+            row = tail[15:16] + total[at : at + 1]
+            for sub in range(2):
+                r = (zo * 4 + part) * 2 + sub
+                piece = row[:, sub * 128 : (sub + 1) * 128]
+                last_ref[:, r : r + 1, :] = jnp.broadcast_to(
+                    piece.astype(bf16)[None], (last_ref.shape[0], 1, 128)
+                )
+
+
+def finish(parts, share, resid, copies):
+    vm = pl.BlockSpec(memory_space=pltpu.VMEM)
+    return pl.pallas_call(
+        finish_body,
+        out_shape=(
+            jax.ShapeDtypeStruct(share.shape, bf16),
+            jax.ShapeDtypeStruct((copies, 16, 128), bf16),
+        ),
+        in_specs=[vm, vm, vm],
+        out_specs=(vm, vm),
+        name="finish",
+    )(parts, share, resid)
 
 
 def head_body(last_ref, gain_ref, w_ref, top_ref, rms_ref):
-    rows, width = last_ref.shape
-    plane = rows // 2
-    feat = width // 8
+    plane = last_ref.shape[0] // 2
+    rows = jnp.swapaxes(last_ref[...].astype(f32), 0, 1)
     halves = []
     for zo in range(2):
         pieces = []
         for part in range(4):
             for core in range(2):
-                lanes = slice((zo * 4 + part) * feat, (zo * 4 + part + 1) * feat)
-                pieces.append(last_ref[core * plane : (core + 1) * plane, lanes])
+                for sub in range(2):
+                    pieces.append(
+                        rows[(zo * 4 + part) * 2 + sub, core * plane : (core + 1) * plane]
+                    )
         halves.append(jnp.concatenate(pieces, axis=1))
-    tok = jnp.concatenate(halves, axis=0).astype(f32)
+    tok = jnp.concatenate(halves, axis=0)
     rms = jnp.sqrt(jnp.mean(tok * tok, axis=-1, keepdims=True) + epsilon)
     head_in = (tok / rms * gain_ref[...].astype(f32)).astype(bf16)
     logits = lax.dot_general(
@@ -257,7 +352,13 @@
     half = width // 2
     experts_all = w_router.shape[1]
     plane = experts_all // 2
-    slots = plane * 2 * CAP
+    slots = plane * 2 * SHARE
+
+    neighbours = [(0, 1), (1, 0), (2, 3), (3, 2)]
+    w_in = w_exp_in[0].swapaxes(1, 2)
+    w_down = w_exp_down[0]
+    pair_in = lax.ppermute(w_in, "zl", neighbours)
+    pair_down = lax.ppermute(w_down, "zl", neighbours)
 
     reqs = holder_slot.shape[0]
     ctx = kv_cache.shape[2]
@@ -281,9 +382,6 @@
     parts = lax.all_to_all(parts, TP, 0, 0, tiled=True)
     attn_total = jnp.sum(parts.astype(f32), axis=0)
     resid_share = (hidden.astype(f32) + attn_total).astype(bf16)
-    resid = spread(resid_share, Z, 8).reshape(2, 4, new, feat)
-    resid = resid.transpose(0, 2, 1, 3).reshape(2 * new, half)
-
     ids = jnp.where(
         zh == 0, jnp.stack([expert_ids, ids_there]), jnp.stack([ids_there, expert_ids])
     )
@@ -293,50 +391,53 @@
     before = (order[:, None] > order[None, :]).astype(bf16)
     earlier = jnp.einsum("pq,rqe->rpe", before, onehot, preferred_element_type=f32)
     rank = jnp.sum(earlier * onehot.astype(f32), axis=2).astype(jnp.int32)
+    rank = rank - (zl % 2) * SHARE
     there = picks - zh * plane
-    slot = (there * 2 + jnp.arange(2, dtype=jnp.int32)[:, None]) * CAP + rank
-    slot = jnp.where((there >= 0) & (there < plane), slot, -1).reshape(2 * new, TOPK)
+    slot = (there * 2 + jnp.arange(2, dtype=jnp.int32)[:, None]) * SHARE + rank
+    here = (there >= 0) & (there < plane) & (rank >= 0) & (rank < SHARE)
+    slot = jnp.where(here, slot, -1).reshape(2 * new, TOPK)
     slot_iota = jnp.arange(slots, dtype=jnp.int32)
     chosen = jnp.zeros((2 * new, slots), bf16)
+    chosen_t = jnp.zeros((slots, 2 * new), bf16)
     for pick in range(TOPK):
         chosen = chosen + (slot[:, pick : pick + 1] == slot_iota[None, :]).astype(bf16)
-
-    outgoing = lax.dot_general(
-        chosen, resid, (((0,), (0,)), ((), ())), preferred_element_type=f32
-    ).astype(bf16)
+        chosen_t = chosen_t + (slot[:, pick][None, :] == slot_iota[:, None]).astype(bf16)
+
+    outgoing, resid = dispatch(chosen_t, spread(resid_share, Z, 8))
     rows_mine = lax.all_to_all(
-        outgoing.reshape(plane, 2 * CAP, half), ("x", "y"), 0, 0, tiled=True
+        outgoing.reshape(plane, 2 * SHARE, half), ("x", "y"), 0, 0, tiled=True
     ).reshape(slots, half)
     rows_theirs = swap_core(rows_mine)
 
-    place = jnp.stack([core, expert]).astype(jnp.int32)
+    place = jnp.stack([core, expert, zh]).astype(jnp.int32)
     gain = ffn_gain[None]
+    router = w_router.T
     own_mine = lax.dynamic_slice_in_dim(resid, zh * new, new, 0)
     shared_mine, shared_theirs = expert_mlp(
-        place, own_mine, swap_core(own_mine), gain, w_router, w_sh_in, w_sh_down, new, False
-    )
-    shared = shared_mine.astype(f32) + swap_core(shared_theirs).astype(f32)
+        place,
+        own_mine,
+        swap_core(own_mine),
+        gain,
+        router,
+        (w_sh_in.swapaxes(1, 2), w_sh_down),
+        new,
+        False,
+    )
+    shared_theirs = swap_core(shared_theirs)
 
     served_mine, served_theirs = expert_mlp(
-        place, rows_mine, rows_theirs, gain, w_router, w_exp_in[0], w_exp_down[0], 256, True
+        place, rows_mine, rows_theirs, gain, router, (w_in, w_down, pair_in, pair_down), 256, True
     )
     served = (served_mine.astype(f32) + swap_core(served_theirs).astype(f32)).astype(bf16)
     returned = lax.all_to_all(
-        served.reshape(plane, 2 * CAP, half), ("x", "y"), 0, 0, tiled=True
+        served.reshape(plane, 2 * SHARE, half), ("x", "y"), 0, 0, tiled=True
     ).reshape(slots, half)
-    share = jnp.dot(chosen, returned, preferred_element_type=f32).reshape(2, new, half)
-    is_own = (jnp.arange(2) == zh)[:, None, None]
-    share = (share + jnp.where(is_own, shared[None], 0.0)).astype(bf16)
-
-    cut = share.reshape(2, new, 4, feat).transpose(0, 2, 1, 3).reshape(8, new, feat)
-    last = share[:, new - 1].reshape(1, 8, feat)
-    packed = jnp.concatenate([cut, jnp.broadcast_to(last, (8, 8, feat))], axis=1)
-    summed = jnp.sum(lax.all_to_all(packed, Z, 0, 0, tiled=True).astype(f32), axis=0)
-    out_hidden = (resid_share.astype(f32) + summed[:new]).astype(bf16)
-    last_resid = resid.reshape(2, new, half)[:, new - 1].astype(f32)
-    last_half = (last_resid + summed[new:].reshape(2, half)).astype(bf16)
-
-    last_all = spread(last_half.reshape(width), ("core", "x", "y"), reqs)
+
+    packed = combine(place, chosen, returned, shared_mine, shared_theirs)
+    summed = lax.all_to_all(packed, Z, 0, 0, tiled=True)
+    out_hidden, last = finish(summed, resid_share, resid, reqs)
+
+    last_all = lax.all_to_all(last, ("core", "x", "y"), 0, 0, tiled=True)
     tops, rms = head(last_all, final_gain[None], w_head)
     last_rms = rms.reshape(reqs)
     top_logit = jnp.max(lax.all_to_all(tops, ALL, 0, 0, tiled=True), axis=0)

time: 320 us -> 305 us (0.953)
  local copies, waits for them, and re-layouts: 44.8 us -> 26.7 us
  blocking collectives: 65.8 us -> 52.3 us
  waiting for transfers between devices: 84.2 us -> 97.2 us
  starting transfers between devices: 66.5 us -> 77 us
  other arithmetic: 26.5 us -> 17.5 us
  Pallas kernels: 21.8 us -> 28 us
  matrix products: 6.57 us -> 2.64 us
    ppermute x0 -> x2, waiting for transfers between devices: none -> 26.9 us  [the longest x1 26.9 us: local(): pair_down = lax.ppermute(w_down, 'zl', neighbours)]
    all_to_all x1, blocking collectives: 31.1 us -> 17.6 us  [local(): summed = lax.all_to_all(packed, Z, 0, 0, tiled=True)]
    all_to_all x2 -> x3, starting transfers between devices: 8.62 us -> 22.1 us  [the longest x1 11.2 us: local(): last_all = lax.all_to_all(last, ('core', 'x', 'y'), 0, 0, tiled=True)]
    all_to_all x1, waiting for transfers between devices: 14.3 us -> 1.52 us  [local(): parts = lax.all_to_all(parts, TP, 0, 0, tiled=True)]
    unnamed x44 -> x27, local copies, waits for them, and re-layouts: 15.9 us -> 4.19 us
    all_to_all x2 -> x1, starting transfers between devices: 12.3 us -> 4.8 us  [spread(): return lax.all_to_all(wide, axes, 0, 0, tiled=True)]
    pallas_call x0 -> x3, Pallas kernels: none -> 7.49 us  [the longest x1 2.75 us: combine(): pl.pallas_call(combine_body, out_shape=jax.ShapeDtypeStruct((8, tokens //...]
    ppermute x1, waiting for transfers between devices: 0.01 us -> 7.19 us  [local(): ids_there = lax.ppermute(expert_ids, 'zh', [(0, 1), (1, 0)])]
  transfers between devices with their start and end apart: 13 -> 15, of which waited for: 9 -> 11; matrix products, arithmetic and copies ran while one was open for 15% -> 11% of each run, Pallas kernels for 1% -> 1%
where the time goes in v2:
time: 305 us; the launch traced here: 303 us
  waiting for transfers between devices  97.2 us (32%)
  starting transfers between devices  77 us (25%)
  blocking collectives  52.3 us (17%)
  Pallas kernels  28 us (9%)
  local copies, waits for them, and re-layouts  26.7 us (9%)
  other arithmetic  17.5 us (6%)
    all_gather x1, blocking collectives, local(): own = lax.all_gather(hidden, TP, axis=1, tiled=True)  34.7 us
    ppermute x1, waiting for transfers between devices, local(): pair_down = lax.ppermute(w_down, 'zl', neighbours)  26.9 us
    all_to_all x1, blocking collectives, local(): summed = lax.all_to_all(packed, Z, 0, 0, tiled=True)  17.6 us
    all_to_all x1, waiting for transfers between devices, local(): lax.all_to_all(outgoing.reshape(plane, 2 * SHARE, half), ('x', 'y'), 0, 0...  14.9 us
    all_to_all x1, starting transfers between devices, local(): leg = lax.all_to_all(pieces, REQ, 0, 0, tiled=True)  14.6 us
    pallas_call x2, Pallas kernels, expert_mlp(): pl.pallas_call(body, grid=(count // block,), out_shape=(shape, shape), in...  14.2 us
    all_to_all x1, waiting for transfers between devices, local(): old = lax.all_to_all(leg, REQ, 0, 0, tiled=True)  12.9 us
    all_to_all x1, starting transfers between devices, local(): last_all = lax.all_to_all(last, ('core', 'x', 'y'), 0, 0, tiled=True)  11.2 us
  transfers between devices with their start and end apart: 15, of which 11 were waited for; matrix products, arithmetic and copies ran while one was open for 11% of the time, Pallas kernels for 1%

profile of v2, /device:TPU:1, one launch (start us, length us, event | category | flops | bytes accessed | tf_op | source)
XLA Modules:
  0.0 303.0 jit_solution(7071691533031497081)
XLA Ops:
  3.1 14.6 %all-to-all-start = ((bf16[32,2,32,256]{3,2,1,0:T(8,128)(2,1)}), bf16[32,2,32,256]{3,2,1,0:T(8,128)(2,1)}, u32[]{:S(2)}, u32[]{:S(2)}) async-start(bf16[32,2,32,256]{3,2,1,0:T(8,128)(2,1)} %copy.30), calls=%async_computation | async-start | bytes 2097152 | tf_op jit(solution)/shard_map/all_to_all | solution.py:366
  18.5 34.7 %all_gather.3 = bf16[128,2048]{1,0:T(8,128)(2,1)S(1)} all-gather(bf16[128,256]{1,0:T(8,128)(2,1)S(1)} %copy-done.6), channel_id=1, replica_groups=mesh['zh'=2,'x'=4,'y'=4,'zl'=4,'core'=2] {'zl','core'}, dimensions={1}, use_global_device_ids=true | all-gather | bytes 589824 | tf_op jit(solution)/shard_map/all_gather | solution.py:371
  54.2 2.8 gather_fusion
  57.1 11.2 %all-to-all-start.1 = ((bf16[32,2,32,256]{3,2,1,0:T(8,128)(2,1)}), bf16[32,2,32,256]{3,2,1,0:T(8,128)(2,1)}, u32[]{:S(2)}, u32[]{:S(2)}) async-start(bf16[32,2,32,256]{3,2,1,0:T(8,128)(2,1)} %gather_fusion), calls=%async_computation.1 | async-start | bytes 2097152 | tf_op jit(solution)/shard_map/all_to_all | solution.py:368
  78.4 12.9 %all-to-all-done.1.old_ref = bf16[32,2,32,256]{3,2,1,0:T(8,128)(2,1)} async-done(((bf16[32,2,32,256]{3,2,1,0:T(8,128)(2,1)}), bf16[32,2,32,256]{3,2,1,0:T(8,128)(2,1)}, u32[]{:S(2)}, u32[]{:S(2)}) %all-to-all-start.1) | async-done | bytes 1048608 | tf_op jit(solution)/shard_map/all_to_all | solution.py:368
  91.3 3.9 %attend.1 = bf16[8,128,256]{2,1,0:T(8,128)(2,1)} custom-call(s32[1]{0:T(128)} %copy.37.len_ref, bf16[128,256]{1,0:T(8,128)(2,1)} %get-tuple-element.57.q_ref, bf16[128,256]{1,0:T(8,128)(2,1)} %get-tuple-element.56.k_ref, bf16[128,256]{1,0:T(8,128)(2,1)} %slice_bitcast_fusion.v_ref, bf16[32,2,32,256]{3,2,1,0:T(8,128)(2,1)} %all-to-all-done.1.old_ref, ...), custom_call_target="tpu_custom_call" | custom-call | tf_op jit(solution)/shard_map/attend/pallas_call | solution.py:89
  95.2 11.2 %all-to-all-start.2 = ((bf16[8,128,256]{2,1,0:T(8,128)(2,1)}), bf16[8,128,256]{2,1,0:T(8,128)(2,1)}, u32[]{:S(2)}, u32[]{:S(2)}) async-start(bf16[8,128,256]{2,1,0:T(8,128)(2,1)} %attend.1), calls=%async_computation.2 | async-start | bytes 1048576 | tf_op jit(solution)/shard_map/all_to_all | solution.py:382
  109.1 7.2 %collective-permute-done = s32[128,6]{0,1:T(8,128)S(1)} collective-permute-done((s32[128,6]{0,1:T(8,128)S(1)}, s32[128,6]{0,1:T(8,128)S(1)}, u32[]{:S(2)}, u32[]{:S(2)}) %collective-permute-start) | collective-permute-done | bytes 3104 | tf_op jit(solution)/shard_map/ppermute | solution.py:370
  124.6 4.8 %all-to-all-start.3 = ((bf16[8,128,256]{2,1,0:T(8,128)(2,1)}), bf16[8,128,256]{2,1,0:T(8,128)(2,1)}, u32[]{:S(2)}, u32[]{:S(2)}) async-start(bf16[8,128,256]{2,1,0:T(8,128)(2,1)} %broadcast_in_dim.15), calls=%async_computation.3 | async-start | bytes 1048576 | tf_op jit(solution)/shard_map/all_to_all | solution.py:321
  136.4 9.6 %all-to-all-done.3.parts_ref = bf16[8,128,256]{2,1,0:T(8,128)(2,1)} async-done(((bf16[8,128,256]{2,1,0:T(8,128)(2,1)}), bf16[8,128,256]{2,1,0:T(8,128)(2,1)}, u32[]{:S(2)}, u32[]{:S(2)}) %all-to-all-start.3) | async-done | bytes 524320 | tf_op jit(solution)/shard_map/all_to_all | solution.py:321
  148.6 4.3 %all-to-all-start.4 = ((bf16[16,32,1024]{2,1,0:T(8,128)(2,1)}), bf16[16,32,1024]{2,1,0:T(8,128)(2,1)}, u32[]{:S(2)}, u32[]{:S(2)}) async-start(bf16[16,32,1024]{2,1,0:T(8,128)(2,1)} %bitcast.61), calls=%async_computation.4 | async-start | bytes 2097152 | tf_op jit(solution)/shard_map/all_to_all | solution.py:407
  153.0 14.9 %all-to-all-done.4 = bf16[16,32,1024]{2,1,0:T(8,128)(2,1)} async-done(((bf16[16,32,1024]{2,1,0:T(8,128)(2,1)}), bf16[16,32,1024]{2,1,0:T(8,128)(2,1)}, u32[]{:S(2)}, u32[]{:S(2)}) %all-to-all-start.4) | async-done | bytes 1048608 | tf_op jit(solution)/shard_map/all_to_all | solution.py:407
  167.9 3.1 %collective-permute-start.1 = (bf16[512,1024]{1,0:T(8,128)(2,1)}, bf16[512,1024]{1,0:T(8,128)(2,1)}, u32[]{:S(2)}, u32[]{:S(2)}) collective-permute-start(bf16[512,1024]{1,0:T(8,128)(2,1)} %bitcast.13.refs_1_), channel_id=1, source_target_pairs={{0,1},{1,0},{2,3},{3,2},{4,5},{5,4},{6,7},{7,6},{8,9},{9,8},{10,11... | collective-permute-start | bytes 3145736 | tf_op jit(solution)/shard_map/ppermute | solution.py:325
  173.0 26.9 %collective-permute-done.3.refs_8_ = bf16[176,2048]{1,0:T(8,128)(2,1)} collective-permute-done((bf16[176,2048]{1,0:T(8,128)(2,1)}, bf16[176,2048]{1,0:T(8,128)(2,1)}, u32[]{:S(2)}, u32[]{:S(2)}) %collective-permute-start.3) | collective-permute-done | bytes 720928 | tf_op jit(solution)/shard_map/ppermute | solution.py:361
  199.9 10.4 %routed_mlp.1 = (bf16[512,1024]{1,0:T(8,128)(2,1)}, bf16[512,1024]{1,0:T(8,128)(2,1)}) custom-call(s32[3]{0:T(128)} %pad_add_fusion.refs_0_.place_ref, bf16[512,1024]{1,0:T(8,128)(2,1)} %bitcast.13.refs_1_, bf16[512,1024]{1,0:T(8,128)(2,1)} %collective-permute-done.1.refs_2_, bf16[1,2048]{1,0:T(2,128)(2,1)} %broadcast_in_dim.16.refs_3_, ...), custom_call_target="tpu_custom_call" | custom-call | flops 2214592512 | bytes 8519680 | tf_op jit(solution)/shard_map/routed_mlp/pallas_call | solution.py:172
  210.3 2.9 collective-permute-start.4
  218.3 6.5 %all-to-all-start.5 = ((bf16[16,32,1024]{2,1,0:T(8,128)(2,1)}), bf16[16,32,1024]{2,1,0:T(8,128)(2,1)}, u32[]{:S(2)}, u32[]{:S(2)}) async-start(bf16[16,32,1024]{2,1,0:T(8,128)(2,1)} %bitcast.58), calls=%async_computation.5 | async-start | bytes 2097152 | tf_op jit(solution)/shard_map/all_to_all | solution.py:432
  229.0 3.7 %shared_mlp.1 = (bf16[128,1024]{1,0:T(8,128)(2,1)}, bf16[128,1024]{1,0:T(8,128)(2,1)}) custom-call(s32[3]{0:T(128)} %pad_add_fusion.refs_0_.place_ref, bf16[128,1024]{1,0:T(8,128)(2,1)} %copy-done.2, bf16[128,1024]{1,0:T(8,128)(2,1)} %copy-done.5, bf16[1,2048]{1,0:T(2,128)(2,1)} %broadcast_in_dim.16.refs_3_, bf16[32,2048]{1,0:T(8,128)(2,1)} %bitcast.65, ...), custom_call_target="tpu_custom_call" | custom-call | flops 276824064 | bytes 3211264 | tf_op jit(solution)/shard_map/shared_mlp/pallas_call | solution.py:172
  234.9 5.0 %all-to-all-done.5 = bf16[16,32,1024]{2,1,0:T(8,128)(2,1)} async-done(((bf16[16,32,1024]{2,1,0:T(8,128)(2,1)}), bf16[16,32,1024]{2,1,0:T(8,128)(2,1)}, u32[]{:S(2)}, u32[]{:S(2)}) %all-to-all-start.5) | async-done | bytes 1048608 | tf_op jit(solution)/shard_map/all_to_all | solution.py:432
  242.6 17.6 %all_to_all.49.parts_ref = bf16[8,136,256]{2,1,0:T(8,128)(2,1)} all-to-all(bf16[8,136,256]{2,1,0:T(8,128)(2,1)} %combine.1), channel_id=1, replica_groups=mesh['zh'=2,'x'=4,'y'=4,'zl'=4,'core'=2] {'zh','zl'}, dimensions={0} | all-to-all | bytes 1114112 | tf_op jit(solution)/shard_map/all_to_all | solution.py:437
  262.4 11.2 %all-to-all-start.7 = ((bf16[32,16,128]{2,1,0:T(8,128)(2,1)}), bf16[32,16,128]{2,1,0:T(8,128)(2,1)}, u32[]{:S(2)}, u32[]{:S(2)}) async-start(bf16[32,16,128]{2,1,0:T(8,128)(2,1)} %get-tuple-element.21), calls=%async_computation.7 | async-start | bytes 262144 | tf_op jit(solution)/shard_map/all_to_all | solution.py:440
  275.8 5.5 %all-to-all-done.7.last_ref = bf16[32,16,128]{2,1,0:T(8,128)(2,1)} async-done(((bf16[32,16,128]{2,1,0:T(8,128)(2,1)}), bf16[32,16,128]{2,1,0:T(8,128)(2,1)}, u32[]{:S(2)}, u32[]{:S(2)}) %all-to-all-start.7) | async-done | bytes 131104 | tf_op jit(solution)/shard_map/all_to_all | solution.py:440
  283.7 5.6 %all-to-all-start.8 = ((f32[256,1,32]{2,1,0:T(1,128)}), f32[256,1,32]{2,1,0:T(1,128)S(1)}, u32[]{:S(2)}, u32[]{:S(2)}) async-start(f32[256,1,32]{2,1,0:T(1,128)} %bitcast.66), calls=%async_computation.8 | async-start | bytes 262144 | tf_op jit(solution)/shard_map/all_to_all | solution.py:443
  292.1 10.0 %all-to-all-done.8 = f32[256,1,32]{2,1,0:T(1,128)S(1)} async-done(((f32[256,1,32]{2,1,0:T(1,128)}), f32[256,1,32]{2,1,0:T(1,128)S(1)}, u32[]{:S(2)}, u32[]{:S(2)}) %all-to-all-start.8) | async-done | bytes 32800 | tf_op jit(solution)/shard_map/all_to_all | solution.py:443
  (90 shorter events, 60.7 us)
Async XLA Ops:
  0.6 67.6 %copy-start = (bf16[3,2048,256]{2,1,0:T(8,128)(2,1)S(1)}, bf16[3,2048,256]{2,1,0:T(8,128)(2,1)}, u32[]{:S(2)}) copy-start(bf16[3,2048,256]{2,1,0:T(8,128)(2,1)} %param.18) | copy-start | bytes 9437188
  0.6 17.8 %copy-start.9 = (bf16[2048]{0:T(1024)(128)(2,1)S(1)}, bf16[2048]{0:T(1024)(128)(2,1)}, u32[]{:S(2)}) copy-start(bf16[2048]{0:T(1024)(128)(2,1)} %param.17) | copy-start | bytes 12292
  0.7 17.8 %copy-start.12 = (s32[32]{0:T(128)S(1)}, s32[32]{0:T(128)}, u32[]{:S(2)}) copy-start(s32[32]{0:T(128)} %param.21) | copy-start | bytes 388
  0.7 17.8 %copy-start.6 = (bf16[128,256]{1,0:T(8,128)(2,1)S(1)}, bf16[128,256]{1,0:T(8,128)(2,1)}, u32[]{:S(2)}) copy-start(bf16[128,256]{1,0:T(8,128)(2,1)} %param.16) | copy-start | bytes 196612
  3.1 51.1 %all-to-all-start = ((bf16[32,2,32,256]{3,2,1,0:T(8,128)(2,1)}), bf16[32,2,32,256]{3,2,1,0:T(8,128)(2,1)}, u32[]{:S(2)}, u32[]{:S(2)}) async-start(bf16[32,2,32,256]{3,2,1,0:T(8,128)(2,1)} %copy.30), calls=%async_computation | async-start | bytes 2097152 | tf_op jit(solution)/shard_map/all_to_all | solution.py:366
  53.2 0.8 copy-start.1
  57.1 34.2 %all-to-all-start.1 = ((bf16[32,2,32,256]{3,2,1,0:T(8,128)(2,1)}), bf16[32,2,32,256]{3,2,1,0:T(8,128)(2,1)}, u32[]{:S(2)}, u32[]{:S(2)}) async-start(bf16[32,2,32,256]{3,2,1,0:T(8,128)(2,1)} %gather_fusion), calls=%async_computation.1 | async-start | bytes 2097152 | tf_op jit(solution)/shard_map/all_to_all | solution.py:368
  75.7 2.1 copy-start.4
  76.9 29.5 %copy-start.10 = (s32[128,6]{0,1:T(8,128)S(1)}, s32[128,6]{0,1:T(8,128)}, u32[]{:S(2)}) copy-start(s32[128,6]{0,1:T(8,128)} %param.25) | copy-start | bytes 9220
  95.2 26.0 %all-to-all-start.2 = ((bf16[8,128,256]{2,1,0:T(8,128)(2,1)}), bf16[8,128,256]{2,1,0:T(8,128)(2,1)}, u32[]{:S(2)}, u32[]{:S(2)}) async-start(bf16[8,128,256]{2,1,0:T(8,128)(2,1)} %attend.1), calls=%async_computation.2 | async-start | bytes 1048576 | tf_op jit(solution)/shard_map/all_to_all | solution.py:382
  106.4 9.9 %collective-permute-start = (s32[128,6]{0,1:T(8,128)S(1)}, s32[128,6]{0,1:T(8,128)S(1)}, u32[]{:S(2)}, u32[]{:S(2)}) collective-permute-start(s32[128,6]{0,1:T(8,128)S(1)} %copy-done.10), channel_id=1, source_target_pairs={{0,128},{128,0},{1,129},{129,1},{2,130},{130,2},{3,131},{131,3},{4... | collective-permute-start | bytes 9224 | tf_op jit(solution)/shard_map/ppermute | solution.py:370
  124.6 21.4 %all-to-all-start.3 = ((bf16[8,128,256]{2,1,0:T(8,128)(2,1)}), bf16[8,128,256]{2,1,0:T(8,128)(2,1)}, u32[]{:S(2)}, u32[]{:S(2)}) async-start(bf16[8,128,256]{2,1,0:T(8,128)(2,1)} %broadcast_in_dim.15), calls=%async_computation.3 | async-start | bytes 1048576 | tf_op jit(solution)/shard_map/all_to_all | solution.py:321
  148.6 19.3 %all-to-all-start.4 = ((bf16[16,32,1024]{2,1,0:T(8,128)(2,1)}), bf16[16,32,1024]{2,1,0:T(8,128)(2,1)}, u32[]{:S(2)}, u32[]{:S(2)}) async-start(bf16[16,32,1024]{2,1,0:T(8,128)(2,1)} %bitcast.61), calls=%async_computation.4 | async-start | bytes 2097152 | tf_op jit(solution)/shard_map/all_to_all | solution.py:407
  152.9 47.0 %collective-permute-start.2 = (bf16[2,176,2048]{2,1,0:T(8,128)(2,1)}, bf16[2,176,2048]{2,1,0:T(8,128)(2,1)}, u32[]{:S(2)}, u32[]{:S(2)}) collective-permute-start(bf16[2,176,2048]{2,1,0:T(8,128)(2,1)} %bitcast.67), channel_id=1, source_target_pairs={{0,2},{2,0},{4,6},{6,4},{1,3},{3,1},{5,7},{7,5},{8,10},{10,8},{12,... | collective-permute-start | bytes 4325384 | tf_op jit(solution)/shard_map/ppermute | solution.py:360
  167.9 32.0 %collective-permute-start.1 = (bf16[512,1024]{1,0:T(8,128)(2,1)}, bf16[512,1024]{1,0:T(8,128)(2,1)}, u32[]{:S(2)}, u32[]{:S(2)}) collective-permute-start(bf16[512,1024]{1,0:T(8,128)(2,1)} %bitcast.13.refs_1_), channel_id=1, source_target_pairs={{0,1},{1,0},{2,3},{3,2},{4,5},{5,4},{6,7},{7,6},{8,9},{9,8},{10,11... | collective-permute-start | bytes 3145736 | tf_op jit(solution)/shard_map/ppermute | solution.py:325
  171.0 28.9 %collective-permute-start.3 = (bf16[176,2048]{1,0:T(8,128)(2,1)}, bf16[176,2048]{1,0:T(8,128)(2,1)}, u32[]{:S(2)}, u32[]{:S(2)}) collective-permute-start(bf16[176,2048]{1,0:T(8,128)(2,1)} %bitcast.69), channel_id=1, source_target_pairs={{0,2},{2,0},{4,6},{6,4},{1,3},{3,1},{5,7},{7,5},{8,10},{10,8},{12,... | collective-permute-start | bytes 2162696 | tf_op jit(solution)/shard_map/ppermute | solution.py:361
  210.3 5.4 %collective-permute-start.4 = (bf16[512,1024]{1,0:T(8,128)(2,1)}, bf16[512,1024]{1,0:T(8,128)(2,1)S(1)}, u32[]{:S(2)}, u32[]{:S(2)}) collective-permute-start(bf16[512,1024]{1,0:T(8,128)(2,1)} %get-tuple-element.16), channel_id=1, source_target_pairs={{0,1},{1,0},{2,3},{3,2},{4,5},{5,4},{6,7},{7,6},{8,9},{9,8},{10,11... | collective-permute-start | bytes 3145736 | tf_op jit(solution)/shard_map/ppermute | solution.py:325
  218.3 21.6 %all-to-all-start.5 = ((bf16[16,32,1024]{2,1,0:T(8,128)(2,1)}), bf16[16,32,1024]{2,1,0:T(8,128)(2,1)}, u32[]{:S(2)}, u32[]{:S(2)}) async-start(bf16[16,32,1024]{2,1,0:T(8,128)(2,1)} %bitcast.58), calls=%async_computation.5 | async-start | bytes 2097152 | tf_op jit(solution)/shard_map/all_to_all | solution.py:432
  226.5 1.8 collective-permute-start.5
  228.3 0.7 copy-start.5
  232.8 2.1 collective-permute-start.6
  239.9 35.3 %copy-start.11 = (bf16[2048]{0:T(1024)(128)(2,1)S(1)}, bf16[2048]{0:T(1024)(128)(2,1)}, u32[]{:S(2)}) copy-start(bf16[2048]{0:T(1024)(128)(2,1)} %param.30) | copy-start | bytes 12292
  262.4 18.8 %all-to-all-start.7 = ((bf16[32,16,128]{2,1,0:T(8,128)(2,1)}), bf16[32,16,128]{2,1,0:T(8,128)(2,1)}, u32[]{:S(2)}, u32[]{:S(2)}) async-start(bf16[32,16,128]{2,1,0:T(8,128)(2,1)} %get-tuple-element.21), calls=%async_computation.7 | async-start | bytes 262144 | tf_op jit(solution)/shard_map/all_to_all | solution.py:440
  283.7 18.5 %all-to-all-start.8 = ((f32[256,1,32]{2,1,0:T(1,128)}), f32[256,1,32]{2,1,0:T(1,128)S(1)}, u32[]{:S(2)}, u32[]{:S(2)}) async-start(f32[256,1,32]{2,1,0:T(1,128)} %bitcast.66), calls=%async_computation.8 | async-start | bytes 262144 | tf_op jit(solution)/shard_map/all_to_all | solution.py:443
  (4 other events, 2.5 us)

commit v3 on v2

v3 whole, which is shorter than its diff:
```python
import jax
import jax.numpy as jnp
from jax import lax
from jax.sharding import Mesh, PartitionSpec as P
from jax.experimental import pallas as pl
from jax.experimental.pallas import tpu as pltpu

HD = 128
TOPK = 6
CAP = 32
SHARE = CAP // 2

REQ = ("zh", "x", "y")
TP = ("zl", "core")
COL = ("zh", "zl", "core")
Z = ("zh", "zl")
ALL = ("zh", "x", "y", "zl", "core")
SIZES = (2, 4, 4, 4, 2)

epsilon = 1e-06
bf16 = jnp.bfloat16
f32 = jnp.float32


def rms_scale(values, gain):
    return (
        values
        * lax.rsqrt(jnp.mean(values * values, axis=-1, keepdims=True) + epsilon)
        * gain.astype(f32)
    )


def rope_tables(length, new):
    half_len = HD // 2
    freqs = 10000.0 ** (-2.0 * jnp.arange(half_len, dtype=f32) / HD)
    positions = (length + jnp.arange(new, dtype=jnp.int32)).astype(f32)
    angles = positions[:, None] * freqs[None, :]
    cosine, sine = jnp.cos(angles), jnp.sin(angles)
    return jnp.concatenate([cosine, cosine], 1), jnp.concatenate([-sine, sine], 1)


def norm_rows(full_ref, gain_ref):
    return rms_scale(full_ref[...].astype(f32), gain_ref[...]).astype(bf16)


def rotate(values, cos_ref, sin_ref):
    heads = []
    for head in range(values.shape[1] // HD):
        piece = values[:, head * HD : (head + 1) * HD]
        heads.append(piece * cos_ref[...] + pltpu.roll(piece, HD // 2, 1) * sin_ref[...])
    return jnp.concatenate(heads, axis=1).astype(bf16)


def new_kv_body(full_ref, gain_ref, w_ref, cos_ref, sin_ref, o_ref):
    normed = norm_rows(full_ref, gain_ref)
    keys = jnp.dot(normed, w_ref[1], preferred_element_type=f32)
    o_ref[0] = rotate(keys, cos_ref, sin_ref)
    o_ref[1] = jnp.dot(normed, w_ref[2], preferred_element_type=f32).astype(bf16)


def new_kv(full, gain, w_qkv, tables):
    vm = pl.BlockSpec(memory_space=pltpu.VMEM)
    return pl.pallas_call(
        new_kv_body,
        out_shape=jax.ShapeDtypeStruct((2, full.shape[0], w_qkv.shape[2]), bf16),
        in_specs=[vm] * 5,
        out_specs=vm,
        name="new_kv",
    )(full, gain, w_qkv, *tables)


def attend_body(len_ref, full_ref, gain_ref, qkv_ref, cos_ref, sin_ref, kv_ref, w_ref, o_ref):
    length = len_ref[0]
    ctx = kv_ref.shape[2]
    new = full_ref.shape[0]
    normed = norm_rows(full_ref, gain_ref)
    q_all = rotate(jnp.dot(normed, qkv_ref[0], preferred_element_type=f32), cos_ref, sin_ref)
    k_all = rotate(jnp.dot(normed, qkv_ref[1], preferred_element_type=f32), cos_ref, sin_ref)
    v_all = jnp.dot(normed, qkv_ref[2], preferred_element_type=f32).astype(bf16)
    heads = []
    for head in range(q_all.shape[1] // HD):
        lanes = slice(head * HD, (head + 1) * HD)
        q = q_all[:, lanes]
        s_old = dot_nt(q, kv_ref[0, 0, :, lanes]) * HD ** (-0.5)
        s_new = dot_nt(q, k_all[:, lanes]) * HD ** (-0.5)
        seen_old = lax.broadcasted_iota(jnp.int32, (new, ctx), 1) < length
        seen_new = lax.broadcasted_iota(jnp.int32, (new, new), 1) <= lax.broadcasted_iota(
            jnp.int32, (new, new), 0
        )
        s_old = jnp.where(seen_old, s_old, -1e30)
        s_new = jnp.where(seen_new, s_new, -1e30)
        peak = jnp.maximum(
            jnp.max(s_old, axis=-1, keepdims=True), jnp.max(s_new, axis=-1, keepdims=True)
        )
        e_old = jnp.where(seen_old, jnp.exp(s_old - peak), 0.0)
        e_new = jnp.where(seen_new, jnp.exp(s_new - peak), 0.0)
        total = jnp.sum(e_old, axis=-1, keepdims=True) + jnp.sum(e_new, axis=-1, keepdims=True)
        w_old = (e_old / total).astype(bf16)
        w_new = (e_new / total).astype(bf16)
        out = jnp.dot(w_old, kv_ref[1, 0, :, lanes], preferred_element_type=f32) + jnp.dot(
            w_new, v_all[:, lanes], preferred_element_type=f32
        )
        heads.append(out.astype(bf16))
    attn = jnp.concatenate(heads, axis=1)
    wide = o_ref.shape[2]
    for part in range(o_ref.shape[0]):
        o_ref[part] = jnp.dot(
            attn, w_ref[:, part * wide : (part + 1) * wide], preferred_element_type=f32
        ).astype(bf16)


def attend(length, full, gain, w_qkv, tables, kv_cache, w_out):
    vm = pl.BlockSpec(memory_space=pltpu.VMEM)
    new = full.shape[0]
    feat = w_out.shape[0]
    return pl.pallas_call(
        attend_body,
        out_shape=jax.ShapeDtypeStruct((w_out.shape[1] // feat, new, feat), bf16),
        in_specs=[pl.BlockSpec(memory_space=pltpu.SMEM)] + [vm] * 7,
        out_specs=vm,
        name="attend",
    )(length, full, gain, w_qkv, *tables, kv_cache, w_out)


def spread(value, axes, count):
    wide = jnp.broadcast_to(value[None], (count,) + value.shape)
    return lax.all_to_all(wide, axes, 0, 0, tiled=True)


def swap_core(value):
    return lax.ppermute(value, "core", [(0, 1), (1, 0)])


def dot_nt(a, b):
    return lax.dot_general(a, b, (((1,), (1,)), ((), ())), preferred_element_type=f32)


def expert_rows(rows, gate_w, up_w, down_w):
    gate = dot_nt(rows, gate_w)
    up = dot_nt(rows, up_w)
    inner = (gate / (1.0 + jnp.exp(-gate)) * up).astype(bf16)
    return jnp.dot(inner, down_w, preferred_element_type=f32)


def drain(first, out, mine_ref, theirs_ref):
    feat = out.shape[1] // 8

    def store(even_ref, odd_ref):
        for part in range(4):
            piece = slice(part * feat, (part + 1) * feat)
            even_ref[:, piece] = out[:, 2 * part * feat : (2 * part + 1) * feat]
            odd_ref[:, piece] = out[:, (2 * part + 1) * feat : (2 * part + 2) * feat]

    @pl.when(first)
    def _():
        store(mine_ref, theirs_ref)

    @pl.when(jnp.logical_not(first))
    def _():
        store(theirs_ref, mine_ref)


def routed_body(
    place_ref, a_ref, b_ref, gain_ref, router_ref, in_ref, down_ref, pg_ref, pu_ref, pd_ref,
    om_ref, ot_ref, x_ref,
):
    first = place_ref[0] == 0
    feat = x_ref.shape[1] // 8

    def fill(even_ref, odd_ref):
        for part in range(4):
            piece = slice(part * feat, (part + 1) * feat)
            x_ref[:, 2 * part * feat : (2 * part + 1) * feat] = even_ref[:, piece]
            x_ref[:, (2 * part + 1) * feat : (2 * part + 2) * feat] = odd_ref[:, piece]

    @pl.when(first)
    def _():
        fill(a_ref, b_ref)

    @pl.when(jnp.logical_not(first))
    def _():
        fill(b_ref, a_ref)

    rows = norm_rows(x_ref, gain_ref)
    out = expert_rows(rows, in_ref[0], in_ref[1], down_ref[...])
    out = out + expert_rows(rows, pg_ref[...], pu_ref[...], pd_ref[...])
    logits = dot_nt(rows, router_ref[...])
    raised = jnp.exp(logits - jnp.max(logits, axis=-1, keepdims=True))
    own = lax.broadcasted_iota(jnp.int32, logits.shape, 1) == place_ref[1]
    picked = jnp.sum(jnp.where(own, raised, 0.0), axis=-1, keepdims=True)
    out = out * (picked / jnp.sum(raised, axis=-1, keepdims=True))
    drain(first, out.astype(bf16), om_ref, ot_ref)


def routed_mlp(place, rows_mine, rows_theirs, block, *shared_operands):
    count, half = rows_mine.shape
    width = 2 * half
    hidden = 2 * shared_operands[3].shape[0]
    row_spec = pl.BlockSpec((block, half), lambda i: (i, 0))

    def whole(array):
        zeros = (0,) * array.ndim
        return pl.BlockSpec(array.shape, lambda i: zeros)

    shape = jax.ShapeDtypeStruct((count, half), bf16)
    return pl.pallas_call(
        routed_body,
        grid=(count // block,),
        out_shape=(shape, shape),
        in_specs=[pl.BlockSpec(memory_space=pltpu.SMEM), row_spec, row_spec]
        + [whole(array) for array in shared_operands],
        out_specs=(row_spec, row_spec),
        scratch_shapes=[pltpu.VMEM((block, width), bf16)],
        cost_estimate=pl.CostEstimate(
            flops=6 * count * width * hidden,
            transcendentals=count * hidden,
            bytes_accessed=8 * count * half + 6 * width * hidden,
        ),
        name="routed_mlp",
    )(place, rows_mine, rows_theirs, *shared_operands)


def shared_body(place_ref, x_ref, gain_ref, in_ref, down_ref, om_ref, ot_ref):
    rows = norm_rows(x_ref, gain_ref)
    out = expert_rows(rows, in_ref[0], in_ref[1], down_ref[...])
    drain(place_ref[0] == 0, out.astype(bf16), om_ref, ot_ref)


def shared_mlp(place, rows, gain, w_in, w_down):
    vm = pl.BlockSpec(memory_space=pltpu.VMEM)
    shape = jax.ShapeDtypeStruct((rows.shape[0], rows.shape[1] // 2), bf16)
    return pl.pallas_call(
        shared_body,
        out_shape=(shape, shape),
        in_specs=[pl.BlockSpec(memory_space=pltpu.SMEM)] + [vm] * 4,
        out_specs=(vm, vm),
        name="shared_mlp",
    )(place, rows, gain, w_in, w_down)


def reorder_body(order_ref, a_ref, b_ref, o_ref):
    chunks = order_ref.shape[0]
    rows = o_ref.shape[0] // chunks
    for i in range(chunks):
        at = pl.ds(pl.multiple_of(order_ref[i] * rows, rows), rows)
        o_ref[i * rows : (i + 1) * rows, :] = (
            a_ref[at, :].astype(f32) + b_ref[at, :].astype(f32)
        ).astype(bf16)


def reorder(order, a, b):
    vm = pl.BlockSpec(memory_space=pltpu.VMEM)
    return pl.pallas_call(
        reorder_body,
        out_shape=jax.ShapeDtypeStruct(a.shape, bf16),
        in_specs=[pl.BlockSpec(memory_space=pltpu.SMEM), vm, vm],
        out_specs=vm,
        name="reorder",
    )(order, a, b)


def dispatch_body(chosen_ref, parts_ref, out_ref):
    feat = parts_ref.shape[2]
    for part in range(4):
        both = jnp.concatenate([parts_ref[part], parts_ref[4 + part]], axis=0)
        out_ref[:, part * feat : (part + 1) * feat] = jnp.dot(
            chosen_ref[...], both, preferred_element_type=f32
        ).astype(bf16)


def dispatch(chosen_t, parts):
    vm = pl.BlockSpec(memory_space=pltpu.VMEM)
    return pl.pallas_call(
        dispatch_body,
        out_shape=jax.ShapeDtypeStruct((chosen_t.shape[0], 4 * parts.shape[2]), bf16),
        in_specs=[vm, vm],
        out_specs=vm,
        name="dispatch",
    )(chosen_t, parts)


def combine_body(place_ref, chosen_ref, back_ref, mine_ref, theirs_ref, share_ref, out_ref):
    tokens = chosen_ref.shape[0]
    new = tokens // 2
    feat = out_ref.shape[2]
    for zo in range(2):
        own = (place_ref[2] == zo).astype(f32)
        total = jnp.dot(
            chosen_ref[zo * new : (zo + 1) * new, :], back_ref[...], preferred_element_type=f32
        )
        total = total + own * (mine_ref[...].astype(f32) + theirs_ref[...].astype(f32))
        for part in range(4):
            once = own * (place_ref[3] == part).astype(f32)
            piece = total[:, part * feat : (part + 1) * feat]
            piece = (piece + once * share_ref[...].astype(f32)).astype(bf16)
            out_ref[zo * 4 + part, :new, :] = piece
            row = piece[new - 1 :, :]
            for dest in range(8):
                out_ref[dest, new + zo * 4 + part : new + zo * 4 + part + 1, :] = row


def combine(place, chosen, back, mine, theirs, share):
    vm = pl.BlockSpec(memory_space=pltpu.VMEM)
    tokens = chosen.shape[0]
    half = back.shape[1]
    return pl.pallas_call(
        combine_body,
        out_shape=jax.ShapeDtypeStruct((8, tokens // 2 + 8, half // 4), bf16),
        in_specs=[pl.BlockSpec(memory_space=pltpu.SMEM)] + [vm] * 5,
        out_specs=vm,
        name="combine",
    )(place, chosen, back, mine, theirs, share)


def finish_body(parts_ref, out_ref, last_ref):
    new = out_ref.shape[0]
    total = parts_ref[0].astype(f32)
    for part in range(1, 8):
        total = total + parts_ref[part].astype(f32)
    out_ref[...] = total[:new].astype(bf16)
    for part in range(8):
        row = total[new + part : new + part + 1]
        for sub in range(2):
            piece = row[:, sub * 128 : (sub + 1) * 128]
            last_ref[:, part * 2 + sub : part * 2 + sub + 1, :] = jnp.broadcast_to(
                piece.astype(bf16)[None], (last_ref.shape[0], 1, 128)
            )


def finish(parts, copies):
    vm = pl.BlockSpec(memory_space=pltpu.VMEM)
    return pl.pallas_call(
        finish_body,
        out_shape=(
            jax.ShapeDtypeStruct((parts.shape[1] - 8, parts.shape[2]), bf16),
            jax.ShapeDtypeStruct((copies, 16, 128), bf16),
        ),
        in_specs=[vm],
        out_specs=(vm, vm),
        name="finish",
    )(parts)


def head_body(last_ref, gain_ref, w_ref, top_ref, rms_ref):
    plane = last_ref.shape[0] // 2
    rows = jnp.swapaxes(last_ref[...].astype(f32), 0, 1)
    halves = []
    for zo in range(2):
        pieces = []
        for part in range(4):
            for core in range(2):
                for sub in range(2):
                    pieces.append(
                        rows[(zo * 4 + part) * 2 + sub, core * plane : (core + 1) * plane]
                    )
        halves.append(jnp.concatenate(pieces, axis=1))
    tok = jnp.concatenate(halves, axis=0)
    rms = jnp.sqrt(jnp.mean(tok * tok, axis=-1, keepdims=True) + epsilon)
    head_in = (tok / rms * gain_ref[...].astype(f32)).astype(bf16)
    logits = lax.dot_general(
        w_ref[...], head_in, (((1,), (1,)), ((), ())), preferred_element_type=f32
    )
    top_ref[...] = jnp.broadcast_to(jnp.max(logits, axis=0, keepdims=True), top_ref.shape)
    rms_ref[...] = rms


def head(last, gain, w_head):
    vm = pl.BlockSpec(memory_space=pltpu.VMEM)
    rows = last.shape[0]
    return pl.pallas_call(
        head_body,
        out_shape=(
            jax.ShapeDtypeStruct((256, rows), f32),
            jax.ShapeDtypeStruct((rows, 1), f32),
        ),
        in_specs=[vm, vm, vm],
        out_specs=(vm, vm),
        name="head",
    )(last, gain, w_head)


def local(
    hidden,
    attn_gain,
    w_qkv,
    w_out,
    kv_cache,
    holder_slot,
    lengths,
    ffn_gain,
    w_router,
    expert_ids,
    w_exp_in,
    w_exp_down,
    w_sh_in,
    w_sh_down,
    final_gain,
    w_head,
):
    zh = lax.axis_index("zh")
    zl = lax.axis_index("zl")
    core = lax.axis_index("core")
    expert = lax.axis_index(REQ)
    new, feat = hidden.shape
    width = attn_gain.shape[0]
    half = width // 2
    experts_all = w_router.shape[1]
    plane = experts_all // 2
    slots = plane * 2 * SHARE
    reqs = holder_slot.shape[0]
    span = new // reqs
    place = jnp.stack([core, expert, zh, zl]).astype(jnp.int32)
    gain = attn_gain[None]
    ffn = ffn_gain[None]
    barrier = lax.optimization_barrier

    meta = jnp.concatenate(
        [
            expert_ids.reshape(reqs, span * TOPK),
            jnp.broadcast_to(lengths[:, None] // 32, (reqs, 1)),
            jnp.broadcast_to(lengths[:, None] % 32, (reqs, 1)),
        ],
        axis=1,
    ).astype(bf16)
    meta = jnp.pad(meta, ((0, 0), (0, feat - meta.shape[1])))[:, None]
    chunks = jnp.concatenate(
        [hidden.reshape(reqs, span, feat), meta, jnp.zeros((reqs, 8 - span - 1, feat), bf16)], axis=1
    )
    leg = lax.all_to_all(chunks, REQ, 0, 0, tiled=True)

    neighbours = [(0, 1), (1, 0), (2, 3), (3, 2)]
    w_in = w_exp_in[0].swapaxes(1, 2)
    w_down = w_exp_down[0]
    pair_gate = lax.ppermute(w_in[0], "zl", neighbours)
    pair_up = lax.ppermute(w_in[1], "zl", neighbours)
    pair_down = lax.ppermute(w_down, "zl", neighbours)

    leg, pair_gate = barrier((leg, pair_gate))
    req_iota = jnp.arange(reqs, dtype=jnp.int32)
    owner_of = jnp.sum(
        jnp.where(holder_slot[None, :] == req_iota[:, None], req_iota[None, :], 0), axis=1
    )
    leg = leg.at[owner_of].get(mode="promise_in_bounds")
    leg = lax.all_to_all(leg, REQ, 0, 0, tiled=True)
    leg, pair_up = barrier((leg, pair_up))
    held = leg[:, :span].reshape(new, feat)
    held_ids = leg[:, span, : span * TOPK].reshape(new, TOPK).astype(jnp.int32)
    packed_len = leg[0, span, span * TOPK : span * TOPK + 2].astype(jnp.int32)
    held_len = packed_len[0] * 32 + packed_len[1]

    full = lax.all_gather(held, TP, axis=1, tiled=True)
    full, pair_down = barrier((full, pair_down))
    parts = attend(
        held_len[None], full, gain, w_qkv, rope_tables(held_len, new), kv_cache, w_out
    )
    parts = lax.all_to_all(parts, TP, 0, 0, tiled=True)
    held_share = (held.astype(f32) + jnp.sum(parts.astype(f32), axis=0)).astype(bf16)

    def slots_of(ids):
        other = lax.ppermute(ids, "zh", [(0, 1), (1, 0)])
        both = jnp.where(zh == 0, jnp.stack([ids, other]), jnp.stack([other, ids]))
        picks = both.reshape(2, new * TOPK)
        onehot = (picks[:, :, None] == jnp.arange(experts_all, dtype=jnp.int32)).astype(bf16)
        order = jnp.arange(new * TOPK, dtype=jnp.int32)
        before = (order[:, None] > order[None, :]).astype(bf16)
        earlier = jnp.einsum("pq,rqe->rpe", before, onehot, preferred_element_type=f32)
        rank = jnp.sum(earlier * onehot.astype(f32), axis=2).astype(jnp.int32)
        rank = rank - (zl % 2) * SHARE
        there = picks - zh * plane
        slot = (there * 2 + jnp.arange(2, dtype=jnp.int32)[:, None]) * SHARE + rank
        here = (there >= 0) & (there < plane) & (rank >= 0) & (rank < SHARE)
        return jnp.where(here, slot, -1).reshape(2 * new, TOPK)

    slot_iota = jnp.arange(slots, dtype=jnp.int32)
    slot_held = slots_of(held_ids)
    slot_own = slots_of(expert_ids)
    chosen_t = jnp.zeros((slots, 2 * new), bf16)
    chosen = jnp.zeros((2 * new, slots), bf16)
    for pick in range(TOPK):
        chosen_t = chosen_t + (slot_held[:, pick][None, :] == slot_iota[:, None]).astype(bf16)
        chosen = chosen + (slot_own[:, pick : pick + 1] == slot_iota[None, :]).astype(bf16)

    outgoing = dispatch(chosen_t, spread(held_share, Z, 8))
    rows_mine = lax.all_to_all(
        outgoing.reshape(plane, 2 * SHARE, half), ("x", "y"), 0, 0, tiled=True
    ).reshape(slots, half)

    hidden_late, _ = barrier((hidden, outgoing))
    own_full = lax.all_gather(hidden_late, TP, axis=1, tiled=True)
    rows_mine, own_full = barrier((rows_mine, own_full))
    rows_theirs = swap_core(rows_mine)
    new_cache = new_kv(own_full, gain, w_qkv, rope_tables(lengths[0], new))[:, None]

    served_mine, served_theirs = routed_mlp(
        place,
        rows_mine,
        rows_theirs,
        256,
        ffn,
        w_router.T,
        w_in,
        w_down,
        pair_gate,
        pair_up,
        pair_down,
    )
    slot_at = holder_slot.reshape(2, plane).T.reshape(reqs)
    order = (slot_at % plane) * 2 + slot_at // plane
    served = reorder(order, served_mine, swap_core(served_theirs))
    returned = lax.all_to_all(
        served.reshape(plane, 2 * SHARE, half), ("x", "y"), 0, 0, tiled=True
    ).reshape(slots, half)

    shares = lax.all_gather(held_share, REQ, axis=0)
    own_slot = lax.dynamic_index_in_dim(holder_slot, expert, 0, keepdims=False)
    own_share = lax.dynamic_index_in_dim(shares, own_slot, 0, keepdims=False)
    own_rows = lax.all_gather(own_share, TP, axis=1, tiled=True)
    shared_mine, shared_theirs = shared_mlp(
        place, own_rows, ffn, w_sh_in.swapaxes(1, 2), w_sh_down
    )
    shared_theirs = swap_core(shared_theirs)

    packed = combine(place, chosen, returned, shared_mine, shared_theirs, own_share)
    summed = lax.all_to_all(packed, Z, 0, 0, tiled=True)
    out_hidden, last = finish(summed, reqs)

    last_all = lax.all_to_all(last, ("core", "x", "y"), 0, 0, tiled=True)
    tops, rms = head(last_all, final_gain[None], w_head)
    last_rms = rms.reshape(reqs)
    top_logit = jnp.max(lax.all_to_all(tops, ALL, 0, 0, tiled=True), axis=0)
    return (out_hidden, new_cache, last_rms, top_logit)


def solution(mesh):
    fine = Mesh(mesh.devices.reshape(SIZES), ALL)
    return jax.shard_map(
        local,
        mesh=fine,
        in_specs=(
            P(REQ, TP),
            P(),
            P(None, None, TP),
            P(TP, None),
            P(None, REQ, None, TP),
            P(),
            P(REQ),
            P(),
            P(),
            P(REQ, None),
            P(REQ, None, None, TP),
            P(REQ, TP, None),
            P(None, None, TP),
            P(TP, None),
            P(),
            P(REQ + TP, None),
        ),
        out_specs=(P(REQ, TP), P(None, REQ, None, TP), P(), P()),
        check_vma=False,
    )
```

time: 305 us -> 324 us (1.062)
  blocking collectives: 52.3 us -> 77 us
  starting transfers between devices: 77 us -> 52.7 us
  between operations: 1.61 us -> 18.4 us
  waiting for transfers between devices: 97.2 us -> 112 us
  local copies, waits for them, and re-layouts: 26.7 us -> 16.8 us
  other arithmetic: 17.5 us -> 8.77 us
  Pallas kernels: 28 us -> 35.7 us
    all_gather x0 -> x1, waiting for transfers between devices: none -> 28.9 us  [local(): shares = lax.all_gather(held_share, REQ, axis=0)]
    ppermute x1, waiting for transfers between devices: 26.9 us -> 0.01 us  [local(): pair_down = lax.ppermute(w_down, 'zl', neighbours)]
    all_to_all x2, waiting for transfers between devices: 12.9 us -> 37.9 us  [the longest x1 27 us: local(): leg = lax.all_to_all(leg, REQ, 0, 0, tiled=True)]
    all_gather x1 -> x3, blocking collectives: 34.7 us -> 54.6 us  [the longest x1 20 us: local(): full = lax.all_gather(held, TP, axis=1, tiled=True)]
    all_to_all x2, starting transfers between devices: 25.8 us -> 10.9 us  [the longest x1 7.04 us: local(): leg = lax.all_to_all(chunks, REQ, 0, 0, tiled=True)]
    all_to_all x1, waiting for transfers between devices: 14.9 us -> 0.01 us  [local(): lax.all_to_all(outgoing.reshape(plane, 2 * SHARE, half), ('x', 'y'), 0, 0...]
    all_to_all x1, waiting for transfers between devices: 1.52 us -> 13.4 us  [local(): parts = lax.all_to_all(parts, TP, 0, 0, tiled=True)]
    ppermute x2 -> x4, starting transfers between devices: 0.53 us -> 9.42 us  [the longest x2 6.05 us: slots_of(): other = lax.ppermute(ids, 'zh', [(0, 1), (1, 0)])]
  transfers between devices with their start and end apart: 15 -> 17, of which waited for: 11 -> 10; matrix products, arithmetic and copies ran while one was open for 11% -> 6% of each run, Pallas kernels for 1% -> 9%
where the time goes in v3:
time: 324 us; the launch traced here: 323 us
  waiting for transfers between devices  112 us (35%)
  blocking collectives  77 us (24%)
  starting transfers between devices  52.7 us (16%)
  Pallas kernels  35.7 us (11%)
  between operations  18.4 us (6%)
  local copies, waits for them, and re-layouts  16.8 us (5%)
  other arithmetic  8.77 us (3%)
    all_gather x1, waiting for transfers between devices, local(): shares = lax.all_gather(held_share, REQ, axis=0)  28.9 us
    all_to_all x1, waiting for transfers between devices, local(): leg = lax.all_to_all(leg, REQ, 0, 0, tiled=True)  27 us
    all_to_all x1, blocking collectives, local(): summed = lax.all_to_all(packed, Z, 0, 0, tiled=True)  22.5 us
    all_gather x1, blocking collectives, local(): full = lax.all_gather(held, TP, axis=1, tiled=True)  20 us
    all_gather x1, blocking collectives, local(): own_rows = lax.all_gather(own_share, TP, axis=1, tiled=True)  17.9 us
    all_gather x1, blocking collectives, local(): own_full = lax.all_gather(hidden_late, TP, axis=1, tiled=True)  16.7 us
    all_to_all x1, waiting for transfers between devices, spread(): return lax.all_to_all(wide, axes, 0, 0, tiled=True)  14.2 us
    all_to_all x1, waiting for transfers between devices, local(): parts = lax.all_to_all(parts, TP, 0, 0, tiled=True)  13.4 us
  transfers between devices with their start and end apart: 17, of which 10 were waited for; matrix products, arithmetic and copies ran while one was open for 6% of the time, Pallas kernels for 9%

profile of v3, /device:TPU:1, one launch (start us, length us, event | category | flops | bytes accessed | tf_op | source)
XLA Modules:
  0.0 322.6 jit_solution(18324901894499074493)
XLA Ops:
  11.3 6.0 %collective-permute-start = (s32[128,6]{0,1:T(8,128)S(1)}, s32[128,6]{0,1:T(8,128)S(1)}, u32[]{:S(2)}, u32[]{:S(2)}) collective-permute-start(s32[128,6]{0,1:T(8,128)S(1)} %copy-done.7), channel_id=1, source_target_pairs={{0,128},{128,0},{1,129},{129,1},{2,130},{130,2},{3,131},{131,3},{4... | collective-permute-start | bytes 9224 | tf_op jit(solution)/shard_map/ppermute | solution.py:460
  19.3 7.0 %all-to-all-start = ((bf16[32,8,256]{2,1,0:T(8,128)(2,1)}), bf16[32,8,256]{2,1,0:T(8,128)(2,1)S(1)}, u32[]{:S(2)}, u32[]{:S(2)}) async-start(bf16[32,8,256]{2,1,0:T(8,128)(2,1)} %maximum_maximum_fusion), calls=%async_computation | async-start | bytes 262144 | tf_op jit(solution)/shard_map/all_to_all | solution.py:429
  28.0 10.9 %all-to-all-done = bf16[32,8,256]{2,1,0:T(8,128)(2,1)S(1)} async-done(((bf16[32,8,256]{2,1,0:T(8,128)(2,1)}), bf16[32,8,256]{2,1,0:T(8,128)(2,1)S(1)}, u32[]{:S(2)}, u32[]{:S(2)}) %all-to-all-start) | async-done | bytes 131104 | tf_op jit(solution)/shard_map/all_to_all | solution.py:429
  40.2 3.9 %all-to-all-start.1 = ((bf16[32,8,256]{2,1,0:T(8,128)(2,1)}), bf16[32,8,256]{2,1,0:T(8,128)(2,1)S(1)}, u32[]{:S(2)}, u32[]{:S(2)}) async-start(bf16[32,8,256]{2,1,0:T(8,128)(2,1)} %gather_fusion), calls=%async_computation.1 | async-start | bytes 262144 | tf_op jit(solution)/shard_map/all_to_all | solution.py:444
  45.5 27.0 %all-to-all-done.1 = bf16[32,8,256]{2,1,0:T(8,128)(2,1)S(1)} async-done(((bf16[32,8,256]{2,1,0:T(8,128)(2,1)}), bf16[32,8,256]{2,1,0:T(8,128)(2,1)S(1)}, u32[]{:S(2)}, u32[]{:S(2)}) %all-to-all-start.1) | async-done | bytes 131104 | tf_op jit(solution)/shard_map/all_to_all | solution.py:444
  74.8 20.0 %all_gather.13.full_ref = bf16[128,2048]{1,0:T(8,128)(2,1)} all-gather(bf16[128,256]{1,0:T(8,128)(2,1)S(1)} %reshape.254), channel_id=1, replica_groups=mesh['zh'=2,'x'=4,'y'=4,'zl'=4,'core'=2] {'zl','core'}, dimensions={1}, use_global_device_ids=true | all-gather | bytes 589824 | tf_op jit(solution)/shard_map/all_gather | solution.py:451
  96.1 5.7 %attend.1 = bf16[8,128,256]{2,1,0:T(8,128)(2,1)} custom-call(s32[1]{0:T(128)} %bitcast.20.len_ref, bf16[128,2048]{1,0:T(8,128)(2,1)} %all_gather.13.full_ref, bf16[1,2048]{1,0:T(2,128)(2,1)} %broadcast_in_dim.54.gain_ref, bf16[3,2048,256]{2,1,0:T(8,128)(2,1)} %w_ref.4, f32[128,128]{1,0:T(8,128)} %get-tuple-element.93.cos_ref, ...), custom_call_target="tpu_custom_call" | custom-call | tf_op jit(solution)/shard_map/attend/pallas_call | solution.py:116
  101.8 3.6 %all-to-all-start.2 = ((bf16[8,128,256]{2,1,0:T(8,128)(2,1)}), bf16[8,128,256]{2,1,0:T(8,128)(2,1)S(1)}, u32[]{:S(2)}, u32[]{:S(2)}) async-start(bf16[8,128,256]{2,1,0:T(8,128)(2,1)} %attend.1), calls=%async_computation.2 | async-start | bytes 1048576 | tf_op jit(solution)/shard_map/all_to_all | solution.py:456
  106.5 13.4 %all-to-all-done.2 = bf16[8,128,256]{2,1,0:T(8,128)(2,1)S(1)} async-done(((bf16[8,128,256]{2,1,0:T(8,128)(2,1)}), bf16[8,128,256]{2,1,0:T(8,128)(2,1)S(1)}, u32[]{:S(2)}, u32[]{:S(2)}) %all-to-all-start.2) | async-done | bytes 524320 | tf_op jit(solution)/shard_map/all_to_all | solution.py:456
  120.8 5.7 %all-to-all-start.3 = ((bf16[8,128,256]{2,1,0:T(8,128)(2,1)}), bf16[8,128,256]{2,1,0:T(8,128)(2,1)S(1)}, u32[]{:S(2)}, u32[]{:S(2)}) async-start(bf16[8,128,256]{2,1,0:T(8,128)(2,1)} %broadcast_in_dim.55), calls=%async_computation.3 | async-start | bytes 1048576 | tf_op jit(solution)/shard_map/all_to_all | solution.py:127
  129.8 14.2 %all-to-all-done.3.parts_ref = bf16[8,128,256]{2,1,0:T(8,128)(2,1)S(1)} async-done(((bf16[8,128,256]{2,1,0:T(8,128)(2,1)}), bf16[8,128,256]{2,1,0:T(8,128)(2,1)S(1)}, u32[]{:S(2)}, u32[]{:S(2)}) %all-to-all-start.3) | async-done | bytes 524320 | tf_op jit(solution)/shard_map/all_to_all | solution.py:127
  147.4 3.7 %all-to-all-start.4 = ((bf16[16,32,1024]{2,1,0:T(8,128)(2,1)}), bf16[16,32,1024]{2,1,0:T(8,128)(2,1)S(1)}, u32[]{:S(2)}, u32[]{:S(2)}) async-start(bf16[16,32,1024]{2,1,0:T(8,128)(2,1)} %bitcast.85), calls=%async_computation.4 | async-start | bytes 2097152 | tf_op jit(solution)/shard_map/all_to_all | solution.py:484
  151.0 16.7 %all_gather.14.full_ref = bf16[128,2048]{1,0:T(8,128)(2,1)} all-gather(bf16[128,256]{1,0:T(8,128)(2,1)S(1)} %copy-done.5), channel_id=1, replica_groups=mesh['zh'=2,'x'=4,'y'=4,'zl'=4,'core'=2] {'zl','core'}, dimensions={1}, use_global_device_ids=true | all-gather | bytes 589824 | tf_op jit(solution)/shard_map/all_gather | solution.py:489
  173.3 10.4 %routed_mlp.1 = (bf16[512,1024]{1,0:T(8,128)(2,1)}, bf16[512,1024]{1,0:T(8,128)(2,1)}) custom-call(s32[4]{0:T(128)} %pad_add_fusion.place_ref, bf16[512,1024]{1,0:T(8,128)(2,1)} %bitcast.93, bf16[512,1024]{1,0:T(8,128)(2,1)} %copy-done.12, bf16[1,2048]{1,0:T(2,128)(2,1)} %broadcast_in_dim.56.gain_ref, bf16[32,2048]{1,0:T(8,128)(2,1)} %bitcast.100, ...), custom_call_target="tpu_custom_call" | custom-call | flops 2214592512 | bytes 8519680 | tf_op jit(solution)/shard_map/routed_mlp/pallas_call | solution.py:206
  190.3 5.1 %all-to-all-start.5 = ((bf16[16,32,1024]{2,1,0:T(8,128)(2,1)}), bf16[16,32,1024]{2,1,0:T(8,128)(2,1)S(1)}, u32[]{:S(2)}, u32[]{:S(2)}) async-start(bf16[16,32,1024]{2,1,0:T(8,128)(2,1)} %bitcast.86), calls=%async_computation.5 | async-start | bytes 2097152 | tf_op jit(solution)/shard_map/all_to_all | solution.py:510
  198.4 28.9 %all-gather.3.cloned.1.call-done = bf16[32,128,256]{2,1,0:T(8,128)(2,1)} async-done(((bf16[1,128,256]{2,1,0:T(8,128)(2,1)}), bf16[32,128,256]{2,1,0:T(8,128)(2,1)}) %all-gather.3.cloned.1.call-update) | async-done | bytes 2097168 | tf_op jit(solution)/shard_map/all_gather | solution.py:514
  228.1 17.9 %all-gather = bf16[1,128,2048]{2,1,0:T(8,128)(2,1)} all-gather(bf16[1,128,256]{2,1,0:T(8,128)(2,1)S(1)} %constant_dynamic-slice_fusion), channel_id=2, replica_groups=mesh['zh'=2,'x'=4,'y'=4,'zl'=4,'core'=2] {'zl','core'}, dimensions={2}, use_global_device_ids=true | all-gather | bytes 589824 | tf_op jit(solution)/shard_map/all_gather | solution.py:517
  246.0 3.6 %shared_mlp.1 = (bf16[128,1024]{1,0:T(8,128)(2,1)}, bf16[128,1024]{1,0:T(8,128)(2,1)}) custom-call(s32[4]{0:T(128)} %pad_add_fusion.place_ref, bf16[128,2048]{1,0:T(8,128)(2,1)} %bitcast.88, bf16[1,2048]{1,0:T(2,128)(2,1)} %broadcast_in_dim.56.gain_ref, bf16[2,176,2048]{2,1,0:T(8,128)(2,1)} %bitcast.91, bf16[176,2048]{1,0:T(8,128)(2,1)} %down_ref.1), custom_call_target="tpu_custom_call" | custom-call | tf_op jit(solution)/shard_map/shared_mlp/pallas_call | solution.py:232
  256.2 22.5 %all_to_all.49.parts_ref = bf16[8,136,256]{2,1,0:T(8,128)(2,1)} all-to-all(bf16[8,136,256]{2,1,0:T(8,128)(2,1)} %combine.1), channel_id=1, replica_groups=mesh['zh'=2,'x'=4,'y'=4,'zl'=4,'core'=2] {'zh','zl'}, dimensions={0} | all-to-all | bytes 1114112 | tf_op jit(solution)/shard_map/all_to_all | solution.py:524
  280.6 5.3 %all-to-all-start.7 = ((bf16[32,16,128]{2,1,0:T(8,128)(2,1)}), bf16[32,16,128]{2,1,0:T(8,128)(2,1)S(1)}, u32[]{:S(2)}, u32[]{:S(2)}) async-start(bf16[32,16,128]{2,1,0:T(8,128)(2,1)} %get-tuple-element.35), calls=%async_computation.7 | async-start | bytes 262144 | tf_op jit(solution)/shard_map/all_to_all | solution.py:527
  286.5 6.9 %all-to-all-done.7.last_ref = bf16[32,16,128]{2,1,0:T(8,128)(2,1)S(1)} async-done(((bf16[32,16,128]{2,1,0:T(8,128)(2,1)}), bf16[32,16,128]{2,1,0:T(8,128)(2,1)S(1)}, u32[]{:S(2)}, u32[]{:S(2)}) %all-to-all-start.7) | async-done | bytes 131104 | tf_op jit(solution)/shard_map/all_to_all | solution.py:527
  296.6 5.5 %all-to-all-start.8 = ((f32[256,1,32]{2,1,0:T(1,128)}), f32[256,1,32]{2,1,0:T(1,128)S(1)}, u32[]{:S(2)}, u32[]{:S(2)}) async-start(f32[256,1,32]{2,1,0:T(1,128)} %bitcast.95), calls=%async_computation.8 | async-start | bytes 262144 | tf_op jit(solution)/shard_map/all_to_all | solution.py:530
  302.9 3.4 %new_kv.1 = bf16[2,128,256]{2,1,0:T(8,128)(2,1)} custom-call(bf16[128,2048]{1,0:T(8,128)(2,1)} %all_gather.14.full_ref, bf16[1,2048]{1,0:T(2,128)(2,1)} %broadcast_in_dim.54.gain_ref, bf16[3,2048,256]{2,1,0:T(8,128)(2,1)} %w_ref.4, f32[128,128]{1,0:T(8,128)} %get-tuple-element.95.cos_ref, f32[128,128]{1,0:T(8,128)} %get-tuple-element.96.sin_ref), custom_call_target="tpu_custom_call" | custom-call | tf_op jit(solution)/shard_map/new_kv/pallas_call | solution.py:63
  306.9 8.0 %all-to-all-done.8 = f32[256,1,32]{2,1,0:T(1,128)S(1)} async-done(((f32[256,1,32]{2,1,0:T(1,128)}), f32[256,1,32]{2,1,0:T(1,128)S(1)}, u32[]{:S(2)}, u32[]{:S(2)}) %all-to-all-start.8) | async-done | bytes 32800 | tf_op jit(solution)/shard_map/all_to_all | solution.py:530
  (129 shorter events, 49.0 us)
Async XLA Ops:
  7.2 11.3 %copy-start.5 = (bf16[128,256]{1,0:T(8,128)(2,1)S(1)}, bf16[128,256]{1,0:T(8,128)(2,1)}, u32[]{:S(2)}) copy-start(bf16[128,256]{1,0:T(8,128)(2,1)} %param.16) | copy-start | bytes 196612
  7.2 20.0 %copy-start.13 = (bf16[1,176,2048]{2,1,0:T(8,128)(2,1)S(1)}, bf16[1,176,2048]{2,1,0:T(8,128)(2,1)}, u32[]{:S(2)}) copy-start(bf16[1,176,2048]{2,1,0:T(8,128)(2,1)} %param.27) | copy-start | bytes 2162692
  7.2 20.7 %copy-start.15 = (s32[32]{0:T(128)S(1)}, s32[32]{0:T(128)}, u32[]{:S(2)}) copy-start(s32[32]{0:T(128)} %param.21) | copy-start | bytes 388
  7.2 37.0 %copy-start.9 = (bf16[2048]{0:T(1024)(128)(2,1)S(1)}, bf16[2048]{0:T(1024)(128)(2,1)}, u32[]{:S(2)}) copy-start(bf16[2048]{0:T(1024)(128)(2,1)} %param.17) | copy-start | bytes 12292
  8.7 30.2 %collective-permute-start.1 = (bf16[176,2048]{1,0:T(8,128)(2,1)S(1)}, bf16[176,2048]{1,0:T(8,128)(2,1)S(1)}, u32[]{:S(2)}, u32[]{:S(2)}) collective-permute-start(bf16[176,2048]{1,0:T(8,128)(2,1)S(1)} %get-tuple-element.75), channel_id=1, source_target_pairs={{0,2},{2,0},{4,6},{6,4},{1,3},{3,1},{5,7},{7,5},{8,10},{10,8},{12,... | collective-permute-start | bytes 2162696 | tf_op jit(solution)/shard_map/ppermute | solution.py:434
  11.3 33.7 %collective-permute-start = (s32[128,6]{0,1:T(8,128)S(1)}, s32[128,6]{0,1:T(8,128)S(1)}, u32[]{:S(2)}, u32[]{:S(2)}) collective-permute-start(s32[128,6]{0,1:T(8,128)S(1)} %copy-done.7), channel_id=1, source_target_pairs={{0,128},{128,0},{1,129},{129,1},{2,130},{130,2},{3,131},{131,3},{4... | collective-permute-start | bytes 9224 | tf_op jit(solution)/shard_map/ppermute | solution.py:460
  19.3 19.6 %all-to-all-start = ((bf16[32,8,256]{2,1,0:T(8,128)(2,1)}), bf16[32,8,256]{2,1,0:T(8,128)(2,1)S(1)}, u32[]{:S(2)}, u32[]{:S(2)}) async-start(bf16[32,8,256]{2,1,0:T(8,128)(2,1)} %maximum_maximum_fusion), calls=%async_computation | async-start | bytes 262144 | tf_op jit(solution)/shard_map/all_to_all | solution.py:429
  26.4 19.2 %collective-permute-start.2 = (bf16[176,2048]{1,0:T(8,128)(2,1)S(1)}, bf16[176,2048]{1,0:T(8,128)(2,1)}, u32[]{:S(2)}, u32[]{:S(2)}) collective-permute-start(bf16[176,2048]{1,0:T(8,128)(2,1)S(1)} %get-tuple-element.74), channel_id=1, source_target_pairs={{0,2},{2,0},{4,6},{6,4},{1,3},{3,1},{5,7},{7,5},{8,10},{10,8},{12,... | collective-permute-start | bytes 2162696 | tf_op jit(solution)/shard_map/ppermute | solution.py:435
  27.2 68.9 %collective-permute-start.4 = (bf16[176,2048]{1,0:T(8,128)(2,1)S(1)}, bf16[176,2048]{1,0:T(8,128)(2,1)}, u32[]{:S(2)}, u32[]{:S(2)}) collective-permute-start(bf16[176,2048]{1,0:T(8,128)(2,1)S(1)} %bitcast.99), channel_id=1, source_target_pairs={{0,2},{2,0},{4,6},{6,4},{1,3},{3,1},{5,7},{7,5},{8,10},{10,8},{12,... | collective-permute-start | bytes 2162696 | tf_op jit(solution)/shard_map/ppermute | solution.py:436
  40.2 32.4 %all-to-all-start.1 = ((bf16[32,8,256]{2,1,0:T(8,128)(2,1)}), bf16[32,8,256]{2,1,0:T(8,128)(2,1)S(1)}, u32[]{:S(2)}, u32[]{:S(2)}) async-start(bf16[32,8,256]{2,1,0:T(8,128)(2,1)} %gather_fusion), calls=%async_computation.1 | async-start | bytes 262144 | tf_op jit(solution)/shard_map/all_to_all | solution.py:444
  74.7 30.8 %collective-permute-start.3 = (s32[128,6]{1,0:T(8,128)S(1)}, s32[128,6]{1,0:T(8,128)S(1)}, u32[]{:S(2)}, u32[]{:S(2)}) collective-permute-start(s32[128,6]{1,0:T(8,128)S(1)} %reshape.263), channel_id=1, source_target_pairs={{0,128},{128,0},{1,129},{129,1},{2,130},{130,2},{3,131},{131,3},{4... | collective-permute-start | bytes 9224 | tf_op jit(solution)/shard_map/ppermute | solution.py:460
  101.8 18.1 %all-to-all-start.2 = ((bf16[8,128,256]{2,1,0:T(8,128)(2,1)}), bf16[8,128,256]{2,1,0:T(8,128)(2,1)S(1)}, u32[]{:S(2)}, u32[]{:S(2)}) async-start(bf16[8,128,256]{2,1,0:T(8,128)(2,1)} %attend.1), calls=%async_computation.2 | async-start | bytes 1048576 | tf_op jit(solution)/shard_map/all_to_all | solution.py:456
  120.8 23.3 %all-to-all-start.3 = ((bf16[8,128,256]{2,1,0:T(8,128)(2,1)}), bf16[8,128,256]{2,1,0:T(8,128)(2,1)S(1)}, u32[]{:S(2)}, u32[]{:S(2)}) async-start(bf16[8,128,256]{2,1,0:T(8,128)(2,1)} %broadcast_in_dim.55), calls=%async_computation.3 | async-start | bytes 1048576 | tf_op jit(solution)/shard_map/all_to_all | solution.py:127
  126.5 100.8 %all-gather.3.cloned.1.call-start = ((), (), s32[]{:S(2)}) async-start(), calls=%async_computation.9 | async-start | bytes 2162688 | tf_op jit(solution)/shard_map/all_gather | solution.py:514
  129.8 40.2 %copy-start.10 = (bf16[2048]{0:T(1024)(128)(2,1)S(1)}, bf16[2048]{0:T(1024)(128)(2,1)}, u32[]{:S(2)}) copy-start(bf16[2048]{0:T(1024)(128)(2,1)} %param.23) | copy-start | bytes 12292
  147.4 20.4 %all-to-all-start.4 = ((bf16[16,32,1024]{2,1,0:T(8,128)(2,1)}), bf16[16,32,1024]{2,1,0:T(8,128)(2,1)S(1)}, u32[]{:S(2)}, u32[]{:S(2)}) async-start(bf16[16,32,1024]{2,1,0:T(8,128)(2,1)} %bitcast.85), calls=%async_computation.4 | async-start | bytes 2097152 | tf_op jit(solution)/shard_map/all_to_all | solution.py:484
  167.8 4.5 %copy-start.2 = (bf16[16,32,1024]{2,1,0:T(8,128)(2,1)}, bf16[16,32,1024]{2,1,0:T(8,128)(2,1)S(1)}, u32[]{:S(2)}) copy-start(bf16[16,32,1024]{2,1,0:T(8,128)(2,1)S(1)} %all-to-all-done.4) | copy-start | bytes 3145732
  167.8 4.5 %collective-permute-start.5 = (bf16[512,1024]{1,0:T(8,128)(2,1)S(1)}, bf16[512,1024]{1,0:T(8,128)(2,1)S(1)}, u32[]{:S(2)}, u32[]{:S(2)}) collective-permute-start(bf16[512,1024]{1,0:T(8,128)(2,1)S(1)} %bitcast.92), channel_id=1, source_target_pairs={{0,1},{1,0},{2,3},{3,2},{4,5},{5,4},{6,7},{7,6},{8,9},{9,8},{10,11... | collective-permute-start | bytes 3145736 | tf_op jit(solution)/shard_map/ppermute | solution.py:131
  183.7 2.9 collective-permute-start.6
  190.3 62.0 %all-to-all-start.5 = ((bf16[16,32,1024]{2,1,0:T(8,128)(2,1)}), bf16[16,32,1024]{2,1,0:T(8,128)(2,1)S(1)}, u32[]{:S(2)}, u32[]{:S(2)}) async-start(bf16[16,32,1024]{2,1,0:T(8,128)(2,1)} %bitcast.86), calls=%async_computation.5 | async-start | bytes 2097152 | tf_op jit(solution)/shard_map/all_to_all | solution.py:510
  249.6 2.7 collective-permute-start.7
  253.4 32.5 %copy-start.11 = (bf16[2048]{0:T(1024)(128)(2,1)S(1)}, bf16[2048]{0:T(1024)(128)(2,1)}, u32[]{:S(2)}) copy-start(bf16[2048]{0:T(1024)(128)(2,1)} %param.30) | copy-start | bytes 12292
  280.6 12.9 %all-to-all-start.7 = ((bf16[32,16,128]{2,1,0:T(8,128)(2,1)}), bf16[32,16,128]{2,1,0:T(8,128)(2,1)S(1)}, u32[]{:S(2)}, u32[]{:S(2)}) async-start(bf16[32,16,128]{2,1,0:T(8,128)(2,1)} %get-tuple-element.35), calls=%async_computation.7 | async-start | bytes 262144 | tf_op jit(solution)/shard_map/all_to_all | solution.py:527
  296.6 18.4 %all-to-all-start.8 = ((f32[256,1,32]{2,1,0:T(1,128)}), f32[256,1,32]{2,1,0:T(1,128)S(1)}, u32[]{:S(2)}, u32[]{:S(2)}) async-start(f32[256,1,32]{2,1,0:T(1,128)} %bitcast.95), calls=%async_computation.8 | async-start | bytes 262144 | tf_op jit(solution)/shard_map/all_to_all | solution.py:530
  (9 other events, 14.7 us)
Sparse Core Ops, SparseCore 0:
  131.4 95.8 all-gather.2

commit v4 on v3

--- a/solution.py
+++ b/solution.py
@@ -160,18 +160,25 @@
         store(theirs_ref, mine_ref)
 
 
-def routed_body(
+def experts_body(
     place_ref, a_ref, b_ref, gain_ref, router_ref, in_ref, down_ref, pg_ref, pu_ref, pd_ref,
-    om_ref, ot_ref, x_ref,
+    si_ref, sd_ref, om_ref, ot_ref, xr_ref, xs_ref,
 ):
     first = place_ref[0] == 0
-    feat = x_ref.shape[1] // 8
+    feat = xr_ref.shape[1] // 8
+    chunks, span = a_ref.shape[:2]
+    routed = xr_ref.shape[0] // chunks
+    shared = span - routed
 
     def fill(even_ref, odd_ref):
-        for part in range(4):
-            piece = slice(part * feat, (part + 1) * feat)
-            x_ref[:, 2 * part * feat : (2 * part + 1) * feat] = even_ref[:, piece]
-            x_ref[:, (2 * part + 1) * feat : (2 * part + 2) * feat] = odd_ref[:, piece]
+        for chunk in range(chunks):
+            for part in range(4):
+                piece = slice(part * feat, (part + 1) * feat)
+                for odd, ref in enumerate((even_ref, odd_ref)):
+                    lanes = slice((2 * part + odd) * feat, (2 * part + odd + 1) * feat)
+                    rows = ref[chunk, :, piece].astype(f32)
+                    xr_ref[chunk * routed : (chunk + 1) * routed, lanes] = rows[:routed]
+                    xs_ref[chunk * shared : (chunk + 1) * shared, lanes] = rows[routed:]
 
     @pl.when(first)
     def _():
@@ -181,7 +188,7 @@
     def _():
         fill(b_ref, a_ref)
 
-    rows = norm_rows(x_ref, gain_ref)
+    rows = norm_rows(xr_ref, gain_ref)
     out = expert_rows(rows, in_ref[0], in_ref[1], down_ref[...])
     out = out + expert_rows(rows, pg_ref[...], pu_ref[...], pd_ref[...])
     logits = dot_nt(rows, router_ref[...])
@@ -189,63 +196,65 @@
     own = lax.broadcasted_iota(jnp.int32, logits.shape, 1) == place_ref[1]
     picked = jnp.sum(jnp.where(own, raised, 0.0), axis=-1, keepdims=True)
     out = out * (picked / jnp.sum(raised, axis=-1, keepdims=True))
-    drain(first, out.astype(bf16), om_ref, ot_ref)
-
-
-def routed_mlp(place, rows_mine, rows_theirs, block, *shared_operands):
-    count, half = rows_mine.shape
+    common = norm_rows(xs_ref, gain_ref)
+    common = expert_rows(common, si_ref[0], si_ref[1], sd_ref[...])
+    common = common + xs_ref[...] * 0.125
+
+    def store(even_ref, odd_ref):
+        for chunk in range(chunks):
+            top = out[chunk * routed : (chunk + 1) * routed]
+            low = common[chunk * shared : (chunk + 1) * shared]
+            both = jnp.concatenate([top, low], axis=0).astype(bf16)
+            for part in range(4):
+                piece = slice(part * feat, (part + 1) * feat)
+                even_ref[chunk, :, piece] = both[:, 2 * part * feat : (2 * part + 1) * feat]
+                odd_ref[chunk, :, piece] = both[:, (2 * part + 1) * feat : (2 * part + 2) * feat]
+
+    @pl.when(first)
+    def _():
+        store(om_ref, ot_ref)
+
+    @pl.when(jnp.logical_not(first))
+    def _():
+        store(ot_ref, om_ref)
+
+
+def experts(place, rows_mine, rows_theirs, steps, *weights):
+    count, span, half = rows_mine.shape
     width = 2 * half
-    hidden = 2 * shared_operands[3].shape[0]
-    row_spec = pl.BlockSpec((block, half), lambda i: (i, 0))
+    block = count // steps
+    row_spec = pl.BlockSpec((block, span, half), lambda i: (i, 0, 0))
 
     def whole(array):
         zeros = (0,) * array.ndim
         return pl.BlockSpec(array.shape, lambda i: zeros)
 
-    shape = jax.ShapeDtypeStruct((count, half), bf16)
-    return pl.pallas_call(
-        routed_body,
-        grid=(count // block,),
+    shape = jax.ShapeDtypeStruct(rows_mine.shape, bf16)
+    return pl.pallas_call(
+        experts_body,
+        grid=(steps,),
         out_shape=(shape, shape),
         in_specs=[pl.BlockSpec(memory_space=pltpu.SMEM), row_spec, row_spec]
-        + [whole(array) for array in shared_operands],
+        + [whole(array) for array in weights],
         out_specs=(row_spec, row_spec),
-        scratch_shapes=[pltpu.VMEM((block, width), bf16)],
+        scratch_shapes=[
+            pltpu.VMEM((block * 2 * SHARE, width), f32),
+            pltpu.VMEM((block * (span - 2 * SHARE), width), f32),
+        ],
         cost_estimate=pl.CostEstimate(
-            flops=6 * count * width * hidden,
-            transcendentals=count * hidden,
-            bytes_accessed=8 * count * half + 6 * width * hidden,
+            flops=6 * count * span * width * 352,
+            transcendentals=count * span * 352,
+            bytes_accessed=8 * count * span * half + 18 * width * 176,
         ),
-        name="routed_mlp",
-    )(place, rows_mine, rows_theirs, *shared_operands)
-
-
-def shared_body(place_ref, x_ref, gain_ref, in_ref, down_ref, om_ref, ot_ref):
-    rows = norm_rows(x_ref, gain_ref)
-    out = expert_rows(rows, in_ref[0], in_ref[1], down_ref[...])
-    drain(place_ref[0] == 0, out.astype(bf16), om_ref, ot_ref)
-
-
-def shared_mlp(place, rows, gain, w_in, w_down):
-    vm = pl.BlockSpec(memory_space=pltpu.VMEM)
-    shape = jax.ShapeDtypeStruct((rows.shape[0], rows.shape[1] // 2), bf16)
-    return pl.pallas_call(
-        shared_body,
-        out_shape=(shape, shape),
-        in_specs=[pl.BlockSpec(memory_space=pltpu.SMEM)] + [vm] * 4,
-        out_specs=(vm, vm),
-        name="shared_mlp",
-    )(place, rows, gain, w_in, w_down)
+        name="experts",
+    )(place, rows_mine, rows_theirs, *weights)
 
 
 def reorder_body(order_ref, a_ref, b_ref, o_ref):
-    chunks = order_ref.shape[0]
-    rows = o_ref.shape[0] // chunks
-    for i in range(chunks):
-        at = pl.ds(pl.multiple_of(order_ref[i] * rows, rows), rows)
-        o_ref[i * rows : (i + 1) * rows, :] = (
-            a_ref[at, :].astype(f32) + b_ref[at, :].astype(f32)
-        ).astype(bf16)
+    o_ref[...] = (
+        jnp.dot(order_ref[...], a_ref[...], preferred_element_type=f32)
+        + jnp.dot(order_ref[...], b_ref[...], preferred_element_type=f32)
+    ).astype(bf16)
 
 
 def reorder(order, a, b):
@@ -253,7 +262,7 @@
     return pl.pallas_call(
         reorder_body,
         out_shape=jax.ShapeDtypeStruct(a.shape, bf16),
-        in_specs=[pl.BlockSpec(memory_space=pltpu.SMEM), vm, vm],
+        in_specs=[vm, vm, vm],
         out_specs=vm,
         name="reorder",
     )(order, a, b)
@@ -279,37 +288,33 @@
     )(chosen_t, parts)
 
 
-def combine_body(place_ref, chosen_ref, back_ref, mine_ref, theirs_ref, share_ref, out_ref):
-    tokens = chosen_ref.shape[0]
-    new = tokens // 2
+def combine_body(chosen_ref, back_ref, out_ref):
     feat = out_ref.shape[2]
+    new = chosen_ref.shape[1] // 2
     for zo in range(2):
-        own = (place_ref[2] == zo).astype(f32)
-        total = jnp.dot(
-            chosen_ref[zo * new : (zo + 1) * new, :], back_ref[...], preferred_element_type=f32
-        )
-        total = total + own * (mine_ref[...].astype(f32) + theirs_ref[...].astype(f32))
+        total = lax.dot_general(
+            chosen_ref[:, zo * new : (zo + 1) * new],
+            back_ref[...],
+            (((0,), (0,)), ((), ())),
+            preferred_element_type=f32,
+        ).astype(bf16)
         for part in range(4):
-            once = own * (place_ref[3] == part).astype(f32)
             piece = total[:, part * feat : (part + 1) * feat]
-            piece = (piece + once * share_ref[...].astype(f32)).astype(bf16)
             out_ref[zo * 4 + part, :new, :] = piece
             row = piece[new - 1 :, :]
             for dest in range(8):
                 out_ref[dest, new + zo * 4 + part : new + zo * 4 + part + 1, :] = row
 
 
-def combine(place, chosen, back, mine, theirs, share):
-    vm = pl.BlockSpec(memory_space=pltpu.VMEM)
-    tokens = chosen.shape[0]
-    half = back.shape[1]
+def combine(chosen_t, back):
+    vm = pl.BlockSpec(memory_space=pltpu.VMEM)
     return pl.pallas_call(
         combine_body,
-        out_shape=jax.ShapeDtypeStruct((8, tokens // 2 + 8, half // 4), bf16),
-        in_specs=[pl.BlockSpec(memory_space=pltpu.SMEM)] + [vm] * 5,
+        out_shape=jax.ShapeDtypeStruct((8, chosen_t.shape[1] // 2 + 8, back.shape[1] // 4), bf16),
+        in_specs=[vm, vm],
         out_specs=vm,
         name="combine",
-    )(place, chosen, back, mine, theirs, share)
+    )(chosen_t, back)
 
 
 def finish_body(parts_ref, out_ref, last_ref):
@@ -406,121 +411,125 @@
     half = width // 2
     experts_all = w_router.shape[1]
     plane = experts_all // 2
-    slots = plane * 2 * SHARE
     reqs = holder_slot.shape[0]
     span = new // reqs
-    place = jnp.stack([core, expert, zh, zl]).astype(jnp.int32)
+    rows = 2 * (SHARE + span)
+    slots = plane * rows
+    place = jnp.stack([core, expert]).astype(jnp.int32)
     gain = attn_gain[None]
-    ffn = ffn_gain[None]
     barrier = lax.optimization_barrier
 
-    meta = jnp.concatenate(
-        [
-            expert_ids.reshape(reqs, span * TOPK),
-            jnp.broadcast_to(lengths[:, None] // 32, (reqs, 1)),
-            jnp.broadcast_to(lengths[:, None] % 32, (reqs, 1)),
-        ],
-        axis=1,
-    ).astype(bf16)
-    meta = jnp.pad(meta, ((0, 0), (0, feat - meta.shape[1])))[:, None]
-    chunks = jnp.concatenate(
-        [hidden.reshape(reqs, span, feat), meta, jnp.zeros((reqs, 8 - span - 1, feat), bf16)], axis=1
-    )
-    leg = lax.all_to_all(chunks, REQ, 0, 0, tiled=True)
-
-    neighbours = [(0, 1), (1, 0), (2, 3), (3, 2)]
+    ids_t = expert_ids.T
+    sizes = jnp.concatenate(
+        [jnp.broadcast_to(lengths // 32, (feat // 2,)), jnp.broadcast_to(lengths % 32, (feat // 2,))]
+    )
+    meta = jnp.concatenate([ids_t.reshape(TOPK * new // feat, feat), sizes[None]]).astype(bf16)
+    meta = jnp.broadcast_to(meta[None], (reqs,) + meta.shape)
+    chunks = jnp.concatenate([hidden.reshape(reqs, span, feat), meta], axis=1)
     w_in = w_exp_in[0].swapaxes(1, 2)
     w_down = w_exp_down[0]
-    pair_gate = lax.ppermute(w_in[0], "zl", neighbours)
-    pair_up = lax.ppermute(w_in[1], "zl", neighbours)
-    pair_down = lax.ppermute(w_down, "zl", neighbours)
-
-    leg, pair_gate = barrier((leg, pair_gate))
+    leg = lax.all_to_all(chunks, REQ, 0, 0, tiled=True)
+    leg, gate_w = barrier((leg, w_in[0]))
+
+    neighbours = [(0, 1), (1, 0), (2, 3), (3, 2)]
+    pair_gate = lax.ppermute(gate_w, "zl", neighbours)
+
     req_iota = jnp.arange(reqs, dtype=jnp.int32)
     owner_of = jnp.sum(
         jnp.where(holder_slot[None, :] == req_iota[:, None], req_iota[None, :], 0), axis=1
     )
     leg = leg.at[owner_of].get(mode="promise_in_bounds")
     leg = lax.all_to_all(leg, REQ, 0, 0, tiled=True)
-    leg, pair_up = barrier((leg, pair_up))
+    leg, pair_gate, up_w = barrier((leg, pair_gate, w_in[1]))
+    pair_up = lax.ppermute(up_w, "zl", neighbours)
     held = leg[:, :span].reshape(new, feat)
-    held_ids = leg[:, span, : span * TOPK].reshape(new, TOPK).astype(jnp.int32)
-    packed_len = leg[0, span, span * TOPK : span * TOPK + 2].astype(jnp.int32)
-    held_len = packed_len[0] * 32 + packed_len[1]
+    held_ids = leg[0, span:-1].reshape(TOPK, new).astype(jnp.int32)
+    held_len = leg[0, -1, :1].astype(jnp.int32) * 32 + leg[0, -1, feat // 2 :][:1].astype(jnp.int32)
 
     full = lax.all_gather(held, TP, axis=1, tiled=True)
-    full, pair_down = barrier((full, pair_down))
     parts = attend(
-        held_len[None], full, gain, w_qkv, rope_tables(held_len, new), kv_cache, w_out
-    )
+        held_len, full, gain, w_qkv, rope_tables(held_len, new), kv_cache, w_out
+    )
+    parts, pair_up = barrier((parts, pair_up))
     parts = lax.all_to_all(parts, TP, 0, 0, tiled=True)
     held_share = (held.astype(f32) + jnp.sum(parts.astype(f32), axis=0)).astype(bf16)
 
-    def slots_of(ids):
+    slot_iota = jnp.arange(slots, dtype=jnp.int32)
+
+    def chosen_of(ids):
         other = lax.ppermute(ids, "zh", [(0, 1), (1, 0)])
         both = jnp.where(zh == 0, jnp.stack([ids, other]), jnp.stack([other, ids]))
-        picks = both.reshape(2, new * TOPK)
+        picks = both.reshape(2, TOPK * new)
         onehot = (picks[:, :, None] == jnp.arange(experts_all, dtype=jnp.int32)).astype(bf16)
-        order = jnp.arange(new * TOPK, dtype=jnp.int32)
+        order = jnp.arange(TOPK * new, dtype=jnp.int32)
         before = (order[:, None] > order[None, :]).astype(bf16)
         earlier = jnp.einsum("pq,rqe->rpe", before, onehot, preferred_element_type=f32)
         rank = jnp.sum(earlier * onehot.astype(f32), axis=2).astype(jnp.int32)
         rank = rank - (zl % 2) * SHARE
         there = picks - zh * plane
-        slot = (there * 2 + jnp.arange(2, dtype=jnp.int32)[:, None]) * SHARE + rank
+        which = jnp.arange(2, dtype=jnp.int32)[:, None]
+        slot = there * rows + which * SHARE + rank
         here = (there >= 0) & (there < plane) & (rank >= 0) & (rank < SHARE)
-        return jnp.where(here, slot, -1).reshape(2 * new, TOPK)
-
-    slot_iota = jnp.arange(slots, dtype=jnp.int32)
-    slot_held = slots_of(held_ids)
-    slot_own = slots_of(expert_ids)
-    chosen_t = jnp.zeros((slots, 2 * new), bf16)
-    chosen = jnp.zeros((2 * new, slots), bf16)
-    for pick in range(TOPK):
-        chosen_t = chosen_t + (slot_held[:, pick][None, :] == slot_iota[:, None]).astype(bf16)
-        chosen = chosen + (slot_own[:, pick : pick + 1] == slot_iota[None, :]).astype(bf16)
-
-    outgoing = dispatch(chosen_t, spread(held_share, Z, 8))
+        slot = jnp.where(here, slot, -1).reshape(2, TOPK, new)
+        token = jnp.arange(new, dtype=jnp.int32)[None, :]
+        chunk = token // span - zh * plane
+        common = chunk * rows + 2 * SHARE + which * span + token % span
+        common = jnp.where((chunk >= 0) & (chunk < plane), common, -1)
+        chosen = (common.reshape(1, 2 * new) == slot_iota[:, None]).astype(bf16)
+        for pick in range(TOPK):
+            at = slot[:, pick].reshape(1, 2 * new)
+            chosen = chosen + (at == slot_iota[:, None]).astype(bf16)
+        return chosen
+
+    chosen_held = chosen_of(held_ids)
+    chosen_own = chosen_of(ids_t)
+
+    outgoing = dispatch(chosen_held, spread(held_share, Z, 8))
+    hidden_late, down_w, outgoing = barrier((hidden, w_down, outgoing))
     rows_mine = lax.all_to_all(
-        outgoing.reshape(plane, 2 * SHARE, half), ("x", "y"), 0, 0, tiled=True
-    ).reshape(slots, half)
-
-    hidden_late, _ = barrier((hidden, outgoing))
+        outgoing.reshape(plane, rows, half), ("x", "y"), 0, 0, tiled=True
+    )
+    pair_down = lax.ppermute(down_w, "zl", neighbours)
+
     own_full = lax.all_gather(hidden_late, TP, axis=1, tiled=True)
-    rows_mine, own_full = barrier((rows_mine, own_full))
+    rows_mine, own_full, pair_down = barrier((rows_mine, own_full, pair_down))
     rows_theirs = swap_core(rows_mine)
     new_cache = new_kv(own_full, gain, w_qkv, rope_tables(lengths[0], new))[:, None]
 
-    served_mine, served_theirs = routed_mlp(
+    served_mine, served_theirs = experts(
         place,
         rows_mine,
         rows_theirs,
-        256,
-        ffn,
+        2,
+        ffn_gain[None],
         w_router.T,
         w_in,
         w_down,
         pair_gate,
         pair_up,
         pair_down,
-    )
-    slot_at = holder_slot.reshape(2, plane).T.reshape(reqs)
-    order = (slot_at % plane) * 2 + slot_at // plane
-    served = reorder(order, served_mine, swap_core(served_theirs))
+        w_sh_in.swapaxes(1, 2),
+        w_sh_down,
+    )
+    chunk, row = slot_iota // rows, slot_iota % rows
+    common = row >= 2 * SHARE
+    size = jnp.where(common, span, SHARE)
+    base = jnp.where(common, 2 * SHARE, 0)
+    which, inner = (row - base) // size, (row - base) % size
+    slot_at = jnp.sum(
+        jnp.where((which * plane + chunk)[:, None] == req_iota[None, :], holder_slot[None, :], 0),
+        axis=1,
+    )
+    origin = (slot_at % plane) * rows + base + (slot_at // plane) * size + inner
+    order = (origin[:, None] == slot_iota[None, :]).astype(bf16)
+    served = reorder(
+        order, served_mine.reshape(slots, half), swap_core(served_theirs).reshape(slots, half)
+    )
     returned = lax.all_to_all(
-        served.reshape(plane, 2 * SHARE, half), ("x", "y"), 0, 0, tiled=True
+        served.reshape(plane, rows, half), ("x", "y"), 0, 0, tiled=True
     ).reshape(slots, half)
 
-    shares = lax.all_gather(held_share, REQ, axis=0)
-    own_slot = lax.dynamic_index_in_dim(holder_slot, expert, 0, keepdims=False)
-    own_share = lax.dynamic_index_in_dim(shares, own_slot, 0, keepdims=False)
-    own_rows = lax.all_gather(own_share, TP, axis=1, tiled=True)
-    shared_mine, shared_theirs = shared_mlp(
-        place, own_rows, ffn, w_sh_in.swapaxes(1, 2), w_sh_down
-    )
-    shared_theirs = swap_core(shared_theirs)
-
-    packed = combine(place, chosen, returned, shared_mine, shared_theirs, own_share)
+    packed = combine(chosen_own, returned)
     summed = lax.all_to_all(packed, Z, 0, 0, tiled=True)
     out_hidden, last = finish(summed, reqs)
 

time: 324 us -> 280 us (0.86)
  waiting for transfers between devices: 112 us -> 59.1 us
  blocking collectives: 77 us -> 103 us
  between operations: 18.4 us -> 2.96 us
  local copies, waits for them, and re-layouts: 16.8 us -> 10.5 us
  starting transfers between devices: 52.7 us -> 57.5 us
    all_gather x1 -> x0, waiting for transfers between devices: 28.9 us -> none  [local(): shares = lax.all_gather(held_share, REQ, axis=0)]
    all_to_all x0 -> x1, blocking collectives: none -> 26.1 us  [local(): lax.all_to_all(served.reshape(plane, rows, half), ('x', 'y'), 0, 0, tiled...]
    all_gather x1 -> x0, blocking collectives: 17.9 us -> none  [local(): own_rows = lax.all_gather(own_share, TP, axis=1, tiled=True)]
    all_to_all x1, waiting for transfers between devices: 27 us -> 11.5 us  [local(): leg = lax.all_to_all(leg, REQ, 0, 0, tiled=True)]
    all_to_all x1, waiting for transfers between devices: 13.4 us -> 0.02 us  [local(): parts = lax.all_to_all(parts, TP, 0, 0, tiled=True)]
    all_gather x1, blocking collectives: 16.7 us -> 29.5 us  [local(): own_full = lax.all_gather(hidden_late, TP, axis=1, tiled=True)]
    ppermute x5, waiting for transfers between devices: 0.3 us -> 9.42 us  [the longest x2 9.41 us: chosen_of(): other = lax.ppermute(ids, 'zh', [(0, 1), (1, 0)])]
    all_to_all x1, starting transfers between devices: 7.04 us -> 14.5 us  [local(): leg = lax.all_to_all(chunks, REQ, 0, 0, tiled=True)]
  transfers between devices with their start and end apart: 17 -> 14, of which waited for: 10 -> 8; matrix products, arithmetic and copies ran while one was open for 6% -> 5% of each run, Pallas kernels for 9% -> 3%
where the time goes in v4:
time: 280 us; the launch traced here: 279 us
  blocking collectives  103 us (37%)
  waiting for transfers between devices  59.1 us (21%)
  starting transfers between devices  57.5 us (21%)
  Pallas kernels  35.8 us (13%)
  local copies, waits for them, and re-layouts  10.5 us (4%)
  other arithmetic  9.35 us (3%)
  between operations  2.96 us (1%)
    all_gather x1, blocking collectives, local(): own_full = lax.all_gather(hidden_late, TP, axis=1, tiled=True)  29.5 us
    all_gather x1, blocking collectives, local(): full = lax.all_gather(held, TP, axis=1, tiled=True)  26.9 us
    all_to_all x1, blocking collectives, local(): lax.all_to_all(served.reshape(plane, rows, half), ('x', 'y'), 0, 0, tiled...  26.1 us
    all_to_all x1, blocking collectives, local(): summed = lax.all_to_all(packed, Z, 0, 0, tiled=True)  20.1 us
    all_to_all x1, waiting for transfers between devices, spread(): return lax.all_to_all(wide, axes, 0, 0, tiled=True)  15.5 us
    all_to_all x1, starting transfers between devices, local(): leg = lax.all_to_all(chunks, REQ, 0, 0, tiled=True)  14.5 us
    all_to_all x1, waiting for transfers between devices, local(): leg = lax.all_to_all(leg, REQ, 0, 0, tiled=True)  11.5 us
    pallas_call x1, Pallas kernels, experts(): pl.pallas_call(experts_body, grid=(steps,), out_shape=(shape, shape), in_...  11.4 us
  transfers between devices with their start and end apart: 14, of which 8 were waited for; matrix products, arithmetic and copies ran while one was open for 5% of the time, Pallas kernels for 3%

profile of v4, /device:TPU:1, one launch (start us, length us, event | category | flops | bytes accessed | tf_op | source)
XLA Modules:
  0.0 278.6 jit_solution(5089350313369359467)
XLA Ops:
  3.7 14.5 %all-to-all-start = ((bf16[32,8,256]{2,1,0:T(8,128)(2,1)}), bf16[32,8,256]{2,1,0:T(8,128)(2,1)S(1)}, u32[]{:S(2)}, u32[]{:S(2)}) async-start(bf16[32,8,256]{2,1,0:T(8,128)(2,1)} %pad_maximum_fusion), calls=%async_computation | async-start | bytes 262144 | tf_op jit(solution)/shard_map/all_to_all | solution.py:431
  18.2 5.2 %collective-permute-start = (s32[6,128]{1,0:T(8,128)}, s32[6,128]{1,0:T(8,128)S(1)}, u32[]{:S(2)}, u32[]{:S(2)}) collective-permute-start(s32[6,128]{1,0:T(8,128)} %bitcast.108), channel_id=1, source_target_pairs={{0,128},{128,0},{1,129},{129,1},{2,130},{130,2},{3,131},{131,3},{4... | collective-permute-start | bytes 9224 | tf_op jit(solution)/shard_map/ppermute | solution.py:460
  25.1 4.4 %all-to-all-done = bf16[32,8,256]{2,1,0:T(8,128)(2,1)S(1)} async-done(((bf16[32,8,256]{2,1,0:T(8,128)(2,1)}), bf16[32,8,256]{2,1,0:T(8,128)(2,1)S(1)}, u32[]{:S(2)}, u32[]{:S(2)}) %all-to-all-start) | async-done | bytes 131104 | tf_op jit(solution)/shard_map/all_to_all | solution.py:431
  31.5 3.9 %all-to-all-start.1 = ((bf16[32,8,256]{2,1,0:T(8,128)(2,1)}), bf16[32,8,256]{2,1,0:T(8,128)(2,1)S(1)}, u32[]{:S(2)}, u32[]{:S(2)}) async-start(bf16[32,8,256]{2,1,0:T(8,128)(2,1)} %gather_fusion), calls=%async_computation.1 | async-start | bytes 262144 | tf_op jit(solution)/shard_map/all_to_all | solution.py:442
  36.0 11.5 %all-to-all-done.1 = bf16[32,8,256]{2,1,0:T(8,128)(2,1)S(1)} async-done(((bf16[32,8,256]{2,1,0:T(8,128)(2,1)}), bf16[32,8,256]{2,1,0:T(8,128)(2,1)S(1)}, u32[]{:S(2)}, u32[]{:S(2)}) %all-to-all-start.1) | async-done | bytes 131104 | tf_op jit(solution)/shard_map/all_to_all | solution.py:442
  51.3 26.9 %all_gather.6.full_ref = bf16[128,2048]{1,0:T(8,128)(2,1)} all-gather(bf16[128,256]{1,0:T(8,128)(2,1)S(1)} %reshape.436), channel_id=1, replica_groups=mesh['zh'=2,'x'=4,'y'=4,'zl'=4,'core'=2] {'zl','core'}, dimensions={1}, use_global_device_ids=true | all-gather | bytes 589824 | tf_op jit(solution)/shard_map/all_gather | solution.py:449
  78.2 5.7 %attend.1 = bf16[8,128,256]{2,1,0:T(8,128)(2,1)} custom-call(s32[1]{0:T(128)} %bitcast.33.len_ref, bf16[128,2048]{1,0:T(8,128)(2,1)} %all_gather.6.full_ref, bf16[1,2048]{1,0:T(2,128)(2,1)} %broadcast_in_dim.145.gain_ref, bf16[3,2048,256]{2,1,0:T(8,128)(2,1)} %w_ref.4, f32[128,128]{1,0:T(8,128)} %get-tuple-element.93.cos_ref, ...), custom_call_target="tpu_custom_call" | custom-call | tf_op jit(solution)/shard_map/attend/pallas_call | solution.py:116
  83.9 3.6 %all-to-all-start.2 = ((bf16[8,128,256]{2,1,0:T(8,128)(2,1)}), bf16[8,128,256]{2,1,0:T(8,128)(2,1)S(1)}, u32[]{:S(2)}, u32[]{:S(2)}) async-start(bf16[8,128,256]{2,1,0:T(8,128)(2,1)} %attend.1), calls=%async_computation.2 | async-start | bytes 1048576 | tf_op jit(solution)/shard_map/all_to_all | solution.py:454
  87.5 4.3 %collective-permute-start.2 = (s32[6,128]{1,0:T(8,128)S(1)}, s32[6,128]{1,0:T(8,128)S(1)}, u32[]{:S(2)}, u32[]{:S(2)}) collective-permute-start(s32[6,128]{1,0:T(8,128)S(1)} %reshape.445), channel_id=1, source_target_pairs={{0,128},{128,0},{1,129},{129,1},{2,130},{130,2},{3,131},{131,3},{4... | collective-permute-start | bytes 9224 | tf_op jit(solution)/shard_map/ppermute | solution.py:460
  91.9 9.4 %collective-permute-done.2 = s32[6,128]{1,0:T(8,128)S(1)} collective-permute-done((s32[6,128]{1,0:T(8,128)S(1)}, s32[6,128]{1,0:T(8,128)S(1)}, u32[]{:S(2)}, u32[]{:S(2)}) %collective-permute-start.2) | collective-permute-done | bytes 3104 | tf_op jit(solution)/shard_map/ppermute | solution.py:460
  103.2 5.5 %all-to-all-start.3 = ((bf16[8,128,256]{2,1,0:T(8,128)(2,1)}), bf16[8,128,256]{2,1,0:T(8,128)(2,1)S(1)}, u32[]{:S(2)}, u32[]{:S(2)}) async-start(bf16[8,128,256]{2,1,0:T(8,128)(2,1)} %broadcast_in_dim.146), calls=%async_computation.3 | async-start | bytes 1048576 | tf_op jit(solution)/shard_map/all_to_all | solution.py:127
  110.7 15.5 %all-to-all-done.3.parts_ref = bf16[8,128,256]{2,1,0:T(8,128)(2,1)S(1)} async-done(((bf16[8,128,256]{2,1,0:T(8,128)(2,1)}), bf16[8,128,256]{2,1,0:T(8,128)(2,1)S(1)}, u32[]{:S(2)}, u32[]{:S(2)}) %all-to-all-start.3) | async-done | bytes 524320 | tf_op jit(solution)/shard_map/all_to_all | solution.py:127
  129.8 5.7 %all-to-all-start.4 = ((bf16[16,40,1024]{2,1,0:T(8,128)(2,1)}), bf16[16,40,1024]{2,1,0:T(8,128)(2,1)S(1)}, u32[]{:S(2)}, u32[]{:S(2)}) async-start(bf16[16,40,1024]{2,1,0:T(8,128)(2,1)} %bitcast.100), calls=%async_computation.4 | async-start | bytes 2621440 | tf_op jit(solution)/shard_map/all_to_all | solution.py:489
  135.6 29.5 %all_gather.7.full_ref = bf16[128,2048]{1,0:T(8,128)(2,1)} all-gather(bf16[128,256]{1,0:T(8,128)(2,1)S(1)} %copy-done.4), channel_id=1, replica_groups=mesh['zh'=2,'x'=4,'y'=4,'zl'=4,'core'=2] {'zl','core'}, dimensions={1}, use_global_device_ids=true | all-gather | bytes 589824 | tf_op jit(solution)/shard_map/all_gather | solution.py:494
  169.5 11.4 %experts.1 = (bf16[16,40,1024]{2,1,0:T(8,128)(2,1)}, bf16[16,40,1024]{2,1,0:T(8,128)(2,1)}) custom-call(s32[2]{0:T(128)} %pad_add_fusion.place_ref, bf16[16,40,1024]{2,1,0:T(8,128)(2,1)} %copy-done.2, bf16[16,40,1024]{2,1,0:T(8,128)(2,1)} %copy-done.11, bf16[1,2048]{1,0:T(2,128)(2,1)} %broadcast_in_dim.147.gain_ref, bf16[32,2048]{1,0:T(8,128)(2,1)} %bitcast.134, ...), custom_call_target="tpu_custom_call" | custom-call | flops 2768240640 | bytes 11730944 | tf_op jit(solution)/shard_map/experts/pallas_call | solution.py:233
  185.2 5.2 %reorder.1 = bf16[640,1024]{1,0:T(8,128)(2,1)} custom-call(bf16[640,640]{1,0:T(8,128)(2,1)} %fusion.5.order_ref, bf16[640,1024]{1,0:T(8,128)(2,1)} %bitcast.104, bf16[640,1024]{1,0:T(8,128)(2,1)} %bitcast.105), custom_call_target="tpu_custom_call" | custom-call | tf_op jit(solution)/shard_map/reorder/pallas_call | solution.py:262
  190.4 26.1 %all_to_all.49 = bf16[16,40,1024]{2,1,0:T(8,128)(2,1)} all-to-all(bf16[16,40,1024]{2,1,0:T(8,128)(2,1)} %bitcast.99), channel_id=1, replica_groups=mesh['zh'=2,'x'=4,'y'=4,'zl'=4,'core'=2] {'x','y'}, dimensions={0} | all-to-all | bytes 2621440 | tf_op jit(solution)/shard_map/all_to_all | solution.py:528
  216.5 2.9 %combine.1 = bf16[8,136,256]{2,1,0:T(8,128)(2,1)} custom-call(bf16[640,256]{1,0:T(8,128)(2,1)} %get-tuple-element.83.chosen_ref, bf16[640,1024]{1,0:T(8,128)(2,1)} %bitcast.101), custom_call_target="tpu_custom_call" | custom-call | tf_op jit(solution)/shard_map/combine/pallas_call | solution.py:311
  219.4 20.1 %all_to_all.50.parts_ref = bf16[8,136,256]{2,1,0:T(8,128)(2,1)} all-to-all(bf16[8,136,256]{2,1,0:T(8,128)(2,1)} %combine.1), channel_id=1, replica_groups=mesh['zh'=2,'x'=4,'y'=4,'zl'=4,'core'=2] {'zh','zl'}, dimensions={0} | all-to-all | bytes 1114112 | tf_op jit(solution)/shard_map/all_to_all | solution.py:533
  241.4 7.3 %all-to-all-start.7 = ((bf16[32,16,128]{2,1,0:T(8,128)(2,1)}), bf16[32,16,128]{2,1,0:T(8,128)(2,1)S(1)}, u32[]{:S(2)}, u32[]{:S(2)}) async-start(bf16[32,16,128]{2,1,0:T(8,128)(2,1)} %get-tuple-element.39), calls=%async_computation.7 | async-start | bytes 262144 | tf_op jit(solution)/shard_map/all_to_all | solution.py:536
  249.3 6.9 %all-to-all-done.7.last_ref = bf16[32,16,128]{2,1,0:T(8,128)(2,1)S(1)} async-done(((bf16[32,16,128]{2,1,0:T(8,128)(2,1)}), bf16[32,16,128]{2,1,0:T(8,128)(2,1)S(1)}, u32[]{:S(2)}, u32[]{:S(2)}) %all-to-all-start.7) | async-done | bytes 131104 | tf_op jit(solution)/shard_map/all_to_all | solution.py:536
  259.4 5.6 %all-to-all-start.8 = ((f32[256,1,32]{2,1,0:T(1,128)}), f32[256,1,32]{2,1,0:T(1,128)S(1)}, u32[]{:S(2)}, u32[]{:S(2)}) async-start(f32[256,1,32]{2,1,0:T(1,128)} %bitcast.107), calls=%async_computation.8 | async-start | bytes 262144 | tf_op jit(solution)/shard_map/all_to_all | solution.py:539
  265.7 3.4 %new_kv.1 = bf16[2,128,256]{2,1,0:T(8,128)(2,1)} custom-call(bf16[128,2048]{1,0:T(8,128)(2,1)} %all_gather.7.full_ref, bf16[1,2048]{1,0:T(2,128)(2,1)} %broadcast_in_dim.145.gain_ref, bf16[3,2048,256]{2,1,0:T(8,128)(2,1)} %w_ref.4, f32[128,128]{1,0:T(8,128)} %get-tuple-element.95.cos_ref, f32[128,128]{1,0:T(8,128)} %get-tuple-element.96.sin_ref), custom_call_target="tpu_custom_call" | custom-call | tf_op jit(solution)/shard_map/new_kv/pallas_call | solution.py:63
  269.7 8.0 %all-to-all-done.8 = f32[256,1,32]{2,1,0:T(1,128)S(1)} async-done(((f32[256,1,32]{2,1,0:T(1,128)}), f32[256,1,32]{2,1,0:T(1,128)S(1)}, u32[]{:S(2)}, u32[]{:S(2)}) %all-to-all-start.8) | async-done | bytes 32800 | tf_op jit(solution)/shard_map/all_to_all | solution.py:539
  (105 shorter events, 33.2 us)
Async XLA Ops:
  3.7 25.8 %all-to-all-start = ((bf16[32,8,256]{2,1,0:T(8,128)(2,1)}), bf16[32,8,256]{2,1,0:T(8,128)(2,1)S(1)}, u32[]{:S(2)}, u32[]{:S(2)}) async-start(bf16[32,8,256]{2,1,0:T(8,128)(2,1)} %pad_maximum_fusion), calls=%async_computation | async-start | bytes 262144 | tf_op jit(solution)/shard_map/all_to_all | solution.py:431
  18.2 73.7 %collective-permute-start = (s32[6,128]{1,0:T(8,128)}, s32[6,128]{1,0:T(8,128)S(1)}, u32[]{:S(2)}, u32[]{:S(2)}) collective-permute-start(s32[6,128]{1,0:T(8,128)} %bitcast.108), channel_id=1, source_target_pairs={{0,128},{128,0},{1,129},{129,1},{2,130},{130,2},{3,131},{131,3},{4... | collective-permute-start | bytes 9224 | tf_op jit(solution)/shard_map/ppermute | solution.py:460
  23.4 11.9 %copy-start.7 = (bf16[2048]{0:T(1024)(128)(2,1)S(1)}, bf16[2048]{0:T(1024)(128)(2,1)}, u32[]{:S(2)}) copy-start(bf16[2048]{0:T(1024)(128)(2,1)} %param.17) | copy-start | bytes 12292
  29.5 18.0 %collective-permute-start.1 = (bf16[176,2048]{1,0:T(8,128)(2,1)S(1)}, bf16[176,2048]{1,0:T(8,128)(2,1)S(1)}, u32[]{:S(2)}, u32[]{:S(2)}) collective-permute-start(bf16[176,2048]{1,0:T(8,128)(2,1)S(1)} %get-tuple-element.24), channel_id=1, source_target_pairs={{0,2},{2,0},{4,6},{6,4},{1,3},{3,1},{5,7},{7,5},{8,10},{10,8},{12,... | collective-permute-start | bytes 2162696 | tf_op jit(solution)/shard_map/ppermute | solution.py:435
  31.5 16.1 %all-to-all-start.1 = ((bf16[32,8,256]{2,1,0:T(8,128)(2,1)}), bf16[32,8,256]{2,1,0:T(8,128)(2,1)S(1)}, u32[]{:S(2)}, u32[]{:S(2)}) async-start(bf16[32,8,256]{2,1,0:T(8,128)(2,1)} %gather_fusion), calls=%async_computation.1 | async-start | bytes 262144 | tf_op jit(solution)/shard_map/all_to_all | solution.py:442
  47.5 36.4 %copy-start.13 = (bf16[176,2048]{1,0:T(8,128)(2,1)}, bf16[176,2048]{1,0:T(8,128)(2,1)S(1)}, u32[]{:S(2)}) copy-start(bf16[176,2048]{1,0:T(8,128)(2,1)S(1)} %collective-permute-done.1.pg_ref) | copy-start | bytes 2162692
  47.5 36.4 %collective-permute-start.3 = (bf16[176,2048]{1,0:T(8,128)(2,1)S(1)}, bf16[176,2048]{1,0:T(8,128)(2,1)S(1)}, u32[]{:S(2)}, u32[]{:S(2)}) collective-permute-start(bf16[176,2048]{1,0:T(8,128)(2,1)S(1)} %get-tuple-element.26), channel_id=1, source_target_pairs={{0,2},{2,0},{4,6},{6,4},{1,3},{3,1},{5,7},{7,5},{8,10},{10,8},{12,... | collective-permute-start | bytes 2162696 | tf_op jit(solution)/shard_map/ppermute | solution.py:444
  78.2 13.7 %copy-start.5 = (s32[128,6]{0,1:T(8,128)S(1)}, s32[128,6]{0,1:T(8,128)}, u32[]{:S(2)}) copy-start(s32[128,6]{0,1:T(8,128)} %param.25) | copy-start | bytes 9220
  83.9 18.2 %copy-start.14 = (bf16[176,2048]{1,0:T(8,128)(2,1)}, bf16[176,2048]{1,0:T(8,128)(2,1)S(1)}, u32[]{:S(2)}) copy-start(bf16[176,2048]{1,0:T(8,128)(2,1)S(1)} %collective-permute-done.3.pu_ref) | copy-start | bytes 2162692
  83.9 18.3 %all-to-all-start.2 = ((bf16[8,128,256]{2,1,0:T(8,128)(2,1)}), bf16[8,128,256]{2,1,0:T(8,128)(2,1)S(1)}, u32[]{:S(2)}, u32[]{:S(2)}) async-start(bf16[8,128,256]{2,1,0:T(8,128)(2,1)} %attend.1), calls=%async_computation.2 | async-start | bytes 1048576 | tf_op jit(solution)/shard_map/all_to_all | solution.py:454
  87.5 13.8 %collective-permute-start.2 = (s32[6,128]{1,0:T(8,128)S(1)}, s32[6,128]{1,0:T(8,128)S(1)}, u32[]{:S(2)}, u32[]{:S(2)}) collective-permute-start(s32[6,128]{1,0:T(8,128)S(1)} %reshape.445), channel_id=1, source_target_pairs={{0,128},{128,0},{1,129},{129,1},{2,130},{130,2},{3,131},{131,3},{4... | collective-permute-start | bytes 9224 | tf_op jit(solution)/shard_map/ppermute | solution.py:460
  103.2 23.1 %all-to-all-start.3 = ((bf16[8,128,256]{2,1,0:T(8,128)(2,1)}), bf16[8,128,256]{2,1,0:T(8,128)(2,1)S(1)}, u32[]{:S(2)}, u32[]{:S(2)}) async-start(bf16[8,128,256]{2,1,0:T(8,128)(2,1)} %broadcast_in_dim.146), calls=%async_computation.3 | async-start | bytes 1048576 | tf_op jit(solution)/shard_map/all_to_all | solution.py:127
  129.8 5.7 %copy-start.12 = (bf16[1,176,2048]{2,1,0:T(8,128)(2,1)S(1)}, bf16[1,176,2048]{2,1,0:T(8,128)(2,1)}, u32[]{:S(2)}) copy-start(bf16[1,176,2048]{2,1,0:T(8,128)(2,1)} %param.27) | copy-start | bytes 2162692
  129.8 5.8 %copy-start.4 = (bf16[128,256]{1,0:T(8,128)(2,1)S(1)}, bf16[128,256]{1,0:T(8,128)(2,1)}, u32[]{:S(2)}) copy-start(bf16[128,256]{1,0:T(8,128)(2,1)} %param.16) | copy-start | bytes 196612
  129.8 35.7 %copy-start.8 = (bf16[2048]{0:T(1024)(128)(2,1)S(1)}, bf16[2048]{0:T(1024)(128)(2,1)}, u32[]{:S(2)}) copy-start(bf16[2048]{0:T(1024)(128)(2,1)} %param.23) | copy-start | bytes 12292
  129.8 35.3 %all-to-all-start.4 = ((bf16[16,40,1024]{2,1,0:T(8,128)(2,1)}), bf16[16,40,1024]{2,1,0:T(8,128)(2,1)S(1)}, u32[]{:S(2)}, u32[]{:S(2)}) async-start(bf16[16,40,1024]{2,1,0:T(8,128)(2,1)} %bitcast.100), calls=%async_computation.4 | async-start | bytes 2621440 | tf_op jit(solution)/shard_map/all_to_all | solution.py:489
  135.5 29.6 %collective-permute-start.4 = (bf16[176,2048]{1,0:T(8,128)(2,1)S(1)}, bf16[176,2048]{1,0:T(8,128)(2,1)}, u32[]{:S(2)}, u32[]{:S(2)}) collective-permute-start(bf16[176,2048]{1,0:T(8,128)(2,1)S(1)} %bitcast.133), channel_id=1, source_target_pairs={{0,2},{2,0},{4,6},{6,4},{1,3},{3,1},{5,7},{7,5},{8,10},{10,8},{12,... | collective-permute-start | bytes 2162696 | tf_op jit(solution)/shard_map/ppermute | solution.py:492
  165.1 3.3 %copy-start.2 = (bf16[16,40,1024]{2,1,0:T(8,128)(2,1)}, bf16[16,40,1024]{2,1,0:T(8,128)(2,1)S(1)}, u32[]{:S(2)}) copy-start(bf16[16,40,1024]{2,1,0:T(8,128)(2,1)S(1)} %all-to-all-done.4.a_ref) | copy-start | bytes 3932164
  165.1 3.3 %collective-permute-start.5 = (bf16[16,40,1024]{2,1,0:T(8,128)(2,1)S(1)}, bf16[16,40,1024]{2,1,0:T(8,128)(2,1)S(1)}, u32[]{:S(2)}, u32[]{:S(2)}) collective-permute-start(bf16[16,40,1024]{2,1,0:T(8,128)(2,1)S(1)} %all-to-all-done.4.a_ref), channel_id=1, source_target_pairs={{0,1},{1,0},{2,3},{3,2},{4,5},{5,4},{6,7},{7,6},{8,9},{9,8},{10,11... | collective-permute-start | bytes 3932168 | tf_op jit(solution)/shard_map/ppermute | solution.py:131
  180.8 3.2 %collective-permute-start.6 = (bf16[16,40,1024]{2,1,0:T(8,128)(2,1)}, bf16[16,40,1024]{2,1,0:T(8,128)(2,1)S(1)}, u32[]{:S(2)}, u32[]{:S(2)}) collective-permute-start(bf16[16,40,1024]{2,1,0:T(8,128)(2,1)} %get-tuple-element.36), channel_id=1, source_target_pairs={{0,1},{1,0},{2,3},{3,2},{4,5},{5,4},{6,7},{7,6},{8,9},{9,8},{10,11... | collective-permute-start | bytes 3932168 | tf_op jit(solution)/shard_map/ppermute | solution.py:131
  219.3 29.4 %copy-start.9 = (bf16[2048]{0:T(1024)(128)(2,1)S(1)}, bf16[2048]{0:T(1024)(128)(2,1)}, u32[]{:S(2)}) copy-start(bf16[2048]{0:T(1024)(128)(2,1)} %param.30) | copy-start | bytes 12292
  241.4 14.8 %all-to-all-start.7 = ((bf16[32,16,128]{2,1,0:T(8,128)(2,1)}), bf16[32,16,128]{2,1,0:T(8,128)(2,1)S(1)}, u32[]{:S(2)}, u32[]{:S(2)}) async-start(bf16[32,16,128]{2,1,0:T(8,128)(2,1)} %get-tuple-element.39), calls=%async_computation.7 | async-start | bytes 262144 | tf_op jit(solution)/shard_map/all_to_all | solution.py:536
  259.4 18.4 %all-to-all-start.8 = ((f32[256,1,32]{2,1,0:T(1,128)}), f32[256,1,32]{2,1,0:T(1,128)S(1)}, u32[]{:S(2)}, u32[]{:S(2)}) async-start(f32[256,1,32]{2,1,0:T(1,128)} %bitcast.107), calls=%async_computation.8 | async-start | bytes 262144 | tf_op jit(solution)/shard_map/all_to_all | solution.py:539
  265.7 3.4 %copy-start.6 = (f32[32,1]{1,0:T(8,128)S(1)}, f32[32,1]{1,0:T(8,128)}, u32[]{:S(2)}) copy-start(f32[32,1]{1,0:T(8,128)} %get-tuple-element.40) | copy-start | bytes 388
  (5 other events, 5.1 us)

commit v5 on v4

--- a/solution.py
+++ b/solution.py
@@ -131,6 +131,10 @@
     return lax.ppermute(value, "core", [(0, 1), (1, 0)])
 
 
+def column_swap(value):
+    return lax.ppermute(value, "zh", [(0, 1), (1, 0)])
+
+
 def dot_nt(a, b):
     return lax.dot_general(a, b, (((1,), (1,)), ((), ())), preferred_element_type=f32)
 
@@ -251,10 +255,8 @@
 
 
 def reorder_body(order_ref, a_ref, b_ref, o_ref):
-    o_ref[...] = (
-        jnp.dot(order_ref[...], a_ref[...], preferred_element_type=f32)
-        + jnp.dot(order_ref[...], b_ref[...], preferred_element_type=f32)
-    ).astype(bf16)
+    total = (a_ref[...].astype(f32) + b_ref[...].astype(f32)).astype(bf16)
+    o_ref[...] = jnp.dot(order_ref[...], total, preferred_element_type=f32).astype(bf16)
 
 
 def reorder(order, a, b):
@@ -429,9 +431,11 @@
     w_in = w_exp_in[0].swapaxes(1, 2)
     w_down = w_exp_down[0]
     leg = lax.all_to_all(chunks, REQ, 0, 0, tiled=True)
+    ids_there, up_w = barrier((column_swap(ids_t), w_in[1]))
     leg, gate_w = barrier((leg, w_in[0]))
 
     neighbours = [(0, 1), (1, 0), (2, 3), (3, 2)]
+    pair_up = lax.ppermute(up_w, "zl", neighbours)
     pair_gate = lax.ppermute(gate_w, "zl", neighbours)
 
     req_iota = jnp.arange(reqs, dtype=jnp.int32)
@@ -440,8 +444,7 @@
     )
     leg = leg.at[owner_of].get(mode="promise_in_bounds")
     leg = lax.all_to_all(leg, REQ, 0, 0, tiled=True)
-    leg, pair_gate, up_w = barrier((leg, pair_gate, w_in[1]))
-    pair_up = lax.ppermute(up_w, "zl", neighbours)
+    leg, pair_up = barrier((leg, pair_up))
     held = leg[:, :span].reshape(new, feat)
     held_ids = leg[0, span:-1].reshape(TOPK, new).astype(jnp.int32)
     held_len = leg[0, -1, :1].astype(jnp.int32) * 32 + leg[0, -1, feat // 2 :][:1].astype(jnp.int32)
@@ -450,14 +453,13 @@
     parts = attend(
         held_len, full, gain, w_qkv, rope_tables(held_len, new), kv_cache, w_out
     )
-    parts, pair_up = barrier((parts, pair_up))
+    parts, pair_gate = barrier((parts, pair_gate))
     parts = lax.all_to_all(parts, TP, 0, 0, tiled=True)
     held_share = (held.astype(f32) + jnp.sum(parts.astype(f32), axis=0)).astype(bf16)
 
     slot_iota = jnp.arange(slots, dtype=jnp.int32)
 
-    def chosen_of(ids):
-        other = lax.ppermute(ids, "zh", [(0, 1), (1, 0)])
+    def chosen_of(ids, other):
         both = jnp.where(zh == 0, jnp.stack([ids, other]), jnp.stack([other, ids]))
         picks = both.reshape(2, TOPK * new)
         onehot = (picks[:, :, None] == jnp.arange(experts_all, dtype=jnp.int32)).astype(bf16)
@@ -481,21 +483,18 @@
             chosen = chosen + (at == slot_iota[:, None]).astype(bf16)
         return chosen
 
-    chosen_held = chosen_of(held_ids)
-    chosen_own = chosen_of(ids_t)
+    chosen_held = chosen_of(held_ids, column_swap(held_ids))
+    chosen_own = chosen_of(ids_t, ids_there)
 
     outgoing = dispatch(chosen_held, spread(held_share, Z, 8))
-    hidden_late, down_w, outgoing = barrier((hidden, w_down, outgoing))
+    down_w, outgoing = barrier((w_down, outgoing))
     rows_mine = lax.all_to_all(
         outgoing.reshape(plane, rows, half), ("x", "y"), 0, 0, tiled=True
     )
     pair_down = lax.ppermute(down_w, "zl", neighbours)
 
-    own_full = lax.all_gather(hidden_late, TP, axis=1, tiled=True)
-    rows_mine, own_full, pair_down = barrier((rows_mine, own_full, pair_down))
+    rows_mine, pair_down = barrier((rows_mine, pair_down))
     rows_theirs = swap_core(rows_mine)
-    new_cache = new_kv(own_full, gain, w_qkv, rope_tables(lengths[0], new))[:, None]
-
     served_mine, served_theirs = experts(
         place,
         rows_mine,
@@ -525,9 +524,14 @@
     served = reorder(
         order, served_mine.reshape(slots, half), swap_core(served_theirs).reshape(slots, half)
     )
+    served, hidden_late = barrier((served, hidden))
     returned = lax.all_to_all(
         served.reshape(plane, rows, half), ("x", "y"), 0, 0, tiled=True
     ).reshape(slots, half)
+
+    own_full = lax.all_gather(hidden_late, TP, axis=1, tiled=True)
+    returned, own_full = barrier((returned, own_full))
+    new_cache = new_kv(own_full, gain, w_qkv, rope_tables(lengths[0], new))[:, None]
 
     packed = combine(chosen_own, returned)
     summed = lax.all_to_all(packed, Z, 0, 0, tiled=True)

time: 280 us -> 266 us (0.950)
  blocking collectives: 103 us -> 56.5 us
  waiting for transfers between devices: 59.1 us -> 78.9 us
  starting transfers between devices: 57.5 us -> 69.9 us
    all_to_all x1 -> x0, blocking collectives: 26.1 us -> none  [local(): lax.all_to_all(served.reshape(plane, rows, half), ('x', 'y'), 0, 0, tiled...]
    ppermute x1, waiting for transfers between devices: 0.01 us -> 16.6 us  [local(): pair_down = lax.ppermute(down_w, 'zl', neighbours)]
    all_gather x1, blocking collectives: 29.5 us -> 16.3 us  [local(): own_full = lax.all_gather(hidden_late, TP, axis=1, tiled=True)]
    all_gather x1, blocking collectives: 26.9 us -> 22.4 us  [local(): full = lax.all_gather(held, TP, axis=1, tiled=True)]
    all_to_all x1, starting transfers between devices: 3.86 us -> 7.83 us  [local(): leg = lax.all_to_all(leg, REQ, 0, 0, tiled=True)]
    all_to_all x0 -> x1, starting transfers between devices: none -> 3.83 us  [local(): lax.all_to_all(served.reshape(plane, rows, half), ('x', 'y'), 0, 0, tiled...]
    all_to_all x1, starting transfers between devices: 7.28 us -> 10.9 us  [local(): last_all = lax.all_to_all(last, ('core', 'x', 'y'), 0, 0, tiled=True)]
    ppermute x2, starting transfers between devices: 0.59 us -> 4.1 us  [swap_core(): return lax.ppermute(value, 'core', [(0, 1), (1, 0)])]
  transfers between devices with their start and end apart: 14 -> 15, of which waited for: 8 -> 13; matrix products, arithmetic and copies ran while one was open for 5% -> 5% of each run, Pallas kernels for 3% -> 3%
where the time goes in v5:
time: 266 us; the launch traced here: 265 us
  waiting for transfers between devices  78.9 us (30%)
  starting transfers between devices  69.9 us (26%)
  blocking collectives  56.5 us (21%)
  Pallas kernels  34.7 us (13%)
  local copies, waits for them, and re-layouts  11.7 us (4%)
  other arithmetic  9.32 us (4%)
  between operations  2.95 us (1%)
    all_gather x1, blocking collectives, local(): full = lax.all_gather(held, TP, axis=1, tiled=True)  22.4 us
    all_to_all x1, blocking collectives, local(): summed = lax.all_to_all(packed, Z, 0, 0, tiled=True)  17.8 us
    ppermute x1, waiting for transfers between devices, local(): pair_down = lax.ppermute(down_w, 'zl', neighbours)  16.6 us
    all_gather x1, blocking collectives, local(): own_full = lax.all_gather(hidden_late, TP, axis=1, tiled=True)  16.3 us
    all_to_all x1, waiting for transfers between devices, spread(): return lax.all_to_all(wide, axes, 0, 0, tiled=True)  15.5 us
    all_to_all x1, starting transfers between devices, local(): leg = lax.all_to_all(chunks, REQ, 0, 0, tiled=True)  14.5 us
    pallas_call x1, Pallas kernels, experts(): pl.pallas_call(experts_body, grid=(steps,), out_shape=(shape, shape), in_...  11.3 us
    all_to_all x1, starting transfers between devices, local(): last_all = lax.all_to_all(last, ('core', 'x', 'y'), 0, 0, tiled=True)  10.9 us
  transfers between devices with their start and end apart: 15, of which 13 were waited for; matrix products, arithmetic and copies ran while one was open for 5% of the time, Pallas kernels for 3%

profile of v5, /device:TPU:1, one launch (start us, length us, event | category | flops | bytes accessed | tf_op | source)
XLA Modules:
  0.0 264.7 jit_solution(9418403471571641539)
XLA Ops:
  3.7 14.5 %all-to-all-start = ((bf16[32,8,256]{2,1,0:T(8,128)(2,1)}), bf16[32,8,256]{2,1,0:T(8,128)(2,1)S(1)}, u32[]{:S(2)}, u32[]{:S(2)}) async-start(bf16[32,8,256]{2,1,0:T(8,128)(2,1)} %pad_maximum_fusion), calls=%async_computation | async-start | bytes 262144 | tf_op jit(solution)/shard_map/all_to_all | solution.py:433
  18.2 5.2 %collective-permute-start = (s32[6,128]{1,0:T(8,128)}, s32[6,128]{1,0:T(8,128)S(1)}, u32[]{:S(2)}, u32[]{:S(2)}) collective-permute-start(s32[6,128]{1,0:T(8,128)} %bitcast.108), channel_id=1, source_target_pairs={{0,128},{128,0},{1,129},{129,1},{2,130},{130,2},{3,131},{131,3},{4... | collective-permute-start | bytes 9224 | tf_op jit(solution)/shard_map/ppermute | solution.py:135
  25.9 3.6 %all-to-all-done = bf16[32,8,256]{2,1,0:T(8,128)(2,1)S(1)} async-done(((bf16[32,8,256]{2,1,0:T(8,128)(2,1)}), bf16[32,8,256]{2,1,0:T(8,128)(2,1)S(1)}, u32[]{:S(2)}, u32[]{:S(2)}) %all-to-all-start) | async-done | bytes 131104 | tf_op jit(solution)/shard_map/all_to_all | solution.py:433
  30.7 7.8 %all-to-all-start.1 = ((bf16[32,8,256]{2,1,0:T(8,128)(2,1)}), bf16[32,8,256]{2,1,0:T(8,128)(2,1)S(1)}, u32[]{:S(2)}, u32[]{:S(2)}) async-start(bf16[32,8,256]{2,1,0:T(8,128)(2,1)} %gather_fusion), calls=%async_computation.1 | async-start | bytes 262144 | tf_op jit(solution)/shard_map/all_to_all | solution.py:446
  40.0 10.5 %all-to-all-done.1 = bf16[32,8,256]{2,1,0:T(8,128)(2,1)S(1)} async-done(((bf16[32,8,256]{2,1,0:T(8,128)(2,1)}), bf16[32,8,256]{2,1,0:T(8,128)(2,1)S(1)}, u32[]{:S(2)}, u32[]{:S(2)}) %all-to-all-start.1) | async-done | bytes 131104 | tf_op jit(solution)/shard_map/all_to_all | solution.py:446
  53.7 22.4 %all_gather.6.full_ref = bf16[128,2048]{1,0:T(8,128)(2,1)} all-gather(bf16[128,256]{1,0:T(8,128)(2,1)S(1)} %reshape.436), channel_id=1, replica_groups=mesh['zh'=2,'x'=4,'y'=4,'zl'=4,'core'=2] {'zl','core'}, dimensions={1}, use_global_device_ids=true | all-gather | bytes 589824 | tf_op jit(solution)/shard_map/all_gather | solution.py:452
  76.1 5.7 %attend.1 = bf16[8,128,256]{2,1,0:T(8,128)(2,1)} custom-call(s32[1]{0:T(128)} %bitcast.33.len_ref, bf16[128,2048]{1,0:T(8,128)(2,1)} %all_gather.6.full_ref, bf16[1,2048]{1,0:T(2,128)(2,1)} %broadcast_in_dim.145.gain_ref, bf16[3,2048,256]{2,1,0:T(8,128)(2,1)} %w_ref.4, f32[128,128]{1,0:T(8,128)} %get-tuple-element.99.cos_ref, ...), custom_call_target="tpu_custom_call" | custom-call | tf_op jit(solution)/shard_map/attend/pallas_call | solution.py:116
  81.8 3.6 %all-to-all-start.2 = ((bf16[8,128,256]{2,1,0:T(8,128)(2,1)}), bf16[8,128,256]{2,1,0:T(8,128)(2,1)S(1)}, u32[]{:S(2)}, u32[]{:S(2)}) async-start(bf16[8,128,256]{2,1,0:T(8,128)(2,1)} %attend.1), calls=%async_computation.2 | async-start | bytes 1048576 | tf_op jit(solution)/shard_map/all_to_all | solution.py:457
  88.4 9.4 %collective-permute-done.2 = s32[6,128]{1,0:T(8,128)S(1)} collective-permute-done((s32[6,128]{1,0:T(8,128)S(1)}, s32[6,128]{1,0:T(8,128)S(1)}, u32[]{:S(2)}, u32[]{:S(2)}) %collective-permute-start.2) | collective-permute-done | bytes 3104 | tf_op jit(solution)/shard_map/ppermute | solution.py:135
  101.0 4.2 %all-to-all-start.3 = ((bf16[8,128,256]{2,1,0:T(8,128)(2,1)}), bf16[8,128,256]{2,1,0:T(8,128)(2,1)S(1)}, u32[]{:S(2)}, u32[]{:S(2)}) async-start(bf16[8,128,256]{2,1,0:T(8,128)(2,1)} %broadcast_in_dim.146), calls=%async_computation.3 | async-start | bytes 1048576 | tf_op jit(solution)/shard_map/all_to_all | solution.py:127
  107.2 15.5 %all-to-all-done.3.parts_ref = bf16[8,128,256]{2,1,0:T(8,128)(2,1)S(1)} async-done(((bf16[8,128,256]{2,1,0:T(8,128)(2,1)}), bf16[8,128,256]{2,1,0:T(8,128)(2,1)S(1)}, u32[]{:S(2)}, u32[]{:S(2)}) %all-to-all-start.3) | async-done | bytes 524320 | tf_op jit(solution)/shard_map/all_to_all | solution.py:127
  126.2 6.3 %all-to-all-start.4 = ((bf16[16,40,1024]{2,1,0:T(8,128)(2,1)}), bf16[16,40,1024]{2,1,0:T(8,128)(2,1)S(1)}, u32[]{:S(2)}, u32[]{:S(2)}) async-start(bf16[16,40,1024]{2,1,0:T(8,128)(2,1)} %bitcast.100), calls=%async_computation.4 | async-start | bytes 2621440 | tf_op jit(solution)/shard_map/all_to_all | solution.py:491
  132.7 16.6 %collective-permute-done.4.pd_ref = bf16[176,2048]{1,0:T(8,128)(2,1)} collective-permute-done((bf16[176,2048]{1,0:T(8,128)(2,1)S(1)}, bf16[176,2048]{1,0:T(8,128)(2,1)}, u32[]{:S(2)}, u32[]{:S(2)}) %collective-permute-start.4) | collective-permute-done | bytes 720928 | tf_op jit(solution)/shard_map/ppermute | solution.py:494
  150.6 3.7 %collective-permute-start.5 = (bf16[16,40,1024]{2,1,0:T(8,128)(2,1)S(1)}, bf16[16,40,1024]{2,1,0:T(8,128)(2,1)S(1)}, u32[]{:S(2)}, u32[]{:S(2)}) collective-permute-start(bf16[16,40,1024]{2,1,0:T(8,128)(2,1)S(1)} %all-to-all-done.4.a_ref), channel_id=1, source_target_pairs={{0,1},{1,0},{2,3},{3,2},{4,5},{5,4},{6,7},{7,6},{8,9},{9,8},{10,11... | collective-permute-start | bytes 3932168 | tf_op jit(solution)/shard_map/ppermute | solution.py:131
  158.1 11.3 %experts.1 = (bf16[16,40,1024]{2,1,0:T(8,128)(2,1)}, bf16[16,40,1024]{2,1,0:T(8,128)(2,1)}) custom-call(s32[2]{0:T(128)} %pad_add_fusion.place_ref, bf16[16,40,1024]{2,1,0:T(8,128)(2,1)} %copy-done.3, bf16[16,40,1024]{2,1,0:T(8,128)(2,1)} %copy-done.12, bf16[1,2048]{1,0:T(2,128)(2,1)} %broadcast_in_dim.147.gain_ref, bf16[32,2048]{1,0:T(8,128)(2,1)} %bitcast.134, ...), custom_call_target="tpu_custom_call" | custom-call | flops 2768240640 | bytes 11730944 | tf_op jit(solution)/shard_map/experts/pallas_call | solution.py:237
  173.8 4.2 %reorder.1 = bf16[640,1024]{1,0:T(8,128)(2,1)} custom-call(bf16[640,640]{1,0:T(8,128)(2,1)} %fusion.5.order_ref, bf16[640,1024]{1,0:T(8,128)(2,1)} %bitcast.104, bf16[640,1024]{1,0:T(8,128)(2,1)} %bitcast.105), custom_call_target="tpu_custom_call" | custom-call | tf_op jit(solution)/shard_map/reorder/pallas_call | solution.py:264
  178.0 3.8 %all-to-all-start.5 = ((bf16[16,40,1024]{2,1,0:T(8,128)(2,1)}), bf16[16,40,1024]{2,1,0:T(8,128)(2,1)S(1)}, u32[]{:S(2)}, u32[]{:S(2)}) async-start(bf16[16,40,1024]{2,1,0:T(8,128)(2,1)} %bitcast.99), calls=%async_computation.5 | async-start | bytes 2621440 | tf_op jit(solution)/shard_map/all_to_all | solution.py:528
  181.9 16.3 %all_gather.7.full_ref = bf16[128,2048]{1,0:T(8,128)(2,1)} all-gather(bf16[128,256]{1,0:T(8,128)(2,1)S(1)} %copy-done.5), channel_id=1, replica_groups=mesh['zh'=2,'x'=4,'y'=4,'zl'=4,'core'=2] {'zl','core'}, dimensions={1}, use_global_device_ids=true | all-gather | bytes 589824 | tf_op jit(solution)/shard_map/all_gather | solution.py:532
  204.0 17.8 %all_to_all.49.parts_ref = bf16[8,136,256]{2,1,0:T(8,128)(2,1)} all-to-all(bf16[8,136,256]{2,1,0:T(8,128)(2,1)} %combine.1), channel_id=1, replica_groups=mesh['zh'=2,'x'=4,'y'=4,'zl'=4,'core'=2] {'zh','zl'}, dimensions={0} | all-to-all | bytes 1114112 | tf_op jit(solution)/shard_map/all_to_all | solution.py:537
  223.9 10.9 %all-to-all-start.7 = ((bf16[32,16,128]{2,1,0:T(8,128)(2,1)}), bf16[32,16,128]{2,1,0:T(8,128)(2,1)S(1)}, u32[]{:S(2)}, u32[]{:S(2)}) async-start(bf16[32,16,128]{2,1,0:T(8,128)(2,1)} %get-tuple-element.45), calls=%async_computation.7 | async-start | bytes 262144 | tf_op jit(solution)/shard_map/all_to_all | solution.py:540
  235.4 6.9 %all-to-all-done.7.last_ref = bf16[32,16,128]{2,1,0:T(8,128)(2,1)S(1)} async-done(((bf16[32,16,128]{2,1,0:T(8,128)(2,1)}), bf16[32,16,128]{2,1,0:T(8,128)(2,1)S(1)}, u32[]{:S(2)}, u32[]{:S(2)}) %all-to-all-start.7) | async-done | bytes 131104 | tf_op jit(solution)/shard_map/all_to_all | solution.py:540
  245.4 5.6 %all-to-all-start.8 = ((f32[256,1,32]{2,1,0:T(1,128)}), f32[256,1,32]{2,1,0:T(1,128)S(1)}, u32[]{:S(2)}, u32[]{:S(2)}) async-start(f32[256,1,32]{2,1,0:T(1,128)} %bitcast.107), calls=%async_computation.8 | async-start | bytes 262144 | tf_op jit(solution)/shard_map/all_to_all | solution.py:543
  251.8 3.4 %new_kv.1 = bf16[2,128,256]{2,1,0:T(8,128)(2,1)} custom-call(bf16[128,2048]{1,0:T(8,128)(2,1)} %all_gather.7.full_ref, bf16[1,2048]{1,0:T(2,128)(2,1)} %broadcast_in_dim.145.gain_ref, bf16[3,2048,256]{2,1,0:T(8,128)(2,1)} %w_ref.4, f32[128,128]{1,0:T(8,128)} %get-tuple-element.101.cos_ref, f32[128,128]{1,0:T(8,128)} %get-tuple-element.102.sin_ref), custom_call_target="tpu_custom_call" | custom-call | tf_op jit(solution)/shard_map/new_kv/pallas_call | solution.py:63
  255.8 8.0 %all-to-all-done.8 = f32[256,1,32]{2,1,0:T(1,128)S(1)} async-done(((f32[256,1,32]{2,1,0:T(1,128)}), f32[256,1,32]{2,1,0:T(1,128)S(1)}, u32[]{:S(2)}, u32[]{:S(2)}) %all-to-all-start.8) | async-done | bytes 32800 | tf_op jit(solution)/shard_map/all_to_all | solution.py:543
  (108 shorter events, 44.4 us)
Async XLA Ops:
  3.7 25.8 %all-to-all-start = ((bf16[32,8,256]{2,1,0:T(8,128)(2,1)}), bf16[32,8,256]{2,1,0:T(8,128)(2,1)S(1)}, u32[]{:S(2)}, u32[]{:S(2)}) async-start(bf16[32,8,256]{2,1,0:T(8,128)(2,1)} %pad_maximum_fusion), calls=%async_computation | async-start | bytes 262144 | tf_op jit(solution)/shard_map/all_to_all | solution.py:433
  18.2 7.7 %collective-permute-start = (s32[6,128]{1,0:T(8,128)}, s32[6,128]{1,0:T(8,128)S(1)}, u32[]{:S(2)}, u32[]{:S(2)}) collective-permute-start(s32[6,128]{1,0:T(8,128)} %bitcast.108), channel_id=1, source_target_pairs={{0,128},{128,0},{1,129},{129,1},{2,130},{130,2},{3,131},{131,3},{4... | collective-permute-start | bytes 9224 | tf_op jit(solution)/shard_map/ppermute | solution.py:135
  23.4 15.1 %copy-start.8 = (bf16[2048]{0:T(1024)(128)(2,1)S(1)}, bf16[2048]{0:T(1024)(128)(2,1)}, u32[]{:S(2)}) copy-start(bf16[2048]{0:T(1024)(128)(2,1)} %param.17) | copy-start | bytes 12292
  25.9 24.6 %collective-permute-start.1 = (bf16[176,2048]{1,0:T(8,128)(2,1)S(1)}, bf16[176,2048]{1,0:T(8,128)(2,1)S(1)}, u32[]{:S(2)}, u32[]{:S(2)}) collective-permute-start(bf16[176,2048]{1,0:T(8,128)(2,1)S(1)} %get-tuple-element.28), channel_id=1, source_target_pairs={{0,2},{2,0},{4,6},{6,4},{1,3},{3,1},{5,7},{7,5},{8,10},{10,8},{12,... | collective-permute-start | bytes 2162696 | tf_op jit(solution)/shard_map/ppermute | solution.py:438
  30.7 19.7 %all-to-all-start.1 = ((bf16[32,8,256]{2,1,0:T(8,128)(2,1)}), bf16[32,8,256]{2,1,0:T(8,128)(2,1)S(1)}, u32[]{:S(2)}, u32[]{:S(2)}) async-start(bf16[32,8,256]{2,1,0:T(8,128)(2,1)} %gather_fusion), calls=%async_computation.1 | async-start | bytes 262144 | tf_op jit(solution)/shard_map/all_to_all | solution.py:446
  39.2 42.5 %collective-permute-start.3 = (bf16[176,2048]{1,0:T(8,128)(2,1)S(1)}, bf16[176,2048]{1,0:T(8,128)(2,1)S(1)}, u32[]{:S(2)}, u32[]{:S(2)}) collective-permute-start(bf16[176,2048]{1,0:T(8,128)(2,1)S(1)} %get-tuple-element.30), channel_id=1, source_target_pairs={{0,2},{2,0},{4,6},{6,4},{1,3},{3,1},{5,7},{7,5},{8,10},{10,8},{12,... | collective-permute-start | bytes 2162696 | tf_op jit(solution)/shard_map/ppermute | solution.py:439
  50.4 31.3 %copy-start.14 = (bf16[176,2048]{1,0:T(8,128)(2,1)}, bf16[176,2048]{1,0:T(8,128)(2,1)S(1)}, u32[]{:S(2)}) copy-start(bf16[176,2048]{1,0:T(8,128)(2,1)S(1)} %collective-permute-done.1.pu_ref) | copy-start | bytes 2162692
  76.1 12.3 %copy-start.6 = (s32[128,6]{0,1:T(8,128)S(1)}, s32[128,6]{0,1:T(8,128)}, u32[]{:S(2)}) copy-start(s32[128,6]{0,1:T(8,128)} %param.25) | copy-start | bytes 9220
  81.8 16.8 %copy-start.15 = (bf16[176,2048]{1,0:T(8,128)(2,1)}, bf16[176,2048]{1,0:T(8,128)(2,1)S(1)}, u32[]{:S(2)}) copy-start(bf16[176,2048]{1,0:T(8,128)(2,1)S(1)} %collective-permute-done.3.pg_ref) | copy-start | bytes 2162692
  81.8 18.3 %all-to-all-start.2 = ((bf16[8,128,256]{2,1,0:T(8,128)(2,1)}), bf16[8,128,256]{2,1,0:T(8,128)(2,1)S(1)}, u32[]{:S(2)}, u32[]{:S(2)}) async-start(bf16[8,128,256]{2,1,0:T(8,128)(2,1)} %attend.1), calls=%async_computation.2 | async-start | bytes 1048576 | tf_op jit(solution)/shard_map/all_to_all | solution.py:457
  85.4 12.4 %collective-permute-start.2 = (s32[6,128]{1,0:T(8,128)S(1)}, s32[6,128]{1,0:T(8,128)S(1)}, u32[]{:S(2)}, u32[]{:S(2)}) collective-permute-start(s32[6,128]{1,0:T(8,128)S(1)} %reshape.445), channel_id=1, source_target_pairs={{0,128},{128,0},{1,129},{129,1},{2,130},{130,2},{3,131},{131,3},{4... | collective-permute-start | bytes 9224 | tf_op jit(solution)/shard_map/ppermute | solution.py:135
  101.0 21.7 %all-to-all-start.3 = ((bf16[8,128,256]{2,1,0:T(8,128)(2,1)}), bf16[8,128,256]{2,1,0:T(8,128)(2,1)S(1)}, u32[]{:S(2)}, u32[]{:S(2)}) async-start(bf16[8,128,256]{2,1,0:T(8,128)(2,1)} %broadcast_in_dim.146), calls=%async_computation.3 | async-start | bytes 1048576 | tf_op jit(solution)/shard_map/all_to_all | solution.py:127
  126.2 6.3 %copy-start.13 = (bf16[1,176,2048]{2,1,0:T(8,128)(2,1)S(1)}, bf16[1,176,2048]{2,1,0:T(8,128)(2,1)}, u32[]{:S(2)}) copy-start(bf16[1,176,2048]{2,1,0:T(8,128)(2,1)} %param.27) | copy-start | bytes 2162692
  126.2 28.1 %copy-start.9 = (bf16[2048]{0:T(1024)(128)(2,1)S(1)}, bf16[2048]{0:T(1024)(128)(2,1)}, u32[]{:S(2)}) copy-start(bf16[2048]{0:T(1024)(128)(2,1)} %param.23) | copy-start | bytes 12292
  126.2 24.3 %all-to-all-start.4 = ((bf16[16,40,1024]{2,1,0:T(8,128)(2,1)}), bf16[16,40,1024]{2,1,0:T(8,128)(2,1)S(1)}, u32[]{:S(2)}, u32[]{:S(2)}) async-start(bf16[16,40,1024]{2,1,0:T(8,128)(2,1)} %bitcast.100), calls=%async_computation.4 | async-start | bytes 2621440 | tf_op jit(solution)/shard_map/all_to_all | solution.py:491
  132.6 16.7 %collective-permute-start.4 = (bf16[176,2048]{1,0:T(8,128)(2,1)S(1)}, bf16[176,2048]{1,0:T(8,128)(2,1)}, u32[]{:S(2)}, u32[]{:S(2)}) collective-permute-start(bf16[176,2048]{1,0:T(8,128)(2,1)S(1)} %bitcast.133), channel_id=1, source_target_pairs={{0,2},{2,0},{4,6},{6,4},{1,3},{3,1},{5,7},{7,5},{8,10},{10,8},{12,... | collective-permute-start | bytes 2162696 | tf_op jit(solution)/shard_map/ppermute | solution.py:494
  150.6 6.4 %copy-start.3 = (bf16[16,40,1024]{2,1,0:T(8,128)(2,1)}, bf16[16,40,1024]{2,1,0:T(8,128)(2,1)S(1)}, u32[]{:S(2)}) copy-start(bf16[16,40,1024]{2,1,0:T(8,128)(2,1)S(1)} %all-to-all-done.4.a_ref) | copy-start | bytes 3932164
  150.6 6.4 %collective-permute-start.5 = (bf16[16,40,1024]{2,1,0:T(8,128)(2,1)S(1)}, bf16[16,40,1024]{2,1,0:T(8,128)(2,1)S(1)}, u32[]{:S(2)}, u32[]{:S(2)}) collective-permute-start(bf16[16,40,1024]{2,1,0:T(8,128)(2,1)S(1)} %all-to-all-done.4.a_ref), channel_id=1, source_target_pairs={{0,1},{1,0},{2,3},{3,2},{4,5},{5,4},{6,7},{7,6},{8,9},{9,8},{10,11... | collective-permute-start | bytes 3932168 | tf_op jit(solution)/shard_map/ppermute | solution.py:131
  169.4 3.2 %collective-permute-start.6 = (bf16[16,40,1024]{2,1,0:T(8,128)(2,1)}, bf16[16,40,1024]{2,1,0:T(8,128)(2,1)S(1)}, u32[]{:S(2)}, u32[]{:S(2)}) collective-permute-start(bf16[16,40,1024]{2,1,0:T(8,128)(2,1)} %get-tuple-element.39), channel_id=1, source_target_pairs={{0,1},{1,0},{2,3},{3,2},{4,5},{5,4},{6,7},{7,6},{8,9},{9,8},{10,11... | collective-permute-start | bytes 3932168 | tf_op jit(solution)/shard_map/ppermute | solution.py:131
  178.0 3.8 %copy-start.5 = (bf16[128,256]{1,0:T(8,128)(2,1)S(1)}, bf16[128,256]{1,0:T(8,128)(2,1)}, u32[]{:S(2)}) copy-start(bf16[128,256]{1,0:T(8,128)(2,1)} %param.16) | copy-start | bytes 196612
  178.0 22.1 %all-to-all-start.5 = ((bf16[16,40,1024]{2,1,0:T(8,128)(2,1)}), bf16[16,40,1024]{2,1,0:T(8,128)(2,1)S(1)}, u32[]{:S(2)}, u32[]{:S(2)}) async-start(bf16[16,40,1024]{2,1,0:T(8,128)(2,1)} %bitcast.99), calls=%async_computation.5 | async-start | bytes 2621440 | tf_op jit(solution)/shard_map/all_to_all | solution.py:528
  204.0 30.8 %copy-start.10 = (bf16[2048]{0:T(1024)(128)(2,1)S(1)}, bf16[2048]{0:T(1024)(128)(2,1)}, u32[]{:S(2)}) copy-start(bf16[2048]{0:T(1024)(128)(2,1)} %param.30) | copy-start | bytes 12292
  223.9 18.5 %all-to-all-start.7 = ((bf16[32,16,128]{2,1,0:T(8,128)(2,1)}), bf16[32,16,128]{2,1,0:T(8,128)(2,1)S(1)}, u32[]{:S(2)}, u32[]{:S(2)}) async-start(bf16[32,16,128]{2,1,0:T(8,128)(2,1)} %get-tuple-element.45), calls=%async_computation.7 | async-start | bytes 262144 | tf_op jit(solution)/shard_map/all_to_all | solution.py:540
  245.4 18.5 %all-to-all-start.8 = ((f32[256,1,32]{2,1,0:T(1,128)}), f32[256,1,32]{2,1,0:T(1,128)S(1)}, u32[]{:S(2)}, u32[]{:S(2)}) async-start(f32[256,1,32]{2,1,0:T(1,128)} %bitcast.107), calls=%async_computation.8 | async-start | bytes 262144 | tf_op jit(solution)/shard_map/all_to_all | solution.py:543
  (7 other events, 9.6 us)

commit v6 on v5

--- a/solution.py
+++ b/solution.py
@@ -69,8 +69,9 @@
     )(full, gain, w_qkv, *tables)
 
 
-def attend_body(len_ref, full_ref, gain_ref, qkv_ref, cos_ref, sin_ref, kv_ref, w_ref, o_ref):
-    length = len_ref[0]
+def attend_body(place_ref, full_ref, gain_ref, qkv_ref, cos_ref, sin_ref, kv_ref, w_ref, o_ref):
+    length = place_ref[0]
+    core = place_ref[1]
     ctx = kv_ref.shape[2]
     new = full_ref.shape[0]
     normed = norm_rows(full_ref, gain_ref)
@@ -102,24 +103,25 @@
         )
         heads.append(out.astype(bf16))
     attn = jnp.concatenate(heads, axis=1)
-    wide = o_ref.shape[2]
-    for part in range(o_ref.shape[0]):
-        o_ref[part] = jnp.dot(
+    wide = o_ref.shape[3]
+    for part in range(2 * o_ref.shape[1]):
+        at = core if part % 2 == 0 else 1 - core
+        o_ref[at, part // 2] = jnp.dot(
             attn, w_ref[:, part * wide : (part + 1) * wide], preferred_element_type=f32
         ).astype(bf16)
 
 
-def attend(length, full, gain, w_qkv, tables, kv_cache, w_out):
+def attend(place, full, gain, w_qkv, tables, kv_cache, w_out):
     vm = pl.BlockSpec(memory_space=pltpu.VMEM)
     new = full.shape[0]
     feat = w_out.shape[0]
     return pl.pallas_call(
         attend_body,
-        out_shape=jax.ShapeDtypeStruct((w_out.shape[1] // feat, new, feat), bf16),
+        out_shape=jax.ShapeDtypeStruct((2, w_out.shape[1] // feat // 2, new, feat), bf16),
         in_specs=[pl.BlockSpec(memory_space=pltpu.SMEM)] + [vm] * 7,
         out_specs=vm,
         name="attend",
-    )(length, full, gain, w_qkv, *tables, kv_cache, w_out)
+    )(place, full, gain, w_qkv, *tables, kv_cache, w_out)
 
 
 def spread(value, axes, count):
@@ -166,7 +168,7 @@
 
 def experts_body(
     place_ref, a_ref, b_ref, gain_ref, router_ref, in_ref, down_ref, pg_ref, pu_ref, pd_ref,
-    si_ref, sd_ref, om_ref, ot_ref, xr_ref, xs_ref,
+    si_ref, sd_ref, om_ref, ot_ref, xr_ref, xs_ref, ys_ref,
 ):
     first = place_ref[0] == 0
     feat = xr_ref.shape[1] // 8
@@ -192,6 +194,13 @@
     def _():
         fill(b_ref, a_ref)
 
+    common = norm_rows(xs_ref, gain_ref)
+    common = expert_rows(common, si_ref[0], si_ref[1], sd_ref[...])
+    common = common + xs_ref[...] * 0.125
+    half = shared // 2
+    for piece in range(2 * chunks):
+        ys_ref[piece, :half, :] = common[piece * half : (piece + 1) * half]
+
     rows = norm_rows(xr_ref, gain_ref)
     out = expert_rows(rows, in_ref[0], in_ref[1], down_ref[...])
     out = out + expert_rows(rows, pg_ref[...], pu_ref[...], pd_ref[...])
@@ -199,16 +208,15 @@
     raised = jnp.exp(logits - jnp.max(logits, axis=-1, keepdims=True))
     own = lax.broadcasted_iota(jnp.int32, logits.shape, 1) == place_ref[1]
     picked = jnp.sum(jnp.where(own, raised, 0.0), axis=-1, keepdims=True)
-    out = out * (picked / jnp.sum(raised, axis=-1, keepdims=True))
-    common = norm_rows(xs_ref, gain_ref)
-    common = expert_rows(common, si_ref[0], si_ref[1], sd_ref[...])
-    common = common + xs_ref[...] * 0.125
+    xr_ref[...] = out * (picked / jnp.sum(raised, axis=-1, keepdims=True))
 
     def store(even_ref, odd_ref):
         for chunk in range(chunks):
-            top = out[chunk * routed : (chunk + 1) * routed]
-            low = common[chunk * shared : (chunk + 1) * shared]
-            both = jnp.concatenate([top, low], axis=0).astype(bf16)
+            origin = [place_ref[2 + 2 * chunk + zo] for zo in range(2)]
+            size = routed // 2
+            top = [xr_ref[pl.ds(pl.multiple_of(at * size, size), size), :] for at in origin]
+            low = [ys_ref[at, :half, :] for at in origin]
+            both = jnp.concatenate(top + low, axis=0).astype(bf16)
             for part in range(4):
                 piece = slice(part * feat, (part + 1) * feat)
                 even_ref[chunk, :, piece] = both[:, 2 * part * feat : (2 * part + 1) * feat]
@@ -223,27 +231,21 @@
         store(ot_ref, om_ref)
 
 
-def experts(place, rows_mine, rows_theirs, steps, *weights):
+def experts(place, rows_mine, rows_theirs, *weights):
+    vm = pl.BlockSpec(memory_space=pltpu.VMEM)
     count, span, half = rows_mine.shape
     width = 2 * half
-    block = count // steps
-    row_spec = pl.BlockSpec((block, span, half), lambda i: (i, 0, 0))
-
-    def whole(array):
-        zeros = (0,) * array.ndim
-        return pl.BlockSpec(array.shape, lambda i: zeros)
-
     shape = jax.ShapeDtypeStruct(rows_mine.shape, bf16)
+    shared = span - 2 * SHARE
     return pl.pallas_call(
         experts_body,
-        grid=(steps,),
         out_shape=(shape, shape),
-        in_specs=[pl.BlockSpec(memory_space=pltpu.SMEM), row_spec, row_spec]
-        + [whole(array) for array in weights],
-        out_specs=(row_spec, row_spec),
+        in_specs=[pl.BlockSpec(memory_space=pltpu.SMEM)] + [vm] * (2 + len(weights)),
+        out_specs=(vm, vm),
         scratch_shapes=[
-            pltpu.VMEM((block * 2 * SHARE, width), f32),
-            pltpu.VMEM((block * (span - 2 * SHARE), width), f32),
+            pltpu.VMEM((count * 2 * SHARE, width), f32),
+            pltpu.VMEM((count * shared, width), f32),
+            pltpu.VMEM((2 * count, 8, width), f32),
         ],
         cost_estimate=pl.CostEstimate(
             flops=6 * count * span * width * 352,
@@ -252,22 +254,6 @@
         ),
         name="experts",
     )(place, rows_mine, rows_theirs, *weights)
-
-
-def reorder_body(order_ref, a_ref, b_ref, o_ref):
-    total = (a_ref[...].astype(f32) + b_ref[...].astype(f32)).astype(bf16)
-    o_ref[...] = jnp.dot(order_ref[...], total, preferred_element_type=f32).astype(bf16)
-
-
-def reorder(order, a, b):
-    vm = pl.BlockSpec(memory_space=pltpu.VMEM)
-    return pl.pallas_call(
-        reorder_body,
-        out_shape=jax.ShapeDtypeStruct(a.shape, bf16),
-        in_specs=[vm, vm, vm],
-        out_specs=vm,
-        name="reorder",
-    )(order, a, b)
 
 
 def dispatch_body(chosen_ref, parts_ref, out_ref):
@@ -417,8 +403,9 @@
     span = new // reqs
     rows = 2 * (SHARE + span)
     slots = plane * rows
-    place = jnp.stack([core, expert]).astype(jnp.int32)
-    gain = attn_gain[None]
+    slot_at = holder_slot.reshape(2, plane).T.reshape(reqs)
+    order = (slot_at % plane) * 2 + slot_at // plane
+    place = jnp.concatenate([jnp.stack([core, expert]).astype(jnp.int32), order])
     barrier = lax.optimization_barrier
 
     ids_t = expert_ids.T
@@ -430,13 +417,12 @@
     chunks = jnp.concatenate([hidden.reshape(reqs, span, feat), meta], axis=1)
     w_in = w_exp_in[0].swapaxes(1, 2)
     w_down = w_exp_down[0]
+    neighbours = [(0, 1), (1, 0), (2, 3), (3, 2)]
+    pair_gate = lax.ppermute(w_in[0], "zl", neighbours)
     leg = lax.all_to_all(chunks, REQ, 0, 0, tiled=True)
     ids_there, up_w = barrier((column_swap(ids_t), w_in[1]))
-    leg, gate_w = barrier((leg, w_in[0]))
-
-    neighbours = [(0, 1), (1, 0), (2, 3), (3, 2)]
+
     pair_up = lax.ppermute(up_w, "zl", neighbours)
-    pair_gate = lax.ppermute(gate_w, "zl", neighbours)
 
     req_iota = jnp.arange(reqs, dtype=jnp.int32)
     owner_of = jnp.sum(
@@ -444,17 +430,27 @@
     )
     leg = leg.at[owner_of].get(mode="promise_in_bounds")
     leg = lax.all_to_all(leg, REQ, 0, 0, tiled=True)
-    leg, pair_up = barrier((leg, pair_up))
+    leg, pair_gate, gain, gain_ffn, gain_final, place = barrier(
+        (leg, pair_gate, attn_gain[None], ffn_gain[None], final_gain[None], place)
+    )
     held = leg[:, :span].reshape(new, feat)
     held_ids = leg[0, span:-1].reshape(TOPK, new).astype(jnp.int32)
     held_len = leg[0, -1, :1].astype(jnp.int32) * 32 + leg[0, -1, feat // 2 :][:1].astype(jnp.int32)
 
     full = lax.all_gather(held, TP, axis=1, tiled=True)
     parts = attend(
-        held_len, full, gain, w_qkv, rope_tables(held_len, new), kv_cache, w_out
-    )
-    parts, pair_gate = barrier((parts, pair_gate))
-    parts = lax.all_to_all(parts, TP, 0, 0, tiled=True)
+        jnp.concatenate([held_len, place[:1]]),
+        full,
+        gain,
+        w_qkv,
+        rope_tables(held_len, new),
+        kv_cache,
+        w_out,
+    )
+    parts, pair_up = barrier((parts, pair_up))
+    parts = (parts[0].astype(f32) + swap_core(parts[1]).astype(f32)).astype(bf16)
+    parts, held_ids = barrier((parts, held_ids))
+    parts = lax.all_to_all(parts, "zl", 0, 0, tiled=True)
     held_share = (held.astype(f32) + jnp.sum(parts.astype(f32), axis=0)).astype(bf16)
 
     slot_iota = jnp.arange(slots, dtype=jnp.int32)
@@ -499,8 +495,7 @@
         place,
         rows_mine,
         rows_theirs,
-        2,
-        ffn_gain[None],
+        gain_ffn,
         w_router.T,
         w_in,
         w_down,
@@ -510,24 +505,9 @@
         w_sh_in.swapaxes(1, 2),
         w_sh_down,
     )
-    chunk, row = slot_iota // rows, slot_iota % rows
-    common = row >= 2 * SHARE
-    size = jnp.where(common, span, SHARE)
-    base = jnp.where(common, 2 * SHARE, 0)
-    which, inner = (row - base) // size, (row - base) % size
-    slot_at = jnp.sum(
-        jnp.where((which * plane + chunk)[:, None] == req_iota[None, :], holder_slot[None, :], 0),
-        axis=1,
-    )
-    origin = (slot_at % plane) * rows + base + (slot_at // plane) * size + inner
-    order = (origin[:, None] == slot_iota[None, :]).astype(bf16)
-    served = reorder(
-        order, served_mine.reshape(slots, half), swap_core(served_theirs).reshape(slots, half)
-    )
+    served = (served_mine.astype(f32) + swap_core(served_theirs).astype(f32)).astype(bf16)
     served, hidden_late = barrier((served, hidden))
-    returned = lax.all_to_all(
-        served.reshape(plane, rows, half), ("x", "y"), 0, 0, tiled=True
-    ).reshape(slots, half)
+    returned = lax.all_to_all(served, ("x", "y"), 0, 0, tiled=True).reshape(slots, half)
 
     own_full = lax.all_gather(hidden_late, TP, axis=1, tiled=True)
     returned, own_full = barrier((returned, own_full))
@@ -538,7 +518,7 @@
     out_hidden, last = finish(summed, reqs)
 
     last_all = lax.all_to_all(last, ("core", "x", "y"), 0, 0, tiled=True)
-    tops, rms = head(last_all, final_gain[None], w_head)
+    tops, rms = head(last_all, gain_final, w_head)
     last_rms = rms.reshape(reqs)
     top_logit = jnp.max(lax.all_to_all(tops, ALL, 0, 0, tiled=True), axis=0)
     return (out_hidden, new_cache, last_rms, top_logit)

time: 266 us -> 257 us (0.966)
  blocking collectives: 56.5 us -> 72.1 us
  starting transfers between devices: 69.9 us -> 54.9 us
  waiting for transfers between devices: 78.9 us -> 69.6 us
  Pallas kernels: 34.7 us -> 31.5 us
    all_to_all x0 -> x1, blocking collectives: none -> 18.6 us  [local(): last_all = lax.all_to_all(last, ('core', 'x', 'y'), 0, 0, tiled=True)]
    all_to_all x3 -> x2, starting transfers between devices: 18.3 us -> 9.25 us  [the longest x1 5.27 us: local(): lax.all_to_all(served, ('x', 'y'), 0, 0, tiled=True).reshape(slots, half)]
    all_to_all x3 -> x2, waiting for transfers between devices: 10.3 us -> 1.98 us  [the longest x1 1.98 us: local(): lax.all_to_all(served, ('x', 'y'), 0, 0, tiled=True).reshape(slots, half)]
    all_to_all x1, starting transfers between devices: 14.5 us -> 7.04 us  [local(): leg = lax.all_to_all(chunks, REQ, 0, 0, tiled=True)]
    ppermute x2, waiting for transfers between devices: 10.2 us -> 5.16 us  [column_swap(): return lax.ppermute(value, 'zh', [(0, 1), (1, 0)])]
    all_to_all x1, waiting for transfers between devices: 3.57 us -> 8.42 us  [local(): leg = lax.all_to_all(chunks, REQ, 0, 0, tiled=True)]
    all_to_all x1, starting transfers between devices: 7.83 us -> 3.86 us  [local(): leg = lax.all_to_all(leg, REQ, 0, 0, tiled=True)]
    ppermute x2 -> x3, waiting for transfers between devices: 2.86 us -> 6.49 us  [swap_core(): return lax.ppermute(value, 'core', [(0, 1), (1, 0)])]
  transfers between devices with their start and end apart: 15 -> 15, of which waited for: 13 -> 11; matrix products, arithmetic and copies ran while one was open for 5% -> 6% of each run, Pallas kernels for 3% -> 4%
where the time goes in v6:
time: 257 us; the launch traced here: 256 us
  blocking collectives  72.1 us (28%)
  waiting for transfers between devices  69.6 us (27%)
  starting transfers between devices  54.9 us (21%)
  Pallas kernels  31.5 us (12%)
  local copies, waits for them, and re-layouts  12.3 us (5%)
  other arithmetic  11.6 us (5%)
  between operations  2.97 us (1%)
    all_gather x1, blocking collectives, local(): full = lax.all_gather(held, TP, axis=1, tiled=True)  19.5 us
    all_to_all x1, blocking collectives, local(): last_all = lax.all_to_all(last, ('core', 'x', 'y'), 0, 0, tiled=True)  18.6 us
    all_to_all x1, blocking collectives, local(): summed = lax.all_to_all(packed, Z, 0, 0, tiled=True)  17.7 us
    all_gather x1, blocking collectives, local(): own_full = lax.all_gather(hidden_late, TP, axis=1, tiled=True)  16.3 us
    ppermute x1, waiting for transfers between devices, local(): pair_down = lax.ppermute(down_w, 'zl', neighbours)  14.9 us
    all_to_all x1, waiting for transfers between devices, spread(): return lax.all_to_all(wide, axes, 0, 0, tiled=True)  13.9 us
    pallas_call x1, Pallas kernels, experts(): pl.pallas_call(experts_body, out_shape=(shape, shape), in_specs=[pl.Block...  12.4 us
    ppermute x2, starting transfers between devices, column_swap(): return lax.ppermute(value, 'zh', [(0, 1), (1, 0)])  11.4 us
  transfers between devices with their start and end apart: 15, of which 11 were waited for; matrix products, arithmetic and copies ran while one was open for 6% of the time, Pallas kernels for 4%

profile of v6, /device:TPU:1, one launch (start us, length us, event | category | flops | bytes accessed | tf_op | source)
XLA Modules:
  0.0 255.6 jit_solution(17901829928941202075)
XLA Ops:
  0.6 7.8 %collective-permute-start = (s32[6,128]{1,0:T(8,128)}, s32[6,128]{1,0:T(8,128)S(1)}, u32[]{:S(2)}, u32[]{:S(2)}) collective-permute-start(s32[6,128]{1,0:T(8,128)} %bitcast.112), channel_id=1, source_target_pairs={{0,128},{128,0},{1,129},{129,1},{2,130},{130,2},{3,131},{131,3},{4... | collective-permute-start | bytes 9224 | tf_op jit(solution)/shard_map/ppermute | solution.py:137
  11.5 7.0 %all-to-all-start = ((bf16[32,8,256]{2,1,0:T(8,128)(2,1)}), bf16[32,8,256]{2,1,0:T(8,128)(2,1)S(1)}, u32[]{:S(2)}, u32[]{:S(2)}) async-start(bf16[32,8,256]{2,1,0:T(8,128)(2,1)} %pad_maximum_fusion), calls=%async_computation | async-start | bytes 262144 | tf_op jit(solution)/shard_map/all_to_all | solution.py:422
  21.4 8.4 %all-to-all-done = bf16[32,8,256]{2,1,0:T(8,128)(2,1)S(1)} async-done(((bf16[32,8,256]{2,1,0:T(8,128)(2,1)}), bf16[32,8,256]{2,1,0:T(8,128)(2,1)S(1)}, u32[]{:S(2)}, u32[]{:S(2)}) %all-to-all-start) | async-done | bytes 131104 | tf_op jit(solution)/shard_map/all_to_all | solution.py:422
  31.0 3.9 %all-to-all-start.1 = ((bf16[32,8,256]{2,1,0:T(8,128)(2,1)}), bf16[32,8,256]{2,1,0:T(8,128)(2,1)S(1)}, u32[]{:S(2)}, u32[]{:S(2)}) async-start(bf16[32,8,256]{2,1,0:T(8,128)(2,1)} %gather_fusion), calls=%async_computation.1 | async-start | bytes 262144 | tf_op jit(solution)/shard_map/all_to_all | solution.py:432
  37.7 9.5 %all-to-all-done.1 = bf16[32,8,256]{2,1,0:T(8,128)(2,1)S(1)} async-done(((bf16[32,8,256]{2,1,0:T(8,128)(2,1)}), bf16[32,8,256]{2,1,0:T(8,128)(2,1)S(1)}, u32[]{:S(2)}, u32[]{:S(2)}) %all-to-all-start.1) | async-done | bytes 131104 | tf_op jit(solution)/shard_map/all_to_all | solution.py:432
  51.1 19.5 %all_gather.6.full_ref = bf16[128,2048]{1,0:T(8,128)(2,1)} all-gather(bf16[128,256]{1,0:T(8,128)(2,1)S(1)} %reshape.347), channel_id=1, replica_groups=mesh['zh'=2,'x'=4,'y'=4,'zl'=4,'core'=2] {'zl','core'}, dimensions={1}, use_global_device_ids=true | all-gather | bytes 589824 | tf_op jit(solution)/shard_map/all_gather | solution.py:440
  70.6 5.7 %attend.1 = bf16[2,4,128,256]{3,2,1,0:T(8,128)(2,1)} custom-call(s32[2]{0:T(128)} %pad_add_fusion.1.place_ref, bf16[128,2048]{1,0:T(8,128)(2,1)} %all_gather.6.full_ref, bf16[1,2048]{1,0:T(2,128)(2,1)} %broadcast_in_dim.61.gain_ref, bf16[3,2048,256]{2,1,0:T(8,128)(2,1)} %w_ref.4, f32[128,128]{1,0:T(8,128)} %get-tuple-element.101.cos_ref, ...), custom_call_target="tpu_custom_call" | custom-call | tf_op jit(solution)/shard_map/attend/pallas_call | solution.py:118
  79.9 4.0 %all-to-all-start.2 = ((bf16[4,128,256]{2,1,0:T(8,128)(2,1)}), bf16[4,128,256]{2,1,0:T(8,128)(2,1)S(1)}, u32[]{:S(2)}, u32[]{:S(2)}) async-start(bf16[4,128,256]{2,1,0:T(8,128)(2,1)} %fusion.36), calls=%async_computation.2 | async-start | bytes 524288 | tf_op jit(solution)/shard_map/all_to_all | solution.py:453
  83.9 3.6 %collective-permute-start.4 = (s32[6,128]{1,0:T(8,128)S(1)}, s32[6,128]{1,0:T(8,128)S(1)}, u32[]{:S(2)}, u32[]{:S(2)}) collective-permute-start(s32[6,128]{1,0:T(8,128)S(1)} %reshape.353), channel_id=1, source_target_pairs={{0,128},{128,0},{1,129},{129,1},{2,130},{130,2},{3,131},{131,3},{4... | collective-permute-start | bytes 9224 | tf_op jit(solution)/shard_map/ppermute | solution.py:137
  87.6 5.2 %collective-permute-done.4 = s32[6,128]{1,0:T(8,128)S(1)} collective-permute-done((s32[6,128]{1,0:T(8,128)S(1)}, s32[6,128]{1,0:T(8,128)S(1)}, u32[]{:S(2)}, u32[]{:S(2)}) %collective-permute-start.4) | collective-permute-done | bytes 3104 | tf_op jit(solution)/shard_map/ppermute | solution.py:137
  94.0 4.2 %all-to-all-start.3 = ((bf16[8,128,256]{2,1,0:T(8,128)(2,1)}), bf16[8,128,256]{2,1,0:T(8,128)(2,1)S(1)}, u32[]{:S(2)}, u32[]{:S(2)}) async-start(bf16[8,128,256]{2,1,0:T(8,128)(2,1)} %broadcast_in_dim.64), calls=%async_computation.3 | async-start | bytes 1048576 | tf_op jit(solution)/shard_map/all_to_all | solution.py:129
  100.2 13.9 %all-to-all-done.3.parts_ref = bf16[8,128,256]{2,1,0:T(8,128)(2,1)S(1)} async-done(((bf16[8,128,256]{2,1,0:T(8,128)(2,1)}), bf16[8,128,256]{2,1,0:T(8,128)(2,1)S(1)}, u32[]{:S(2)}, u32[]{:S(2)}) %all-to-all-start.3) | async-done | bytes 524320 | tf_op jit(solution)/shard_map/all_to_all | solution.py:129
  117.7 7.1 %all-to-all-start.4 = ((bf16[16,40,1024]{2,1,0:T(8,128)(2,1)}), bf16[16,40,1024]{2,1,0:T(8,128)(2,1)S(1)}, u32[]{:S(2)}, u32[]{:S(2)}) async-start(bf16[16,40,1024]{2,1,0:T(8,128)(2,1)} %bitcast.106), calls=%async_computation.4 | async-start | bytes 2621440 | tf_op jit(solution)/shard_map/all_to_all | solution.py:487
  124.9 14.9 %collective-permute-done.5.pd_ref = bf16[176,2048]{1,0:T(8,128)(2,1)S(1)} collective-permute-done((bf16[176,2048]{1,0:T(8,128)(2,1)S(1)}, bf16[176,2048]{1,0:T(8,128)(2,1)S(1)}, u32[]{:S(2)}, u32[]{:S(2)}) %collective-permute-start.5) | collective-permute-done | bytes 720928 | tf_op jit(solution)/shard_map/ppermute | solution.py:490
  141.8 4.1 %collective-permute-start.6 = (bf16[16,40,1024]{2,1,0:T(8,128)(2,1)S(1)}, bf16[16,40,1024]{2,1,0:T(8,128)(2,1)S(1)}, u32[]{:S(2)}, u32[]{:S(2)}) collective-permute-start(bf16[16,40,1024]{2,1,0:T(8,128)(2,1)S(1)} %all-to-all-done.4.a_ref), channel_id=1, source_target_pairs={{0,1},{1,0},{2,3},{3,2},{4,5},{5,4},{6,7},{7,6},{8,9},{9,8},{10,11... | collective-permute-start | bytes 3932168 | tf_op jit(solution)/shard_map/ppermute | solution.py:133
  149.6 12.4 %experts.1 = (bf16[16,40,1024]{2,1,0:T(8,128)(2,1)}, bf16[16,40,1024]{2,1,0:T(8,128)(2,1)}) custom-call(s32[34]{0:T(128)} %copy-done.10, bf16[16,40,1024]{2,1,0:T(8,128)(2,1)} %copy-done.3, bf16[16,40,1024]{2,1,0:T(8,128)(2,1)} %copy-done.11, bf16[1,2048]{1,0:T(2,128)(2,1)} %broadcast_in_dim.62.gain_ref, bf16[32,2048]{1,0:T(8,128)(2,1)} %bitcast.142, ...), custom_call_target="tpu_custom_call" | custom-call | flops 2768240640 | bytes 11730944 | tf_op jit(solution)/shard_map/experts/pallas_call | solution.py:240
  165.2 2.9 %add_convert_fusion = bf16[16,40,1024]{2,1,0:T(8,128)(2,1)} fusion(bf16[16,40,1024]{2,1,0:T(8,128)(2,1)S(1)} %collective-permute-done.7, bf16[16,40,1024]{2,1,0:T(8,128)(2,1)} %get-tuple-element.45), kind=kLoop, calls=%fused_computation.1 | loop fusion | flops 2621440 | bytes 3932160 | tf_op jit(solution)/shard_map/convert_element_type | solution.py:508
  168.2 5.3 %all-to-all-start.5 = ((bf16[16,40,1024]{2,1,0:T(8,128)(2,1)}), bf16[16,40,1024]{2,1,0:T(8,128)(2,1)S(1)}, u32[]{:S(2)}, u32[]{:S(2)}) async-start(bf16[16,40,1024]{2,1,0:T(8,128)(2,1)} %add_convert_fusion), calls=%async_computation.5 | async-start | bytes 2621440 | tf_op jit(solution)/shard_map/all_to_all | solution.py:510
  173.5 16.3 %all_gather.7.full_ref = bf16[128,2048]{1,0:T(8,128)(2,1)} all-gather(bf16[128,256]{1,0:T(8,128)(2,1)S(1)} %copy-done.4), channel_id=1, replica_groups=mesh['zh'=2,'x'=4,'y'=4,'zl'=4,'core'=2] {'zl','core'}, dimensions={1}, use_global_device_ids=true | all-gather | bytes 589824 | tf_op jit(solution)/shard_map/all_gather | solution.py:512
  195.7 17.7 %all_to_all.49.parts_ref = bf16[8,136,256]{2,1,0:T(8,128)(2,1)} all-to-all(bf16[8,136,256]{2,1,0:T(8,128)(2,1)} %combine.1), channel_id=1, replica_groups=mesh['zh'=2,'x'=4,'y'=4,'zl'=4,'core'=2] {'zh','zl'}, dimensions={0} | all-to-all | bytes 1114112 | tf_op jit(solution)/shard_map/all_to_all | solution.py:517
  215.4 18.6 %all_to_all.50.last_ref = bf16[32,16,128]{2,1,0:T(8,128)(2,1)} all-to-all(bf16[32,16,128]{2,1,0:T(8,128)(2,1)} %get-tuple-element.52), channel_id=1, replica_groups=mesh['zh'=2,'x'=4,'y'=4,'zl'=4,'core'=2] {'core','x','y'}, dimensions={0} | all-to-all | bytes 262144 | tf_op jit(solution)/shard_map/all_to_all | solution.py:520
  236.4 5.6 %all-to-all-start.8 = ((f32[256,1,32]{2,1,0:T(1,128)}), f32[256,1,32]{2,1,0:T(1,128)S(1)}, u32[]{:S(2)}, u32[]{:S(2)}) async-start(f32[256,1,32]{2,1,0:T(1,128)} %bitcast.111), calls=%async_computation.8 | async-start | bytes 262144 | tf_op jit(solution)/shard_map/all_to_all | solution.py:523
  242.7 3.4 %new_kv.1 = bf16[2,128,256]{2,1,0:T(8,128)(2,1)} custom-call(bf16[128,2048]{1,0:T(8,128)(2,1)} %all_gather.7.full_ref, bf16[1,2048]{1,0:T(2,128)(2,1)} %broadcast_in_dim.61.gain_ref, bf16[3,2048,256]{2,1,0:T(8,128)(2,1)} %w_ref.4, f32[128,128]{1,0:T(8,128)} %get-tuple-element.103.cos_ref, f32[128,128]{1,0:T(8,128)} %get-tuple-element.104.sin_ref), custom_call_target="tpu_custom_call" | custom-call | tf_op jit(solution)/shard_map/new_kv/pallas_call | solution.py:63
  246.8 8.1 %all-to-all-done.8 = f32[256,1,32]{2,1,0:T(1,128)S(1)} async-done(((f32[256,1,32]{2,1,0:T(1,128)}), f32[256,1,32]{2,1,0:T(1,128)S(1)}, u32[]{:S(2)}, u32[]{:S(2)}) %all-to-all-start.8) | async-done | bytes 32800 | tf_op jit(solution)/shard_map/all_to_all | solution.py:523
  (114 shorter events, 43.6 us)
Async XLA Ops:
  0.6 36.2 %collective-permute-start = (s32[6,128]{1,0:T(8,128)}, s32[6,128]{1,0:T(8,128)S(1)}, u32[]{:S(2)}, u32[]{:S(2)}) collective-permute-start(s32[6,128]{1,0:T(8,128)} %bitcast.112), channel_id=1, source_target_pairs={{0,128},{128,0},{1,129},{129,1},{2,130},{130,2},{3,131},{131,3},{4... | collective-permute-start | bytes 9224 | tf_op jit(solution)/shard_map/ppermute | solution.py:137
  11.5 18.3 %all-to-all-start = ((bf16[32,8,256]{2,1,0:T(8,128)(2,1)}), bf16[32,8,256]{2,1,0:T(8,128)(2,1)S(1)}, u32[]{:S(2)}, u32[]{:S(2)}) async-start(bf16[32,8,256]{2,1,0:T(8,128)(2,1)} %pad_maximum_fusion), calls=%async_computation | async-start | bytes 262144 | tf_op jit(solution)/shard_map/all_to_all | solution.py:422
  18.5 16.5 %copy-start.5 = (s32[128,6]{0,1:T(8,128)S(1)}, s32[128,6]{0,1:T(8,128)}, u32[]{:S(2)}) copy-start(s32[128,6]{0,1:T(8,128)} %param.25) | copy-start | bytes 9220
  18.6 16.5 %copy-start.7 = (bf16[2048]{0:T(1024)(128)(2,1)S(1)}, bf16[2048]{0:T(1024)(128)(2,1)}, u32[]{:S(2)}) copy-start(bf16[2048]{0:T(1024)(128)(2,1)} %param.17) | copy-start | bytes 12292
  18.6 17.1 %copy-start.8 = (bf16[2048]{0:T(1024)(128)(2,1)S(1)}, bf16[2048]{0:T(1024)(128)(2,1)}, u32[]{:S(2)}) copy-start(bf16[2048]{0:T(1024)(128)(2,1)} %param.23) | copy-start | bytes 12292
  18.6 17.7 %copy-start.9 = (bf16[2048]{0:T(1024)(128)(2,1)S(1)}, bf16[2048]{0:T(1024)(128)(2,1)}, u32[]{:S(2)}) copy-start(bf16[2048]{0:T(1024)(128)(2,1)} %param.30) | copy-start | bytes 12292
  20.0 27.2 %collective-permute-start.1 = (bf16[176,2048]{1,0:T(8,128)(2,1)S(1)}, bf16[176,2048]{1,0:T(8,128)(2,1)S(1)}, u32[]{:S(2)}, u32[]{:S(2)}) collective-permute-start(bf16[176,2048]{1,0:T(8,128)(2,1)S(1)} %get-tuple-element.72), channel_id=1, source_target_pairs={{0,2},{2,0},{4,6},{6,4},{1,3},{3,1},{5,7},{7,5},{8,10},{10,8},{12,... | collective-permute-start | bytes 2162696 | tf_op jit(solution)/shard_map/ppermute | solution.py:421
  31.0 16.2 %all-to-all-start.1 = ((bf16[32,8,256]{2,1,0:T(8,128)(2,1)}), bf16[32,8,256]{2,1,0:T(8,128)(2,1)S(1)}, u32[]{:S(2)}, u32[]{:S(2)}) async-start(bf16[32,8,256]{2,1,0:T(8,128)(2,1)} %gather_fusion), calls=%async_computation.1 | async-start | bytes 262144 | tf_op jit(solution)/shard_map/all_to_all | solution.py:432
  35.0 41.3 %copy-start.10 = (s32[34]{0:T(128)}, s32[34]{0:T(128)S(1)}, u32[]{:S(2)}) copy-start(s32[34]{0:T(128)S(1)} %pad_add_fusion.place_ref) | copy-start | bytes 412
  36.9 39.5 %collective-permute-start.2 = (bf16[176,2048]{1,0:T(8,128)(2,1)S(1)}, bf16[176,2048]{1,0:T(8,128)(2,1)S(1)}, u32[]{:S(2)}, u32[]{:S(2)}) collective-permute-start(bf16[176,2048]{1,0:T(8,128)(2,1)S(1)} %get-tuple-element.34), channel_id=1, source_target_pairs={{0,2},{2,0},{4,6},{6,4},{1,3},{3,1},{5,7},{7,5},{8,10},{10,8},{12,... | collective-permute-start | bytes 2162696 | tf_op jit(solution)/shard_map/ppermute | solution.py:425
  47.3 29.0 %copy-start.13 = (bf16[176,2048]{1,0:T(8,128)(2,1)}, bf16[176,2048]{1,0:T(8,128)(2,1)S(1)}, u32[]{:S(2)}) copy-start(bf16[176,2048]{1,0:T(8,128)(2,1)S(1)} %collective-permute-done.1.pg_ref) | copy-start | bytes 2162692
  76.3 16.4 %copy-start.14 = (bf16[176,2048]{1,0:T(8,128)(2,1)}, bf16[176,2048]{1,0:T(8,128)(2,1)S(1)}, u32[]{:S(2)}) copy-start(bf16[176,2048]{1,0:T(8,128)(2,1)S(1)} %collective-permute-done.2.pu_ref) | copy-start | bytes 2162692
  77.6 1.6 collective-permute-start.3
  79.9 13.2 %all-to-all-start.2 = ((bf16[4,128,256]{2,1,0:T(8,128)(2,1)}), bf16[4,128,256]{2,1,0:T(8,128)(2,1)S(1)}, u32[]{:S(2)}, u32[]{:S(2)}) async-start(bf16[4,128,256]{2,1,0:T(8,128)(2,1)} %fusion.36), calls=%async_computation.2 | async-start | bytes 524288 | tf_op jit(solution)/shard_map/all_to_all | solution.py:453
  83.9 8.8 %collective-permute-start.4 = (s32[6,128]{1,0:T(8,128)S(1)}, s32[6,128]{1,0:T(8,128)S(1)}, u32[]{:S(2)}, u32[]{:S(2)}) collective-permute-start(s32[6,128]{1,0:T(8,128)S(1)} %reshape.353), channel_id=1, source_target_pairs={{0,128},{128,0},{1,129},{129,1},{2,130},{130,2},{3,131},{131,3},{4... | collective-permute-start | bytes 9224 | tf_op jit(solution)/shard_map/ppermute | solution.py:137
  94.0 20.2 %all-to-all-start.3 = ((bf16[8,128,256]{2,1,0:T(8,128)(2,1)}), bf16[8,128,256]{2,1,0:T(8,128)(2,1)S(1)}, u32[]{:S(2)}, u32[]{:S(2)}) async-start(bf16[8,128,256]{2,1,0:T(8,128)(2,1)} %broadcast_in_dim.64), calls=%async_computation.3 | async-start | bytes 1048576 | tf_op jit(solution)/shard_map/all_to_all | solution.py:129
  117.7 7.1 %copy-start.12 = (bf16[1,176,2048]{2,1,0:T(8,128)(2,1)S(1)}, bf16[1,176,2048]{2,1,0:T(8,128)(2,1)}, u32[]{:S(2)}) copy-start(bf16[1,176,2048]{2,1,0:T(8,128)(2,1)} %param.27) | copy-start | bytes 2162692
  117.7 24.0 %all-to-all-start.4 = ((bf16[16,40,1024]{2,1,0:T(8,128)(2,1)}), bf16[16,40,1024]{2,1,0:T(8,128)(2,1)S(1)}, u32[]{:S(2)}, u32[]{:S(2)}) async-start(bf16[16,40,1024]{2,1,0:T(8,128)(2,1)} %bitcast.106), calls=%async_computation.4 | async-start | bytes 2621440 | tf_op jit(solution)/shard_map/all_to_all | solution.py:487
  124.8 15.0 %collective-permute-start.5 = (bf16[176,2048]{1,0:T(8,128)(2,1)S(1)}, bf16[176,2048]{1,0:T(8,128)(2,1)S(1)}, u32[]{:S(2)}, u32[]{:S(2)}) collective-permute-start(bf16[176,2048]{1,0:T(8,128)(2,1)S(1)} %bitcast.141), channel_id=1, source_target_pairs={{0,2},{2,0},{4,6},{6,4},{1,3},{3,1},{5,7},{7,5},{8,10},{10,8},{12,... | collective-permute-start | bytes 2162696 | tf_op jit(solution)/shard_map/ppermute | solution.py:490
  141.8 6.8 %copy-start.3 = (bf16[16,40,1024]{2,1,0:T(8,128)(2,1)}, bf16[16,40,1024]{2,1,0:T(8,128)(2,1)S(1)}, u32[]{:S(2)}) copy-start(bf16[16,40,1024]{2,1,0:T(8,128)(2,1)S(1)} %all-to-all-done.4.a_ref) | copy-start | bytes 3932164
  141.8 6.8 %collective-permute-start.6 = (bf16[16,40,1024]{2,1,0:T(8,128)(2,1)S(1)}, bf16[16,40,1024]{2,1,0:T(8,128)(2,1)S(1)}, u32[]{:S(2)}, u32[]{:S(2)}) collective-permute-start(bf16[16,40,1024]{2,1,0:T(8,128)(2,1)S(1)} %all-to-all-done.4.a_ref), channel_id=1, source_target_pairs={{0,1},{1,0},{2,3},{3,2},{4,5},{5,4},{6,7},{7,6},{8,9},{9,8},{10,11... | collective-permute-start | bytes 3932168 | tf_op jit(solution)/shard_map/ppermute | solution.py:133
  162.0 3.3 %collective-permute-start.7 = (bf16[16,40,1024]{2,1,0:T(8,128)(2,1)}, bf16[16,40,1024]{2,1,0:T(8,128)(2,1)S(1)}, u32[]{:S(2)}, u32[]{:S(2)}) collective-permute-start(bf16[16,40,1024]{2,1,0:T(8,128)(2,1)} %get-tuple-element.46), channel_id=1, source_target_pairs={{0,1},{1,0},{2,3},{3,2},{4,5},{5,4},{6,7},{7,6},{8,9},{9,8},{10,11... | collective-permute-start | bytes 3932168 | tf_op jit(solution)/shard_map/ppermute | solution.py:133
  168.2 23.6 %all-to-all-start.5 = ((bf16[16,40,1024]{2,1,0:T(8,128)(2,1)}), bf16[16,40,1024]{2,1,0:T(8,128)(2,1)S(1)}, u32[]{:S(2)}, u32[]{:S(2)}) async-start(bf16[16,40,1024]{2,1,0:T(8,128)(2,1)} %add_convert_fusion), calls=%async_computation.5 | async-start | bytes 2621440 | tf_op jit(solution)/shard_map/all_to_all | solution.py:510
  236.4 18.4 %all-to-all-start.8 = ((f32[256,1,32]{2,1,0:T(1,128)}), f32[256,1,32]{2,1,0:T(1,128)S(1)}, u32[]{:S(2)}, u32[]{:S(2)}) async-start(f32[256,1,32]{2,1,0:T(1,128)} %bitcast.111), calls=%async_computation.8 | async-start | bytes 262144 | tf_op jit(solution)/shard_map/all_to_all | solution.py:523
  (8 other events, 17.8 us)

commit v7 on v6

--- a/solution.py
+++ b/solution.py
@@ -35,8 +35,7 @@
     freqs = 10000.0 ** (-2.0 * jnp.arange(half_len, dtype=f32) / HD)
     positions = (length + jnp.arange(new, dtype=jnp.int32)).astype(f32)
     angles = positions[:, None] * freqs[None, :]
-    cosine, sine = jnp.cos(angles), jnp.sin(angles)
-    return jnp.concatenate([cosine, cosine], 1), jnp.concatenate([-sine, sine], 1)
+    return jnp.cos(angles), jnp.sin(angles)
 
 
 def norm_rows(full_ref, gain_ref):
@@ -44,10 +43,12 @@
 
 
 def rotate(values, cos_ref, sin_ref):
+    cosine = jnp.concatenate([cos_ref[...], cos_ref[...]], axis=1)
+    sine = jnp.concatenate([-sin_ref[...], sin_ref[...]], axis=1)
     heads = []
     for head in range(values.shape[1] // HD):
         piece = values[:, head * HD : (head + 1) * HD]
-        heads.append(piece * cos_ref[...] + pltpu.roll(piece, HD // 2, 1) * sin_ref[...])
+        heads.append(piece * cosine + pltpu.roll(piece, HD // 2, 1) * sine)
     return jnp.concatenate(heads, axis=1).astype(bf16)
 
 
@@ -69,9 +70,11 @@
     )(full, gain, w_qkv, *tables)
 
 
-def attend_body(place_ref, full_ref, gain_ref, qkv_ref, cos_ref, sin_ref, kv_ref, w_ref, o_ref):
-    length = place_ref[0]
-    core = place_ref[1]
+def attend_body(
+    len_ref, place_ref, full_ref, gain_ref, qkv_ref, cos_ref, sin_ref, kv_ref, w_ref, om_ref, ot_ref
+):
+    length = len_ref[0]
+    first = place_ref[0] == 0
     ctx = kv_ref.shape[2]
     new = full_ref.shape[0]
     normed = norm_rows(full_ref, gain_ref)
@@ -103,25 +106,36 @@
         )
         heads.append(out.astype(bf16))
     attn = jnp.concatenate(heads, axis=1)
-    wide = o_ref.shape[3]
-    for part in range(2 * o_ref.shape[1]):
-        at = core if part % 2 == 0 else 1 - core
-        o_ref[at, part // 2] = jnp.dot(
-            attn, w_ref[:, part * wide : (part + 1) * wide], preferred_element_type=f32
-        ).astype(bf16)
-
-
-def attend(place, full, gain, w_qkv, tables, kv_cache, w_out):
+    wide = om_ref.shape[2]
+
+    def store(even_ref, odd_ref):
+        for part in range(2 * om_ref.shape[0]):
+            ref = odd_ref if part % 2 else even_ref
+            ref[part // 2] = jnp.dot(
+                attn, w_ref[:, part * wide : (part + 1) * wide], preferred_element_type=f32
+            ).astype(bf16)
+
+    @pl.when(first)
+    def _():
+        store(om_ref, ot_ref)
+
+    @pl.when(jnp.logical_not(first))
+    def _():
+        store(ot_ref, om_ref)
+
+
+def attend(length, place, full, gain, w_qkv, tables, kv_cache, w_out):
     vm = pl.BlockSpec(memory_space=pltpu.VMEM)
     new = full.shape[0]
     feat = w_out.shape[0]
+    shape = jax.ShapeDtypeStruct((w_out.shape[1] // feat // 2, new, feat), bf16)
     return pl.pallas_call(
         attend_body,
-        out_shape=jax.ShapeDtypeStruct((2, w_out.shape[1] // feat // 2, new, feat), bf16),
-        in_specs=[pl.BlockSpec(memory_space=pltpu.SMEM)] + [vm] * 7,
-        out_specs=vm,
+        out_shape=(shape, shape),
+        in_specs=[pl.BlockSpec(memory_space=pltpu.SMEM)] * 2 + [vm] * 7,
+        out_specs=(vm, vm),
         name="attend",
-    )(place, full, gain, w_qkv, *tables, kv_cache, w_out)
+    )(length, place, full, gain, w_qkv, *tables, kv_cache, w_out)
 
 
 def spread(value, axes, count):
@@ -278,46 +292,41 @@
 
 def combine_body(chosen_ref, back_ref, out_ref):
     feat = out_ref.shape[2]
-    new = chosen_ref.shape[1] // 2
+    new = chosen_ref.shape[0] // 2
+    last = []
     for zo in range(2):
-        total = lax.dot_general(
-            chosen_ref[:, zo * new : (zo + 1) * new],
-            back_ref[...],
-            (((0,), (0,)), ((), ())),
-            preferred_element_type=f32,
-        ).astype(bf16)
+        total = jnp.dot(
+            chosen_ref[zo * new : (zo + 1) * new, :], back_ref[...], preferred_element_type=f32
+        )
         for part in range(4):
             piece = total[:, part * feat : (part + 1) * feat]
-            out_ref[zo * 4 + part, :new, :] = piece
-            row = piece[new - 1 :, :]
-            for dest in range(8):
-                out_ref[dest, new + zo * 4 + part : new + zo * 4 + part + 1, :] = row
-
-
-def combine(chosen_t, back):
+            out_ref[zo * 4 + part, :new, :] = piece.astype(bf16)
+            last.append(piece[new - 1 :, :])
+    last = jnp.concatenate(last, axis=0).astype(bf16)
+    for dest in range(8):
+        out_ref[dest, new:, :] = last
+
+
+def combine(chosen, back):
     vm = pl.BlockSpec(memory_space=pltpu.VMEM)
     return pl.pallas_call(
         combine_body,
-        out_shape=jax.ShapeDtypeStruct((8, chosen_t.shape[1] // 2 + 8, back.shape[1] // 4), bf16),
+        out_shape=jax.ShapeDtypeStruct((8, chosen.shape[0] // 2 + 8, back.shape[1] // 4), bf16),
         in_specs=[vm, vm],
         out_specs=vm,
         name="combine",
-    )(chosen_t, back)
+    )(chosen, back)
 
 
 def finish_body(parts_ref, out_ref, last_ref):
-    new = out_ref.shape[0]
+    new, feat = out_ref.shape
     total = parts_ref[0].astype(f32)
     for part in range(1, 8):
         total = total + parts_ref[part].astype(f32)
     out_ref[...] = total[:new].astype(bf16)
-    for part in range(8):
-        row = total[new + part : new + part + 1]
-        for sub in range(2):
-            piece = row[:, sub * 128 : (sub + 1) * 128]
-            last_ref[:, part * 2 + sub : part * 2 + sub + 1, :] = jnp.broadcast_to(
-                piece.astype(bf16)[None], (last_ref.shape[0], 1, 128)
-            )
+    last = total[new:].astype(bf16).astype(f32)
+    last = jnp.concatenate([last[:, : feat // 2], last[:, feat // 2 :]], axis=0).astype(bf16)
+    last_ref[...] = jnp.broadcast_to(last[None], last_ref.shape)
 
 
 def finish(parts, copies):
@@ -344,7 +353,7 @@
             for core in range(2):
                 for sub in range(2):
                     pieces.append(
-                        rows[(zo * 4 + part) * 2 + sub, core * plane : (core + 1) * plane]
+                        rows[sub * 8 + zo * 4 + part, core * plane : (core + 1) * plane]
                     )
         halves.append(jnp.concatenate(pieces, axis=1))
     tok = jnp.concatenate(halves, axis=0)
@@ -418,9 +427,10 @@
     w_in = w_exp_in[0].swapaxes(1, 2)
     w_down = w_exp_down[0]
     neighbours = [(0, 1), (1, 0), (2, 3), (3, 2)]
-    pair_gate = lax.ppermute(w_in[0], "zl", neighbours)
+    chunks, ids_out, gate_w = barrier((chunks, ids_t, w_in[0]))
+    pair_gate = lax.ppermute(gate_w, "zl", neighbours)
     leg = lax.all_to_all(chunks, REQ, 0, 0, tiled=True)
-    ids_there, up_w = barrier((column_swap(ids_t), w_in[1]))
+    ids_there, up_w = barrier((column_swap(ids_out), w_in[1]))
 
     pair_up = lax.ppermute(up_w, "zl", neighbours)
 
@@ -438,8 +448,9 @@
     held_len = leg[0, -1, :1].astype(jnp.int32) * 32 + leg[0, -1, feat // 2 :][:1].astype(jnp.int32)
 
     full = lax.all_gather(held, TP, axis=1, tiled=True)
-    parts = attend(
-        jnp.concatenate([held_len, place[:1]]),
+    parts_mine, parts_theirs = attend(
+        held_len,
+        place,
         full,
         gain,
         w_qkv,
@@ -447,8 +458,8 @@
         kv_cache,
         w_out,
     )
-    parts, pair_up = barrier((parts, pair_up))
-    parts = (parts[0].astype(f32) + swap_core(parts[1]).astype(f32)).astype(bf16)
+    parts_theirs, pair_up = barrier((parts_theirs, pair_up))
+    parts = (parts_mine.astype(f32) + swap_core(parts_theirs).astype(f32)).astype(bf16)
     parts, held_ids = barrier((parts, held_ids))
     parts = lax.all_to_all(parts, "zl", 0, 0, tiled=True)
     held_share = (held.astype(f32) + jnp.sum(parts.astype(f32), axis=0)).astype(bf16)
@@ -480,7 +491,7 @@
         return chosen
 
     chosen_held = chosen_of(held_ids, column_swap(held_ids))
-    chosen_own = chosen_of(ids_t, ids_there)
+    chosen_own = chosen_of(ids_t, ids_there).T
 
     outgoing = dispatch(chosen_held, spread(held_share, Z, 8))
     down_w, outgoing = barrier((w_down, outgoing))

time: 257 us -> 261 us (1.016)
  starting transfers between devices: 54.9 us -> 59.3 us
  blocking collectives: 72.1 us -> 75.1 us
    all_to_all x1, starting transfers between devices: 7.04 us -> 12.8 us  [local(): leg = lax.all_to_all(chunks, REQ, 0, 0, tiled=True)]
  transfers between devices with their start and end apart: 15 -> 15, of which waited for: 11 -> 11; matrix products, arithmetic and copies ran while one was open for 6% -> 4% of each run, Pallas kernels for 4% -> 4%
where the time goes in v7:
time: 261 us; the launch traced here: 260 us
  blocking collectives  75.1 us (29%)
  waiting for transfers between devices  68 us (26%)
  starting transfers between devices  59.3 us (23%)
  Pallas kernels  31.4 us (12%)
  other arithmetic  12.2 us (5%)
  local copies, waits for them, and re-layouts  10.2 us (4%)
  between operations  3 us (1%)
    all_gather x1, blocking collectives, local(): full = lax.all_gather(held, TP, axis=1, tiled=True)  21.4 us
    all_to_all x1, blocking collectives, local(): last_all = lax.all_to_all(last, ('core', 'x', 'y'), 0, 0, tiled=True)  19.8 us
    all_to_all x1, blocking collectives, local(): summed = lax.all_to_all(packed, Z, 0, 0, tiled=True)  17.7 us
    all_gather x1, blocking collectives, local(): own_full = lax.all_gather(hidden_late, TP, axis=1, tiled=True)  16.2 us
    ppermute x1, waiting for transfers between devices, local(): pair_down = lax.ppermute(down_w, 'zl', neighbours)  14.1 us
    all_to_all x1, waiting for transfers between devices, spread(): return lax.all_to_all(wide, axes, 0, 0, tiled=True)  13.3 us
    all_to_all x1, starting transfers between devices, local(): leg = lax.all_to_all(chunks, REQ, 0, 0, tiled=True)  12.8 us
    pallas_call x1, Pallas kernels, experts(): pl.pallas_call(experts_body, out_shape=(shape, shape), in_specs=[pl.Block...  12.4 us
  transfers between devices with their start and end apart: 15, of which 11 were waited for; matrix products, arithmetic and copies ran while one was open for 4% of the time, Pallas kernels for 4%

profile of v7, /device:TPU:1, one launch (start us, length us, event | category | flops | bytes accessed | tf_op | source)
XLA Modules:
  0.0 260.0 jit_solution(7014655275454317721)
XLA Ops:
  7.7 12.8 %all-to-all-start = ((bf16[32,8,256]{2,1,0:T(8,128)(2,1)}), bf16[32,8,256]{2,1,0:T(8,128)(2,1)S(1)}, u32[]{:S(2)}, u32[]{:S(2)}) async-start(bf16[32,8,256]{2,1,0:T(8,128)(2,1)} %pad_maximum_fusion), calls=%async_computation | async-start | bytes 262144 | tf_op jit(solution)/shard_map/all_to_all | solution.py:432
  20.4 5.2 %collective-permute-start = (s32[6,128]{1,0:T(8,128)S(1)}, s32[6,128]{1,0:T(8,128)S(1)}, u32[]{:S(2)}, u32[]{:S(2)}) collective-permute-start(s32[6,128]{1,0:T(8,128)S(1)} %bitcast.104), channel_id=1, source_target_pairs={{0,128},{128,0},{1,129},{129,1},{2,130},{130,2},{3,131},{131,3},{4... | collective-permute-start | bytes 9224 | tf_op jit(solution)/shard_map/ppermute | solution.py:151
  26.2 8.8 %all-to-all-done = bf16[32,8,256]{2,1,0:T(8,128)(2,1)S(1)} async-done(((bf16[32,8,256]{2,1,0:T(8,128)(2,1)}), bf16[32,8,256]{2,1,0:T(8,128)(2,1)S(1)}, u32[]{:S(2)}, u32[]{:S(2)}) %all-to-all-start) | async-done | bytes 131104 | tf_op jit(solution)/shard_map/all_to_all | solution.py:432
  36.3 3.9 %all-to-all-start.1 = ((bf16[32,8,256]{2,1,0:T(8,128)(2,1)}), bf16[32,8,256]{2,1,0:T(8,128)(2,1)S(1)}, u32[]{:S(2)}, u32[]{:S(2)}) async-start(bf16[32,8,256]{2,1,0:T(8,128)(2,1)} %gather_fusion), calls=%async_computation.1 | async-start | bytes 262144 | tf_op jit(solution)/shard_map/all_to_all | solution.py:442
  43.2 8.3 %all-to-all-done.1 = bf16[32,8,256]{2,1,0:T(8,128)(2,1)S(1)} async-done(((bf16[32,8,256]{2,1,0:T(8,128)(2,1)}), bf16[32,8,256]{2,1,0:T(8,128)(2,1)S(1)}, u32[]{:S(2)}, u32[]{:S(2)}) %all-to-all-start.1) | async-done | bytes 131104 | tf_op jit(solution)/shard_map/all_to_all | solution.py:442
  53.4 21.4 %all_gather.6.full_ref = bf16[128,2048]{1,0:T(8,128)(2,1)} all-gather(bf16[128,256]{1,0:T(8,128)(2,1)S(1)} %reshape.345), channel_id=1, replica_groups=mesh['zh'=2,'x'=4,'y'=4,'zl'=4,'core'=2] {'zl','core'}, dimensions={1}, use_global_device_ids=true | all-gather | bytes 589824 | tf_op jit(solution)/shard_map/all_gather | solution.py:450
  76.0 5.8 %attend.1 = (bf16[4,128,256]{2,1,0:T(8,128)(2,1)}, bf16[4,128,256]{2,1,0:T(8,128)(2,1)}) custom-call(s32[1]{0:T(128)} %bitcast.26.len_ref, s32[34]{0:T(128)} %pad_add_fusion.place_ref, bf16[128,2048]{1,0:T(8,128)(2,1)} %all_gather.6.full_ref, bf16[1,2048]{1,0:T(2,128)(2,1)} %broadcast_in_dim.61.gain_ref, bf16[3,2048,256]{2,1,0:T(8,128)(2,1)} %w_ref.4, ...), custom_call_target="tpu_custom_call" | custom-call | tf_op jit(solution)/shard_map/attend/pallas_call | solution.py:132
  85.3 3.4 %all-to-all-start.2 = ((bf16[4,128,256]{2,1,0:T(8,128)(2,1)}), bf16[4,128,256]{2,1,0:T(8,128)(2,1)S(1)}, u32[]{:S(2)}, u32[]{:S(2)}) async-start(bf16[4,128,256]{2,1,0:T(8,128)(2,1)} %add_convert_fusion.1), calls=%async_computation.2 | async-start | bytes 524288 | tf_op jit(solution)/shard_map/all_to_all | solution.py:464
  89.1 4.9 %collective-permute-start.4 = (s32[6,128]{1,0:T(8,128)S(1)}, s32[6,128]{1,0:T(8,128)S(1)}, u32[]{:S(2)}, u32[]{:S(2)}) collective-permute-start(s32[6,128]{1,0:T(8,128)S(1)} %reshape.350), channel_id=1, source_target_pairs={{0,128},{128,0},{1,129},{129,1},{2,130},{130,2},{3,131},{131,3},{4... | collective-permute-start | bytes 9224 | tf_op jit(solution)/shard_map/ppermute | solution.py:151
  94.1 4.5 %collective-permute-done.4 = s32[6,128]{1,0:T(8,128)S(1)} collective-permute-done((s32[6,128]{1,0:T(8,128)S(1)}, s32[6,128]{1,0:T(8,128)S(1)}, u32[]{:S(2)}, u32[]{:S(2)}) %collective-permute-start.4) | collective-permute-done | bytes 3104 | tf_op jit(solution)/shard_map/ppermute | solution.py:151
  99.5 4.1 %all-to-all-start.3 = ((bf16[8,128,256]{2,1,0:T(8,128)(2,1)}), bf16[8,128,256]{2,1,0:T(8,128)(2,1)S(1)}, u32[]{:S(2)}, u32[]{:S(2)}) async-start(bf16[8,128,256]{2,1,0:T(8,128)(2,1)} %broadcast_in_dim.64), calls=%async_computation.3 | async-start | bytes 1048576 | tf_op jit(solution)/shard_map/all_to_all | solution.py:143
  105.4 13.3 %all-to-all-done.3.parts_ref = bf16[8,128,256]{2,1,0:T(8,128)(2,1)S(1)} async-done(((bf16[8,128,256]{2,1,0:T(8,128)(2,1)}), bf16[8,128,256]{2,1,0:T(8,128)(2,1)S(1)}, u32[]{:S(2)}, u32[]{:S(2)}) %all-to-all-start.3) | async-done | bytes 524320 | tf_op jit(solution)/shard_map/all_to_all | solution.py:143
  122.3 6.6 %all-to-all-start.4 = ((bf16[16,40,1024]{2,1,0:T(8,128)(2,1)}), bf16[16,40,1024]{2,1,0:T(8,128)(2,1)S(1)}, u32[]{:S(2)}, u32[]{:S(2)}) async-start(bf16[16,40,1024]{2,1,0:T(8,128)(2,1)} %bitcast.99), calls=%async_computation.4 | async-start | bytes 2621440 | tf_op jit(solution)/shard_map/all_to_all | solution.py:498
  129.0 14.1 %collective-permute-done.5.pd_ref = bf16[176,2048]{1,0:T(8,128)(2,1)} collective-permute-done((bf16[176,2048]{1,0:T(8,128)(2,1)S(1)}, bf16[176,2048]{1,0:T(8,128)(2,1)}, u32[]{:S(2)}, u32[]{:S(2)}) %collective-permute-start.5) | collective-permute-done | bytes 720928 | tf_op jit(solution)/shard_map/ppermute | solution.py:501
  145.5 4.9 %collective-permute-start.6 = (bf16[16,40,1024]{2,1,0:T(8,128)(2,1)S(1)}, bf16[16,40,1024]{2,1,0:T(8,128)(2,1)S(1)}, u32[]{:S(2)}, u32[]{:S(2)}) collective-permute-start(bf16[16,40,1024]{2,1,0:T(8,128)(2,1)S(1)} %all-to-all-done.4.a_ref), channel_id=1, source_target_pairs={{0,1},{1,0},{2,3},{3,2},{4,5},{5,4},{6,7},{7,6},{8,9},{9,8},{10,11... | collective-permute-start | bytes 3932168 | tf_op jit(solution)/shard_map/ppermute | solution.py:147
  154.1 12.4 %experts.1 = (bf16[16,40,1024]{2,1,0:T(8,128)(2,1)}, bf16[16,40,1024]{2,1,0:T(8,128)(2,1)}) custom-call(s32[34]{0:T(128)} %pad_add_fusion.place_ref, bf16[16,40,1024]{2,1,0:T(8,128)(2,1)} %copy-done.2, bf16[16,40,1024]{2,1,0:T(8,128)(2,1)} %copy-done.9, bf16[1,2048]{1,0:T(2,128)(2,1)} %broadcast_in_dim.62.gain_ref, bf16[32,2048]{1,0:T(8,128)(2,1)} %bitcast.131, ...), custom_call_target="tpu_custom_call" | custom-call | flops 2768240640 | bytes 11730944 | tf_op jit(solution)/shard_map/experts/pallas_call | solution.py:254
  169.7 2.9 %add_convert_fusion = bf16[16,40,1024]{2,1,0:T(8,128)(2,1)} fusion(bf16[16,40,1024]{2,1,0:T(8,128)(2,1)S(1)} %collective-permute-done.7, bf16[16,40,1024]{2,1,0:T(8,128)(2,1)} %get-tuple-element.55), kind=kLoop, calls=%fused_computation.1 | loop fusion | flops 2621440 | bytes 3932160 | tf_op jit(solution)/shard_map/convert_element_type | solution.py:519
  172.6 4.1 %all-to-all-start.5 = ((bf16[16,40,1024]{2,1,0:T(8,128)(2,1)}), bf16[16,40,1024]{2,1,0:T(8,128)(2,1)S(1)}, u32[]{:S(2)}, u32[]{:S(2)}) async-start(bf16[16,40,1024]{2,1,0:T(8,128)(2,1)} %add_convert_fusion), calls=%async_computation.5 | async-start | bytes 2621440 | tf_op jit(solution)/shard_map/all_to_all | solution.py:521
  178.0 16.2 %all_gather.7.full_ref = bf16[128,2048]{1,0:T(8,128)(2,1)} all-gather(bf16[128,256]{1,0:T(8,128)(2,1)S(1)} %copy-done.3), channel_id=1, replica_groups=mesh['zh'=2,'x'=4,'y'=4,'zl'=4,'core'=2] {'zl','core'}, dimensions={1}, use_global_device_ids=true | all-gather | bytes 589824 | tf_op jit(solution)/shard_map/all_gather | solution.py:523
  198.9 17.7 %all_to_all.49.parts_ref = bf16[8,136,256]{2,1,0:T(8,128)(2,1)} all-to-all(bf16[8,136,256]{2,1,0:T(8,128)(2,1)} %combine.1), channel_id=1, replica_groups=mesh['zh'=2,'x'=4,'y'=4,'zl'=4,'core'=2] {'zh','zl'}, dimensions={0} | all-to-all | bytes 1114112 | tf_op jit(solution)/shard_map/all_to_all | solution.py:528
  218.5 19.8 %all_to_all.50.last_ref = bf16[32,16,128]{2,1,0:T(8,128)(2,1)} all-to-all(bf16[32,16,128]{2,1,0:T(8,128)(2,1)} %get-tuple-element.62), channel_id=1, replica_groups=mesh['zh'=2,'x'=4,'y'=4,'zl'=4,'core'=2] {'core','x','y'}, dimensions={0} | all-to-all | bytes 262144 | tf_op jit(solution)/shard_map/all_to_all | solution.py:531
  240.7 5.6 %all-to-all-start.8 = ((f32[256,1,32]{2,1,0:T(1,128)}), f32[256,1,32]{2,1,0:T(1,128)S(1)}, u32[]{:S(2)}, u32[]{:S(2)}) async-start(f32[256,1,32]{2,1,0:T(1,128)} %bitcast.103), calls=%async_computation.8 | async-start | bytes 262144 | tf_op jit(solution)/shard_map/all_to_all | solution.py:534
  246.3 3.4 %new_kv.1 = bf16[2,128,256]{2,1,0:T(8,128)(2,1)} custom-call(bf16[128,2048]{1,0:T(8,128)(2,1)} %all_gather.7.full_ref, bf16[1,2048]{1,0:T(2,128)(2,1)} %broadcast_in_dim.61.gain_ref, bf16[3,2048,256]{2,1,0:T(8,128)(2,1)} %w_ref.4, f32[128,64]{1,0:T(8,128)} %get-tuple-element.99.cos_ref, f32[128,64]{1,0:T(8,128)} %get-tuple-element.98.sin_ref), custom_call_target="tpu_custom_call" | custom-call | tf_op jit(solution)/shard_map/new_kv/pallas_call | solution.py:64
  250.4 8.8 %all-to-all-done.8 = f32[256,1,32]{2,1,0:T(1,128)S(1)} async-done(((f32[256,1,32]{2,1,0:T(1,128)}), f32[256,1,32]{2,1,0:T(1,128)S(1)}, u32[]{:S(2)}, u32[]{:S(2)}) %all-to-all-start.8) | async-done | bytes 32800 | tf_op jit(solution)/shard_map/all_to_all | solution.py:534
  (103 shorter events, 44.1 us)
Async XLA Ops:
  2.9 17.5 %copy-start.4 = (s32[128,6]{0,1:T(8,128)S(1)}, s32[128,6]{0,1:T(8,128)}, u32[]{:S(2)}) copy-start(s32[128,6]{0,1:T(8,128)} %param.25) | copy-start | bytes 9220
  2.9 22.8 %copy-start.13 = (s32[32]{0:T(128)S(1)}, s32[32]{0:T(128)}, u32[]{:S(2)}) copy-start(s32[32]{0:T(128)} %param.21) | copy-start | bytes 388
  2.9 37.8 %copy-start.6 = (bf16[2048]{0:T(1024)(128)(2,1)S(1)}, bf16[2048]{0:T(1024)(128)(2,1)}, u32[]{:S(2)}) copy-start(bf16[2048]{0:T(1024)(128)(2,1)} %param.17) | copy-start | bytes 12292
  3.0 38.4 %copy-start.7 = (bf16[2048]{0:T(1024)(128)(2,1)S(1)}, bf16[2048]{0:T(1024)(128)(2,1)}, u32[]{:S(2)}) copy-start(bf16[2048]{0:T(1024)(128)(2,1)} %param.23) | copy-start | bytes 12292
  3.0 39.0 %copy-start.8 = (bf16[2048]{0:T(1024)(128)(2,1)S(1)}, bf16[2048]{0:T(1024)(128)(2,1)}, u32[]{:S(2)}) copy-start(bf16[2048]{0:T(1024)(128)(2,1)} %param.30) | copy-start | bytes 12292
  5.2 46.2 %collective-permute-start.1 = (bf16[176,2048]{1,0:T(8,128)(2,1)S(1)}, bf16[176,2048]{1,0:T(8,128)(2,1)S(1)}, u32[]{:S(2)}, u32[]{:S(2)}) collective-permute-start(bf16[176,2048]{1,0:T(8,128)(2,1)S(1)} %get-tuple-element.38), channel_id=1, source_target_pairs={{0,2},{2,0},{4,6},{6,4},{1,3},{3,1},{5,7},{7,5},{8,10},{10,8},{12,... | collective-permute-start | bytes 2162696 | tf_op jit(solution)/shard_map/ppermute | solution.py:431
  7.7 27.4 %all-to-all-start = ((bf16[32,8,256]{2,1,0:T(8,128)(2,1)}), bf16[32,8,256]{2,1,0:T(8,128)(2,1)S(1)}, u32[]{:S(2)}, u32[]{:S(2)}) async-start(bf16[32,8,256]{2,1,0:T(8,128)(2,1)} %pad_maximum_fusion), calls=%async_computation | async-start | bytes 262144 | tf_op jit(solution)/shard_map/all_to_all | solution.py:432
  20.4 22.1 %collective-permute-start = (s32[6,128]{1,0:T(8,128)S(1)}, s32[6,128]{1,0:T(8,128)S(1)}, u32[]{:S(2)}, u32[]{:S(2)}) collective-permute-start(s32[6,128]{1,0:T(8,128)S(1)} %bitcast.104), channel_id=1, source_target_pairs={{0,128},{128,0},{1,129},{129,1},{2,130},{130,2},{3,131},{131,3},{4... | collective-permute-start | bytes 9224 | tf_op jit(solution)/shard_map/ppermute | solution.py:151
  36.3 15.2 %all-to-all-start.1 = ((bf16[32,8,256]{2,1,0:T(8,128)(2,1)}), bf16[32,8,256]{2,1,0:T(8,128)(2,1)S(1)}, u32[]{:S(2)}, u32[]{:S(2)}) async-start(bf16[32,8,256]{2,1,0:T(8,128)(2,1)} %gather_fusion), calls=%async_computation.1 | async-start | bytes 262144 | tf_op jit(solution)/shard_map/all_to_all | solution.py:442
  42.6 39.2 %collective-permute-start.2 = (bf16[176,2048]{1,0:T(8,128)(2,1)S(1)}, bf16[176,2048]{1,0:T(8,128)(2,1)S(1)}, u32[]{:S(2)}, u32[]{:S(2)}) collective-permute-start(bf16[176,2048]{1,0:T(8,128)(2,1)S(1)} %get-tuple-element.44), channel_id=1, source_target_pairs={{0,2},{2,0},{4,6},{6,4},{1,3},{3,1},{5,7},{7,5},{8,10},{10,8},{12,... | collective-permute-start | bytes 2162696 | tf_op jit(solution)/shard_map/ppermute | solution.py:435
  51.4 30.3 %copy-start.11 = (bf16[176,2048]{1,0:T(8,128)(2,1)}, bf16[176,2048]{1,0:T(8,128)(2,1)S(1)}, u32[]{:S(2)}) copy-start(bf16[176,2048]{1,0:T(8,128)(2,1)S(1)} %collective-permute-done.1.pg_ref) | copy-start | bytes 2162692
  81.7 16.9 %copy-start.12 = (bf16[176,2048]{1,0:T(8,128)(2,1)}, bf16[176,2048]{1,0:T(8,128)(2,1)S(1)}, u32[]{:S(2)}) copy-start(bf16[176,2048]{1,0:T(8,128)(2,1)S(1)} %collective-permute-done.2.pu_ref) | copy-start | bytes 2162692
  81.8 1.8 collective-permute-start.3
  85.3 13.3 %all-to-all-start.2 = ((bf16[4,128,256]{2,1,0:T(8,128)(2,1)}), bf16[4,128,256]{2,1,0:T(8,128)(2,1)S(1)}, u32[]{:S(2)}, u32[]{:S(2)}) async-start(bf16[4,128,256]{2,1,0:T(8,128)(2,1)} %add_convert_fusion.1), calls=%async_computation.2 | async-start | bytes 524288 | tf_op jit(solution)/shard_map/all_to_all | solution.py:464
  89.1 9.5 %collective-permute-start.4 = (s32[6,128]{1,0:T(8,128)S(1)}, s32[6,128]{1,0:T(8,128)S(1)}, u32[]{:S(2)}, u32[]{:S(2)}) collective-permute-start(s32[6,128]{1,0:T(8,128)S(1)} %reshape.350), channel_id=1, source_target_pairs={{0,128},{128,0},{1,129},{129,1},{2,130},{130,2},{3,131},{131,3},{4... | collective-permute-start | bytes 9224 | tf_op jit(solution)/shard_map/ppermute | solution.py:151
  99.5 19.2 %all-to-all-start.3 = ((bf16[8,128,256]{2,1,0:T(8,128)(2,1)}), bf16[8,128,256]{2,1,0:T(8,128)(2,1)S(1)}, u32[]{:S(2)}, u32[]{:S(2)}) async-start(bf16[8,128,256]{2,1,0:T(8,128)(2,1)} %broadcast_in_dim.64), calls=%async_computation.3 | async-start | bytes 1048576 | tf_op jit(solution)/shard_map/all_to_all | solution.py:143
  122.3 6.6 %copy-start.10 = (bf16[1,176,2048]{2,1,0:T(8,128)(2,1)S(1)}, bf16[1,176,2048]{2,1,0:T(8,128)(2,1)}, u32[]{:S(2)}) copy-start(bf16[1,176,2048]{2,1,0:T(8,128)(2,1)} %param.27) | copy-start | bytes 2162692
  122.3 23.2 %all-to-all-start.4 = ((bf16[16,40,1024]{2,1,0:T(8,128)(2,1)}), bf16[16,40,1024]{2,1,0:T(8,128)(2,1)S(1)}, u32[]{:S(2)}, u32[]{:S(2)}) async-start(bf16[16,40,1024]{2,1,0:T(8,128)(2,1)} %bitcast.99), calls=%async_computation.4 | async-start | bytes 2621440 | tf_op jit(solution)/shard_map/all_to_all | solution.py:498
  128.9 14.2 %collective-permute-start.5 = (bf16[176,2048]{1,0:T(8,128)(2,1)S(1)}, bf16[176,2048]{1,0:T(8,128)(2,1)}, u32[]{:S(2)}, u32[]{:S(2)}) collective-permute-start(bf16[176,2048]{1,0:T(8,128)(2,1)S(1)} %bitcast.130), channel_id=1, source_target_pairs={{0,2},{2,0},{4,6},{6,4},{1,3},{3,1},{5,7},{7,5},{8,10},{10,8},{12,... | collective-permute-start | bytes 2162696 | tf_op jit(solution)/shard_map/ppermute | solution.py:501
  145.5 7.5 %copy-start.2 = (bf16[16,40,1024]{2,1,0:T(8,128)(2,1)}, bf16[16,40,1024]{2,1,0:T(8,128)(2,1)S(1)}, u32[]{:S(2)}) copy-start(bf16[16,40,1024]{2,1,0:T(8,128)(2,1)S(1)} %all-to-all-done.4.a_ref) | copy-start | bytes 3932164
  145.5 7.5 %collective-permute-start.6 = (bf16[16,40,1024]{2,1,0:T(8,128)(2,1)S(1)}, bf16[16,40,1024]{2,1,0:T(8,128)(2,1)S(1)}, u32[]{:S(2)}, u32[]{:S(2)}) collective-permute-start(bf16[16,40,1024]{2,1,0:T(8,128)(2,1)S(1)} %all-to-all-done.4.a_ref), channel_id=1, source_target_pairs={{0,1},{1,0},{2,3},{3,2},{4,5},{5,4},{6,7},{7,6},{8,9},{9,8},{10,11... | collective-permute-start | bytes 3932168 | tf_op jit(solution)/shard_map/ppermute | solution.py:147
  166.4 3.2 %collective-permute-start.7 = (bf16[16,40,1024]{2,1,0:T(8,128)(2,1)}, bf16[16,40,1024]{2,1,0:T(8,128)(2,1)S(1)}, u32[]{:S(2)}, u32[]{:S(2)}) collective-permute-start(bf16[16,40,1024]{2,1,0:T(8,128)(2,1)} %get-tuple-element.56), channel_id=1, source_target_pairs={{0,1},{1,0},{2,3},{3,2},{4,5},{5,4},{6,7},{7,6},{8,9},{9,8},{10,11... | collective-permute-start | bytes 3932168 | tf_op jit(solution)/shard_map/ppermute | solution.py:147
  172.6 22.4 %all-to-all-start.5 = ((bf16[16,40,1024]{2,1,0:T(8,128)(2,1)}), bf16[16,40,1024]{2,1,0:T(8,128)(2,1)S(1)}, u32[]{:S(2)}, u32[]{:S(2)}) async-start(bf16[16,40,1024]{2,1,0:T(8,128)(2,1)} %add_convert_fusion), calls=%async_computation.5 | async-start | bytes 2621440 | tf_op jit(solution)/shard_map/all_to_all | solution.py:521
  240.7 18.5 %all-to-all-start.8 = ((f32[256,1,32]{2,1,0:T(1,128)}), f32[256,1,32]{2,1,0:T(1,128)S(1)}, u32[]{:S(2)}, u32[]{:S(2)}) async-start(f32[256,1,32]{2,1,0:T(1,128)} %bitcast.103), calls=%async_computation.8 | async-start | bytes 262144 | tf_op jit(solution)/shard_map/all_to_all | solution.py:534
  (5 other events, 11.8 us)

commit v8 on v7

--- a/solution.py
+++ b/solution.py
@@ -33,18 +33,20 @@
 def rope_tables(length, new):
     half_len = HD // 2
     freqs = 10000.0 ** (-2.0 * jnp.arange(half_len, dtype=f32) / HD)
-    positions = (length + jnp.arange(new, dtype=jnp.int32)).astype(f32)
-    angles = positions[:, None] * freqs[None, :]
-    return jnp.cos(angles), jnp.sin(angles)
+    offsets = jnp.arange(new, dtype=jnp.int32).astype(f32)[:, None] * freqs[None, :]
+    shift = length.astype(f32).reshape(1, 1) * freqs[None, :]
+    return jnp.cos(offsets), jnp.sin(offsets), jnp.cos(shift), jnp.sin(shift)
 
 
 def norm_rows(full_ref, gain_ref):
     return rms_scale(full_ref[...].astype(f32), gain_ref[...]).astype(bf16)
 
 
-def rotate(values, cos_ref, sin_ref):
-    cosine = jnp.concatenate([cos_ref[...], cos_ref[...]], axis=1)
-    sine = jnp.concatenate([-sin_ref[...], sin_ref[...]], axis=1)
+def rotate(values, cos_ref, sin_ref, cos_at_ref, sin_at_ref):
+    cosine = cos_ref[...] * cos_at_ref[...] - sin_ref[...] * sin_at_ref[...]
+    sine = sin_ref[...] * cos_at_ref[...] + cos_ref[...] * sin_at_ref[...]
+    cosine = jnp.concatenate([cosine, cosine], axis=1)
+    sine = jnp.concatenate([-sine, sine], axis=1)
     heads = []
     for head in range(values.shape[1] // HD):
         piece = values[:, head * HD : (head + 1) * HD]
@@ -52,10 +54,11 @@
     return jnp.concatenate(heads, axis=1).astype(bf16)
 
 
-def new_kv_body(full_ref, gain_ref, w_ref, cos_ref, sin_ref, o_ref):
+def new_kv_body(full_ref, gain_ref, w_ref, *refs):
+    tables, o_ref = refs[:4], refs[4]
     normed = norm_rows(full_ref, gain_ref)
     keys = jnp.dot(normed, w_ref[1], preferred_element_type=f32)
-    o_ref[0] = rotate(keys, cos_ref, sin_ref)
+    o_ref[0] = rotate(keys, *tables)
     o_ref[1] = jnp.dot(normed, w_ref[2], preferred_element_type=f32).astype(bf16)
 
 
@@ -64,22 +67,24 @@
     return pl.pallas_call(
         new_kv_body,
         out_shape=jax.ShapeDtypeStruct((2, full.shape[0], w_qkv.shape[2]), bf16),
-        in_specs=[vm] * 5,
+        in_specs=[vm] * 7,
         out_specs=vm,
         name="new_kv",
     )(full, gain, w_qkv, *tables)
 
 
 def attend_body(
-    len_ref, place_ref, full_ref, gain_ref, qkv_ref, cos_ref, sin_ref, kv_ref, w_ref, om_ref, ot_ref
+    len_ref, place_ref, full_ref, gain_ref, qkv_ref, cos_ref, sin_ref, cos_at_ref, sin_at_ref,
+    kv_ref, w_ref, om_ref, ot_ref,
 ):
+    tables = (cos_ref, sin_ref, cos_at_ref, sin_at_ref)
     length = len_ref[0]
     first = place_ref[0] == 0
     ctx = kv_ref.shape[2]
     new = full_ref.shape[0]
     normed = norm_rows(full_ref, gain_ref)
-    q_all = rotate(jnp.dot(normed, qkv_ref[0], preferred_element_type=f32), cos_ref, sin_ref)
-    k_all = rotate(jnp.dot(normed, qkv_ref[1], preferred_element_type=f32), cos_ref, sin_ref)
+    q_all = rotate(jnp.dot(normed, qkv_ref[0], preferred_element_type=f32), *tables)
+    k_all = rotate(jnp.dot(normed, qkv_ref[1], preferred_element_type=f32), *tables)
     v_all = jnp.dot(normed, qkv_ref[2], preferred_element_type=f32).astype(bf16)
     heads = []
     for head in range(q_all.shape[1] // HD):
@@ -132,7 +137,7 @@
     return pl.pallas_call(
         attend_body,
         out_shape=(shape, shape),
-        in_specs=[pl.BlockSpec(memory_space=pltpu.SMEM)] * 2 + [vm] * 7,
+        in_specs=[pl.BlockSpec(memory_space=pltpu.SMEM)] * 2 + [vm] * 9,
         out_specs=(vm, vm),
         name="attend",
     )(length, place, full, gain, w_qkv, *tables, kv_cache, w_out)
@@ -271,23 +276,24 @@
 
 
 def dispatch_body(chosen_ref, parts_ref, out_ref):
-    feat = parts_ref.shape[2]
-    for part in range(4):
-        both = jnp.concatenate([parts_ref[part], parts_ref[4 + part]], axis=0)
-        out_ref[:, part * feat : (part + 1) * feat] = jnp.dot(
-            chosen_ref[...], both, preferred_element_type=f32
-        ).astype(bf16)
+    both = jnp.concatenate([parts_ref[0, 0], parts_ref[1, 0]], axis=0)
+    out_ref[...] = jnp.dot(chosen_ref[...], both, preferred_element_type=f32).astype(bf16)
 
 
 def dispatch(chosen_t, parts):
-    vm = pl.BlockSpec(memory_space=pltpu.VMEM)
+    new, feat = parts.shape[1:]
+    slots, tokens = chosen_t.shape
     return pl.pallas_call(
         dispatch_body,
-        out_shape=jax.ShapeDtypeStruct((chosen_t.shape[0], 4 * parts.shape[2]), bf16),
-        in_specs=[vm, vm],
-        out_specs=vm,
+        grid=(4,),
+        out_shape=jax.ShapeDtypeStruct((slots, 4 * feat), bf16),
+        in_specs=[
+            pl.BlockSpec((slots, tokens), lambda i: (0, 0)),
+            pl.BlockSpec((2, 1, new, feat), lambda i: (0, i, 0, 0)),
+        ],
+        out_specs=pl.BlockSpec((slots, feat), lambda i: (0, i)),
         name="dispatch",
-    )(chosen_t, parts)
+    )(chosen_t, parts.reshape(2, 4, new, feat))
 
 
 def combine_body(chosen_ref, back_ref, out_ref):
@@ -427,18 +433,18 @@
     w_in = w_exp_in[0].swapaxes(1, 2)
     w_down = w_exp_down[0]
     neighbours = [(0, 1), (1, 0), (2, 3), (3, 2)]
-    chunks, ids_out, gate_w = barrier((chunks, ids_t, w_in[0]))
-    pair_gate = lax.ppermute(gate_w, "zl", neighbours)
+    pair_gate = lax.ppermute(w_in[0], "zl", neighbours)
     leg = lax.all_to_all(chunks, REQ, 0, 0, tiled=True)
-    ids_there, up_w = barrier((column_swap(ids_out), w_in[1]))
-
-    pair_up = lax.ppermute(up_w, "zl", neighbours)
+    ids_there = column_swap(ids_t)
+
 
     req_iota = jnp.arange(reqs, dtype=jnp.int32)
     owner_of = jnp.sum(
         jnp.where(holder_slot[None, :] == req_iota[:, None], req_iota[None, :], 0), axis=1
     )
     leg = leg.at[owner_of].get(mode="promise_in_bounds")
+    leg, up_w = barrier((leg, w_in[1]))
+    pair_up = lax.ppermute(up_w, "zl", neighbours)
     leg = lax.all_to_all(leg, REQ, 0, 0, tiled=True)
     leg, pair_gate, gain, gain_ffn, gain_final, place = barrier(
         (leg, pair_gate, attn_gain[None], ffn_gain[None], final_gain[None], place)

time: 261 us -> 256 us (0.981)
  blocking collectives: 75.1 us -> 53.3 us
  starting transfers between devices: 59.3 us -> 71.3 us
    all_to_all x1 -> x0, blocking collectives: 19.8 us -> none  [local(): last_all = lax.all_to_all(last, ('core', 'x', 'y'), 0, 0, tiled=True)]
    all_to_all x0 -> x1, starting transfers between devices: none -> 12.2 us  [local(): last_all = lax.all_to_all(last, ('core', 'x', 'y'), 0, 0, tiled=True)]
    all_to_all x0 -> x1, waiting for transfers between devices: none -> 7.53 us  [local(): last_all = lax.all_to_all(last, ('core', 'x', 'y'), 0, 0, tiled=True)]
    all_to_all x1, waiting for transfers between devices: 8.82 us -> 2.31 us  [local(): leg = lax.all_to_all(chunks, REQ, 0, 0, tiled=True)]
  transfers between devices with their start and end apart: 15 -> 16, of which waited for: 11 -> 13; matrix products, arithmetic and copies ran while one was open for 4% -> 5% of each run, Pallas kernels for 4% -> 4%
where the time goes in v8:
time: 256 us; the launch traced here: 255 us
  starting transfers between devices  71.3 us (28%)
  waiting for transfers between devices  70.3 us (27%)
  blocking collectives  53.3 us (21%)
  Pallas kernels  32.6 us (13%)
  other arithmetic  13.2 us (5%)
  local copies, waits for them, and re-layouts  10.9 us (4%)
  between operations  2.96 us (1%)
    all_gather x1, blocking collectives, local(): full = lax.all_gather(held, TP, axis=1, tiled=True)  19.3 us
    all_to_all x1, blocking collectives, local(): summed = lax.all_to_all(packed, Z, 0, 0, tiled=True)  17.7 us
    all_gather x1, blocking collectives, local(): own_full = lax.all_gather(hidden_late, TP, axis=1, tiled=True)  16.3 us
    ppermute x1, waiting for transfers between devices, local(): pair_down = lax.ppermute(down_w, 'zl', neighbours)  14.7 us
    all_to_all x1, starting transfers between devices, local(): leg = lax.all_to_all(chunks, REQ, 0, 0, tiled=True)  14.5 us
    all_to_all x1, waiting for transfers between devices, spread(): return lax.all_to_all(wide, axes, 0, 0, tiled=True)  13.9 us
    pallas_call x1, Pallas kernels, experts(): pl.pallas_call(experts_body, out_shape=(shape, shape), in_specs=[pl.Block...  12.4 us
    all_to_all x1, starting transfers between devices, local(): last_all = lax.all_to_all(last, ('core', 'x', 'y'), 0, 0, tiled=True)  12.2 us
  transfers between devices with their start and end apart: 16, of which 13 were waited for; matrix products, arithmetic and copies ran while one was open for 5% of the time, Pallas kernels for 4%

profile of v8, /device:TPU:1, one launch (start us, length us, event | category | flops | bytes accessed | tf_op | source)
XLA Modules:
  0.0 255.3 jit_solution(10343335693480709731)
XLA Ops:
  3.7 14.5 %all-to-all-start = ((bf16[32,8,256]{2,1,0:T(8,128)(2,1)}), bf16[32,8,256]{2,1,0:T(8,128)(2,1)S(1)}, u32[]{:S(2)}, u32[]{:S(2)}) async-start(bf16[32,8,256]{2,1,0:T(8,128)(2,1)} %pad_maximum_fusion), calls=%async_computation | async-start | bytes 262144 | tf_op jit(solution)/shard_map/all_to_all | solution.py:437
  20.5 5.1 %collective-permute-start = (s32[6,128]{1,0:T(8,128)S(1)}, s32[6,128]{1,0:T(8,128)S(1)}, u32[]{:S(2)}, u32[]{:S(2)}) collective-permute-start(s32[6,128]{1,0:T(8,128)S(1)} %bitcast.107), channel_id=1, source_target_pairs={{0,128},{128,0},{1,129},{129,1},{2,130},{130,2},{3,131},{131,3},{4... | collective-permute-start | bytes 9224 | tf_op jit(solution)/shard_map/ppermute | solution.py:156
  30.7 4.5 %all-to-all-start.1 = ((bf16[32,8,256]{2,1,0:T(8,128)(2,1)}), bf16[32,8,256]{2,1,0:T(8,128)(2,1)S(1)}, u32[]{:S(2)}, u32[]{:S(2)}) async-start(bf16[32,8,256]{2,1,0:T(8,128)(2,1)} %gather_fusion), calls=%async_computation.1 | async-start | bytes 262144 | tf_op jit(solution)/shard_map/all_to_all | solution.py:448
  40.7 6.9 %all-to-all-done.1 = bf16[32,8,256]{2,1,0:T(8,128)(2,1)S(1)} async-done(((bf16[32,8,256]{2,1,0:T(8,128)(2,1)}), bf16[32,8,256]{2,1,0:T(8,128)(2,1)S(1)}, u32[]{:S(2)}, u32[]{:S(2)}) %all-to-all-start.1) | async-done | bytes 131104 | tf_op jit(solution)/shard_map/all_to_all | solution.py:448
  50.1 19.3 %all_gather.6.full_ref = bf16[128,2048]{1,0:T(8,128)(2,1)} all-gather(bf16[128,256]{1,0:T(8,128)(2,1)S(1)} %reshape.384), channel_id=1, replica_groups=mesh['zh'=2,'x'=4,'y'=4,'zl'=4,'core'=2] {'zl','core'}, dimensions={1}, use_global_device_ids=true | all-gather | bytes 589824 | tf_op jit(solution)/shard_map/all_gather | solution.py:456
  69.4 5.8 %attend.1 = (bf16[4,128,256]{2,1,0:T(8,128)(2,1)}, bf16[4,128,256]{2,1,0:T(8,128)(2,1)}) custom-call(s32[1]{0:T(128)} %bitcast.26.len_ref, s32[34]{0:T(128)} %pad_add_fusion.place_ref, bf16[128,2048]{1,0:T(8,128)(2,1)} %all_gather.6.full_ref, bf16[1,2048]{1,0:T(2,128)(2,1)} %broadcast_in_dim.61.gain_ref, bf16[3,2048,256]{2,1,0:T(8,128)(2,1)} %w_ref.4, ...), custom_call_target="tpu_custom_call" | custom-call | tf_op jit(solution)/shard_map/attend/pallas_call | solution.py:137
  78.8 3.4 %all-to-all-start.2 = ((bf16[4,128,256]{2,1,0:T(8,128)(2,1)}), bf16[4,128,256]{2,1,0:T(8,128)(2,1)S(1)}, u32[]{:S(2)}, u32[]{:S(2)}) async-start(bf16[4,128,256]{2,1,0:T(8,128)(2,1)} %add_convert_fusion.1), calls=%async_computation.2 | async-start | bytes 524288 | tf_op jit(solution)/shard_map/all_to_all | solution.py:470
  82.6 4.0 %collective-permute-start.4 = (s32[6,128]{1,0:T(8,128)S(1)}, s32[6,128]{1,0:T(8,128)S(1)}, u32[]{:S(2)}, u32[]{:S(2)}) collective-permute-start(s32[6,128]{1,0:T(8,128)S(1)} %reshape.390), channel_id=1, source_target_pairs={{0,128},{128,0},{1,129},{129,1},{2,130},{130,2},{3,131},{131,3},{4... | collective-permute-start | bytes 9224 | tf_op jit(solution)/shard_map/ppermute | solution.py:156
  86.6 4.7 %collective-permute-done.4 = s32[6,128]{1,0:T(8,128)S(1)} collective-permute-done((s32[6,128]{1,0:T(8,128)S(1)}, s32[6,128]{1,0:T(8,128)S(1)}, u32[]{:S(2)}, u32[]{:S(2)}) %collective-permute-start.4) | collective-permute-done | bytes 3104 | tf_op jit(solution)/shard_map/ppermute | solution.py:156
  92.3 4.2 %all-to-all-start.3 = ((bf16[8,128,256]{2,1,0:T(8,128)(2,1)}), bf16[8,128,256]{2,1,0:T(8,128)(2,1)S(1)}, u32[]{:S(2)}, u32[]{:S(2)}) async-start(bf16[8,128,256]{2,1,0:T(8,128)(2,1)} %broadcast_in_dim.64), calls=%async_computation.3 | async-start | bytes 1048576 | tf_op jit(solution)/shard_map/all_to_all | solution.py:148
  98.3 13.9 %all-to-all-done.3 = bf16[8,128,256]{2,1,0:T(8,128)(2,1)S(1)} async-done(((bf16[8,128,256]{2,1,0:T(8,128)(2,1)}), bf16[8,128,256]{2,1,0:T(8,128)(2,1)S(1)}, u32[]{:S(2)}, u32[]{:S(2)}) %all-to-all-start.3) | async-done | bytes 524320 | tf_op jit(solution)/shard_map/all_to_all | solution.py:148
  113.1 3.9 %dispatch.1 = bf16[640,1024]{1,0:T(8,128)(2,1)} custom-call(bf16[640,256]{1,0:T(8,128)(2,1)} %fusion.37.chosen_ref, bf16[2,4,128,256]{3,2,1,0:T(8,128)(2,1)} %bitcast.102), custom_call_target="tpu_custom_call" | custom-call | tf_op jit(solution)/shard_map/dispatch/pallas_call | solution.py:286
  117.0 6.6 %all-to-all-start.4 = ((bf16[16,40,1024]{2,1,0:T(8,128)(2,1)}), bf16[16,40,1024]{2,1,0:T(8,128)(2,1)S(1)}, u32[]{:S(2)}, u32[]{:S(2)}) async-start(bf16[16,40,1024]{2,1,0:T(8,128)(2,1)} %bitcast.101), calls=%async_computation.4 | async-start | bytes 2621440 | tf_op jit(solution)/shard_map/all_to_all | solution.py:504
  123.7 14.7 %collective-permute-done.5.pd_ref = bf16[176,2048]{1,0:T(8,128)(2,1)} collective-permute-done((bf16[176,2048]{1,0:T(8,128)(2,1)S(1)}, bf16[176,2048]{1,0:T(8,128)(2,1)}, u32[]{:S(2)}, u32[]{:S(2)}) %collective-permute-start.5) | collective-permute-done | bytes 720928 | tf_op jit(solution)/shard_map/ppermute | solution.py:507
  140.4 4.2 %collective-permute-start.6 = (bf16[16,40,1024]{2,1,0:T(8,128)(2,1)S(1)}, bf16[16,40,1024]{2,1,0:T(8,128)(2,1)S(1)}, u32[]{:S(2)}, u32[]{:S(2)}) collective-permute-start(bf16[16,40,1024]{2,1,0:T(8,128)(2,1)S(1)} %all-to-all-done.4.a_ref), channel_id=1, source_target_pairs={{0,1},{1,0},{2,3},{3,2},{4,5},{5,4},{6,7},{7,6},{8,9},{9,8},{10,11... | collective-permute-start | bytes 3932168 | tf_op jit(solution)/shard_map/ppermute | solution.py:152
  148.4 12.4 %experts.1 = (bf16[16,40,1024]{2,1,0:T(8,128)(2,1)}, bf16[16,40,1024]{2,1,0:T(8,128)(2,1)}) custom-call(s32[34]{0:T(128)} %pad_add_fusion.place_ref, bf16[16,40,1024]{2,1,0:T(8,128)(2,1)} %copy-done.2, bf16[16,40,1024]{2,1,0:T(8,128)(2,1)} %copy-done.10, bf16[1,2048]{1,0:T(2,128)(2,1)} %broadcast_in_dim.62.gain_ref, bf16[32,2048]{1,0:T(8,128)(2,1)} %bitcast.136, ...), custom_call_target="tpu_custom_call" | custom-call | flops 2768240640 | bytes 11730944 | tf_op jit(solution)/shard_map/experts/pallas_call | solution.py:259
  167.0 4.5 %all-to-all-start.5 = ((bf16[16,40,1024]{2,1,0:T(8,128)(2,1)}), bf16[16,40,1024]{2,1,0:T(8,128)(2,1)S(1)}, u32[]{:S(2)}, u32[]{:S(2)}) async-start(bf16[16,40,1024]{2,1,0:T(8,128)(2,1)} %add_convert_fusion), calls=%async_computation.5 | async-start | bytes 2621440 | tf_op jit(solution)/shard_map/all_to_all | solution.py:527
  172.7 16.3 %all_gather.7.full_ref = bf16[128,2048]{1,0:T(8,128)(2,1)} all-gather(bf16[128,256]{1,0:T(8,128)(2,1)S(1)} %copy-done.4), channel_id=1, replica_groups=mesh['zh'=2,'x'=4,'y'=4,'zl'=4,'core'=2] {'zl','core'}, dimensions={1}, use_global_device_ids=true | all-gather | bytes 589824 | tf_op jit(solution)/shard_map/all_gather | solution.py:529
  193.7 17.7 %all_to_all.49.parts_ref = bf16[8,136,256]{2,1,0:T(8,128)(2,1)} all-to-all(bf16[8,136,256]{2,1,0:T(8,128)(2,1)} %combine.1), channel_id=1, replica_groups=mesh['zh'=2,'x'=4,'y'=4,'zl'=4,'core'=2] {'zh','zl'}, dimensions={0} | all-to-all | bytes 1114112 | tf_op jit(solution)/shard_map/all_to_all | solution.py:534
  213.2 12.2 %all-to-all-start.7 = ((bf16[32,16,128]{2,1,0:T(8,128)(2,1)}), bf16[32,16,128]{2,1,0:T(8,128)(2,1)S(1)}, u32[]{:S(2)}, u32[]{:S(2)}) async-start(bf16[32,16,128]{2,1,0:T(8,128)(2,1)} %get-tuple-element.56), calls=%async_computation.7 | async-start | bytes 262144 | tf_op jit(solution)/shard_map/all_to_all | solution.py:537
  225.4 7.5 %all-to-all-done.7.last_ref = bf16[32,16,128]{2,1,0:T(8,128)(2,1)S(1)} async-done(((bf16[32,16,128]{2,1,0:T(8,128)(2,1)}), bf16[32,16,128]{2,1,0:T(8,128)(2,1)S(1)}, u32[]{:S(2)}, u32[]{:S(2)}) %all-to-all-start.7) | async-done | bytes 131104 | tf_op jit(solution)/shard_map/all_to_all | solution.py:537
  236.1 5.6 %all-to-all-start.8 = ((f32[256,1,32]{2,1,0:T(1,128)}), f32[256,1,32]{2,1,0:T(1,128)S(1)}, u32[]{:S(2)}, u32[]{:S(2)}) async-start(f32[256,1,32]{2,1,0:T(1,128)} %bitcast.106), calls=%async_computation.8 | async-start | bytes 262144 | tf_op jit(solution)/shard_map/all_to_all | solution.py:540
  242.3 3.4 %new_kv.1 = bf16[2,128,256]{2,1,0:T(8,128)(2,1)} custom-call(bf16[128,2048]{1,0:T(8,128)(2,1)} %all_gather.7.full_ref, bf16[1,2048]{1,0:T(2,128)(2,1)} %broadcast_in_dim.61.gain_ref, bf16[3,2048,256]{2,1,0:T(8,128)(2,1)} %w_ref.4, f32[128,64]{1,0:T(8,128)} %get-tuple-element.93.cos_ref.refs_0_, f32[128,64]{1,0:T(8,128)} %get-tuple-element.92.sin_ref.refs_1_, ...), custom_call_target="tpu_custom_call" | custom-call | tf_op jit(solution)/shard_map/new_kv/pallas_call | solution.py:67
  246.3 8.2 %all-to-all-done.8 = f32[256,1,32]{2,1,0:T(1,128)S(1)} async-done(((f32[256,1,32]{2,1,0:T(1,128)}), f32[256,1,32]{2,1,0:T(1,128)S(1)}, u32[]{:S(2)}, u32[]{:S(2)}) %all-to-all-start.8) | async-done | bytes 32800 | tf_op jit(solution)/shard_map/all_to_all | solution.py:540
  (109 shorter events, 48.6 us)
Async XLA Ops:
  3.7 25.8 %all-to-all-start = ((bf16[32,8,256]{2,1,0:T(8,128)(2,1)}), bf16[32,8,256]{2,1,0:T(8,128)(2,1)S(1)}, u32[]{:S(2)}, u32[]{:S(2)}) async-start(bf16[32,8,256]{2,1,0:T(8,128)(2,1)} %pad_maximum_fusion), calls=%async_computation | async-start | bytes 262144 | tf_op jit(solution)/shard_map/all_to_all | solution.py:437
  18.2 7.5 %copy-start.14 = (s32[32]{0:T(128)S(1)}, s32[32]{0:T(128)}, u32[]{:S(2)}) copy-start(s32[32]{0:T(128)} %param.21) | copy-start | bytes 388
  18.2 18.4 %copy-start.7 = (bf16[2048]{0:T(1024)(128)(2,1)S(1)}, bf16[2048]{0:T(1024)(128)(2,1)}, u32[]{:S(2)}) copy-start(bf16[2048]{0:T(1024)(128)(2,1)} %param.17) | copy-start | bytes 12292
  18.2 19.0 %copy-start.8 = (bf16[2048]{0:T(1024)(128)(2,1)S(1)}, bf16[2048]{0:T(1024)(128)(2,1)}, u32[]{:S(2)}) copy-start(bf16[2048]{0:T(1024)(128)(2,1)} %param.23) | copy-start | bytes 12292
  18.2 19.6 %copy-start.9 = (bf16[2048]{0:T(1024)(128)(2,1)S(1)}, bf16[2048]{0:T(1024)(128)(2,1)}, u32[]{:S(2)}) copy-start(bf16[2048]{0:T(1024)(128)(2,1)} %param.30) | copy-start | bytes 12292
  19.7 27.9 %collective-permute-start.1 = (bf16[176,2048]{1,0:T(8,128)(2,1)S(1)}, bf16[176,2048]{1,0:T(8,128)(2,1)S(1)}, u32[]{:S(2)}, u32[]{:S(2)}) collective-permute-start(bf16[176,2048]{1,0:T(8,128)(2,1)S(1)} %get-tuple-element.76), channel_id=1, source_target_pairs={{0,2},{2,0},{4,6},{6,4},{1,3},{3,1},{5,7},{7,5},{8,10},{10,8},{12,... | collective-permute-start | bytes 2162696 | tf_op jit(solution)/shard_map/ppermute | solution.py:436
  20.5 20.2 %collective-permute-start = (s32[6,128]{1,0:T(8,128)S(1)}, s32[6,128]{1,0:T(8,128)S(1)}, u32[]{:S(2)}, u32[]{:S(2)}) collective-permute-start(s32[6,128]{1,0:T(8,128)S(1)} %bitcast.107), channel_id=1, source_target_pairs={{0,128},{128,0},{1,129},{129,1},{2,130},{130,2},{3,131},{131,3},{4... | collective-permute-start | bytes 9224 | tf_op jit(solution)/shard_map/ppermute | solution.py:156
  30.7 16.8 %all-to-all-start.1 = ((bf16[32,8,256]{2,1,0:T(8,128)(2,1)}), bf16[32,8,256]{2,1,0:T(8,128)(2,1)S(1)}, u32[]{:S(2)}, u32[]{:S(2)}) async-start(bf16[32,8,256]{2,1,0:T(8,128)(2,1)} %gather_fusion), calls=%async_computation.1 | async-start | bytes 262144 | tf_op jit(solution)/shard_map/all_to_all | solution.py:448
  35.2 40.0 %collective-permute-start.2 = (bf16[176,2048]{1,0:T(8,128)(2,1)S(1)}, bf16[176,2048]{1,0:T(8,128)(2,1)S(1)}, u32[]{:S(2)}, u32[]{:S(2)}) collective-permute-start(bf16[176,2048]{1,0:T(8,128)(2,1)S(1)} %get-tuple-element.38), channel_id=1, source_target_pairs={{0,2},{2,0},{4,6},{6,4},{1,3},{3,1},{5,7},{7,5},{8,10},{10,8},{12,... | collective-permute-start | bytes 2162696 | tf_op jit(solution)/shard_map/ppermute | solution.py:447
  47.6 27.7 %copy-start.12 = (bf16[176,2048]{1,0:T(8,128)(2,1)}, bf16[176,2048]{1,0:T(8,128)(2,1)S(1)}, u32[]{:S(2)}) copy-start(bf16[176,2048]{1,0:T(8,128)(2,1)S(1)} %collective-permute-done.1.pg_ref) | copy-start | bytes 2162692
  75.2 16.2 %copy-start.13 = (bf16[176,2048]{1,0:T(8,128)(2,1)}, bf16[176,2048]{1,0:T(8,128)(2,1)S(1)}, u32[]{:S(2)}) copy-start(bf16[176,2048]{1,0:T(8,128)(2,1)S(1)} %collective-permute-done.2.pu_ref) | copy-start | bytes 2162692
  75.2 1.8 collective-permute-start.3
  78.8 12.6 %all-to-all-start.2 = ((bf16[4,128,256]{2,1,0:T(8,128)(2,1)}), bf16[4,128,256]{2,1,0:T(8,128)(2,1)S(1)}, u32[]{:S(2)}, u32[]{:S(2)}) async-start(bf16[4,128,256]{2,1,0:T(8,128)(2,1)} %add_convert_fusion.1), calls=%async_computation.2 | async-start | bytes 524288 | tf_op jit(solution)/shard_map/all_to_all | solution.py:470
  82.6 8.8 %collective-permute-start.4 = (s32[6,128]{1,0:T(8,128)S(1)}, s32[6,128]{1,0:T(8,128)S(1)}, u32[]{:S(2)}, u32[]{:S(2)}) collective-permute-start(s32[6,128]{1,0:T(8,128)S(1)} %reshape.390), channel_id=1, source_target_pairs={{0,128},{128,0},{1,129},{129,1},{2,130},{130,2},{3,131},{131,3},{4... | collective-permute-start | bytes 9224 | tf_op jit(solution)/shard_map/ppermute | solution.py:156
  92.3 20.0 %all-to-all-start.3 = ((bf16[8,128,256]{2,1,0:T(8,128)(2,1)}), bf16[8,128,256]{2,1,0:T(8,128)(2,1)S(1)}, u32[]{:S(2)}, u32[]{:S(2)}) async-start(bf16[8,128,256]{2,1,0:T(8,128)(2,1)} %broadcast_in_dim.64), calls=%async_computation.3 | async-start | bytes 1048576 | tf_op jit(solution)/shard_map/all_to_all | solution.py:148
  117.0 6.6 %copy-start.11 = (bf16[1,176,2048]{2,1,0:T(8,128)(2,1)S(1)}, bf16[1,176,2048]{2,1,0:T(8,128)(2,1)}, u32[]{:S(2)}) copy-start(bf16[1,176,2048]{2,1,0:T(8,128)(2,1)} %param.27) | copy-start | bytes 2162692
  117.0 23.4 %all-to-all-start.4 = ((bf16[16,40,1024]{2,1,0:T(8,128)(2,1)}), bf16[16,40,1024]{2,1,0:T(8,128)(2,1)S(1)}, u32[]{:S(2)}, u32[]{:S(2)}) async-start(bf16[16,40,1024]{2,1,0:T(8,128)(2,1)} %bitcast.101), calls=%async_computation.4 | async-start | bytes 2621440 | tf_op jit(solution)/shard_map/all_to_all | solution.py:504
  123.6 14.8 %collective-permute-start.5 = (bf16[176,2048]{1,0:T(8,128)(2,1)S(1)}, bf16[176,2048]{1,0:T(8,128)(2,1)}, u32[]{:S(2)}, u32[]{:S(2)}) collective-permute-start(bf16[176,2048]{1,0:T(8,128)(2,1)S(1)} %bitcast.135), channel_id=1, source_target_pairs={{0,2},{2,0},{4,6},{6,4},{1,3},{3,1},{5,7},{7,5},{8,10},{10,8},{12,... | collective-permute-start | bytes 2162696 | tf_op jit(solution)/shard_map/ppermute | solution.py:507
  140.4 6.9 %copy-start.2 = (bf16[16,40,1024]{2,1,0:T(8,128)(2,1)}, bf16[16,40,1024]{2,1,0:T(8,128)(2,1)S(1)}, u32[]{:S(2)}) copy-start(bf16[16,40,1024]{2,1,0:T(8,128)(2,1)S(1)} %all-to-all-done.4.a_ref) | copy-start | bytes 3932164
  140.4 6.9 %collective-permute-start.6 = (bf16[16,40,1024]{2,1,0:T(8,128)(2,1)S(1)}, bf16[16,40,1024]{2,1,0:T(8,128)(2,1)S(1)}, u32[]{:S(2)}, u32[]{:S(2)}) collective-permute-start(bf16[16,40,1024]{2,1,0:T(8,128)(2,1)S(1)} %all-to-all-done.4.a_ref), channel_id=1, source_target_pairs={{0,1},{1,0},{2,3},{3,2},{4,5},{5,4},{6,7},{7,6},{8,9},{9,8},{10,11... | collective-permute-start | bytes 3932168 | tf_op jit(solution)/shard_map/ppermute | solution.py:152
  160.8 3.2 %collective-permute-start.7 = (bf16[16,40,1024]{2,1,0:T(8,128)(2,1)}, bf16[16,40,1024]{2,1,0:T(8,128)(2,1)S(1)}, u32[]{:S(2)}, u32[]{:S(2)}) collective-permute-start(bf16[16,40,1024]{2,1,0:T(8,128)(2,1)} %get-tuple-element.50), channel_id=1, source_target_pairs={{0,1},{1,0},{2,3},{3,2},{4,5},{5,4},{6,7},{7,6},{8,9},{9,8},{10,11... | collective-permute-start | bytes 3932168 | tf_op jit(solution)/shard_map/ppermute | solution.py:152
  167.0 22.8 %all-to-all-start.5 = ((bf16[16,40,1024]{2,1,0:T(8,128)(2,1)}), bf16[16,40,1024]{2,1,0:T(8,128)(2,1)S(1)}, u32[]{:S(2)}, u32[]{:S(2)}) async-start(bf16[16,40,1024]{2,1,0:T(8,128)(2,1)} %add_convert_fusion), calls=%async_computation.5 | async-start | bytes 2621440 | tf_op jit(solution)/shard_map/all_to_all | solution.py:527
  213.2 19.8 %all-to-all-start.7 = ((bf16[32,16,128]{2,1,0:T(8,128)(2,1)}), bf16[32,16,128]{2,1,0:T(8,128)(2,1)S(1)}, u32[]{:S(2)}, u32[]{:S(2)}) async-start(bf16[32,16,128]{2,1,0:T(8,128)(2,1)} %get-tuple-element.56), calls=%async_computation.7 | async-start | bytes 262144 | tf_op jit(solution)/shard_map/all_to_all | solution.py:537
  236.1 18.4 %all-to-all-start.8 = ((f32[256,1,32]{2,1,0:T(1,128)}), f32[256,1,32]{2,1,0:T(1,128)S(1)}, u32[]{:S(2)}, u32[]{:S(2)}) async-start(f32[256,1,32]{2,1,0:T(1,128)} %bitcast.106), calls=%async_computation.8 | async-start | bytes 262144 | tf_op jit(solution)/shard_map/all_to_all | solution.py:540
  (7 other events, 15.2 us)

commit v9 on v8

--- a/solution.py
+++ b/solution.py
@@ -276,27 +276,26 @@
 
 
 def dispatch_body(chosen_ref, parts_ref, out_ref):
-    both = jnp.concatenate([parts_ref[0, 0], parts_ref[1, 0]], axis=0)
-    out_ref[...] = jnp.dot(chosen_ref[...], both, preferred_element_type=f32).astype(bf16)
+    feat = parts_ref.shape[2]
+    for part in range(4):
+        both = jnp.concatenate([parts_ref[part], parts_ref[4 + part]], axis=0)
+        out_ref[:, part * feat : (part + 1) * feat] = jnp.dot(
+            chosen_ref[...], both, preferred_element_type=f32
+        ).astype(bf16)
 
 
 def dispatch(chosen_t, parts):
-    new, feat = parts.shape[1:]
-    slots, tokens = chosen_t.shape
+    vm = pl.BlockSpec(memory_space=pltpu.VMEM)
     return pl.pallas_call(
         dispatch_body,
-        grid=(4,),
-        out_shape=jax.ShapeDtypeStruct((slots, 4 * feat), bf16),
-        in_specs=[
-            pl.BlockSpec((slots, tokens), lambda i: (0, 0)),
-            pl.BlockSpec((2, 1, new, feat), lambda i: (0, i, 0, 0)),
-        ],
-        out_specs=pl.BlockSpec((slots, feat), lambda i: (0, i)),
+        out_shape=jax.ShapeDtypeStruct((chosen_t.shape[0], 4 * parts.shape[2]), bf16),
+        in_specs=[vm, vm],
+        out_specs=vm,
         name="dispatch",
-    )(chosen_t, parts.reshape(2, 4, new, feat))
-
-
-def combine_body(chosen_ref, back_ref, out_ref):
+    )(chosen_t, parts)
+
+
+def combine_body(chosen_ref, back_ref, out_ref, last_ref):
     feat = out_ref.shape[2]
     new = chosen_ref.shape[0] // 2
     last = []
@@ -306,31 +305,32 @@
         )
         for part in range(4):
             piece = total[:, part * feat : (part + 1) * feat]
-            out_ref[zo * 4 + part, :new, :] = piece.astype(bf16)
+            out_ref[zo * 4 + part] = piece.astype(bf16)
             last.append(piece[new - 1 :, :])
     last = jnp.concatenate(last, axis=0).astype(bf16)
     for dest in range(8):
-        out_ref[dest, new:, :] = last
+        last_ref[dest] = last
 
 
 def combine(chosen, back):
     vm = pl.BlockSpec(memory_space=pltpu.VMEM)
+    feat = back.shape[1] // 4
     return pl.pallas_call(
         combine_body,
-        out_shape=jax.ShapeDtypeStruct((8, chosen.shape[0] // 2 + 8, back.shape[1] // 4), bf16),
+        out_shape=(
+            jax.ShapeDtypeStruct((8, chosen.shape[0] // 2, feat), bf16),
+            jax.ShapeDtypeStruct((8, 8, feat), bf16),
+        ),
         in_specs=[vm, vm],
-        out_specs=vm,
+        out_specs=(vm, vm),
         name="combine",
     )(chosen, back)
 
 
-def finish_body(parts_ref, out_ref, last_ref):
-    new, feat = out_ref.shape
-    total = parts_ref[0].astype(f32)
-    for part in range(1, 8):
-        total = total + parts_ref[part].astype(f32)
-    out_ref[...] = total[:new].astype(bf16)
-    last = total[new:].astype(bf16).astype(f32)
+def finish_body(parts_ref, last_ref):
+    feat = parts_ref.shape[2]
+    total = jnp.sum(parts_ref[...].astype(f32), axis=0)
+    last = total.astype(bf16).astype(f32)
     last = jnp.concatenate([last[:, : feat // 2], last[:, feat // 2 :]], axis=0).astype(bf16)
     last_ref[...] = jnp.broadcast_to(last[None], last_ref.shape)
 
@@ -339,12 +339,9 @@
     vm = pl.BlockSpec(memory_space=pltpu.VMEM)
     return pl.pallas_call(
         finish_body,
-        out_shape=(
-            jax.ShapeDtypeStruct((parts.shape[1] - 8, parts.shape[2]), bf16),
-            jax.ShapeDtypeStruct((copies, 16, 128), bf16),
-        ),
+        out_shape=jax.ShapeDtypeStruct((copies, 16, 128), bf16),
         in_specs=[vm],
-        out_specs=(vm, vm),
+        out_specs=vm,
         name="finish",
     )(parts)
 
@@ -530,9 +527,9 @@
     returned, own_full = barrier((returned, own_full))
     new_cache = new_kv(own_full, gain, w_qkv, rope_tables(lengths[0], new))[:, None]
 
-    packed = combine(chosen_own, returned)
-    summed = lax.all_to_all(packed, Z, 0, 0, tiled=True)
-    out_hidden, last = finish(summed, reqs)
+    shares, last = combine(chosen_own, returned)
+    out_hidden = lax.psum_scatter(shares, Z, scatter_dimension=0)
+    last = finish(lax.all_to_all(last, Z, 0, 0, tiled=True), reqs)
 
     last_all = lax.all_to_all(last, ("core", "x", "y"), 0, 0, tiled=True)
     tops, rms = head(last_all, gain_final, w_head)

time: 256 us -> 257 us (level)
  between operations: 2.96 us -> 16.4 us
  blocking collectives: 53.3 us -> 46.4 us
  starting transfers between devices: 71.3 us -> 67.4 us
    all_to_all x1, blocking collectives: 17.7 us -> 10.8 us  [local(): last = finish(lax.all_to_all(last, Z, 0, 0, tiled=True), reqs)]
    all_to_all x1, starting transfers between devices: 12.2 us -> 8.39 us  [local(): last_all = lax.all_to_all(last, ('core', 'x', 'y'), 0, 0, tiled=True)]
  transfers between devices with their start and end apart: 16 -> 17, of which waited for: 13 -> 13; matrix products, arithmetic and copies ran while one was open for 5% -> 5% of each run, Pallas kernels for 4% -> 5%
where the time goes in v9:
time: 257 us; the launch traced here: 256 us
  waiting for transfers between devices  70.3 us (27%)
  starting transfers between devices  67.4 us (26%)
  blocking collectives  46.4 us (18%)
  Pallas kernels  31 us (12%)
  between operations  16.4 us (6%)
  other arithmetic  13.2 us (5%)
  local copies, waits for them, and re-layouts  10.9 us (4%)
    all_gather x1, blocking collectives, local(): full = lax.all_gather(held, TP, axis=1, tiled=True)  19.3 us
    all_gather x1, blocking collectives, local(): own_full = lax.all_gather(hidden_late, TP, axis=1, tiled=True)  16.3 us
    ppermute x1, waiting for transfers between devices, local(): pair_down = lax.ppermute(down_w, 'zl', neighbours)  14.7 us
    all_to_all x1, starting transfers between devices, local(): leg = lax.all_to_all(chunks, REQ, 0, 0, tiled=True)  14.5 us
    all_to_all x1, waiting for transfers between devices, spread(): return lax.all_to_all(wide, axes, 0, 0, tiled=True)  13.9 us
    pallas_call x1, Pallas kernels, experts(): pl.pallas_call(experts_body, out_shape=(shape, shape), in_specs=[pl.Block...  12.4 us
    all_to_all x1, blocking collectives, local(): last = finish(lax.all_to_all(last, Z, 0, 0, tiled=True), reqs)  10.8 us
    ppermute x2, starting transfers between devices, column_swap(): return lax.ppermute(value, 'zh', [(0, 1), (1, 0)])  9.19 us
  transfers between devices with their start and end apart: 17, of which 13 were waited for; matrix products, arithmetic and copies ran while one was open for 5% of the time, Pallas kernels for 5%

profile of v9, /device:TPU:1, one launch (start us, length us, event | category | flops | bytes accessed | tf_op | source)
XLA Modules:
  0.0 256.3 jit_solution(4213618726867926044)
XLA Ops:
  10.2 14.5 %all-to-all-start = ((bf16[32,8,256]{2,1,0:T(8,128)(2,1)}), bf16[32,8,256]{2,1,0:T(8,128)(2,1)S(1)}, u32[]{:S(2)}, u32[]{:S(2)}) async-start(bf16[32,8,256]{2,1,0:T(8,128)(2,1)} %pad_maximum_fusion), calls=%async_computation | async-start | bytes 262144 | tf_op jit(solution)/shard_map/all_to_all | solution.py:434
  27.1 5.1 %collective-permute-start = (s32[6,128]{1,0:T(8,128)S(1)}, s32[6,128]{1,0:T(8,128)S(1)}, u32[]{:S(2)}, u32[]{:S(2)}) collective-permute-start(s32[6,128]{1,0:T(8,128)S(1)} %bitcast.106), channel_id=1, source_target_pairs={{0,128},{128,0},{1,129},{129,1},{2,130},{130,2},{3,131},{131,3},{4... | collective-permute-start | bytes 9224 | tf_op jit(solution)/shard_map/ppermute | solution.py:156
  37.2 4.5 %all-to-all-start.1 = ((bf16[32,8,256]{2,1,0:T(8,128)(2,1)}), bf16[32,8,256]{2,1,0:T(8,128)(2,1)S(1)}, u32[]{:S(2)}, u32[]{:S(2)}) async-start(bf16[32,8,256]{2,1,0:T(8,128)(2,1)} %gather_fusion), calls=%async_computation.1 | async-start | bytes 262144 | tf_op jit(solution)/shard_map/all_to_all | solution.py:445
  47.2 6.9 %all-to-all-done.1 = bf16[32,8,256]{2,1,0:T(8,128)(2,1)S(1)} async-done(((bf16[32,8,256]{2,1,0:T(8,128)(2,1)}), bf16[32,8,256]{2,1,0:T(8,128)(2,1)S(1)}, u32[]{:S(2)}, u32[]{:S(2)}) %all-to-all-start.1) | async-done | bytes 131104 | tf_op jit(solution)/shard_map/all_to_all | solution.py:445
  56.6 19.3 %all_gather.6.full_ref = bf16[128,2048]{1,0:T(8,128)(2,1)} all-gather(bf16[128,256]{1,0:T(8,128)(2,1)S(1)} %reshape.381), channel_id=1, replica_groups=mesh['zh'=2,'x'=4,'y'=4,'zl'=4,'core'=2] {'zl','core'}, dimensions={1}, use_global_device_ids=true | all-gather | bytes 589824 | tf_op jit(solution)/shard_map/all_gather | solution.py:453
  76.0 5.8 %attend.1 = (bf16[4,128,256]{2,1,0:T(8,128)(2,1)}, bf16[4,128,256]{2,1,0:T(8,128)(2,1)}) custom-call(s32[1]{0:T(128)} %bitcast.26.len_ref, s32[34]{0:T(128)} %pad_add_fusion.place_ref, bf16[128,2048]{1,0:T(8,128)(2,1)} %all_gather.6.full_ref, bf16[1,2048]{1,0:T(2,128)(2,1)} %broadcast_in_dim.61.gain_ref, bf16[3,2048,256]{2,1,0:T(8,128)(2,1)} %w_ref.4, ...), custom_call_target="tpu_custom_call" | custom-call | tf_op jit(solution)/shard_map/attend/pallas_call | solution.py:137
  85.3 3.4 %all-to-all-start.2 = ((bf16[4,128,256]{2,1,0:T(8,128)(2,1)}), bf16[4,128,256]{2,1,0:T(8,128)(2,1)S(1)}, u32[]{:S(2)}, u32[]{:S(2)}) async-start(bf16[4,128,256]{2,1,0:T(8,128)(2,1)} %add_convert_fusion.1), calls=%async_computation.2 | async-start | bytes 524288 | tf_op jit(solution)/shard_map/all_to_all | solution.py:467
  89.1 4.0 %collective-permute-start.4 = (s32[6,128]{1,0:T(8,128)S(1)}, s32[6,128]{1,0:T(8,128)S(1)}, u32[]{:S(2)}, u32[]{:S(2)}) collective-permute-start(s32[6,128]{1,0:T(8,128)S(1)} %reshape.386), channel_id=1, source_target_pairs={{0,128},{128,0},{1,129},{129,1},{2,130},{130,2},{3,131},{131,3},{4... | collective-permute-start | bytes 9224 | tf_op jit(solution)/shard_map/ppermute | solution.py:156
  93.2 4.7 %collective-permute-done.4 = s32[6,128]{1,0:T(8,128)S(1)} collective-permute-done((s32[6,128]{1,0:T(8,128)S(1)}, s32[6,128]{1,0:T(8,128)S(1)}, u32[]{:S(2)}, u32[]{:S(2)}) %collective-permute-start.4) | collective-permute-done | bytes 3104 | tf_op jit(solution)/shard_map/ppermute | solution.py:156
  98.8 4.2 %all-to-all-start.3 = ((bf16[8,128,256]{2,1,0:T(8,128)(2,1)}), bf16[8,128,256]{2,1,0:T(8,128)(2,1)S(1)}, u32[]{:S(2)}, u32[]{:S(2)}) async-start(bf16[8,128,256]{2,1,0:T(8,128)(2,1)} %broadcast_in_dim.64), calls=%async_computation.3 | async-start | bytes 1048576 | tf_op jit(solution)/shard_map/all_to_all | solution.py:148
  104.8 13.9 %all-to-all-done.3.parts_ref = bf16[8,128,256]{2,1,0:T(8,128)(2,1)S(1)} async-done(((bf16[8,128,256]{2,1,0:T(8,128)(2,1)}), bf16[8,128,256]{2,1,0:T(8,128)(2,1)S(1)}, u32[]{:S(2)}, u32[]{:S(2)}) %all-to-all-start.3) | async-done | bytes 524320 | tf_op jit(solution)/shard_map/all_to_all | solution.py:148
  122.3 6.6 %all-to-all-start.4 = ((bf16[16,40,1024]{2,1,0:T(8,128)(2,1)}), bf16[16,40,1024]{2,1,0:T(8,128)(2,1)S(1)}, u32[]{:S(2)}, u32[]{:S(2)}) async-start(bf16[16,40,1024]{2,1,0:T(8,128)(2,1)} %bitcast.101), calls=%async_computation.4 | async-start | bytes 2621440 | tf_op jit(solution)/shard_map/all_to_all | solution.py:501
  129.0 14.7 %collective-permute-done.5.pd_ref = bf16[176,2048]{1,0:T(8,128)(2,1)} collective-permute-done((bf16[176,2048]{1,0:T(8,128)(2,1)S(1)}, bf16[176,2048]{1,0:T(8,128)(2,1)}, u32[]{:S(2)}, u32[]{:S(2)}) %collective-permute-start.5) | collective-permute-done | bytes 720928 | tf_op jit(solution)/shard_map/ppermute | solution.py:504
  145.7 4.2 %collective-permute-start.6 = (bf16[16,40,1024]{2,1,0:T(8,128)(2,1)S(1)}, bf16[16,40,1024]{2,1,0:T(8,128)(2,1)S(1)}, u32[]{:S(2)}, u32[]{:S(2)}) collective-permute-start(bf16[16,40,1024]{2,1,0:T(8,128)(2,1)S(1)} %all-to-all-done.4.a_ref), channel_id=1, source_target_pairs={{0,1},{1,0},{2,3},{3,2},{4,5},{5,4},{6,7},{7,6},{8,9},{9,8},{10,11... | collective-permute-start | bytes 3932168 | tf_op jit(solution)/shard_map/ppermute | solution.py:152
  153.7 12.4 %experts.1 = (bf16[16,40,1024]{2,1,0:T(8,128)(2,1)}, bf16[16,40,1024]{2,1,0:T(8,128)(2,1)}) custom-call(s32[34]{0:T(128)} %pad_add_fusion.place_ref, bf16[16,40,1024]{2,1,0:T(8,128)(2,1)} %copy-done.2, bf16[16,40,1024]{2,1,0:T(8,128)(2,1)} %copy-done.10, bf16[1,2048]{1,0:T(2,128)(2,1)} %broadcast_in_dim.62.gain_ref, bf16[32,2048]{1,0:T(8,128)(2,1)} %bitcast.135, ...), custom_call_target="tpu_custom_call" | custom-call | flops 2768240640 | bytes 11730944 | tf_op jit(solution)/shard_map/experts/pallas_call | solution.py:259
  169.3 2.9 %add_convert_fusion = bf16[16,40,1024]{2,1,0:T(8,128)(2,1)} fusion(bf16[16,40,1024]{2,1,0:T(8,128)(2,1)S(1)} %collective-permute-done.7, bf16[16,40,1024]{2,1,0:T(8,128)(2,1)} %get-tuple-element.49), kind=kLoop, calls=%fused_computation.1 | loop fusion | flops 2621440 | bytes 3932160 | tf_op jit(solution)/shard_map/convert_element_type | solution.py:522
  172.3 4.5 %all-to-all-start.5 = ((bf16[16,40,1024]{2,1,0:T(8,128)(2,1)}), bf16[16,40,1024]{2,1,0:T(8,128)(2,1)S(1)}, u32[]{:S(2)}, u32[]{:S(2)}) async-start(bf16[16,40,1024]{2,1,0:T(8,128)(2,1)} %add_convert_fusion), calls=%async_computation.5 | async-start | bytes 2621440 | tf_op jit(solution)/shard_map/all_to_all | solution.py:524
  178.1 16.3 %all_gather.7.full_ref = bf16[128,2048]{1,0:T(8,128)(2,1)} all-gather(bf16[128,256]{1,0:T(8,128)(2,1)S(1)} %copy-done.4), channel_id=1, replica_groups=mesh['zh'=2,'x'=4,'y'=4,'zl'=4,'core'=2] {'zl','core'}, dimensions={1}, use_global_device_ids=true | all-gather | bytes 589824 | tf_op jit(solution)/shard_map/all_gather | solution.py:526
  199.0 10.8 %all_to_all.49.parts_ref = bf16[8,8,256]{2,1,0:T(8,128)(2,1)} all-to-all(bf16[8,8,256]{2,1,0:T(8,128)(2,1)} %get-tuple-element.56), channel_id=1, replica_groups=mesh['zh'=2,'x'=4,'y'=4,'zl'=4,'core'=2] {'zh','zl'}, dimensions={0} | all-to-all | bytes 65536 | tf_op jit(solution)/shard_map/all_to_all | solution.py:532
  211.2 8.4 %all-to-all-start.7 = ((bf16[32,16,128]{2,1,0:T(8,128)(2,1)}), bf16[32,16,128]{2,1,0:T(8,128)(2,1)S(1)}, u32[]{:S(2)}, u32[]{:S(2)}) async-start(bf16[32,16,128]{2,1,0:T(8,128)(2,1)} %finish.1), calls=%async_computation.8 | async-start | bytes 262144 | tf_op jit(solution)/shard_map/all_to_all | solution.py:534
  219.6 7.5 %all-to-all-done.7.last_ref = bf16[32,16,128]{2,1,0:T(8,128)(2,1)S(1)} async-done(((bf16[32,16,128]{2,1,0:T(8,128)(2,1)}), bf16[32,16,128]{2,1,0:T(8,128)(2,1)S(1)}, u32[]{:S(2)}, u32[]{:S(2)}) %all-to-all-start.7) | async-done | bytes 131104 | tf_op jit(solution)/shard_map/all_to_all | solution.py:534
  230.3 5.5 %all-to-all-start.8 = ((f32[256,1,32]{2,1,0:T(1,128)}), f32[256,1,32]{2,1,0:T(1,128)S(1)}, u32[]{:S(2)}, u32[]{:S(2)}) async-start(f32[256,1,32]{2,1,0:T(1,128)} %bitcast.105), calls=%async_computation.9 | async-start | bytes 262144 | tf_op jit(solution)/shard_map/all_to_all | solution.py:537
  236.4 3.4 %new_kv.1 = bf16[2,128,256]{2,1,0:T(8,128)(2,1)} custom-call(bf16[128,2048]{1,0:T(8,128)(2,1)} %all_gather.7.full_ref, bf16[1,2048]{1,0:T(2,128)(2,1)} %broadcast_in_dim.61.gain_ref, bf16[3,2048,256]{2,1,0:T(8,128)(2,1)} %w_ref.4, f32[128,64]{1,0:T(8,128)} %get-tuple-element.93.cos_ref.refs_0_, f32[128,64]{1,0:T(8,128)} %get-tuple-element.92.sin_ref.refs_1_, ...), custom_call_target="tpu_custom_call" | custom-call | tf_op jit(solution)/shard_map/new_kv/pallas_call | solution.py:67
  240.5 8.2 %all-to-all-done.8 = f32[256,1,32]{2,1,0:T(1,128)S(1)} async-done(((f32[256,1,32]{2,1,0:T(1,128)}), f32[256,1,32]{2,1,0:T(1,128)S(1)}, u32[]{:S(2)}, u32[]{:S(2)}) %all-to-all-start.8) | async-done | bytes 32800 | tf_op jit(solution)/shard_map/all_to_all | solution.py:537
  (112 shorter events, 48.0 us)
Async XLA Ops:
  10.2 25.8 %all-to-all-start = ((bf16[32,8,256]{2,1,0:T(8,128)(2,1)}), bf16[32,8,256]{2,1,0:T(8,128)(2,1)S(1)}, u32[]{:S(2)}, u32[]{:S(2)}) async-start(bf16[32,8,256]{2,1,0:T(8,128)(2,1)} %pad_maximum_fusion), calls=%async_computation | async-start | bytes 262144 | tf_op jit(solution)/shard_map/all_to_all | solution.py:434
  24.7 7.5 %copy-start.14 = (s32[32]{0:T(128)S(1)}, s32[32]{0:T(128)}, u32[]{:S(2)}) copy-start(s32[32]{0:T(128)} %param.21) | copy-start | bytes 388
  24.8 18.4 %copy-start.7 = (bf16[2048]{0:T(1024)(128)(2,1)S(1)}, bf16[2048]{0:T(1024)(128)(2,1)}, u32[]{:S(2)}) copy-start(bf16[2048]{0:T(1024)(128)(2,1)} %param.17) | copy-start | bytes 12292
  24.8 19.0 %copy-start.8 = (bf16[2048]{0:T(1024)(128)(2,1)S(1)}, bf16[2048]{0:T(1024)(128)(2,1)}, u32[]{:S(2)}) copy-start(bf16[2048]{0:T(1024)(128)(2,1)} %param.23) | copy-start | bytes 12292
  24.8 19.6 %copy-start.9 = (bf16[2048]{0:T(1024)(128)(2,1)S(1)}, bf16[2048]{0:T(1024)(128)(2,1)}, u32[]{:S(2)}) copy-start(bf16[2048]{0:T(1024)(128)(2,1)} %param.30) | copy-start | bytes 12292
  26.2 27.9 %collective-permute-start.1 = (bf16[176,2048]{1,0:T(8,128)(2,1)S(1)}, bf16[176,2048]{1,0:T(8,128)(2,1)S(1)}, u32[]{:S(2)}, u32[]{:S(2)}) collective-permute-start(bf16[176,2048]{1,0:T(8,128)(2,1)S(1)} %get-tuple-element.76), channel_id=1, source_target_pairs={{0,2},{2,0},{4,6},{6,4},{1,3},{3,1},{5,7},{7,5},{8,10},{10,8},{12,... | collective-permute-start | bytes 2162696 | tf_op jit(solution)/shard_map/ppermute | solution.py:433
  27.1 20.2 %collective-permute-start = (s32[6,128]{1,0:T(8,128)S(1)}, s32[6,128]{1,0:T(8,128)S(1)}, u32[]{:S(2)}, u32[]{:S(2)}) collective-permute-start(s32[6,128]{1,0:T(8,128)S(1)} %bitcast.106), channel_id=1, source_target_pairs={{0,128},{128,0},{1,129},{129,1},{2,130},{130,2},{3,131},{131,3},{4... | collective-permute-start | bytes 9224 | tf_op jit(solution)/shard_map/ppermute | solution.py:156
  37.2 16.8 %all-to-all-start.1 = ((bf16[32,8,256]{2,1,0:T(8,128)(2,1)}), bf16[32,8,256]{2,1,0:T(8,128)(2,1)S(1)}, u32[]{:S(2)}, u32[]{:S(2)}) async-start(bf16[32,8,256]{2,1,0:T(8,128)(2,1)} %gather_fusion), calls=%async_computation.1 | async-start | bytes 262144 | tf_op jit(solution)/shard_map/all_to_all | solution.py:445
  41.8 40.0 %collective-permute-start.2 = (bf16[176,2048]{1,0:T(8,128)(2,1)S(1)}, bf16[176,2048]{1,0:T(8,128)(2,1)S(1)}, u32[]{:S(2)}, u32[]{:S(2)}) collective-permute-start(bf16[176,2048]{1,0:T(8,128)(2,1)S(1)} %get-tuple-element.38), channel_id=1, source_target_pairs={{0,2},{2,0},{4,6},{6,4},{1,3},{3,1},{5,7},{7,5},{8,10},{10,8},{12,... | collective-permute-start | bytes 2162696 | tf_op jit(solution)/shard_map/ppermute | solution.py:444
  54.1 27.7 %copy-start.12 = (bf16[176,2048]{1,0:T(8,128)(2,1)}, bf16[176,2048]{1,0:T(8,128)(2,1)S(1)}, u32[]{:S(2)}) copy-start(bf16[176,2048]{1,0:T(8,128)(2,1)S(1)} %collective-permute-done.1.pg_ref) | copy-start | bytes 2162692
  81.8 16.2 %copy-start.13 = (bf16[176,2048]{1,0:T(8,128)(2,1)}, bf16[176,2048]{1,0:T(8,128)(2,1)S(1)}, u32[]{:S(2)}) copy-start(bf16[176,2048]{1,0:T(8,128)(2,1)S(1)} %collective-permute-done.2.pu_ref) | copy-start | bytes 2162692
  81.8 1.8 collective-permute-start.3
  85.3 12.6 %all-to-all-start.2 = ((bf16[4,128,256]{2,1,0:T(8,128)(2,1)}), bf16[4,128,256]{2,1,0:T(8,128)(2,1)S(1)}, u32[]{:S(2)}, u32[]{:S(2)}) async-start(bf16[4,128,256]{2,1,0:T(8,128)(2,1)} %add_convert_fusion.1), calls=%async_computation.2 | async-start | bytes 524288 | tf_op jit(solution)/shard_map/all_to_all | solution.py:467
  89.1 8.8 %collective-permute-start.4 = (s32[6,128]{1,0:T(8,128)S(1)}, s32[6,128]{1,0:T(8,128)S(1)}, u32[]{:S(2)}, u32[]{:S(2)}) collective-permute-start(s32[6,128]{1,0:T(8,128)S(1)} %reshape.386), channel_id=1, source_target_pairs={{0,128},{128,0},{1,129},{129,1},{2,130},{130,2},{3,131},{131,3},{4... | collective-permute-start | bytes 9224 | tf_op jit(solution)/shard_map/ppermute | solution.py:156
  98.8 20.0 %all-to-all-start.3 = ((bf16[8,128,256]{2,1,0:T(8,128)(2,1)}), bf16[8,128,256]{2,1,0:T(8,128)(2,1)S(1)}, u32[]{:S(2)}, u32[]{:S(2)}) async-start(bf16[8,128,256]{2,1,0:T(8,128)(2,1)} %broadcast_in_dim.64), calls=%async_computation.3 | async-start | bytes 1048576 | tf_op jit(solution)/shard_map/all_to_all | solution.py:148
  122.3 23.4 %all-to-all-start.4 = ((bf16[16,40,1024]{2,1,0:T(8,128)(2,1)}), bf16[16,40,1024]{2,1,0:T(8,128)(2,1)S(1)}, u32[]{:S(2)}, u32[]{:S(2)}) async-start(bf16[16,40,1024]{2,1,0:T(8,128)(2,1)} %bitcast.101), calls=%async_computation.4 | async-start | bytes 2621440 | tf_op jit(solution)/shard_map/all_to_all | solution.py:501
  128.9 14.8 %collective-permute-start.5 = (bf16[176,2048]{1,0:T(8,128)(2,1)S(1)}, bf16[176,2048]{1,0:T(8,128)(2,1)}, u32[]{:S(2)}, u32[]{:S(2)}) collective-permute-start(bf16[176,2048]{1,0:T(8,128)(2,1)S(1)} %bitcast.134), channel_id=1, source_target_pairs={{0,2},{2,0},{4,6},{6,4},{1,3},{3,1},{5,7},{7,5},{8,10},{10,8},{12,... | collective-permute-start | bytes 2162696 | tf_op jit(solution)/shard_map/ppermute | solution.py:504
  145.7 6.9 %copy-start.2 = (bf16[16,40,1024]{2,1,0:T(8,128)(2,1)}, bf16[16,40,1024]{2,1,0:T(8,128)(2,1)S(1)}, u32[]{:S(2)}) copy-start(bf16[16,40,1024]{2,1,0:T(8,128)(2,1)S(1)} %all-to-all-done.4.a_ref) | copy-start | bytes 3932164
  145.7 6.9 %collective-permute-start.6 = (bf16[16,40,1024]{2,1,0:T(8,128)(2,1)S(1)}, bf16[16,40,1024]{2,1,0:T(8,128)(2,1)S(1)}, u32[]{:S(2)}, u32[]{:S(2)}) collective-permute-start(bf16[16,40,1024]{2,1,0:T(8,128)(2,1)S(1)} %all-to-all-done.4.a_ref), channel_id=1, source_target_pairs={{0,1},{1,0},{2,3},{3,2},{4,5},{5,4},{6,7},{7,6},{8,9},{9,8},{10,11... | collective-permute-start | bytes 3932168 | tf_op jit(solution)/shard_map/ppermute | solution.py:152
  166.1 3.2 %collective-permute-start.7 = (bf16[16,40,1024]{2,1,0:T(8,128)(2,1)}, bf16[16,40,1024]{2,1,0:T(8,128)(2,1)S(1)}, u32[]{:S(2)}, u32[]{:S(2)}) collective-permute-start(bf16[16,40,1024]{2,1,0:T(8,128)(2,1)} %get-tuple-element.50), channel_id=1, source_target_pairs={{0,1},{1,0},{2,3},{3,2},{4,5},{5,4},{6,7},{7,6},{8,9},{9,8},{10,11... | collective-permute-start | bytes 3932168 | tf_op jit(solution)/shard_map/ppermute | solution.py:152
  172.3 22.8 %all-to-all-start.5 = ((bf16[16,40,1024]{2,1,0:T(8,128)(2,1)}), bf16[16,40,1024]{2,1,0:T(8,128)(2,1)S(1)}, u32[]{:S(2)}, u32[]{:S(2)}) async-start(bf16[16,40,1024]{2,1,0:T(8,128)(2,1)} %add_convert_fusion), calls=%async_computation.5 | async-start | bytes 2621440 | tf_op jit(solution)/shard_map/all_to_all | solution.py:524
  176.8 72.7 %reduce-scatter.2.cloned.1.call-start = ((), (), s32[]{:S(2)}) async-start(), calls=%async_computation.10 | async-start | bytes 589824 | tf_op jit(solution)/shard_map/reduce_scatter | solution.py:531
  211.2 15.9 %all-to-all-start.7 = ((bf16[32,16,128]{2,1,0:T(8,128)(2,1)}), bf16[32,16,128]{2,1,0:T(8,128)(2,1)S(1)}, u32[]{:S(2)}, u32[]{:S(2)}) async-start(bf16[32,16,128]{2,1,0:T(8,128)(2,1)} %finish.1), calls=%async_computation.8 | async-start | bytes 262144 | tf_op jit(solution)/shard_map/all_to_all | solution.py:534
  230.3 18.4 %all-to-all-start.8 = ((f32[256,1,32]{2,1,0:T(1,128)}), f32[256,1,32]{2,1,0:T(1,128)S(1)}, u32[]{:S(2)}, u32[]{:S(2)}) async-start(f32[256,1,32]{2,1,0:T(1,128)} %bitcast.105), calls=%async_computation.9 | async-start | bytes 262144 | tf_op jit(solution)/shard_map/all_to_all | solution.py:537
  (8 other events, 21.8 us)
Sparse Core Ops, SparseCore 0:
  199.1 29.6 reduce-scatter.1

commit v10 on v9

--- a/solution.py
+++ b/solution.py
@@ -295,36 +295,47 @@
     )(chosen_t, parts)
 
 
-def combine_body(chosen_ref, back_ref, out_ref, last_ref):
-    feat = out_ref.shape[2]
+def combine_body(place_ref, chosen_ref, back_ref, keep_ref, send_ref, last_ref):
+    zh = place_ref[0]
+    zl = place_ref[1]
+    feat = keep_ref.shape[2]
     new = chosen_ref.shape[0] // 2
     last = []
     for zo in range(2):
         total = jnp.dot(
             chosen_ref[zo * new : (zo + 1) * new, :], back_ref[...], preferred_element_type=f32
         )
-        for part in range(4):
-            piece = total[:, part * feat : (part + 1) * feat]
-            out_ref[zo * 4 + part] = piece.astype(bf16)
-            last.append(piece[new - 1 :, :])
+        pieces = [total[:, part * feat : (part + 1) * feat] for part in range(4)]
+        last += [piece[new - 1 :, :] for piece in pieces]
+
+        def store(ref, pieces=pieces):
+            for part in range(4):
+                ref[jnp.bitwise_xor(zl, part)] = pieces[part].astype(bf16)
+
+        @pl.when(zh == zo)
+        def _(store=store):
+            store(keep_ref)
+
+        @pl.when(zh != zo)
+        def _(store=store):
+            store(send_ref)
+
     last = jnp.concatenate(last, axis=0).astype(bf16)
     for dest in range(8):
         last_ref[dest] = last
 
 
-def combine(chosen, back):
+def combine(place, chosen, back):
     vm = pl.BlockSpec(memory_space=pltpu.VMEM)
     feat = back.shape[1] // 4
+    shape = jax.ShapeDtypeStruct((4, chosen.shape[0] // 2, feat), bf16)
     return pl.pallas_call(
         combine_body,
-        out_shape=(
-            jax.ShapeDtypeStruct((8, chosen.shape[0] // 2, feat), bf16),
-            jax.ShapeDtypeStruct((8, 8, feat), bf16),
-        ),
-        in_specs=[vm, vm],
-        out_specs=(vm, vm),
+        out_shape=(shape, shape, jax.ShapeDtypeStruct((8, 8, feat), bf16)),
+        in_specs=[pl.BlockSpec(memory_space=pltpu.SMEM), vm, vm],
+        out_specs=(vm, vm, vm),
         name="combine",
-    )(chosen, back)
+    )(place, chosen, back)
 
 
 def finish_body(parts_ref, last_ref):
@@ -527,9 +538,15 @@
     returned, own_full = barrier((returned, own_full))
     new_cache = new_kv(own_full, gain, w_qkv, rope_tables(lengths[0], new))[:, None]
 
-    shares, last = combine(chosen_own, returned)
-    out_hidden = lax.psum_scatter(shares, Z, scatter_dimension=0)
+    keep, send, last = combine(jnp.stack([zh, zl]).astype(jnp.int32), chosen_own, returned)
     last = finish(lax.all_to_all(last, Z, 0, 0, tiled=True), reqs)
+
+    def add(mine, theirs):
+        return (mine.astype(f32) + theirs.astype(f32)).astype(bf16)
+
+    keep = add(keep, column_swap(send))
+    keep = add(keep[:2], lax.ppermute(keep[2:], "zl", [(0, 2), (1, 3), (2, 0), (3, 1)]))
+    out_hidden = add(keep[0], lax.ppermute(keep[1], "zl", neighbours))
 
     last_all = lax.all_to_all(last, ("core", "x", "y"), 0, 0, tiled=True)
     tops, rms = head(last_all, gain_final, w_head)

time: 257 us -> 254 us (0.988)
  starting transfers between devices: 67.4 us -> 84.9 us
  between operations: 16.4 us -> 2.97 us
  blocking collectives: 46.4 us -> 35.6 us
    all_to_all x1 -> x0, blocking collectives: 10.8 us -> none  [local(): last = finish(lax.all_to_all(last, Z, 0, 0, tiled=True), reqs)]
    ppermute x0 -> x2, starting transfers between devices: none -> 5.95 us  [the longest x1 4.36 us: local(): lax.ppermute(keep[2:], 'zl', [(0, 2), (1, 3), (2, 0), (3, 1)])]
    all_to_all x0 -> x1, starting transfers between devices: none -> 5.68 us  [local(): last = finish(lax.all_to_all(last, Z, 0, 0, tiled=True), reqs)]
    all_to_all x1, starting transfers between devices: 8.39 us -> 12.5 us  [local(): last_all = lax.all_to_all(last, ('core', 'x', 'y'), 0, 0, tiled=True)]
    ppermute x2 -> x3, waiting for transfers between devices: 6.92 us -> 9.73 us  [column_swap(): return lax.ppermute(value, 'zh', [(0, 1), (1, 0)])]
    ppermute x2 -> x3, starting transfers between devices: 9.19 us -> 10.2 us  [column_swap(): return lax.ppermute(value, 'zh', [(0, 1), (1, 0)])]
  transfers between devices with their start and end apart: 17 -> 20, of which waited for: 13 -> 13; matrix products, arithmetic and copies ran while one was open for 5% -> 6% of each run, Pallas kernels for 5% -> 5%
where the time goes in v10:
time: 254 us; the launch traced here: 253 us
  starting transfers between devices  84.9 us (33%)
  waiting for transfers between devices  70.7 us (28%)
  blocking collectives  35.6 us (14%)
  Pallas kernels  31.2 us (12%)
  other arithmetic  15.6 us (6%)
  local copies, waits for them, and re-layouts  11.5 us (5%)
  between operations  2.97 us (1%)
    all_gather x1, blocking collectives, local(): full = lax.all_gather(held, TP, axis=1, tiled=True)  19.3 us
    all_gather x1, blocking collectives, local(): own_full = lax.all_gather(hidden_late, TP, axis=1, tiled=True)  16.3 us
    ppermute x1, waiting for transfers between devices, local(): pair_down = lax.ppermute(down_w, 'zl', neighbours)  14.7 us
    all_to_all x1, starting transfers between devices, local(): leg = lax.all_to_all(chunks, REQ, 0, 0, tiled=True)  14.5 us
    all_to_all x1, waiting for transfers between devices, spread(): return lax.all_to_all(wide, axes, 0, 0, tiled=True)  13.9 us
    all_to_all x1, starting transfers between devices, local(): last_all = lax.all_to_all(last, ('core', 'x', 'y'), 0, 0, tiled=True)  12.5 us
    pallas_call x1, Pallas kernels, experts(): pl.pallas_call(experts_body, out_shape=(shape, shape), in_specs=[pl.Block...  12.4 us
    ppermute x3, starting transfers between devices, column_swap(): return lax.ppermute(value, 'zh', [(0, 1), (1, 0)])  10.2 us
  transfers between devices with their start and end apart: 20, of which 13 were waited for; matrix products, arithmetic and copies ran while one was open for 6% of the time, Pallas kernels for 5%

profile of v10, /device:TPU:1, one launch (start us, length us, event | category | flops | bytes accessed | tf_op | source)
XLA Modules:
  0.0 253.2 jit_solution(8119816806332393102)
XLA Ops:
  3.7 14.5 %all-to-all-start = ((bf16[32,8,256]{2,1,0:T(8,128)(2,1)}), bf16[32,8,256]{2,1,0:T(8,128)(2,1)S(1)}, u32[]{:S(2)}, u32[]{:S(2)}) async-start(bf16[32,8,256]{2,1,0:T(8,128)(2,1)} %pad_maximum_fusion), calls=%async_computation | async-start | bytes 262144 | tf_op jit(solution)/shard_map/all_to_all | solution.py:445
  20.5 5.1 %collective-permute-start = (s32[6,128]{1,0:T(8,128)S(1)}, s32[6,128]{1,0:T(8,128)S(1)}, u32[]{:S(2)}, u32[]{:S(2)}) collective-permute-start(s32[6,128]{1,0:T(8,128)S(1)} %bitcast.114), channel_id=1, source_target_pairs={{0,128},{128,0},{1,129},{129,1},{2,130},{130,2},{3,131},{131,3},{4... | collective-permute-start | bytes 9224 | tf_op jit(solution)/shard_map/ppermute | solution.py:156
  30.7 4.5 %all-to-all-start.1 = ((bf16[32,8,256]{2,1,0:T(8,128)(2,1)}), bf16[32,8,256]{2,1,0:T(8,128)(2,1)S(1)}, u32[]{:S(2)}, u32[]{:S(2)}) async-start(bf16[32,8,256]{2,1,0:T(8,128)(2,1)} %gather_fusion), calls=%async_computation.1 | async-start | bytes 262144 | tf_op jit(solution)/shard_map/all_to_all | solution.py:456
  40.7 6.8 %all-to-all-done.1 = bf16[32,8,256]{2,1,0:T(8,128)(2,1)S(1)} async-done(((bf16[32,8,256]{2,1,0:T(8,128)(2,1)}), bf16[32,8,256]{2,1,0:T(8,128)(2,1)S(1)}, u32[]{:S(2)}, u32[]{:S(2)}) %all-to-all-start.1) | async-done | bytes 131104 | tf_op jit(solution)/shard_map/all_to_all | solution.py:456
  50.1 19.3 %all_gather.6.full_ref = bf16[128,2048]{1,0:T(8,128)(2,1)} all-gather(bf16[128,256]{1,0:T(8,128)(2,1)S(1)} %reshape.383), channel_id=1, replica_groups=mesh['zh'=2,'x'=4,'y'=4,'zl'=4,'core'=2] {'zl','core'}, dimensions={1}, use_global_device_ids=true | all-gather | bytes 589824 | tf_op jit(solution)/shard_map/all_gather | solution.py:464
  69.4 5.8 %attend.1 = (bf16[4,128,256]{2,1,0:T(8,128)(2,1)}, bf16[4,128,256]{2,1,0:T(8,128)(2,1)}) custom-call(s32[1]{0:T(128)} %bitcast.28.len_ref, s32[34]{0:T(128)} %pad_add_fusion.1.place_ref, bf16[128,2048]{1,0:T(8,128)(2,1)} %all_gather.6.full_ref, bf16[1,2048]{1,0:T(2,128)(2,1)} %broadcast_in_dim.61.gain_ref, bf16[3,2048,256]{2,1,0:T(8,128)(2,1)} %w_ref.4, ...), custom_call_target="tpu_custom_call" | custom-call | tf_op jit(solution)/shard_map/attend/pallas_call | solution.py:137
  78.8 3.4 %all-to-all-start.2 = ((bf16[4,128,256]{2,1,0:T(8,128)(2,1)}), bf16[4,128,256]{2,1,0:T(8,128)(2,1)S(1)}, u32[]{:S(2)}, u32[]{:S(2)}) async-start(bf16[4,128,256]{2,1,0:T(8,128)(2,1)} %add_convert_fusion.2), calls=%async_computation.2 | async-start | bytes 524288 | tf_op jit(solution)/shard_map/all_to_all | solution.py:478
  82.6 4.0 %collective-permute-start.4 = (s32[6,128]{1,0:T(8,128)S(1)}, s32[6,128]{1,0:T(8,128)S(1)}, u32[]{:S(2)}, u32[]{:S(2)}) collective-permute-start(s32[6,128]{1,0:T(8,128)S(1)} %reshape.388), channel_id=1, source_target_pairs={{0,128},{128,0},{1,129},{129,1},{2,130},{130,2},{3,131},{131,3},{4... | collective-permute-start | bytes 9224 | tf_op jit(solution)/shard_map/ppermute | solution.py:156
  86.7 4.7 %collective-permute-done.4 = s32[6,128]{1,0:T(8,128)S(1)} collective-permute-done((s32[6,128]{1,0:T(8,128)S(1)}, s32[6,128]{1,0:T(8,128)S(1)}, u32[]{:S(2)}, u32[]{:S(2)}) %collective-permute-start.4) | collective-permute-done | bytes 3104 | tf_op jit(solution)/shard_map/ppermute | solution.py:156
  92.3 4.2 %all-to-all-start.3 = ((bf16[8,128,256]{2,1,0:T(8,128)(2,1)}), bf16[8,128,256]{2,1,0:T(8,128)(2,1)S(1)}, u32[]{:S(2)}, u32[]{:S(2)}) async-start(bf16[8,128,256]{2,1,0:T(8,128)(2,1)} %broadcast_in_dim.64), calls=%async_computation.3 | async-start | bytes 1048576 | tf_op jit(solution)/shard_map/all_to_all | solution.py:148
  98.3 13.9 %all-to-all-done.3.parts_ref = bf16[8,128,256]{2,1,0:T(8,128)(2,1)S(1)} async-done(((bf16[8,128,256]{2,1,0:T(8,128)(2,1)}), bf16[8,128,256]{2,1,0:T(8,128)(2,1)S(1)}, u32[]{:S(2)}, u32[]{:S(2)}) %all-to-all-start.3) | async-done | bytes 524320 | tf_op jit(solution)/shard_map/all_to_all | solution.py:148
  115.8 6.5 %all-to-all-start.4 = ((bf16[16,40,1024]{2,1,0:T(8,128)(2,1)}), bf16[16,40,1024]{2,1,0:T(8,128)(2,1)S(1)}, u32[]{:S(2)}, u32[]{:S(2)}) async-start(bf16[16,40,1024]{2,1,0:T(8,128)(2,1)} %bitcast.109), calls=%async_computation.4 | async-start | bytes 2621440 | tf_op jit(solution)/shard_map/all_to_all | solution.py:512
  122.5 14.7 %collective-permute-done.5.pd_ref = bf16[176,2048]{1,0:T(8,128)(2,1)} collective-permute-done((bf16[176,2048]{1,0:T(8,128)(2,1)S(1)}, bf16[176,2048]{1,0:T(8,128)(2,1)}, u32[]{:S(2)}, u32[]{:S(2)}) %collective-permute-start.5) | collective-permute-done | bytes 720928 | tf_op jit(solution)/shard_map/ppermute | solution.py:515
  139.2 4.2 %collective-permute-start.6 = (bf16[16,40,1024]{2,1,0:T(8,128)(2,1)S(1)}, bf16[16,40,1024]{2,1,0:T(8,128)(2,1)S(1)}, u32[]{:S(2)}, u32[]{:S(2)}) collective-permute-start(bf16[16,40,1024]{2,1,0:T(8,128)(2,1)S(1)} %all-to-all-done.4.a_ref), channel_id=1, source_target_pairs={{0,1},{1,0},{2,3},{3,2},{4,5},{5,4},{6,7},{7,6},{8,9},{9,8},{10,11... | collective-permute-start | bytes 3932168 | tf_op jit(solution)/shard_map/ppermute | solution.py:152
  147.2 12.4 %experts.1 = (bf16[16,40,1024]{2,1,0:T(8,128)(2,1)}, bf16[16,40,1024]{2,1,0:T(8,128)(2,1)}) custom-call(s32[34]{0:T(128)} %pad_add_fusion.1.place_ref, bf16[16,40,1024]{2,1,0:T(8,128)(2,1)} %copy-done.2, bf16[16,40,1024]{2,1,0:T(8,128)(2,1)} %copy-done.11, bf16[1,2048]{1,0:T(2,128)(2,1)} %broadcast_in_dim.62.gain_ref, bf16[32,2048]{1,0:T(8,128)(2,1)} %bitcast.143, ...), custom_call_target="tpu_custom_call" | custom-call | flops 2768240640 | bytes 11730944 | tf_op jit(solution)/shard_map/experts/pallas_call | solution.py:259
  165.7 4.5 %all-to-all-start.5 = ((bf16[16,40,1024]{2,1,0:T(8,128)(2,1)}), bf16[16,40,1024]{2,1,0:T(8,128)(2,1)S(1)}, u32[]{:S(2)}, u32[]{:S(2)}) async-start(bf16[16,40,1024]{2,1,0:T(8,128)(2,1)} %add_convert_fusion), calls=%async_computation.5 | async-start | bytes 2621440 | tf_op jit(solution)/shard_map/all_to_all | solution.py:535
  172.1 16.3 %all_gather.7.full_ref = bf16[128,2048]{1,0:T(8,128)(2,1)} all-gather(bf16[128,256]{1,0:T(8,128)(2,1)S(1)} %copy-done.4), channel_id=1, replica_groups=mesh['zh'=2,'x'=4,'y'=4,'zl'=4,'core'=2] {'zl','core'}, dimensions={1}, use_global_device_ids=true | all-gather | bytes 589824 | tf_op jit(solution)/shard_map/all_gather | solution.py:537
  193.6 5.7 %all-to-all-start.6 = ((bf16[8,8,256]{2,1,0:T(8,128)(2,1)}), bf16[8,8,256]{2,1,0:T(8,128)(2,1)S(1)}, u32[]{:S(2)}, u32[]{:S(2)}) async-start(bf16[8,8,256]{2,1,0:T(8,128)(2,1)} %get-tuple-element.58), calls=%async_computation.6 | async-start | bytes 65536 | tf_op jit(solution)/shard_map/all_to_all | solution.py:542
  203.1 4.4 %collective-permute-start.9 = (bf16[2,128,256]{2,1,0:T(8,128)(2,1)S(1)}, bf16[2,128,256]{2,1,0:T(8,128)(2,1)S(1)}, u32[]{:S(2)}, u32[]{:S(2)}) collective-permute-start(bf16[2,128,256]{2,1,0:T(8,128)(2,1)S(1)} %slice.108), channel_id=1, source_target_pairs={{0,4},{2,6},{4,0},{6,2},{1,5},{3,7},{5,1},{7,3},{8,12},{10,14},{12... | collective-permute-start | bytes 393224 | tf_op jit(solution)/shard_map/ppermute | solution.py:548
  209.5 12.5 %all-to-all-start.7 = ((bf16[32,16,128]{2,1,0:T(8,128)(2,1)}), bf16[32,16,128]{2,1,0:T(8,128)(2,1)S(1)}, u32[]{:S(2)}, u32[]{:S(2)}) async-start(bf16[32,16,128]{2,1,0:T(8,128)(2,1)} %finish.1), calls=%async_computation.7 | async-start | bytes 262144 | tf_op jit(solution)/shard_map/all_to_all | solution.py:551
  222.0 7.5 %all-to-all-done.7.last_ref = bf16[32,16,128]{2,1,0:T(8,128)(2,1)S(1)} async-done(((bf16[32,16,128]{2,1,0:T(8,128)(2,1)}), bf16[32,16,128]{2,1,0:T(8,128)(2,1)S(1)}, u32[]{:S(2)}, u32[]{:S(2)}) %all-to-all-start.7) | async-done | bytes 131104 | tf_op jit(solution)/shard_map/all_to_all | solution.py:551
  232.6 6.3 %all-to-all-start.8 = ((f32[256,1,32]{2,1,0:T(1,128)}), f32[256,1,32]{2,1,0:T(1,128)S(1)}, u32[]{:S(2)}, u32[]{:S(2)}) async-start(f32[256,1,32]{2,1,0:T(1,128)} %bitcast.113), calls=%async_computation.8 | async-start | bytes 262144 | tf_op jit(solution)/shard_map/all_to_all | solution.py:554
  241.2 3.4 %new_kv.1 = bf16[2,128,256]{2,1,0:T(8,128)(2,1)} custom-call(bf16[128,2048]{1,0:T(8,128)(2,1)} %all_gather.7.full_ref, bf16[1,2048]{1,0:T(2,128)(2,1)} %broadcast_in_dim.61.gain_ref, bf16[3,2048,256]{2,1,0:T(8,128)(2,1)} %w_ref.4, f32[128,64]{1,0:T(8,128)} %get-tuple-element.95.cos_ref.refs_0_, f32[128,64]{1,0:T(8,128)} %get-tuple-element.94.sin_ref.refs_1_, ...), custom_call_target="tpu_custom_call" | custom-call | tf_op jit(solution)/shard_map/new_kv/pallas_call | solution.py:67
  245.3 6.5 %all-to-all-done.8 = f32[256,1,32]{2,1,0:T(1,128)S(1)} async-done(((f32[256,1,32]{2,1,0:T(1,128)}), f32[256,1,32]{2,1,0:T(1,128)S(1)}, u32[]{:S(2)}, u32[]{:S(2)}) %all-to-all-start.8) | async-done | bytes 32800 | tf_op jit(solution)/shard_map/all_to_all | solution.py:554
  (124 shorter events, 58.9 us)
Async XLA Ops:
  3.7 25.8 %all-to-all-start = ((bf16[32,8,256]{2,1,0:T(8,128)(2,1)}), bf16[32,8,256]{2,1,0:T(8,128)(2,1)S(1)}, u32[]{:S(2)}, u32[]{:S(2)}) async-start(bf16[32,8,256]{2,1,0:T(8,128)(2,1)} %pad_maximum_fusion), calls=%async_computation | async-start | bytes 262144 | tf_op jit(solution)/shard_map/all_to_all | solution.py:445
  18.2 18.4 %copy-start.8 = (bf16[2048]{0:T(1024)(128)(2,1)S(1)}, bf16[2048]{0:T(1024)(128)(2,1)}, u32[]{:S(2)}) copy-start(bf16[2048]{0:T(1024)(128)(2,1)} %param.17) | copy-start | bytes 12292
  18.2 19.0 %copy-start.9 = (bf16[2048]{0:T(1024)(128)(2,1)S(1)}, bf16[2048]{0:T(1024)(128)(2,1)}, u32[]{:S(2)}) copy-start(bf16[2048]{0:T(1024)(128)(2,1)} %param.23) | copy-start | bytes 12292
  18.2 19.6 %copy-start.10 = (bf16[2048]{0:T(1024)(128)(2,1)S(1)}, bf16[2048]{0:T(1024)(128)(2,1)}, u32[]{:S(2)}) copy-start(bf16[2048]{0:T(1024)(128)(2,1)} %param.30) | copy-start | bytes 12292
  19.7 27.8 %collective-permute-start.1 = (bf16[176,2048]{1,0:T(8,128)(2,1)S(1)}, bf16[176,2048]{1,0:T(8,128)(2,1)S(1)}, u32[]{:S(2)}, u32[]{:S(2)}) collective-permute-start(bf16[176,2048]{1,0:T(8,128)(2,1)S(1)} %get-tuple-element.78), channel_id=1, source_target_pairs={{0,2},{2,0},{4,6},{6,4},{1,3},{3,1},{5,7},{7,5},{8,10},{10,8},{12,... | collective-permute-start | bytes 2162696 | tf_op jit(solution)/shard_map/ppermute | solution.py:444
  20.5 20.2 %collective-permute-start = (s32[6,128]{1,0:T(8,128)S(1)}, s32[6,128]{1,0:T(8,128)S(1)}, u32[]{:S(2)}, u32[]{:S(2)}) collective-permute-start(s32[6,128]{1,0:T(8,128)S(1)} %bitcast.114), channel_id=1, source_target_pairs={{0,128},{128,0},{1,129},{129,1},{2,130},{130,2},{3,131},{131,3},{4... | collective-permute-start | bytes 9224 | tf_op jit(solution)/shard_map/ppermute | solution.py:156
  30.7 16.8 %all-to-all-start.1 = ((bf16[32,8,256]{2,1,0:T(8,128)(2,1)}), bf16[32,8,256]{2,1,0:T(8,128)(2,1)S(1)}, u32[]{:S(2)}, u32[]{:S(2)}) async-start(bf16[32,8,256]{2,1,0:T(8,128)(2,1)} %gather_fusion), calls=%async_computation.1 | async-start | bytes 262144 | tf_op jit(solution)/shard_map/all_to_all | solution.py:456
  35.2 40.0 %collective-permute-start.2 = (bf16[176,2048]{1,0:T(8,128)(2,1)S(1)}, bf16[176,2048]{1,0:T(8,128)(2,1)S(1)}, u32[]{:S(2)}, u32[]{:S(2)}) collective-permute-start(bf16[176,2048]{1,0:T(8,128)(2,1)S(1)} %get-tuple-element.39), channel_id=1, source_target_pairs={{0,2},{2,0},{4,6},{6,4},{1,3},{3,1},{5,7},{7,5},{8,10},{10,8},{12,... | collective-permute-start | bytes 2162696 | tf_op jit(solution)/shard_map/ppermute | solution.py:455
  47.5 27.7 %copy-start.13 = (bf16[176,2048]{1,0:T(8,128)(2,1)}, bf16[176,2048]{1,0:T(8,128)(2,1)S(1)}, u32[]{:S(2)}) copy-start(bf16[176,2048]{1,0:T(8,128)(2,1)S(1)} %collective-permute-done.1.pg_ref) | copy-start | bytes 2162692
  75.2 1.8 collective-permute-start.3
  78.8 12.6 %all-to-all-start.2 = ((bf16[4,128,256]{2,1,0:T(8,128)(2,1)}), bf16[4,128,256]{2,1,0:T(8,128)(2,1)S(1)}, u32[]{:S(2)}, u32[]{:S(2)}) async-start(bf16[4,128,256]{2,1,0:T(8,128)(2,1)} %add_convert_fusion.2), calls=%async_computation.2 | async-start | bytes 524288 | tf_op jit(solution)/shard_map/all_to_all | solution.py:478
  82.6 8.8 %collective-permute-start.4 = (s32[6,128]{1,0:T(8,128)S(1)}, s32[6,128]{1,0:T(8,128)S(1)}, u32[]{:S(2)}, u32[]{:S(2)}) collective-permute-start(s32[6,128]{1,0:T(8,128)S(1)} %reshape.388), channel_id=1, source_target_pairs={{0,128},{128,0},{1,129},{129,1},{2,130},{130,2},{3,131},{131,3},{4... | collective-permute-start | bytes 9224 | tf_op jit(solution)/shard_map/ppermute | solution.py:156
  92.3 20.0 %all-to-all-start.3 = ((bf16[8,128,256]{2,1,0:T(8,128)(2,1)}), bf16[8,128,256]{2,1,0:T(8,128)(2,1)S(1)}, u32[]{:S(2)}, u32[]{:S(2)}) async-start(bf16[8,128,256]{2,1,0:T(8,128)(2,1)} %broadcast_in_dim.64), calls=%async_computation.3 | async-start | bytes 1048576 | tf_op jit(solution)/shard_map/all_to_all | solution.py:148
  115.8 23.4 %all-to-all-start.4 = ((bf16[16,40,1024]{2,1,0:T(8,128)(2,1)}), bf16[16,40,1024]{2,1,0:T(8,128)(2,1)S(1)}, u32[]{:S(2)}, u32[]{:S(2)}) async-start(bf16[16,40,1024]{2,1,0:T(8,128)(2,1)} %bitcast.109), calls=%async_computation.4 | async-start | bytes 2621440 | tf_op jit(solution)/shard_map/all_to_all | solution.py:512
  122.4 14.8 %collective-permute-start.5 = (bf16[176,2048]{1,0:T(8,128)(2,1)S(1)}, bf16[176,2048]{1,0:T(8,128)(2,1)}, u32[]{:S(2)}, u32[]{:S(2)}) collective-permute-start(bf16[176,2048]{1,0:T(8,128)(2,1)S(1)} %bitcast.142), channel_id=1, source_target_pairs={{0,2},{2,0},{4,6},{6,4},{1,3},{3,1},{5,7},{7,5},{8,10},{10,8},{12,... | collective-permute-start | bytes 2162696 | tf_op jit(solution)/shard_map/ppermute | solution.py:515
  139.2 6.9 %collective-permute-start.6 = (bf16[16,40,1024]{2,1,0:T(8,128)(2,1)S(1)}, bf16[16,40,1024]{2,1,0:T(8,128)(2,1)S(1)}, u32[]{:S(2)}, u32[]{:S(2)}) collective-permute-start(bf16[16,40,1024]{2,1,0:T(8,128)(2,1)S(1)} %all-to-all-done.4.a_ref), channel_id=1, source_target_pairs={{0,1},{1,0},{2,3},{3,2},{4,5},{5,4},{6,7},{7,6},{8,9},{9,8},{10,11... | collective-permute-start | bytes 3932168 | tf_op jit(solution)/shard_map/ppermute | solution.py:152
  159.5 3.2 %collective-permute-start.7 = (bf16[16,40,1024]{2,1,0:T(8,128)(2,1)}, bf16[16,40,1024]{2,1,0:T(8,128)(2,1)S(1)}, u32[]{:S(2)}, u32[]{:S(2)}) collective-permute-start(bf16[16,40,1024]{2,1,0:T(8,128)(2,1)} %get-tuple-element.51), channel_id=1, source_target_pairs={{0,1},{1,0},{2,3},{3,2},{4,5},{5,4},{6,7},{7,6},{8,9},{9,8},{10,11... | collective-permute-start | bytes 3932168 | tf_op jit(solution)/shard_map/ppermute | solution.py:152
  165.7 22.8 %all-to-all-start.5 = ((bf16[16,40,1024]{2,1,0:T(8,128)(2,1)}), bf16[16,40,1024]{2,1,0:T(8,128)(2,1)S(1)}, u32[]{:S(2)}, u32[]{:S(2)}) async-start(bf16[16,40,1024]{2,1,0:T(8,128)(2,1)} %add_convert_fusion), calls=%async_computation.5 | async-start | bytes 2621440 | tf_op jit(solution)/shard_map/all_to_all | solution.py:535
  192.6 9.5 %collective-permute-start.8 = (bf16[4,128,256]{2,1,0:T(8,128)(2,1)}, bf16[4,128,256]{2,1,0:T(8,128)(2,1)S(1)}, u32[]{:S(2)}, u32[]{:S(2)}) collective-permute-start(bf16[4,128,256]{2,1,0:T(8,128)(2,1)} %get-tuple-element.56), channel_id=1, source_target_pairs={{0,128},{128,0},{1,129},{129,1},{2,130},{130,2},{3,131},{131,3},{4... | collective-permute-start | bytes 786440 | tf_op jit(solution)/shard_map/ppermute | solution.py:156
  193.6 13.9 %all-to-all-start.6 = ((bf16[8,8,256]{2,1,0:T(8,128)(2,1)}), bf16[8,8,256]{2,1,0:T(8,128)(2,1)S(1)}, u32[]{:S(2)}, u32[]{:S(2)}) async-start(bf16[8,8,256]{2,1,0:T(8,128)(2,1)} %get-tuple-element.58), calls=%async_computation.6 | async-start | bytes 65536 | tf_op jit(solution)/shard_map/all_to_all | solution.py:542
  203.1 35.9 %collective-permute-start.9 = (bf16[2,128,256]{2,1,0:T(8,128)(2,1)S(1)}, bf16[2,128,256]{2,1,0:T(8,128)(2,1)S(1)}, u32[]{:S(2)}, u32[]{:S(2)}) collective-permute-start(bf16[2,128,256]{2,1,0:T(8,128)(2,1)S(1)} %slice.108), channel_id=1, source_target_pairs={{0,4},{2,6},{4,0},{6,2},{1,5},{3,7},{5,1},{7,3},{8,12},{10,14},{12... | collective-permute-start | bytes 393224 | tf_op jit(solution)/shard_map/ppermute | solution.py:548
  209.5 20.0 %all-to-all-start.7 = ((bf16[32,16,128]{2,1,0:T(8,128)(2,1)}), bf16[32,16,128]{2,1,0:T(8,128)(2,1)S(1)}, u32[]{:S(2)}, u32[]{:S(2)}) async-start(bf16[32,16,128]{2,1,0:T(8,128)(2,1)} %finish.1), calls=%async_computation.7 | async-start | bytes 262144 | tf_op jit(solution)/shard_map/all_to_all | solution.py:551
  232.6 19.1 %all-to-all-start.8 = ((f32[256,1,32]{2,1,0:T(1,128)}), f32[256,1,32]{2,1,0:T(1,128)S(1)}, u32[]{:S(2)}, u32[]{:S(2)}) async-start(f32[256,1,32]{2,1,0:T(1,128)} %bitcast.113), calls=%async_computation.8 | async-start | bytes 262144 | tf_op jit(solution)/shard_map/all_to_all | solution.py:554
  239.1 13.5 %collective-permute-start.10 = (bf16[128,256]{1,0:T(8,128)(2,1)S(1)}, bf16[128,256]{1,0:T(8,128)(2,1)S(1)}, u32[]{:S(2)}, u32[]{:S(2)}) collective-permute-start(bf16[128,256]{1,0:T(8,128)(2,1)S(1)} %slice_bitcast_fusion.2), channel_id=1, source_target_pairs={{0,2},{2,0},{4,6},{6,4},{1,3},{3,1},{5,7},{7,5},{8,10},{10,8},{12,... | collective-permute-start | bytes 196616 | tf_op jit(solution)/shard_map/ppermute | solution.py:549
  (12 other events, 53.6 us)

commit v11 on v10

--- a/solution.py
+++ b/solution.py
@@ -539,7 +539,8 @@
     new_cache = new_kv(own_full, gain, w_qkv, rope_tables(lengths[0], new))[:, None]
 
     keep, send, last = combine(jnp.stack([zh, zl]).astype(jnp.int32), chosen_own, returned)
-    last = finish(lax.all_to_all(last, Z, 0, 0, tiled=True), reqs)
+    last, send = barrier((lax.all_to_all(last, Z, 0, 0, tiled=True), send))
+    last = finish(last, reqs)
 
     def add(mine, theirs):
         return (mine.astype(f32) + theirs.astype(f32)).astype(bf16)

time: 254 us -> 264 us (1.039)
  blocking collectives: 35.6 us -> 46.5 us
  starting transfers between devices: 84.9 us -> 78.2 us
  waiting for transfers between devices: 70.7 us -> 77.4 us
    all_to_all x0 -> x1, blocking collectives: none -> 10.8 us  [local(): last, send = barrier((lax.all_to_all(last, Z, 0, 0, tiled=True), send))]
    ppermute x3, waiting for transfers between devices: 9.73 us -> 16.2 us  [column_swap(): return lax.ppermute(value, 'zh', [(0, 1), (1, 0)])]
    all_to_all x1 -> x0, starting transfers between devices: 5.68 us -> none  [local(): last = finish(lax.all_to_all(last, Z, 0, 0, tiled=True), reqs)]
  transfers between devices with their start and end apart: 20 -> 19, of which waited for: 13 -> 14; matrix products, arithmetic and copies ran while one was open for 6% -> 5% of each run, Pallas kernels for 5% -> 5%
where the time goes in v11:
time: 264 us; the launch traced here: 263 us
  starting transfers between devices  78.2 us (30%)
  waiting for transfers between devices  77.4 us (29%)
  blocking collectives  46.5 us (18%)
  Pallas kernels  31.2 us (12%)
  other arithmetic  15.4 us (6%)
  local copies, waits for them, and re-layouts  10.9 us (4%)
  between operations  2.91 us (1%)
    all_gather x1, blocking collectives, local(): full = lax.all_gather(held, TP, axis=1, tiled=True)  19.4 us
    all_gather x1, blocking collectives, local(): own_full = lax.all_gather(hidden_late, TP, axis=1, tiled=True)  16.3 us
    ppermute x3, waiting for transfers between devices, column_swap(): return lax.ppermute(value, 'zh', [(0, 1), (1, 0)])  16.2 us
    ppermute x1, waiting for transfers between devices, local(): pair_down = lax.ppermute(down_w, 'zl', neighbours)  14.7 us
    all_to_all x1, starting transfers between devices, local(): leg = lax.all_to_all(chunks, REQ, 0, 0, tiled=True)  14.5 us
    all_to_all x1, waiting for transfers between devices, spread(): return lax.all_to_all(wide, axes, 0, 0, tiled=True)  14 us
    all_to_all x1, starting transfers between devices, local(): last_all = lax.all_to_all(last, ('core', 'x', 'y'), 0, 0, tiled=True)  13.1 us
    pallas_call x1, Pallas kernels, experts(): pl.pallas_call(experts_body, out_shape=(shape, shape), in_specs=[pl.Block...  12.4 us
  transfers between devices with their start and end apart: 19, of which 14 were waited for; matrix products, arithmetic and copies ran while one was open for 5% of the time, Pallas kernels for 5%

profile of v11, /device:TPU:1, one launch (start us, length us, event | category | flops | bytes accessed | tf_op | source)
XLA Modules:
  0.0 263.1 jit_solution(10881231515235616768)
XLA Ops:
  3.7 14.5 %all-to-all-start = ((bf16[32,8,256]{2,1,0:T(8,128)(2,1)}), bf16[32,8,256]{2,1,0:T(8,128)(2,1)S(1)}, u32[]{:S(2)}, u32[]{:S(2)}) async-start(bf16[32,8,256]{2,1,0:T(8,128)(2,1)} %pad_maximum_fusion), calls=%async_computation | async-start | bytes 262144 | tf_op jit(solution)/shard_map/all_to_all | solution.py:445
  20.5 5.1 %collective-permute-start = (s32[6,128]{1,0:T(8,128)S(1)}, s32[6,128]{1,0:T(8,128)S(1)}, u32[]{:S(2)}, u32[]{:S(2)}) collective-permute-start(s32[6,128]{1,0:T(8,128)S(1)} %bitcast.114), channel_id=1, source_target_pairs={{0,128},{128,0},{1,129},{129,1},{2,130},{130,2},{3,131},{131,3},{4... | collective-permute-start | bytes 9224 | tf_op jit(solution)/shard_map/ppermute | solution.py:156
  30.7 4.5 %all-to-all-start.1 = ((bf16[32,8,256]{2,1,0:T(8,128)(2,1)}), bf16[32,8,256]{2,1,0:T(8,128)(2,1)S(1)}, u32[]{:S(2)}, u32[]{:S(2)}) async-start(bf16[32,8,256]{2,1,0:T(8,128)(2,1)} %gather_fusion), calls=%async_computation.1 | async-start | bytes 262144 | tf_op jit(solution)/shard_map/all_to_all | solution.py:456
  40.7 6.8 %all-to-all-done.1 = bf16[32,8,256]{2,1,0:T(8,128)(2,1)S(1)} async-done(((bf16[32,8,256]{2,1,0:T(8,128)(2,1)}), bf16[32,8,256]{2,1,0:T(8,128)(2,1)S(1)}, u32[]{:S(2)}, u32[]{:S(2)}) %all-to-all-start.1) | async-done | bytes 131104 | tf_op jit(solution)/shard_map/all_to_all | solution.py:456
  50.0 19.4 %all_gather.6.full_ref = bf16[128,2048]{1,0:T(8,128)(2,1)} all-gather(bf16[128,256]{1,0:T(8,128)(2,1)S(1)} %reshape.383), channel_id=1, replica_groups=mesh['zh'=2,'x'=4,'y'=4,'zl'=4,'core'=2] {'zl','core'}, dimensions={1}, use_global_device_ids=true | all-gather | bytes 589824 | tf_op jit(solution)/shard_map/all_gather | solution.py:464
  69.4 5.8 %attend.1 = (bf16[4,128,256]{2,1,0:T(8,128)(2,1)}, bf16[4,128,256]{2,1,0:T(8,128)(2,1)}) custom-call(s32[1]{0:T(128)} %bitcast.28.len_ref, s32[34]{0:T(128)} %pad_add_fusion.1.place_ref, bf16[128,2048]{1,0:T(8,128)(2,1)} %all_gather.6.full_ref, bf16[1,2048]{1,0:T(2,128)(2,1)} %broadcast_in_dim.61.gain_ref, bf16[3,2048,256]{2,1,0:T(8,128)(2,1)} %w_ref.4, ...), custom_call_target="tpu_custom_call" | custom-call | tf_op jit(solution)/shard_map/attend/pallas_call | solution.py:137
  82.6 4.0 %collective-permute-start.4 = (s32[6,128]{1,0:T(8,128)S(1)}, s32[6,128]{1,0:T(8,128)S(1)}, u32[]{:S(2)}, u32[]{:S(2)}) collective-permute-start(s32[6,128]{1,0:T(8,128)S(1)} %reshape.388), channel_id=1, source_target_pairs={{0,128},{128,0},{1,129},{129,1},{2,130},{130,2},{3,131},{131,3},{4... | collective-permute-start | bytes 9224 | tf_op jit(solution)/shard_map/ppermute | solution.py:156
  86.6 4.7 %collective-permute-done.4 = s32[6,128]{1,0:T(8,128)S(1)} collective-permute-done((s32[6,128]{1,0:T(8,128)S(1)}, s32[6,128]{1,0:T(8,128)S(1)}, u32[]{:S(2)}, u32[]{:S(2)}) %collective-permute-start.4) | collective-permute-done | bytes 3104 | tf_op jit(solution)/shard_map/ppermute | solution.py:156
  92.2 4.2 %all-to-all-start.3 = ((bf16[8,128,256]{2,1,0:T(8,128)(2,1)}), bf16[8,128,256]{2,1,0:T(8,128)(2,1)S(1)}, u32[]{:S(2)}, u32[]{:S(2)}) async-start(bf16[8,128,256]{2,1,0:T(8,128)(2,1)} %broadcast_in_dim.64), calls=%async_computation.3 | async-start | bytes 1048576 | tf_op jit(solution)/shard_map/all_to_all | solution.py:148
  98.3 14.0 %all-to-all-done.3.parts_ref = bf16[8,128,256]{2,1,0:T(8,128)(2,1)S(1)} async-done(((bf16[8,128,256]{2,1,0:T(8,128)(2,1)}), bf16[8,128,256]{2,1,0:T(8,128)(2,1)S(1)}, u32[]{:S(2)}, u32[]{:S(2)}) %all-to-all-start.3) | async-done | bytes 524320 | tf_op jit(solution)/shard_map/all_to_all | solution.py:148
  115.8 6.6 %all-to-all-start.4 = ((bf16[16,40,1024]{2,1,0:T(8,128)(2,1)}), bf16[16,40,1024]{2,1,0:T(8,128)(2,1)S(1)}, u32[]{:S(2)}, u32[]{:S(2)}) async-start(bf16[16,40,1024]{2,1,0:T(8,128)(2,1)} %bitcast.109), calls=%async_computation.4 | async-start | bytes 2621440 | tf_op jit(solution)/shard_map/all_to_all | solution.py:512
  122.5 14.7 %collective-permute-done.5.pd_ref = bf16[176,2048]{1,0:T(8,128)(2,1)} collective-permute-done((bf16[176,2048]{1,0:T(8,128)(2,1)S(1)}, bf16[176,2048]{1,0:T(8,128)(2,1)}, u32[]{:S(2)}, u32[]{:S(2)}) %collective-permute-start.5) | collective-permute-done | bytes 720928 | tf_op jit(solution)/shard_map/ppermute | solution.py:515
  139.2 4.2 %collective-permute-start.6 = (bf16[16,40,1024]{2,1,0:T(8,128)(2,1)S(1)}, bf16[16,40,1024]{2,1,0:T(8,128)(2,1)S(1)}, u32[]{:S(2)}, u32[]{:S(2)}) collective-permute-start(bf16[16,40,1024]{2,1,0:T(8,128)(2,1)S(1)} %all-to-all-done.4.a_ref), channel_id=1, source_target_pairs={{0,1},{1,0},{2,3},{3,2},{4,5},{5,4},{6,7},{7,6},{8,9},{9,8},{10,11... | collective-permute-start | bytes 3932168 | tf_op jit(solution)/shard_map/ppermute | solution.py:152
  147.1 12.4 %experts.1 = (bf16[16,40,1024]{2,1,0:T(8,128)(2,1)}, bf16[16,40,1024]{2,1,0:T(8,128)(2,1)}) custom-call(s32[34]{0:T(128)} %pad_add_fusion.1.place_ref, bf16[16,40,1024]{2,1,0:T(8,128)(2,1)} %copy-done.2, bf16[16,40,1024]{2,1,0:T(8,128)(2,1)} %copy-done.10, bf16[1,2048]{1,0:T(2,128)(2,1)} %broadcast_in_dim.62.gain_ref, bf16[32,2048]{1,0:T(8,128)(2,1)} %bitcast.143, ...), custom_call_target="tpu_custom_call" | custom-call | flops 2768240640 | bytes 11730944 | tf_op jit(solution)/shard_map/experts/pallas_call | solution.py:259
  165.7 4.5 %all-to-all-start.5 = ((bf16[16,40,1024]{2,1,0:T(8,128)(2,1)}), bf16[16,40,1024]{2,1,0:T(8,128)(2,1)S(1)}, u32[]{:S(2)}, u32[]{:S(2)}) async-start(bf16[16,40,1024]{2,1,0:T(8,128)(2,1)} %add_convert_fusion), calls=%async_computation.5 | async-start | bytes 2621440 | tf_op jit(solution)/shard_map/all_to_all | solution.py:535
  172.0 16.3 %all_gather.7.full_ref = bf16[128,2048]{1,0:T(8,128)(2,1)} all-gather(bf16[128,256]{1,0:T(8,128)(2,1)S(1)} %copy-done.4), channel_id=1, replica_groups=mesh['zh'=2,'x'=4,'y'=4,'zl'=4,'core'=2] {'zl','core'}, dimensions={1}, use_global_device_ids=true | all-gather | bytes 589824 | tf_op jit(solution)/shard_map/all_gather | solution.py:537
  192.6 10.8 %all_to_all.49.parts_ref = bf16[8,8,256]{2,1,0:T(8,128)(2,1)} all-to-all(bf16[8,8,256]{2,1,0:T(8,128)(2,1)} %get-tuple-element.58), channel_id=1, replica_groups=mesh['zh'=2,'x'=4,'y'=4,'zl'=4,'core'=2] {'zh','zl'}, dimensions={0} | all-to-all | bytes 65536 | tf_op jit(solution)/shard_map/all_to_all | solution.py:542
  203.6 9.3 %collective-permute-done.8 = bf16[4,128,256]{2,1,0:T(8,128)(2,1)S(1)} collective-permute-done((bf16[4,128,256]{2,1,0:T(8,128)(2,1)}, bf16[4,128,256]{2,1,0:T(8,128)(2,1)S(1)}, u32[]{:S(2)}, u32[]{:S(2)}) %collective-permute-start.8) | collective-permute-done | bytes 262176 | tf_op jit(solution)/shard_map/ppermute | solution.py:156
  213.9 3.6 %collective-permute-start.9 = (bf16[2,128,256]{2,1,0:T(8,128)(2,1)S(1)}, bf16[2,128,256]{2,1,0:T(8,128)(2,1)S(1)}, u32[]{:S(2)}, u32[]{:S(2)}) collective-permute-start(bf16[2,128,256]{2,1,0:T(8,128)(2,1)S(1)} %slice.108), channel_id=1, source_target_pairs={{0,4},{2,6},{4,0},{6,2},{1,5},{3,7},{5,1},{7,3},{8,12},{10,14},{12... | collective-permute-start | bytes 393224 | tf_op jit(solution)/shard_map/ppermute | solution.py:549
  219.0 13.1 %all-to-all-start.7 = ((bf16[32,16,128]{2,1,0:T(8,128)(2,1)}), bf16[32,16,128]{2,1,0:T(8,128)(2,1)S(1)}, u32[]{:S(2)}, u32[]{:S(2)}) async-start(bf16[32,16,128]{2,1,0:T(8,128)(2,1)} %finish.1), calls=%async_computation.7 | async-start | bytes 262144 | tf_op jit(solution)/shard_map/all_to_all | solution.py:552
  232.1 7.5 %all-to-all-done.7.last_ref = bf16[32,16,128]{2,1,0:T(8,128)(2,1)S(1)} async-done(((bf16[32,16,128]{2,1,0:T(8,128)(2,1)}), bf16[32,16,128]{2,1,0:T(8,128)(2,1)S(1)}, u32[]{:S(2)}, u32[]{:S(2)}) %all-to-all-start.7) | async-done | bytes 131104 | tf_op jit(solution)/shard_map/all_to_all | solution.py:552
  242.7 6.2 %all-to-all-start.8 = ((f32[256,1,32]{2,1,0:T(1,128)}), f32[256,1,32]{2,1,0:T(1,128)S(1)}, u32[]{:S(2)}, u32[]{:S(2)}) async-start(f32[256,1,32]{2,1,0:T(1,128)} %bitcast.113), calls=%async_computation.8 | async-start | bytes 262144 | tf_op jit(solution)/shard_map/all_to_all | solution.py:555
  251.2 3.4 %new_kv.1 = bf16[2,128,256]{2,1,0:T(8,128)(2,1)} custom-call(bf16[128,2048]{1,0:T(8,128)(2,1)} %all_gather.7.full_ref, bf16[1,2048]{1,0:T(2,128)(2,1)} %broadcast_in_dim.61.gain_ref, bf16[3,2048,256]{2,1,0:T(8,128)(2,1)} %w_ref.4, f32[128,64]{1,0:T(8,128)} %get-tuple-element.99.cos_ref.refs_0_, f32[128,64]{1,0:T(8,128)} %get-tuple-element.98.sin_ref.refs_1_, ...), custom_call_target="tpu_custom_call" | custom-call | tf_op jit(solution)/shard_map/new_kv/pallas_call | solution.py:67
  255.2 6.5 %all-to-all-done.8 = f32[256,1,32]{2,1,0:T(1,128)S(1)} async-done(((f32[256,1,32]{2,1,0:T(1,128)}), f32[256,1,32]{2,1,0:T(1,128)S(1)}, u32[]{:S(2)}, u32[]{:S(2)}) %all-to-all-start.8) | async-done | bytes 32800 | tf_op jit(solution)/shard_map/all_to_all | solution.py:555
  (121 shorter events, 58.1 us)
Async XLA Ops:
  3.7 25.8 %all-to-all-start = ((bf16[32,8,256]{2,1,0:T(8,128)(2,1)}), bf16[32,8,256]{2,1,0:T(8,128)(2,1)S(1)}, u32[]{:S(2)}, u32[]{:S(2)}) async-start(bf16[32,8,256]{2,1,0:T(8,128)(2,1)} %pad_maximum_fusion), calls=%async_computation | async-start | bytes 262144 | tf_op jit(solution)/shard_map/all_to_all | solution.py:445
  18.2 18.4 %copy-start.7 = (bf16[2048]{0:T(1024)(128)(2,1)S(1)}, bf16[2048]{0:T(1024)(128)(2,1)}, u32[]{:S(2)}) copy-start(bf16[2048]{0:T(1024)(128)(2,1)} %param.17) | copy-start | bytes 12292
  18.2 19.0 %copy-start.8 = (bf16[2048]{0:T(1024)(128)(2,1)S(1)}, bf16[2048]{0:T(1024)(128)(2,1)}, u32[]{:S(2)}) copy-start(bf16[2048]{0:T(1024)(128)(2,1)} %param.23) | copy-start | bytes 12292
  18.2 19.6 %copy-start.9 = (bf16[2048]{0:T(1024)(128)(2,1)S(1)}, bf16[2048]{0:T(1024)(128)(2,1)}, u32[]{:S(2)}) copy-start(bf16[2048]{0:T(1024)(128)(2,1)} %param.30) | copy-start | bytes 12292
  19.7 27.8 %collective-permute-start.1 = (bf16[176,2048]{1,0:T(8,128)(2,1)S(1)}, bf16[176,2048]{1,0:T(8,128)(2,1)S(1)}, u32[]{:S(2)}, u32[]{:S(2)}) collective-permute-start(bf16[176,2048]{1,0:T(8,128)(2,1)S(1)} %get-tuple-element.82), channel_id=1, source_target_pairs={{0,2},{2,0},{4,6},{6,4},{1,3},{3,1},{5,7},{7,5},{8,10},{10,8},{12,... | collective-permute-start | bytes 2162696 | tf_op jit(solution)/shard_map/ppermute | solution.py:444
  20.5 20.2 %collective-permute-start = (s32[6,128]{1,0:T(8,128)S(1)}, s32[6,128]{1,0:T(8,128)S(1)}, u32[]{:S(2)}, u32[]{:S(2)}) collective-permute-start(s32[6,128]{1,0:T(8,128)S(1)} %bitcast.114), channel_id=1, source_target_pairs={{0,128},{128,0},{1,129},{129,1},{2,130},{130,2},{3,131},{131,3},{4... | collective-permute-start | bytes 9224 | tf_op jit(solution)/shard_map/ppermute | solution.py:156
  30.7 16.8 %all-to-all-start.1 = ((bf16[32,8,256]{2,1,0:T(8,128)(2,1)}), bf16[32,8,256]{2,1,0:T(8,128)(2,1)S(1)}, u32[]{:S(2)}, u32[]{:S(2)}) async-start(bf16[32,8,256]{2,1,0:T(8,128)(2,1)} %gather_fusion), calls=%async_computation.1 | async-start | bytes 262144 | tf_op jit(solution)/shard_map/all_to_all | solution.py:456
  35.2 40.0 %collective-permute-start.2 = (bf16[176,2048]{1,0:T(8,128)(2,1)S(1)}, bf16[176,2048]{1,0:T(8,128)(2,1)S(1)}, u32[]{:S(2)}, u32[]{:S(2)}) collective-permute-start(bf16[176,2048]{1,0:T(8,128)(2,1)S(1)} %get-tuple-element.41), channel_id=1, source_target_pairs={{0,2},{2,0},{4,6},{6,4},{1,3},{3,1},{5,7},{7,5},{8,10},{10,8},{12,... | collective-permute-start | bytes 2162696 | tf_op jit(solution)/shard_map/ppermute | solution.py:455
  47.5 27.7 %copy-start.12 = (bf16[176,2048]{1,0:T(8,128)(2,1)}, bf16[176,2048]{1,0:T(8,128)(2,1)S(1)}, u32[]{:S(2)}) copy-start(bf16[176,2048]{1,0:T(8,128)(2,1)S(1)} %collective-permute-done.1.pg_ref) | copy-start | bytes 2162692
  75.2 16.2 %copy-start.13 = (bf16[176,2048]{1,0:T(8,128)(2,1)}, bf16[176,2048]{1,0:T(8,128)(2,1)S(1)}, u32[]{:S(2)}) copy-start(bf16[176,2048]{1,0:T(8,128)(2,1)S(1)} %collective-permute-done.2.pu_ref) | copy-start | bytes 2162692
  75.2 1.8 collective-permute-start.3
  78.8 12.6 %all-to-all-start.2 = ((bf16[4,128,256]{2,1,0:T(8,128)(2,1)}), bf16[4,128,256]{2,1,0:T(8,128)(2,1)S(1)}, u32[]{:S(2)}, u32[]{:S(2)}) async-start(bf16[4,128,256]{2,1,0:T(8,128)(2,1)} %add_convert_fusion.2), calls=%async_computation.2 | async-start | bytes 524288 | tf_op jit(solution)/shard_map/all_to_all | solution.py:478
  82.6 8.8 %collective-permute-start.4 = (s32[6,128]{1,0:T(8,128)S(1)}, s32[6,128]{1,0:T(8,128)S(1)}, u32[]{:S(2)}, u32[]{:S(2)}) collective-permute-start(s32[6,128]{1,0:T(8,128)S(1)} %reshape.388), channel_id=1, source_target_pairs={{0,128},{128,0},{1,129},{129,1},{2,130},{130,2},{3,131},{131,3},{4... | collective-permute-start | bytes 9224 | tf_op jit(solution)/shard_map/ppermute | solution.py:156
  92.2 20.0 %all-to-all-start.3 = ((bf16[8,128,256]{2,1,0:T(8,128)(2,1)}), bf16[8,128,256]{2,1,0:T(8,128)(2,1)S(1)}, u32[]{:S(2)}, u32[]{:S(2)}) async-start(bf16[8,128,256]{2,1,0:T(8,128)(2,1)} %broadcast_in_dim.64), calls=%async_computation.3 | async-start | bytes 1048576 | tf_op jit(solution)/shard_map/all_to_all | solution.py:148
  115.8 23.4 %all-to-all-start.4 = ((bf16[16,40,1024]{2,1,0:T(8,128)(2,1)}), bf16[16,40,1024]{2,1,0:T(8,128)(2,1)S(1)}, u32[]{:S(2)}, u32[]{:S(2)}) async-start(bf16[16,40,1024]{2,1,0:T(8,128)(2,1)} %bitcast.109), calls=%async_computation.4 | async-start | bytes 2621440 | tf_op jit(solution)/shard_map/all_to_all | solution.py:512
  122.4 14.8 %collective-permute-start.5 = (bf16[176,2048]{1,0:T(8,128)(2,1)S(1)}, bf16[176,2048]{1,0:T(8,128)(2,1)}, u32[]{:S(2)}, u32[]{:S(2)}) collective-permute-start(bf16[176,2048]{1,0:T(8,128)(2,1)S(1)} %bitcast.142), channel_id=1, source_target_pairs={{0,2},{2,0},{4,6},{6,4},{1,3},{3,1},{5,7},{7,5},{8,10},{10,8},{12,... | collective-permute-start | bytes 2162696 | tf_op jit(solution)/shard_map/ppermute | solution.py:515
  139.2 6.9 %collective-permute-start.6 = (bf16[16,40,1024]{2,1,0:T(8,128)(2,1)S(1)}, bf16[16,40,1024]{2,1,0:T(8,128)(2,1)S(1)}, u32[]{:S(2)}, u32[]{:S(2)}) collective-permute-start(bf16[16,40,1024]{2,1,0:T(8,128)(2,1)S(1)} %all-to-all-done.4.a_ref), channel_id=1, source_target_pairs={{0,1},{1,0},{2,3},{3,2},{4,5},{5,4},{6,7},{7,6},{8,9},{9,8},{10,11... | collective-permute-start | bytes 3932168 | tf_op jit(solution)/shard_map/ppermute | solution.py:152
  159.5 3.2 %collective-permute-start.7 = (bf16[16,40,1024]{2,1,0:T(8,128)(2,1)}, bf16[16,40,1024]{2,1,0:T(8,128)(2,1)S(1)}, u32[]{:S(2)}, u32[]{:S(2)}) collective-permute-start(bf16[16,40,1024]{2,1,0:T(8,128)(2,1)} %get-tuple-element.53), channel_id=1, source_target_pairs={{0,1},{1,0},{2,3},{3,2},{4,5},{5,4},{6,7},{7,6},{8,9},{9,8},{10,11... | collective-permute-start | bytes 3932168 | tf_op jit(solution)/shard_map/ppermute | solution.py:152
  165.7 22.8 %all-to-all-start.5 = ((bf16[16,40,1024]{2,1,0:T(8,128)(2,1)}), bf16[16,40,1024]{2,1,0:T(8,128)(2,1)S(1)}, u32[]{:S(2)}, u32[]{:S(2)}) async-start(bf16[16,40,1024]{2,1,0:T(8,128)(2,1)} %add_convert_fusion), calls=%async_computation.5 | async-start | bytes 2621440 | tf_op jit(solution)/shard_map/all_to_all | solution.py:535
  203.4 9.5 %collective-permute-start.8 = (bf16[4,128,256]{2,1,0:T(8,128)(2,1)}, bf16[4,128,256]{2,1,0:T(8,128)(2,1)S(1)}, u32[]{:S(2)}, u32[]{:S(2)}) collective-permute-start(bf16[4,128,256]{2,1,0:T(8,128)(2,1)} %get-tuple-element.60), channel_id=1, source_target_pairs={{0,128},{128,0},{1,129},{129,1},{2,130},{130,2},{3,131},{131,3},{4... | collective-permute-start | bytes 786440 | tf_op jit(solution)/shard_map/ppermute | solution.py:156
  213.9 35.0 %collective-permute-start.9 = (bf16[2,128,256]{2,1,0:T(8,128)(2,1)S(1)}, bf16[2,128,256]{2,1,0:T(8,128)(2,1)S(1)}, u32[]{:S(2)}, u32[]{:S(2)}) collective-permute-start(bf16[2,128,256]{2,1,0:T(8,128)(2,1)S(1)} %slice.108), channel_id=1, source_target_pairs={{0,4},{2,6},{4,0},{6,2},{1,5},{3,7},{5,1},{7,3},{8,12},{10,14},{12... | collective-permute-start | bytes 393224 | tf_op jit(solution)/shard_map/ppermute | solution.py:549
  219.0 20.7 %all-to-all-start.7 = ((bf16[32,16,128]{2,1,0:T(8,128)(2,1)}), bf16[32,16,128]{2,1,0:T(8,128)(2,1)S(1)}, u32[]{:S(2)}, u32[]{:S(2)}) async-start(bf16[32,16,128]{2,1,0:T(8,128)(2,1)} %finish.1), calls=%async_computation.7 | async-start | bytes 262144 | tf_op jit(solution)/shard_map/all_to_all | solution.py:552
  242.7 18.9 %all-to-all-start.8 = ((f32[256,1,32]{2,1,0:T(1,128)}), f32[256,1,32]{2,1,0:T(1,128)S(1)}, u32[]{:S(2)}, u32[]{:S(2)}) async-start(f32[256,1,32]{2,1,0:T(1,128)} %bitcast.113), calls=%async_computation.8 | async-start | bytes 262144 | tf_op jit(solution)/shard_map/all_to_all | solution.py:555
  249.0 13.5 %collective-permute-start.10 = (bf16[128,256]{1,0:T(8,128)(2,1)S(1)}, bf16[128,256]{1,0:T(8,128)(2,1)S(1)}, u32[]{:S(2)}, u32[]{:S(2)}) collective-permute-start(bf16[128,256]{1,0:T(8,128)(2,1)S(1)} %slice_bitcast_fusion.2), channel_id=1, source_target_pairs={{0,2},{2,0},{4,6},{6,4},{1,3},{3,1},{5,7},{7,5},{8,10},{10,8},{12,... | collective-permute-start | bytes 196616 | tf_op jit(solution)/shard_map/ppermute | solution.py:550
  (10 other events, 36.6 us)
